TPU v7x, 32 devices: a whole 2x2x4 slice. The times are simulated.
32 devices in a mesh: fsdp: 8 (over y, x, core), tensor: 4 (over z).
Axes of the slice: x: 2, y: 2, z: 4, core: 2. Of those that a mesh axis runs over, the one named last changes fastest.
Arguments:
- tokens: bfloat16 [8192, 2048], P(('fsdp', 'tensor')), may hold values from -6 to 6
- segments: int32 [8, 1024], P('fsdp'), may hold values from 0 to 23, never falling along the last dimension, each value on 1 to 256 neighbouring positions
- routes: int32 [8192, 8], P(('fsdp', 'tensor')), may hold values from 0 to 31, all different within a row; in each aligned block of 256 rows (0 to 255, 256 to 511, ...) at most 80 rows name the same one
- adapter_index: int32 [8], replicated, may hold values from 0 to 7
- cotangent: bfloat16 [8192, 2048], P(('fsdp', 'tensor')), may hold values from -6 to 6
- attn_gain: bfloat16 [2048], replicated, may hold values from 0.25 to 1.75
- moe_gain: bfloat16 [2048], replicated, may hold values from 0.25 to 1.75
- q_gain: bfloat16 [128], replicated, may hold values from 0.25 to 1.75
- key_norm_gain: bfloat16 [128], replicated, may hold values from 0.25 to 1.75
- w_query: bfloat16 [2048, 4096], P('fsdp', 'tensor'), may hold values from -0.125 to 0.125
- key_projection_weight: bfloat16 [2048, 512], P('fsdp', 'tensor'), may hold values from -0.125 to 0.125
- value_projection_weight: bfloat16 [2048, 512], P('fsdp', 'tensor'), may hold values from -0.125 to 0.125
- w_out: bfloat16 [4096, 2048], P('tensor', 'fsdp'), may hold values from -0.25 to 0.25
- w_router: bfloat16 [2048, 32], P('fsdp'), may hold values from -0.0625 to 0.0625
- expert_gate_weight: bfloat16 [32, 2048, 768], P(('fsdp', 'tensor')), may hold values from -0.125 to 0.125
- expert_up_weight: bfloat16 [32, 2048, 768], P(('fsdp', 'tensor')), may hold values from -0.125 to 0.125
- expert_down_weight: bfloat16 [32, 768, 2048], P(('fsdp', 'tensor')), may hold values from -1 to 1
- query_in: bfloat16 [8, 2048, 16], replicated, may hold values from -0.125 to 0.125
- query_out: bfloat16 [8, 16, 4096], P(None, None, 'tensor'), may hold values from -0.5 to 0.5
- key_in: bfloat16 [8, 2048, 16], replicated, may hold values from -0.125 to 0.125
- key_second_weight: bfloat16 [8, 16, 512], P(None, None, 'tensor'), may hold values from -0.5 to 0.5
- value_in: bfloat16 [8, 2048, 16], replicated, may hold values from -0.125 to 0.125
- value_second_weight: bfloat16 [8, 16, 512], P(None, None, 'tensor'), may hold values from -0.5 to 0.5
- attn_in: bfloat16 [8, 4096, 16], P(None, 'tensor'), may hold values from -0.09375 to 0.09375
- attn_out: bfloat16 [8, 16, 2048], replicated, may hold values from -1.5 to 1.5
- router_in: bfloat16 [8, 2048, 16], replicated, may hold values from -0.125 to 0.125
- router_out: bfloat16 [8, 16, 32], replicated, may hold values from -0.25 to 0.25
- gate_in: bfloat16 [32, 8, 2048, 16], P(('fsdp', 'tensor')), may hold values from -0.125 to 0.125
- gate_out: bfloat16 [32, 8, 16, 768], P(('fsdp', 'tensor')), may hold values from -0.5 to 0.5
- upward_in: bfloat16 [32, 8, 2048, 16], P(('fsdp', 'tensor')), may hold values from -0.125 to 0.125
- upward_out: bfloat16 [32, 8, 16, 768], P(('fsdp', 'tensor')), may hold values from -0.5 to 0.5
- downward_in: bfloat16 [32, 8, 768, 16], P(('fsdp', 'tensor')), may hold values from -0.21875 to 0.21875
- downward_out: bfloat16 [32, 8, 16, 2048], P(('fsdp', 'tensor')), may hold values from -2.5 to 2.5
Outputs:
- output: bfloat16 [8192, 2048], P(('fsdp', 'tensor'))
- input_grad: float32 [8192, 2048], P(('fsdp', 'tensor'))
- grad_query_in: float32 [8, 2048, 16], P(None, ('fsdp', 'tensor'))
- grad_query_out: float32 [8, 16, 4096], P(None, None, ('fsdp', 'tensor'))
- grad_key_in: float32 [8, 2048, 16], P(None, ('fsdp', 'tensor'))
- grad_key_out: float32 [8, 16, 512], P(None, None, ('fsdp', 'tensor'))
- grad_value_in: float32 [8, 2048, 16], P(None, ('fsdp', 'tensor'))
- grad_value_out: float32 [8, 16, 512], P(None, None, ('fsdp', 'tensor'))
- grad_attn_in: float32 [8, 4096, 16], P(None, ('fsdp', 'tensor'))
- grad_attn_out: float32 [8, 16, 2048], P(None, None, ('fsdp', 'tensor'))
- grad_router_in: float32 [8, 2048, 16], P(None, ('fsdp', 'tensor'))
- grad_router_out: float32 [8, 16, 32], P(None, None, ('fsdp', 'tensor'))
- grad_gate_in: float32 [32, 8, 2048, 16], P(('fsdp', 'tensor'))
- grad_gate_out: float32 [32, 8, 16, 768], P(('fsdp', 'tensor'))
- grad_upward_in: float32 [32, 8, 2048, 16], P(('fsdp', 'tensor'))
- grad_upward_out: float32 [32, 8, 16, 768], P(('fsdp', 'tensor'))
- grad_downward_in: float32 [32, 8, 768, 16], P(('fsdp', 'tensor'))
- grad_downward_out: float32 [32, 8, 16, 2048], P(('fsdp', 'tensor'))
Inputs may be any that keep to these rules, and one draw needn't show every extreme that they name: `routes`: every row names 8 different experts; among the rows of one device no expert is named more than 80 times, a bound that some block reaches. `segments`: along each sequence segment numbers never fall; segment 0 is padding; every segment holds 1 to 256 positions and one holds exactly that many.
All inputs are finite; a program needn't handle non-finite values.
Results may differ from a plain program's by a relative error of at most 0.025.
Values may be sent and summed in bfloat16 or wider, within the bound.
A program may use at most 448 MiB of HBM per device.

v0:
```python
import math

import jax
import jax.numpy as jnp
from jax import lax
from jax.sharding import PartitionSpec as P

NORM_EPSILON = 1e-06
ROPE_THETA = 1000000.0


def matrix_product(first_op, second_op):
    return jnp.dot(first_op, second_op, preferred_element_type=jnp.float32)


def flipped_left_operand(first_op, second_op):
    return lax.dot_general(
        first_op, second_op, (((0,), (0,)), ((), ())), preferred_element_type=jnp.float32
    )


def flipped_right_operand(first_op, second_op):
    return lax.dot_general(
        first_op, second_op, (((1,), (1,)), ((), ())), preferred_element_type=jnp.float32
    )


def norm_forward(values, gain_vec):
    factor = lax.rsqrt(jnp.mean(values * values, axis=-1, keepdims=True) + NORM_EPSILON)
    return (values * factor * gain_vec, factor)


def norm_backward(values, factor, gain_vec, upstream):
    scaled = upstream * gain_vec
    return factor * scaled - values * (factor * factor * factor) * jnp.mean(
        values * scaled, axis=-1, keepdims=True
    )


def rope_tables(sequence_length, head_width):
    half_width = head_width // 2
    inverse = jnp.power(ROPE_THETA, -2.0 * jnp.arange(half_width, dtype=jnp.float32) / head_width)
    angles = jnp.arange(sequence_length, dtype=jnp.float32)[:, None] * inverse[None, :]
    return (jnp.cos(angles)[:, None, :], jnp.sin(angles)[:, None, :])


def rotated_rows(values, cosine_table, sine_table):
    half_width = values.shape[-1] // 2
    leading = values[..., :half_width]
    trailing = values[..., half_width:]
    return jnp.concatenate(
        [
            leading * cosine_table - trailing * sine_table,
            trailing * cosine_table + leading * sine_table,
        ],
        axis=-1,
    )


def unrotated(upstream, cosine_table, sine_table):
    half_width = upstream.shape[-1] // 2
    leading = upstream[..., :half_width]
    trailing = upstream[..., half_width:]
    return jnp.concatenate(
        [
            leading * cosine_table + trailing * sine_table,
            trailing * cosine_table - leading * sine_table,
        ],
        axis=-1,
    )


def route_rows(block_rows):
    return lax.all_to_all(block_rows, ("fsdp", "tensor"), split_axis=0, concat_axis=0, tiled=True)


def per_device(
    tokens,
    segments,
    routes,
    adapter_index,
    cotangent,
    attn_gain,
    moe_gain,
    q_gain,
    key_norm_gain,
    w_query,
    key_projection_weight,
    value_projection_weight,
    w_out,
    w_router,
    expert_gate_weight,
    expert_up_weight,
    expert_down_weight,
    query_in,
    query_out,
    key_in,
    key_second_weight,
    value_in,
    value_second_weight,
    attn_in,
    attn_out,
    router_in,
    router_out,
    gate_in,
    gate_out,
    upward_in,
    upward_out,
    downward_in,
    downward_out,
):
    tensor_count = lax.axis_size("tensor")
    tensor_pos = lax.axis_index("tensor")
    fsdp_pos = lax.axis_index("fsdp")
    zero_pos = fsdp_pos * 0
    tok_rows, model_width = tokens.shape
    seq_rows = tok_rows * tensor_count
    rank_columns = query_in.shape[2]
    adapter_count = query_in.shape[0]
    head_dim = q_gain.shape[0]
    local_cols = query_out.shape[2]
    local_kv_cols = key_second_weight.shape[2]
    local_heads = local_cols // head_dim
    local_groups = local_kv_cols // head_dim
    group_size = local_heads // local_groups
    expert_count = w_router.shape[1]
    top_count = routes.shape[1]
    capacity = 5 * tok_rows * top_count // (4 * expert_count)
    score_scale = 1.0 / math.sqrt(head_dim)
    broad_columns = adapter_count * rank_columns
    adapter_pick = lax.dynamic_index_in_dim(adapter_index, fsdp_pos, 0, keepdims=False)

    def select_adapter(adapter_table):
        return lax.dynamic_index_in_dim(adapter_table, adapter_pick, 0, keepdims=False)

    input_first_factor = jnp.concatenate(
        [select_adapter(query_in), select_adapter(key_in), select_adapter(value_in)], axis=1
    )
    query_second_factor = select_adapter(query_out)
    key_second_factor = select_adapter(key_second_weight)
    value_second_factor = select_adapter(value_second_weight)
    attention_down_factor = select_adapter(attn_in)
    attention_up_factor = select_adapter(attn_out)
    router_first_factor = select_adapter(router_in)
    router_second_factor = select_adapter(router_out)
    gain_attn = attn_gain.astype(jnp.float32)
    gain_moe = moe_gain.astype(jnp.float32)
    gain_query = q_gain.astype(jnp.float32)
    gain_key = key_norm_gain.astype(jnp.float32)
    gathered = (
        lax.all_gather(w_query, "fsdp", axis=0, tiled=True),
        lax.all_gather(key_projection_weight, "fsdp", axis=0, tiled=True),
        lax.all_gather(value_projection_weight, "fsdp", axis=0, tiled=True),
        lax.all_gather(w_out, "fsdp", axis=1, tiled=True),
        lax.all_gather(w_router, "fsdp", axis=0, tiled=True),
    )
    complete_query, complete_key, complete_value, full_out, complete_router = gathered
    token_value_rows = tokens.astype(jnp.float32)
    attn_normed, attn_factor = norm_forward(token_value_rows, gain_attn)
    attention_narrow = attn_normed.astype(jnp.bfloat16)
    input_adapter = matrix_product(attention_narrow, input_first_factor).astype(jnp.bfloat16)
    sequence_normalized, sequence_adapter = (
        lax.all_gather(attention_narrow, "tensor", axis=0, tiled=True),
        lax.all_gather(input_adapter, "tensor", axis=0, tiled=True),
    )
    query_linear = matrix_product(sequence_normalized, complete_query) + matrix_product(
        sequence_adapter[:, :rank_columns], query_second_factor
    )
    key_linear = matrix_product(sequence_normalized, complete_key) + matrix_product(
        sequence_adapter[:, rank_columns : 2 * rank_columns], key_second_factor
    )
    value_narrow = (
        matrix_product(sequence_normalized, complete_value)
        + matrix_product(sequence_adapter[:, 2 * rank_columns :], value_second_factor)
    ).astype(jnp.bfloat16)
    cosine_table, sine_table = rope_tables(seq_rows, head_dim)
    query_heads = query_linear.reshape(seq_rows, local_heads, head_dim)
    query_normed, query_factor = norm_forward(query_heads, gain_query)
    query_narrow = rotated_rows(query_normed, cosine_table, sine_table).astype(jnp.bfloat16)
    key_heads = key_linear.reshape(seq_rows, local_groups, head_dim)
    key_normed, key_factor = norm_forward(key_heads, gain_key)
    key_narrow = rotated_rows(key_normed, cosine_table, sine_table).astype(jnp.bfloat16)
    value_heads = value_narrow.reshape(seq_rows, local_groups, head_dim)
    seg_ids = segments[0]
    block_rows = min(512, seq_rows)
    block_count = seq_rows // block_rows
    key_pos = jnp.arange(seq_rows, dtype=jnp.int32)

    def block_scores(row_start):
        query_pos = row_start + jnp.arange(block_rows, dtype=jnp.int32)
        query_seg = seg_ids[row_start : row_start + block_rows]
        allowed = (key_pos[None, :] == query_pos[:, None]) | (
            key_pos[None, :] < query_pos[:, None]
        ) & (query_seg[:, None] == seg_ids[None, :]) & (seg_ids[None, :] != 0)
        query_block = query_narrow[row_start : row_start + block_rows].reshape(
            block_rows, local_groups, group_size, head_dim
        )
        raw_scores = (
            jnp.einsum(
                "ikgd,jkd->kgij", query_block, key_narrow, preferred_element_type=jnp.float32
            )
            * score_scale
        )
        return (jnp.where(allowed[None, None], raw_scores, -1e30), query_block)

    block_outputs = []
    block_lse = []
    for block_idx in range(block_count):
        row_start = block_idx * block_rows
        masked, query_block = block_scores(row_start)
        row_peak = jnp.max(masked, axis=-1, keepdims=True)
        expo_scores = jnp.exp(masked - row_peak)
        row_total = jnp.sum(expo_scores, axis=-1, keepdims=True)
        probs_low = (expo_scores / row_total).astype(jnp.bfloat16)
        block_lse.append(row_peak + jnp.log(row_total))
        block_outputs.append(
            jnp.einsum(
                "qnzb,bqs->zqns", probs_low, value_heads, preferred_element_type=jnp.float32
            ).reshape(block_rows, local_cols)
        )
    heads_narrow = jnp.concatenate(block_outputs, axis=0).astype(jnp.bfloat16)
    out_part = matrix_product(heads_narrow, full_out)
    attention_adapter_share = matrix_product(heads_narrow, attention_down_factor)
    attention_total, attention_adapter_total = (
        lax.psum_scatter(
            out_part.astype(jnp.bfloat16), "tensor", scatter_dimension=0, tiled=True
        ).astype(jnp.float32),
        lax.psum_scatter(
            attention_adapter_share.astype(jnp.bfloat16), "tensor", scatter_dimension=0, tiled=True
        ).astype(jnp.float32),
    )
    attention_adapter_narrow = attention_adapter_total.astype(jnp.bfloat16)
    residual_stream = (
        token_value_rows
        + attention_total
        + matrix_product(attention_adapter_narrow, attention_up_factor)
    )
    moe_normed, moe_factor = norm_forward(residual_stream, gain_moe)
    experts_narrow = moe_normed.astype(jnp.bfloat16)
    router_adapter = matrix_product(experts_narrow, router_first_factor).astype(jnp.bfloat16)
    router_logits = matrix_product(experts_narrow, complete_router) + matrix_product(
        router_adapter, router_second_factor
    )
    expert_ids = jnp.arange(expert_count, dtype=jnp.int32)
    onehot = (routes[:, :, None] == expert_ids[None, None, :]).astype(jnp.float32)
    chosen = jnp.sum(onehot * router_logits[:, None, :], axis=-1)
    chosen_exp = jnp.exp(chosen - jnp.max(chosen, axis=-1, keepdims=True))
    gate_weights = chosen_exp / jnp.sum(chosen_exp, axis=-1, keepdims=True)
    flat_routes = routes.reshape(-1)
    entries = flat_routes.shape[0]
    flat_onehot = (flat_routes[:, None] == expert_ids[None, :]).astype(jnp.int32)
    slot_rank = jnp.sum(
        (jnp.cumsum(flat_onehot, axis=0, dtype=jnp.int32) - flat_onehot) * flat_onehot,
        axis=1,
        dtype=jnp.int32,
    )
    destination = flat_routes * capacity + slot_rank
    slot_entry = (
        jnp.full((expert_count * capacity,), entries, jnp.int32)
        .at[destination]
        .set(jnp.arange(entries, dtype=jnp.int32))
    )
    slot_token = slot_entry // top_count
    padded_low = jnp.concatenate(
        [experts_narrow, jnp.zeros((1, model_width), jnp.bfloat16)], axis=0
    )
    send_rows = padded_low[slot_token].reshape(expert_count, capacity, model_width)
    expert_input = route_rows(send_rows).reshape(expert_count * capacity, model_width)
    source_seq = jnp.arange(expert_count, dtype=jnp.int32) // tensor_count
    source_adapter = adapter_index[source_seq]
    column_adapter = jnp.arange(broad_columns, dtype=jnp.int32) // rank_columns
    source_mask = (source_adapter[:, None] == column_adapter[None, :]).astype(jnp.float32)
    row_validity_mask = jnp.broadcast_to(
        source_mask[:, None, :], (expert_count, capacity, broad_columns)
    ).reshape(expert_count * capacity, broad_columns)
    paired_mask = jnp.concatenate([row_validity_mask, row_validity_mask], axis=1)

    def flat_down(adapter_table):
        return jnp.transpose(adapter_table[0], (1, 0, 2)).reshape(
            adapter_table.shape[2], broad_columns
        )

    def flat_up(adapter_table):
        return adapter_table[0].reshape(broad_columns, adapter_table.shape[3])

    paired_first_factor = jnp.concatenate([flat_down(gate_in), flat_down(upward_in)], axis=1)
    gate_second_factor = flat_up(gate_out)
    upward_second_factor = flat_up(upward_out)
    down_first_factor = flat_down(downward_in)
    down_second_factor = flat_up(downward_out)
    paired_adapter = (matrix_product(expert_input, paired_first_factor) * paired_mask).astype(
        jnp.bfloat16
    )
    gate_linear = matrix_product(expert_input, expert_gate_weight[0]) + matrix_product(
        paired_adapter[:, :broad_columns], gate_second_factor
    )
    up_linear = matrix_product(expert_input, expert_up_weight[0]) + matrix_product(
        paired_adapter[:, broad_columns:], upward_second_factor
    )
    gate_sig = jax.nn.sigmoid(gate_linear)
    gate_act = gate_linear * gate_sig
    inner_narrow = (gate_act * up_linear).astype(jnp.bfloat16)
    down_adapter = (matrix_product(inner_narrow, down_first_factor) * row_validity_mask).astype(
        jnp.bfloat16
    )
    expert_output = (
        matrix_product(inner_narrow, expert_down_weight[0])
        + matrix_product(down_adapter, down_second_factor)
    ).astype(jnp.bfloat16)
    back_rows = route_rows(expert_output.reshape(expert_count, capacity, model_width)).reshape(
        expert_count * capacity, model_width
    )
    route_out = back_rows[destination].reshape(tok_rows, top_count, model_width)
    final_rows = residual_stream + jnp.sum(gate_weights[:, :, None] * route_out, axis=1)
    output = final_rows.astype(jnp.bfloat16)
    out_grad = cotangent.astype(jnp.float32)
    back_weights = (
        lax.all_gather(w_query, "fsdp", axis=0, tiled=True),
        lax.all_gather(key_projection_weight, "fsdp", axis=0, tiled=True),
        lax.all_gather(value_projection_weight, "fsdp", axis=0, tiled=True),
        lax.all_gather(w_out, "fsdp", axis=1, tiled=True),
        lax.all_gather(w_router, "fsdp", axis=0, tiled=True),
    )
    complete_query, complete_key, complete_value, full_out, complete_router = back_weights
    gate_grad = jnp.sum(out_grad[:, None, :] * route_out, axis=-1)
    route_grad = (
        (gate_weights[:, :, None] * out_grad[:, None, :])
        .astype(jnp.bfloat16)
        .reshape(entries, model_width)
    )
    padded_grad = jnp.concatenate([route_grad, jnp.zeros((1, model_width), jnp.bfloat16)], axis=0)
    grad_send = padded_grad[slot_entry].reshape(expert_count, capacity, model_width)
    expert_gradient = route_rows(grad_send).reshape(expert_count * capacity, model_width)
    down_adapter_gradient = (
        flipped_right_operand(expert_gradient, down_second_factor) * row_validity_mask
    ).astype(jnp.bfloat16)
    inner_grad = flipped_right_operand(
        expert_gradient, expert_down_weight[0]
    ) + flipped_right_operand(down_adapter_gradient, down_first_factor)
    down_first_gradient = flipped_left_operand(inner_narrow, down_adapter_gradient)
    down_second_gradient = flipped_left_operand(down_adapter, expert_gradient)
    gate_linear_gradient = (
        inner_grad * up_linear * (gate_sig * (1.0 + gate_linear * (1.0 - gate_sig)))
    ).astype(jnp.bfloat16)
    up_linear_gradient = (inner_grad * gate_act).astype(jnp.bfloat16)
    pair_grad = (
        jnp.concatenate(
            [
                flipped_right_operand(gate_linear_gradient, gate_second_factor),
                flipped_right_operand(up_linear_gradient, upward_second_factor),
            ],
            axis=1,
        )
        * paired_mask
    ).astype(jnp.bfloat16)
    rows_grad = (
        flipped_right_operand(gate_linear_gradient, expert_gate_weight[0])
        + flipped_right_operand(up_linear_gradient, expert_up_weight[0])
        + flipped_right_operand(pair_grad, paired_first_factor)
    )
    grad_pair_down = flipped_left_operand(expert_input, pair_grad)
    gate_second_gradient = flipped_left_operand(
        paired_adapter[:, :broad_columns], gate_linear_gradient
    )
    upward_second_gradient = flipped_left_operand(
        paired_adapter[:, broad_columns:], up_linear_gradient
    )
    back_grad = route_rows(
        rows_grad.astype(jnp.bfloat16).reshape(expert_count, capacity, model_width)
    ).reshape(expert_count * capacity, model_width)
    moe_grad = jnp.sum(
        back_grad[destination].reshape(tok_rows, top_count, model_width), axis=1, dtype=jnp.float32
    )
    chosen_grad = gate_weights * (
        gate_grad - jnp.sum(gate_weights * gate_grad, axis=-1, keepdims=True)
    )
    logit_gradient = jnp.sum(onehot * chosen_grad[:, :, None], axis=1).astype(jnp.bfloat16)
    router_adapter_gradient = flipped_right_operand(logit_gradient, router_second_factor).astype(
        jnp.bfloat16
    )
    moe_grad = (
        moe_grad
        + flipped_right_operand(logit_gradient, complete_router)
        + flipped_right_operand(router_adapter_gradient, router_first_factor)
    )
    router_first_gradient = flipped_left_operand(experts_narrow, router_adapter_gradient)
    router_second_gradient = flipped_left_operand(router_adapter, logit_gradient)
    residual_grad = out_grad + norm_backward(residual_stream, moe_factor, gain_moe, moe_grad)
    branch_gradient = residual_grad.astype(jnp.bfloat16)
    attention_adapter_grad = flipped_right_operand(branch_gradient, attention_up_factor).astype(
        jnp.bfloat16
    )
    attention_up_gradient = flipped_left_operand(attention_adapter_narrow, branch_gradient)
    sequence_branch_gradient, sequence_attention_adapter_grad = (
        lax.all_gather(branch_gradient, "tensor", axis=0, tiled=True),
        lax.all_gather(attention_adapter_grad, "tensor", axis=0, tiled=True),
    )
    heads_grad = (
        flipped_right_operand(sequence_branch_gradient, full_out)
        + flipped_right_operand(sequence_attention_adapter_grad, attention_down_factor)
    ).astype(jnp.bfloat16)
    attention_down_gradient = flipped_left_operand(heads_narrow, sequence_attention_adapter_grad)
    heads_grad_view = heads_grad.reshape(seq_rows, local_groups, group_size, head_dim)
    value_grad = jnp.zeros((seq_rows, local_groups, head_dim), jnp.float32)
    key_grad = jnp.zeros((seq_rows, local_groups, head_dim), jnp.float32)
    query_grads = []
    for block_idx in range(block_count):
        row_start = block_idx * block_rows
        masked, query_block = block_scores(row_start)
        block_probs = jnp.exp(masked - block_lse[block_idx])
        probs_low = block_probs.astype(jnp.bfloat16)
        grad_block = heads_grad_view[row_start : row_start + block_rows]
        prob_grad = jnp.einsum(
            "ikgd,jkd->kgij", grad_block, value_heads, preferred_element_type=jnp.float32
        )
        score_grad = (
            block_probs * (prob_grad - jnp.sum(block_probs * prob_grad, axis=-1, keepdims=True))
        ).astype(jnp.bfloat16)
        value_grad = value_grad + jnp.einsum(
            "kgij,ikgd->jkd", probs_low, grad_block, preferred_element_type=jnp.float32
        )
        key_grad = (
            key_grad
            + jnp.einsum(
                "kgij,ikgd->jkd", score_grad, query_block, preferred_element_type=jnp.float32
            )
            * score_scale
        )
        query_grads.append(
            jnp.einsum(
                "qnzb,bqs->zqns", score_grad, key_narrow, preferred_element_type=jnp.float32
            ).reshape(block_rows, local_heads, head_dim)
            * score_scale
        )
    query_grad = jnp.concatenate(query_grads, axis=0)
    query_linear_gradient = (
        norm_backward(
            query_heads, query_factor, gain_query, unrotated(query_grad, cosine_table, sine_table)
        )
        .reshape(seq_rows, local_cols)
        .astype(jnp.bfloat16)
    )
    key_linear_gradient = (
        norm_backward(
            key_heads, key_factor, gain_key, unrotated(key_grad, cosine_table, sine_table)
        )
        .reshape(seq_rows, local_kv_cols)
        .astype(jnp.bfloat16)
    )
    value_linear_gradient = value_grad.reshape(seq_rows, local_kv_cols).astype(jnp.bfloat16)
    normed_part = (
        flipped_right_operand(query_linear_gradient, complete_query)
        + flipped_right_operand(key_linear_gradient, complete_key)
        + flipped_right_operand(value_linear_gradient, complete_value)
    )
    adapter_share = jnp.concatenate(
        [
            flipped_right_operand(query_linear_gradient, query_second_factor),
            flipped_right_operand(key_linear_gradient, key_second_factor),
            flipped_right_operand(value_linear_gradient, value_second_factor),
        ],
        axis=1,
    )
    query_second_gradient = flipped_left_operand(
        sequence_adapter[:, :rank_columns], query_linear_gradient
    )
    key_second_gradient = flipped_left_operand(
        sequence_adapter[:, rank_columns : 2 * rank_columns], key_linear_gradient
    )
    value_second_gradient = flipped_left_operand(
        sequence_adapter[:, 2 * rank_columns :], value_linear_gradient
    )
    normalized_gradient, input_adapter_gradient = (
        lax.psum_scatter(
            normed_part.astype(jnp.bfloat16), "tensor", scatter_dimension=0, tiled=True
        ).astype(jnp.float32),
        lax.psum_scatter(
            adapter_share.astype(jnp.bfloat16), "tensor", scatter_dimension=0, tiled=True
        ).astype(jnp.float32),
    )
    input_adapter_narrow = input_adapter_gradient.astype(jnp.bfloat16)
    normalized_gradient = normalized_gradient + flipped_right_operand(
        input_adapter_narrow, input_first_factor
    )
    input_first_gradient = flipped_left_operand(attention_narrow, input_adapter_narrow)
    input_grad = residual_grad + norm_backward(
        token_value_rows, attn_factor, gain_attn, normalized_gradient
    )
    all_cols = local_cols * tensor_count
    all_kv_cols = local_kv_cols * tensor_count

    def placed(full_shape, addend, offsets):
        holder = jnp.zeros(full_shape, jnp.float32)
        return lax.dynamic_update_slice(holder, addend[None], (adapter_pick,) + offsets)

    summed = (
        lax.psum_scatter(
            placed(
                (adapter_count, model_width, rank_columns),
                input_first_gradient[:, :rank_columns],
                (zero_pos, zero_pos),
            ),
            ("fsdp", "tensor"),
            scatter_dimension=1,
            tiled=True,
        ),
        lax.psum_scatter(
            placed(
                (adapter_count, rank_columns, all_cols),
                query_second_gradient,
                (zero_pos, tensor_pos * local_cols),
            ),
            ("fsdp", "tensor"),
            scatter_dimension=2,
            tiled=True,
        ),
        lax.psum_scatter(
            placed(
                (adapter_count, model_width, rank_columns),
                input_first_gradient[:, rank_columns : 2 * rank_columns],
                (zero_pos, zero_pos),
            ),
            ("fsdp", "tensor"),
            scatter_dimension=1,
            tiled=True,
        ),
        lax.psum_scatter(
            placed(
                (adapter_count, rank_columns, all_kv_cols),
                key_second_gradient,
                (zero_pos, tensor_pos * local_kv_cols),
            ),
            ("fsdp", "tensor"),
            scatter_dimension=2,
            tiled=True,
        ),
        lax.psum_scatter(
            placed(
                (adapter_count, model_width, rank_columns),
                input_first_gradient[:, 2 * rank_columns :],
                (zero_pos, zero_pos),
            ),
            ("fsdp", "tensor"),
            scatter_dimension=1,
            tiled=True,
        ),
        lax.psum_scatter(
            placed(
                (adapter_count, rank_columns, all_kv_cols),
                value_second_gradient,
                (zero_pos, tensor_pos * local_kv_cols),
            ),
            ("fsdp", "tensor"),
            scatter_dimension=2,
            tiled=True,
        ),
        lax.psum_scatter(
            placed(
                (adapter_count, all_cols, rank_columns),
                attention_down_gradient,
                (tensor_pos * local_cols, zero_pos),
            ),
            ("fsdp", "tensor"),
            scatter_dimension=1,
            tiled=True,
        ),
        lax.psum_scatter(
            placed(
                (adapter_count, rank_columns, model_width),
                attention_up_gradient,
                (zero_pos, zero_pos),
            ),
            ("fsdp", "tensor"),
            scatter_dimension=2,
            tiled=True,
        ),
        lax.psum_scatter(
            placed(
                (adapter_count, model_width, rank_columns),
                router_first_gradient,
                (zero_pos, zero_pos),
            ),
            ("fsdp", "tensor"),
            scatter_dimension=1,
            tiled=True,
        ),
        lax.psum_scatter(
            placed(
                (adapter_count, rank_columns, expert_count),
                router_second_gradient,
                (zero_pos, zero_pos),
            ),
            ("fsdp", "tensor"),
            scatter_dimension=2,
            tiled=True,
        ),
    )
    grad_gate_in = jnp.transpose(
        grad_pair_down[:, :broad_columns].reshape(model_width, adapter_count, rank_columns),
        (1, 0, 2),
    )[None]
    grad_upward_in = jnp.transpose(
        grad_pair_down[:, broad_columns:].reshape(model_width, adapter_count, rank_columns),
        (1, 0, 2),
    )[None]
    grad_gate_out = gate_second_gradient.reshape(
        adapter_count, rank_columns, gate_second_factor.shape[1]
    )[None]
    grad_upward_out = upward_second_gradient.reshape(
        adapter_count, rank_columns, upward_second_factor.shape[1]
    )[None]
    grad_downward_in = jnp.transpose(
        down_first_gradient.reshape(down_first_factor.shape[0], adapter_count, rank_columns),
        (1, 0, 2),
    )[None]
    grad_downward_out = down_second_gradient.reshape(adapter_count, rank_columns, model_width)[None]
    return (
        output,
        input_grad,
        summed[0],
        summed[1],
        summed[2],
        summed[3],
        summed[4],
        summed[5],
        summed[6],
        summed[7],
        summed[8],
        summed[9],
        grad_gate_in,
        grad_gate_out,
        grad_upward_in,
        grad_upward_out,
        grad_downward_in,
        grad_downward_out,
    )


def solution(mesh):
    placed = (
        P(("fsdp", "tensor"), None),
        P("fsdp", None),
        P(("fsdp", "tensor"), None),
        P(),
        P(("fsdp", "tensor"), None),
        P(),
        P(),
        P(),
        P(),
        P("fsdp", "tensor"),
        P("fsdp", "tensor"),
        P("fsdp", "tensor"),
        P("tensor", "fsdp"),
        P("fsdp", None),
        P(("fsdp", "tensor"), None, None),
        P(("fsdp", "tensor"), None, None),
        P(("fsdp", "tensor"), None, None),
        P(),
        P(None, None, "tensor"),
        P(),
        P(None, None, "tensor"),
        P(),
        P(None, None, "tensor"),
        P(None, "tensor", None),
        P(),
        P(),
        P(),
        P(("fsdp", "tensor"), None, None, None),
        P(("fsdp", "tensor"), None, None, None),
        P(("fsdp", "tensor"), None, None, None),
        P(("fsdp", "tensor"), None, None, None),
        P(("fsdp", "tensor"), None, None, None),
        P(("fsdp", "tensor"), None, None, None),
    )
    return jax.shard_map(
        per_device,
        mesh=mesh,
        in_specs=placed,
        out_specs=(
            P(("fsdp", "tensor"), None),
            P(("fsdp", "tensor"), None),
            P(None, ("fsdp", "tensor"), None),
            P(None, None, ("fsdp", "tensor")),
            P(None, ("fsdp", "tensor"), None),
            P(None, None, ("fsdp", "tensor")),
            P(None, ("fsdp", "tensor"), None),
            P(None, None, ("fsdp", "tensor")),
            P(None, ("fsdp", "tensor"), None),
            P(None, None, ("fsdp", "tensor")),
            P(None, ("fsdp", "tensor"), None),
            P(None, None, ("fsdp", "tensor")),
            P(("fsdp", "tensor"), None, None, None),
            P(("fsdp", "tensor"), None, None, None),
            P(("fsdp", "tensor"), None, None, None),
            P(("fsdp", "tensor"), None, None, None),
            P(("fsdp", "tensor"), None, None, None),
            P(("fsdp", "tensor"), None, None, None),
        ),
        check_vma=False,
    )
```

profile of v0, /device:TPU:16, one launch (start us, length us, event | category | flops | bytes accessed | tf_op | source)
XLA Modules:
  0.0 2920.8 jit_solution(14198556197839117842)
XLA Ops:
  17.0 10.9 all_gather.35
  27.9 10.7 all_gather.33
  42.8 14.5 all_gather.34
  66.1 29.4 %all-gather.5.cloned.1.call-done = bf16[1024,2048]{1,0:T(8,128)(2,1)} async-done(((bf16[256,2048]{1,0:T(8,128)(2,1)}), bf16[1024,2048]{1,0:T(8,128)(2,1)}) %all-gather.5.cloned.1.call-update) | async-done | bytes 4194320 | tf_op jit(solution)/shard_map/all_gather | solution.py:163
  104.0 30.1 %all-gather.7.cloned.1.call-done = bf16[2048,1024]{1,0:T(8,128)(2,1)} async-done(((bf16[256,1024]{1,0:T(8,128)(2,1)}), bf16[2048,1024]{1,0:T(8,128)(2,1)}) %all-gather.7.cloned.1.call-update) | async-done | bytes 4194320 | tf_op jit(solution)/shard_map/all_gather | solution.py:151
  157.9 8.2 fusion.184
  181.9 8.1 fusion.9
  208.7 9.5 convolution_convert_fusion
  220.3 15.9 reduce-window.6
  238.8 8.1 scatter_custom_fusion
  246.9 58.4 %reduce-scatter.28.cloned.1.call-done = bf16[256,2048]{1,0:T(8,128)(2,1)} async-done(((bf16[1024,2048]{1,0:T(8,128)(2,1)}), bf16[256,2048]{1,0:T(8,128)(2,1)}) %reduce-scatter.28.cloned.1.call-update) | async-done | bytes 1048592 | tf_op jit(solution)/shard_map/reduce_scatter | solution.py:225
  311.2 21.5 gather_fusion
  340.7 53.7 %all_gather.38 = bf16[2048,32]{0,1:T(8,128)(2,1)S(1)} all-gather(bf16[256,32]{0,1:T(8,128)(2,1)S(1)} %copy-done.124), channel_id=1, replica_groups=mesh['fsdp'=8,'tensor'=4] {'fsdp'}, dimensions={0}, use_global_device_ids=true | all-gather | bytes 147456 | tf_op jit(solution)/shard_map/all_gather | solution.py:155
  404.8 8.4 concatenate.69
  413.2 24.7 gather_fusion.3
  437.8 130.5 %all-to-all-done = bf16[32,80,2048]{2,1,0:T(8,128)(2,1)} async-done(((bf16[32,80,2048]{2,1,0:T(8,128)(2,1)}), bf16[32,80,2048]{2,1,0:T(8,128)(2,1)}, u32[]{:S(2)}, u32[]{:S(2)}) %all-to-all-start) | async-done | bytes 10485792 | tf_op jit(solution)/shard_map/all_to_all | solution.py:74
  575.2 13.9 fusion.40
  589.1 13.0 fusion.44
  602.1 202.7 %all-to-all-done.2 = bf16[32,80,2048]{2,1,0:T(8,128)(2,1)} async-done(((bf16[32,80,2048]{2,1,0:T(8,128)(2,1)}), bf16[32,80,2048]{2,1,0:T(8,128)(2,1)}, u32[]{:S(2)}, u32[]{:S(2)}) %all-to-all-start.2) | async-done | bytes 10485792 | tf_op jit(solution)/shard_map/all_to_all | solution.py:74
  804.8 14.2 fusion.34
  844.8 11.6 multiply_convert_fusion
  857.5 11.9 fusion.42
  871.3 11.7 fusion.38
  883.0 18.7 add_convert_fusion
  911.4 11.6 fusion.36
  923.0 11.9 add_convert_fusion.1
  934.9 202.8 %all-to-all-done.3 = bf16[32,80,2048]{2,1,0:T(8,128)(2,1)} async-done(((bf16[32,80,2048]{2,1,0:T(8,128)(2,1)}), bf16[32,80,2048]{2,1,0:T(8,128)(2,1)}, u32[]{:S(2)}, u32[]{:S(2)}) %all-to-all-start.3) | async-done | bytes 10485792 | tf_op jit(solution)/shard_map/all_to_all | solution.py:74
  1143.7 21.6 gather_fusion.4
  1165.3 11.3 convert_reduce_fusion
  1176.6 197.2 %all-to-all-done.1 = bf16[32,80,2048]{2,1,0:T(8,128)(2,1)} async-done(((bf16[32,80,2048]{2,1,0:T(8,128)(2,1)}), bf16[32,80,2048]{2,1,0:T(8,128)(2,1)}, u32[]{:S(2)}, u32[]{:S(2)}) %all-to-all-start.1) | async-done | bytes 10485792 | tf_op jit(solution)/shard_map/all_to_all | solution.py:74
  1373.8 21.8 gather_fusion.2
  1395.7 9.6 fusion.1
  1415.5 11.3 all_gather.40
  1426.9 66.5 %all-gather.11.cloned.1.call-done = bf16[1024,2048]{1,0:T(8,128)(2,1)} async-done(((bf16[256,2048]{1,0:T(8,128)(2,1)}), bf16[1024,2048]{1,0:T(8,128)(2,1)}) %all-gather.11.cloned.1.call-update) | async-done | bytes 4194320 | tf_op jit(solution)/shard_map/all_gather | solution.py:395
  1510.8 16.2 fusion.20
  1533.9 8.1 multiply_bitcast_fusion
  1552.4 8.7 fusion.88
  1562.7 10.9 fusion.19
  1726.9 41.0 %all-reduce.2 = f32[8,16,32]{1,0,2:T(8,128)S(1)} all-reduce(f32[8,16,32]{1,0,2:T(8,128)S(1)} %dynamic_update_slice.39), channel_id=15, replica_groups=mesh['fsdp'=8,'tensor'=4] {'fsdp','tensor'}, use_global_device_ids=true, to_apply=%region_39.40.clone | all-reduce | flops 4096 | bytes 32768
  1770.1 121.0 %reduce-scatter.52.cloned.1.call-done = f32[64,128]{1,0:T(8,128)} async-done(((f32[2048,128]{1,0:T(8,128)}), f32[64,128]{1,0:T(8,128)}) %reduce-scatter.52.cloned.1.call-update) | async-done | bytes 32784
  1892.7 130.6 %reduce-scatter.48.cloned.1.call-done = f32[16,128]{1,0:T(8,128)} async-done(((f32[512,128]{1,0:T(8,128)}), f32[16,128]{1,0:T(8,128)}) %reduce-scatter.48.cloned.1.call-update) | async-done | bytes 8208
  2024.8 130.5 %reduce-scatter.44.cloned.1.call-done = f32[16,128]{1,0:T(8,128)} async-done(((f32[512,128]{1,0:T(8,128)}), f32[16,128]{1,0:T(8,128)}) %reduce-scatter.44.cloned.1.call-update) | async-done | bytes 8208
  2156.8 132.3 %reduce-scatter.40.cloned.1.call-done = f32[64,128]{1,0:T(8,128)} async-done(((f32[2048,128]{1,0:T(8,128)}), f32[64,128]{1,0:T(8,128)}) %reduce-scatter.40.cloned.1.call-update) | async-done | bytes 32784
  2290.8 132.7 %reduce-scatter.42.cloned.1.call-done = f32[64,128]{1,0:T(8,128)} async-done(((f32[2048,128]{1,0:T(8,128)}), f32[64,128]{1,0:T(8,128)}) %reduce-scatter.42.cloned.1.call-update) | async-done | bytes 32784
  2425.2 132.4 %reduce-scatter.46.cloned.1.call-done = f32[64,128]{1,0:T(8,128)} async-done(((f32[2048,128]{1,0:T(8,128)}), f32[64,128]{1,0:T(8,128)}) %reduce-scatter.46.cloned.1.call-update) | async-done | bytes 32784
  2559.2 78.1 %reduce-scatter.32.cloned.1.call-done = bf16[256,2048]{1,0:T(8,128)(2,1)} async-done(((bf16[1024,2048]{1,0:T(8,128)(2,1)}), bf16[256,2048]{1,0:T(8,128)(2,1)}) %reduce-scatter.32.cloned.1.call-update) | async-done | bytes 1048592 | tf_op jit(solution)/shard_map/reduce_scatter | solution.py:474
  2643.5 131.2 %reduce-scatter.38.cloned.1.call-done = f32[8,128,16]{1,2,0:T(8,128)} async-done(((f32[8,4096,16]{1,2,0:T(8,128)}), f32[8,128,16]{1,2,0:T(8,128)}) %reduce-scatter.38.cloned.1.call-update) | async-done | bytes 65552 | tf_op jit(solution)/shard_map/reduce_scatter | solution.py:557
  2774.7 139.3 %reduce-scatter.36.cloned.1.call-done = f32[8,16,128]{2,1,0:T(8,128)} async-done(((f32[8,16,4096]{2,1,0:T(8,128)}), f32[8,16,128]{2,1,0:T(8,128)}) %reduce-scatter.36.cloned.1.call-update) | async-done | bytes 65552 | tf_op jit(solution)/shard_map/reduce_scatter | solution.py:507
  (542 shorter events, 383.7 us)
Async XLA Ops:
  7.2 581.9 %copy-start = (bf16[1,2048,768]{2,1,0:T(8,128)(2,1)S(1)}, bf16[1,2048,768]{2,1,0:T(8,128)(2,1)}, u32[]{:S(2)}) copy-start(bf16[1,2048,768]{2,1,0:T(8,128)(2,1)} %param.47) | copy-start | bytes 9437188
  7.3 88.2 %all-gather.5.cloned.1.call-start = ((), (), s32[]{:S(2)}) async-start(), calls=%async_computation.17 | async-start | bytes 5242880 | tf_op jit(solution)/shard_map/all_gather | solution.py:163
  13.4 120.7 %all-gather.7.cloned.1.call-start = ((), (), s32[]{:S(2)}) async-start(), calls=%async_computation.18 | async-start | bytes 4718592 | tf_op jit(solution)/shard_map/all_gather | solution.py:151
  14.1 194.6 %all-gather.9.cloned.1.call-start = ((), (), s32[]{:S(2)}) async-start(), calls=%async_computation.19 | async-start | bytes 4718592 | tf_op jit(solution)/shard_map/all_gather | solution.py:154
  14.9 232.0 %reduce-scatter.30.cloned.1.call-start = ((), (), s32[]{:S(2)}) async-start(), calls=%async_computation.21 | async-start | bytes 40960 | tf_op jit(solution)/shard_map/reduce_scatter | solution.py:228
  16.8 83.7 %copy-start.134 = (f32[64]{0:T(128)}, f32[64]{0:T(128)S(1)}, u32[]{:S(2)}) copy-start(f32[64]{0:T(128)S(1)} %multiply_power_fusion) | copy-start | bytes 772
  16.9 134.2 %copy-start.129 = (f32[128]{0:T(128)}, f32[128]{0:T(128)S(1)}, u32[]{:S(2)}) copy-start(f32[128]{0:T(128)S(1)} %convert_element_type.190) | copy-start | bytes 1540
  16.9 83.3 %copy-start.132 = (f32[128]{0:T(128)}, f32[128]{0:T(128)S(1)}, u32[]{:S(2)}) copy-start(f32[128]{0:T(128)S(1)} %convert_element_type.189) | copy-start | bytes 1540
  57.3 84.5 %copy-start.71 = (bf16[1024,48]{0,1:T(8,128)(2,1)}, bf16[1024,48]{0,1:T(8,128)(2,1)S(1)}, u32[]{:S(2)}) copy-start(bf16[1024,48]{0,1:T(8,128)(2,1)S(1)} %all_gather.34) | copy-start | bytes 294916
  102.0 64.0 %copy-start.52 = (bf16[1024,64]{0,1:T(8,128)(2,1)}, bf16[1024,64]{0,1:T(8,128)(2,1)S(1)}, u32[]{:S(2)}) copy-start(bf16[1024,64]{0,1:T(8,128)(2,1)S(1)} %get-tuple-element.92) | copy-start | bytes 393220
  102.1 64.0 %copy-start.54 = (bf16[1024,64]{0,1:T(8,128)(2,1)}, bf16[1024,64]{0,1:T(8,128)(2,1)S(1)}, u32[]{:S(2)}) copy-start(bf16[1024,64]{0,1:T(8,128)(2,1)S(1)} %get-tuple-element.93) | copy-start | bytes 393220
  166.1 31.6 %copy-start.90 = (f32[8,512]{1,0:T(8,128)}, f32[8,512]{1,0:T(8,128)S(1)}, u32[]{:S(2)}) copy-start(f32[8,512]{1,0:T(8,128)S(1)} %get-tuple-element.116) | copy-start | bytes 49156
  208.5 96.9 %reduce-scatter.28.cloned.1.call-start = ((), (), s32[]{:S(2)}) async-start(), calls=%async_computation.20 | async-start | bytes 5242880 | tf_op jit(solution)/shard_map/reduce_scatter | solution.py:225
  219.3 89.8 %copy-start.103 = (f32[2048]{0:T(1024)}, f32[2048]{0:T(1024)S(1)}, u32[]{:S(2)}) copy-start(f32[2048]{0:T(1024)S(1)} %convert_element_type.196) | copy-start | bytes 24580
  238.8 72.5 %copy-start.117 = (s32[2048,1]{0,1:T(1,128)}, s32[2048,1]{0,1:T(1,128)S(1)}, u32[]{:S(2)}) copy-start(s32[2048,1]{0,1:T(1,128)S(1)} %compare_select_fusion) | copy-start | bytes 24580
  308.2 24.6 copy-start.127
  332.8 235.5 %all-to-all-start = ((bf16[32,80,2048]{2,1,0:T(8,128)(2,1)}), bf16[32,80,2048]{2,1,0:T(8,128)(2,1)}, u32[]{:S(2)}, u32[]{:S(2)}) async-start(bf16[32,80,2048]{2,1,0:T(8,128)(2,1)} %bitcast.462), calls=%async_computation.2 | async-start | bytes 20971520 | tf_op jit(solution)/shard_map/all_to_all | solution.py:74
  337.7 58.3 %copy-start.16 = (bf16[256,2048]{1,0:T(8,128)(2,1)S(1)}, bf16[256,2048]{1,0:T(8,128)(2,1)}, u32[]{:S(2)}) copy-start(bf16[256,2048]{1,0:T(8,128)(2,1)} %copy-done.15) | copy-start | bytes 3145732
  568.3 236.5 %all-to-all-start.2 = ((bf16[32,80,2048]{2,1,0:T(8,128)(2,1)}), bf16[32,80,2048]{2,1,0:T(8,128)(2,1)}, u32[]{:S(2)}, u32[]{:S(2)}) async-start(bf16[32,80,2048]{2,1,0:T(8,128)(2,1)} %bitcast.463), calls=%async_computation.4 | async-start | bytes 20971520 | tf_op jit(solution)/shard_map/all_to_all | solution.py:74
  819.0 64.0 %copy-start.12 = (f32[32,80,128]{2,1,0:T(8,128)}, f32[32,80,128]{2,1,0:T(8,128)S(1)}, u32[]{:S(2)}) copy-start(f32[32,80,128]{2,1,0:T(8,128)S(1)} %broadcast_in_dim.73) | copy-start | bytes 3932164
  857.5 25.5 copy-start.36
  901.7 236.1 %all-to-all-start.3 = ((bf16[32,80,2048]{2,1,0:T(8,128)(2,1)}), bf16[32,80,2048]{2,1,0:T(8,128)(2,1)}, u32[]{:S(2)}, u32[]{:S(2)}) async-start(bf16[32,80,2048]{2,1,0:T(8,128)(2,1)} %bitcast.461), calls=%async_computation.5 | async-start | bytes 20971520 | tf_op jit(solution)/shard_map/all_to_all | solution.py:74
  1137.8 236.1 %all-to-all-start.1 = ((bf16[32,80,2048]{2,1,0:T(8,128)(2,1)}), bf16[32,80,2048]{2,1,0:T(8,128)(2,1)}, u32[]{:S(2)}, u32[]{:S(2)}) async-start(bf16[32,80,2048]{2,1,0:T(8,128)(2,1)} %bitcast.464), calls=%async_computation.3 | async-start | bytes 20971520 | tf_op jit(solution)/shard_map/all_to_all | solution.py:74
  1143.2 350.1 %all-gather.11.cloned.1.call-start = ((), (), s32[]{:S(2)}) async-start(), calls=%async_computation.22 | async-start | bytes 5242880 | tf_op jit(solution)/shard_map/all_gather | solution.py:395
  1413.2 233.6 %reduce-scatter.34.cloned.1.call-start = ((), (), s32[]{:S(2)}) async-start(), calls=%async_computation.24 | async-start | bytes 122880 | tf_op jit(solution)/shard_map/reduce_scatter | solution.py:477
  1426.9 74.2 %copy-start.95 = (bf16[1024,16]{0,1:T(8,128)(2,1)}, bf16[1024,16]{0,1:T(8,128)(2,1)S(1)}, u32[]{:S(2)}) copy-start(bf16[1024,16]{0,1:T(8,128)(2,1)S(1)} %all_gather.40) | copy-start | bytes 98308
  1510.8 31.2 %slice-start = ((s8[16777216]{0:T(1024)(128)(4,1)}), s8[4194304]{0:T(1024)(128)(4,1)S(1)}, s32[]{:S(2)}) async-start(s8[16777216]{0:T(1024)(128)(4,1)} %bitcast.457), calls=%async_computation.34 | async-start | bytes 8388608
  1510.8 31.2 %slice-start.1 = ((s8[16777216]{0:T(1024)(128)(4,1)}), s8[4194304]{0:T(1024)(128)(4,1)S(1)}, s32[]{:S(2)}) async-start(s8[16777216]{0:T(1024)(128)(4,1)} %bitcast.457), calls=%async_computation.35 | async-start | bytes 8388608
  1510.8 31.2 %slice-start.2 = ((s8[16777216]{0:T(1024)(128)(4,1)}), s8[4194304]{0:T(1024)(128)(4,1)S(1)}, s32[]{:S(2)}) async-start(s8[16777216]{0:T(1024)(128)(4,1)} %bitcast.457), calls=%async_computation.36 | async-start | bytes 8388608
  1603.1 82.9 %copy-start.20 = (bf16[1024,1024]{0,1:T(8,128)(2,1)}, bf16[1024,1024]{0,1:T(8,128)(2,1)S(1)}, u32[]{:S(2)}) copy-start(bf16[1024,1024]{0,1:T(8,128)(2,1)S(1)} %fusion.29) | copy-start | bytes 6291460
  1605.0 163.4 %reduce-scatter.50.cloned.1.call-start = ((), (), s32[]{:S(2)}) async-start(), calls=%async_computation.32 | async-start | bytes 1081344
  1619.7 271.3 %reduce-scatter.52.cloned.1.call-start = ((), (), s32[]{:S(2)}) async-start(), calls=%async_computation.33 | async-start | bytes 1081344
  1634.4 388.9 %reduce-scatter.48.cloned.1.call-start = ((), (), s32[]{:S(2)}) async-start(), calls=%async_computation.31 | async-start | bytes 270336
  1639.5 515.8 %reduce-scatter.44.cloned.1.call-start = ((), (), s32[]{:S(2)}) async-start(), calls=%async_computation.29 | async-start | bytes 270336
  1646.7 642.4 %reduce-scatter.40.cloned.1.call-start = ((), (), s32[]{:S(2)}) async-start(), calls=%async_computation.27 | async-start | bytes 1081344
  1659.8 763.7 %reduce-scatter.42.cloned.1.call-start = ((), (), s32[]{:S(2)}) async-start(), calls=%async_computation.28 | async-start | bytes 1081344
  1672.1 885.5 %reduce-scatter.46.cloned.1.call-start = ((), (), s32[]{:S(2)}) async-start(), calls=%async_computation.30 | async-start | bytes 1081344
  1684.4 952.9 %reduce-scatter.32.cloned.1.call-start = ((), (), s32[]{:S(2)}) async-start(), calls=%async_computation.23 | async-start | bytes 5242880 | tf_op jit(solution)/shard_map/reduce_scatter | solution.py:474
  1694.8 1079.9 %reduce-scatter.38.cloned.1.call-start = ((), (), s32[]{:S(2)}) async-start(), calls=%async_computation.26 | async-start | bytes 2162688 | tf_op jit(solution)/shard_map/reduce_scatter | solution.py:557
  1699.1 1214.9 %reduce-scatter.36.cloned.1.call-start = ((), (), s32[]{:S(2)}) async-start(), calls=%async_computation.25 | async-start | bytes 2162688 | tf_op jit(solution)/shard_map/reduce_scatter | solution.py:507
  1720.0 917.3 %copy-start.82 = (bf16[2048,16]{0,1:T(8,128)(2,1)S(1)}, bf16[2048,16]{0,1:T(8,128)(2,1)}, u32[]{:S(2)}) copy-start(bf16[2048,16]{0,1:T(8,128)(2,1)} %copy-done.81) | copy-start | bytes 196612
  1720.0 917.3 %copy-start.84 = (bf16[2048,16]{0,1:T(8,128)(2,1)S(1)}, bf16[2048,16]{0,1:T(8,128)(2,1)}, u32[]{:S(2)}) copy-start(bf16[2048,16]{0,1:T(8,128)(2,1)} %copy-done.83) | copy-start | bytes 196612
  1720.0 917.3 %copy-start.86 = (bf16[2048,16]{0,1:T(8,128)(2,1)S(1)}, bf16[2048,16]{0,1:T(8,128)(2,1)}, u32[]{:S(2)}) copy-start(bf16[2048,16]{0,1:T(8,128)(2,1)} %copy-done.85) | copy-start | bytes 196612
  1720.0 917.3 %copy-start.100 = (bf16[256,48]{0,1:T(8,128)(2,1)S(1)}, bf16[256,48]{0,1:T(8,128)(2,1)}, u32[]{:S(2)}) copy-start(bf16[256,48]{0,1:T(8,128)(2,1)} %reduce-scatter.34.cloned.1.call-done) | copy-start | bytes 73732
  1720.0 917.3 %copy-start.102 = (f32[2048]{0:T(1024)S(1)}, f32[2048]{0:T(1024)}, u32[]{:S(2)}) copy-start(f32[2048]{0:T(1024)} %copy-done.101) | copy-start | bytes 24580
  1726.7 913.0 %copy-start.126 = (f32[256]{0:T(256)S(1)}, f32[256]{0:T(256)}, u32[]{:S(2)}) copy-start(f32[256]{0:T(256)} %copy-done.125) | copy-start | bytes 3076
  1726.7 913.0 %copy-start.136 = (f32[256]{0:T(256)S(1)}, f32[256]{0:T(256)}, u32[]{:S(2)}) copy-start(f32[256]{0:T(256)} %get-tuple-element.104) | copy-start | bytes 3076
  2637.3 276.7 %copy-start.1 = (bf16[1,2048,768]{2,1,0:T(8,128)(2,1)S(1)}, bf16[1,2048,768]{2,1,0:T(8,128)(2,1)}, u32[]{:S(2)}) copy-start(bf16[1,2048,768]{2,1,0:T(8,128)(2,1)} %param.47) | copy-start | bytes 9437188
  (131 other events, 825.1 us)
Sparse Core Ops, SparseCore 0:
  13.5 81.9 all-gather.4
  97.3 36.7 all-gather.6
  136.0 37.4 all-gather.8
  208.6 17.1 reduce-scatter.29
  228.0 77.3 reduce-scatter.27
  1413.3 79.9 all-gather.10
  1605.1 17.2 reduce-scatter.33
  1624.8 131.7 reduce-scatter.49
  1758.8 132.1 reduce-scatter.51
  1893.2 130.0 reduce-scatter.47
  2025.5 129.7 reduce-scatter.43
  2157.5 131.5 reduce-scatter.39
  2291.3 132.1 reduce-scatter.41
  2425.7 131.8 reduce-scatter.45
  2559.7 77.5 reduce-scatter.31
  2640.1 134.5 reduce-scatter.37
  2777.4 136.5 reduce-scatter.35
where the time goes:
time: 2930 us; the launch traced here: 2920 us
  waiting for transfers between devices  2050 us (70%)
  matrix products  332 us (11%)
  local copies, waits for them, and re-layouts  230 us (8%)
  blocking collectives  142 us (5%)
  other arithmetic  128 us (4%)
    unnamed x24, waiting for transfers between devices  781 us
    all_to_all x4, waiting for transfers between devices, route_rows(): lax.all_to_all(block_rows, ('fsdp', 'tensor'), split_axis=0, concat_axis=...  733 us
    reduce_scatter x1, waiting for transfers between devices, per_device(): lax.psum_scatter(placed((adapter_count, rank_columns, all_cols), query_se...  139 us
    reduce_scatter x1, waiting for transfers between devices, per_device(): lax.psum_scatter(placed((adapter_count, all_cols, rank_columns), attentio...  131 us
    dot_general x21, matrix products, matrix_product(): return jnp.dot(first_op, second_op, preferred_element_type=jnp.float32)  109 us
    dot_general x21, matrix products, flipped_right_operand(): lax.dot_general(first_op, second_op, (((1,), (1,)), ((), ())), preferred_...  108 us
    unnamed x346, local copies, waits for them, and re-layouts  95.4 us
    reduce_scatter x1, waiting for transfers between devices, per_device(): lax.psum_scatter(normed_part.astype(jnp.bfloat16), 'tensor', scatter_dime...  78.1 us
  transfers between devices with their start and end apart: 21, of which 17 were waited for; matrix products, arithmetic and copies ran while one was open for 14% of the time, Pallas kernels for 0%

commit v1 on v0

--- a/solution.py
+++ b/solution.py
@@ -486,114 +486,84 @@
     input_grad = residual_grad + norm_backward(
         token_value_rows, attn_factor, gain_attn, normalized_gradient
     )
-    all_cols = local_cols * tensor_count
-    all_kv_cols = local_kv_cols * tensor_count
-
-    def placed(full_shape, addend, offsets):
-        holder = jnp.zeros(full_shape, jnp.float32)
-        return lax.dynamic_update_slice(holder, addend[None], (adapter_pick,) + offsets)
+    device_count = lax.axis_size("fsdp") * tensor_count
+    fsdp_count = lax.axis_size("fsdp")
+    adapter_ids = jnp.arange(adapter_count, dtype=jnp.int32)
+    source_rows = jnp.arange(device_count, dtype=jnp.int32) // tensor_count
+    owner_onehot = (adapter_ids[:, None] == adapter_index[source_rows][None, :]).astype(
+        jnp.bfloat16
+    )
+
+    def everywhere(addend):
+        return addend.reshape(device_count, -1)
+
+    def columns_everywhere(addend):
+        ranks = addend.shape[0]
+        return jnp.transpose(addend.reshape(ranks, device_count, -1), (1, 0, 2)).reshape(
+            device_count, -1
+        )
+
+    def from_heads(pieces):
+        holder = jnp.zeros((device_count, pieces.shape[1]), pieces.dtype)
+        return lax.dynamic_update_slice(
+            holder, pieces, (tensor_pos * fsdp_count, zero_pos)
+        )
+
+    def owner_sums(parts):
+        widths = [part.shape[1] for part in parts]
+        packed = jnp.concatenate([part.astype(jnp.bfloat16) for part in parts], axis=1)
+        received = route_rows(packed)
+        total = matrix_product(owner_onehot, received)
+        pieces = []
+        start = 0
+        for width in widths:
+            pieces.append(total[:, start : start + width])
+            start += width
+        return pieces
+
+    def head_columns(addend):
+        ranks = addend.shape[0]
+        return from_heads(
+            jnp.transpose(addend.reshape(ranks, fsdp_count, -1), (1, 0, 2)).reshape(
+                fsdp_count, -1
+            )
+        )
+
+    early = owner_sums(
+        [
+            everywhere(router_first_gradient),
+            columns_everywhere(attention_up_gradient),
+            columns_everywhere(router_second_gradient),
+            from_heads(attention_down_gradient.reshape(fsdp_count, -1)),
+        ]
+    )
+    late = owner_sums(
+        [
+            everywhere(input_first_gradient),
+            head_columns(query_second_gradient),
+            head_columns(key_second_gradient),
+            head_columns(value_second_gradient),
+        ]
+    )
+    first_sums = late[0].reshape(adapter_count, -1, 3 * rank_columns)
+
+    def by_row(piece):
+        return piece.reshape(adapter_count, -1, rank_columns)
+
+    def by_column(piece):
+        return piece.reshape(adapter_count, rank_columns, -1)
 
     summed = (
-        lax.psum_scatter(
-            placed(
-                (adapter_count, model_width, rank_columns),
-                input_first_gradient[:, :rank_columns],
-                (zero_pos, zero_pos),
-            ),
-            ("fsdp", "tensor"),
-            scatter_dimension=1,
-            tiled=True,
-        ),
-        lax.psum_scatter(
-            placed(
-                (adapter_count, rank_columns, all_cols),
-                query_second_gradient,
-                (zero_pos, tensor_pos * local_cols),
-            ),
-            ("fsdp", "tensor"),
-            scatter_dimension=2,
-            tiled=True,
-        ),
-        lax.psum_scatter(
-            placed(
-                (adapter_count, model_width, rank_columns),
-                input_first_gradient[:, rank_columns : 2 * rank_columns],
-                (zero_pos, zero_pos),
-            ),
-            ("fsdp", "tensor"),
-            scatter_dimension=1,
-            tiled=True,
-        ),
-        lax.psum_scatter(
-            placed(
-                (adapter_count, rank_columns, all_kv_cols),
-                key_second_gradient,
-                (zero_pos, tensor_pos * local_kv_cols),
-            ),
-            ("fsdp", "tensor"),
-            scatter_dimension=2,
-            tiled=True,
-        ),
-        lax.psum_scatter(
-            placed(
-                (adapter_count, model_width, rank_columns),
-                input_first_gradient[:, 2 * rank_columns :],
-                (zero_pos, zero_pos),
-            ),
-            ("fsdp", "tensor"),
-            scatter_dimension=1,
-            tiled=True,
-        ),
-        lax.psum_scatter(
-            placed(
-                (adapter_count, rank_columns, all_kv_cols),
-                value_second_gradient,
-                (zero_pos, tensor_pos * local_kv_cols),
-            ),
-            ("fsdp", "tensor"),
-            scatter_dimension=2,
-            tiled=True,
-        ),
-        lax.psum_scatter(
-            placed(
-                (adapter_count, all_cols, rank_columns),
-                attention_down_gradient,
-                (tensor_pos * local_cols, zero_pos),
-            ),
-            ("fsdp", "tensor"),
-            scatter_dimension=1,
-            tiled=True,
-        ),
-        lax.psum_scatter(
-            placed(
-                (adapter_count, rank_columns, model_width),
-                attention_up_gradient,
-                (zero_pos, zero_pos),
-            ),
-            ("fsdp", "tensor"),
-            scatter_dimension=2,
-            tiled=True,
-        ),
-        lax.psum_scatter(
-            placed(
-                (adapter_count, model_width, rank_columns),
-                router_first_gradient,
-                (zero_pos, zero_pos),
-            ),
-            ("fsdp", "tensor"),
-            scatter_dimension=1,
-            tiled=True,
-        ),
-        lax.psum_scatter(
-            placed(
-                (adapter_count, rank_columns, expert_count),
-                router_second_gradient,
-                (zero_pos, zero_pos),
-            ),
-            ("fsdp", "tensor"),
-            scatter_dimension=2,
-            tiled=True,
-        ),
+        first_sums[:, :, :rank_columns],
+        by_column(late[1]),
+        first_sums[:, :, rank_columns : 2 * rank_columns],
+        by_column(late[2]),
+        first_sums[:, :, 2 * rank_columns :],
+        by_column(late[3]),
+        by_row(early[3]),
+        by_column(early[1]),
+        by_row(early[0]),
+        by_column(early[2]),
     )
     grad_gate_in = jnp.transpose(
         grad_pair_down[:, :broad_columns].reshape(model_width, adapter_count, rank_columns),

time: 2930 us -> 1750 us (0.60)
  waiting for transfers between devices: 2050 us -> 939 us
  local copies, waits for them, and re-layouts: 230 us -> 168 us
  blocking collectives: 142 us -> 101 us
    unnamed x24 -> x8, waiting for transfers between devices: 781 us -> 1.47 us
    reduce_scatter x2 -> x0, waiting for transfers between devices: 271 us -> none  [the longest x1 139 us: per_device(): lax.psum_scatter(placed((adapter_count, rank_columns, all_cols), query_se...]
    reduce_scatter x1, waiting for transfers between devices: 78.1 us -> 0.01 us  [per_device(): lax.psum_scatter(normed_part.astype(jnp.bfloat16), 'tensor', scatter_dime...]
    unnamed x346 -> x315, local copies, waits for them, and re-layouts: 95.4 us -> 21.4 us
    unnamed x1 -> x0, blocking collectives: 41 us -> none
    all_to_all x4 -> x6, waiting for transfers between devices: 733 us -> 753 us  [route_rows(): lax.all_to_all(block_rows, ('fsdp', 'tensor'), split_axis=0, concat_axis=...]
    dot_general x21 -> x23, matrix products: 109 us -> 110 us  [matrix_product(): return jnp.dot(first_op, second_op, preferred_element_type=jnp.float32)]
  transfers between devices with their start and end apart: 21 -> 14, of which waited for: 17 -> 10; matrix products, arithmetic and copies ran while one was open for 14% -> 20% of each run, Pallas kernels for 0% -> 0%
where the time goes in v1:
time: 1750 us
  waiting for transfers between devices  939 us (54%)
  matrix products  354 us (20%)
  local copies, waits for them, and re-layouts  168 us (10%)
  other arithmetic  134 us (8%)
  blocking collectives  101 us (6%)
  starting transfers between devices  32.7 us (2%)
  between operations  18.5 us (1%)
    all_to_all x6, waiting for transfers between devices, route_rows(): lax.all_to_all(block_rows, ('fsdp', 'tensor'), split_axis=0, concat_axis=...  753 us
    dot_general x21, matrix products, flipped_right_operand(): lax.dot_general(first_op, second_op, (((1,), (1,)), ((), ())), preferred_...  117 us
    dot_general x23, matrix products, matrix_product(): return jnp.dot(first_op, second_op, preferred_element_type=jnp.float32)  110 us
    all_gather x1, waiting for transfers between devices, per_device(): lax.all_gather(branch_gradient, 'tensor', axis=0, tiled=True)  66.5 us
    reduce_scatter x1, waiting for transfers between devices, per_device(): lax.psum_scatter(out_part.astype(jnp.bfloat16), 'tensor', scatter_dimensi...  58.5 us
    all_gather x1, blocking collectives, per_device(): lax.all_gather(w_router, 'fsdp', axis=0, tiled=True)  53.8 us
    another operation x6, other arithmetic  44.2 us
  transfers between devices with their start and end apart: 14, of which 10 were waited for; matrix products, arithmetic and copies ran while one was open for 20% of the time, Pallas kernels for 0%

profile of v1, /device:TPU:16, one launch (start us, length us, event | category | flops | bytes accessed | tf_op | source)
XLA Modules:
  0.0 1746.7 jit_solution(14592550469543175790)
XLA Ops:
  17.0 10.9 all_gather.35
  27.9 10.7 all_gather.33
  42.8 14.5 all_gather.34
  66.1 29.3 %all-gather.5.cloned.1.call-done = bf16[1024,2048]{1,0:T(8,128)(2,1)} async-done(((bf16[256,2048]{1,0:T(8,128)(2,1)}), bf16[1024,2048]{1,0:T(8,128)(2,1)}) %all-gather.5.cloned.1.call-update) | async-done | bytes 4194320 | tf_op jit(solution)/shard_map/all_gather | solution.py:163
  104.1 30.1 %all-gather.7.cloned.1.call-done = bf16[2048,1024]{1,0:T(8,128)(2,1)} async-done(((bf16[256,1024]{1,0:T(8,128)(2,1)}), bf16[2048,1024]{1,0:T(8,128)(2,1)}) %all-gather.7.cloned.1.call-update) | async-done | bytes 4194320 | tf_op jit(solution)/shard_map/all_gather | solution.py:151
  134.1 7.6 fusion.187
  158.0 8.1 fusion.186
  166.1 7.7 fusion.185
  173.9 8.0 fusion.10
  181.9 8.1 fusion.9
  190.1 7.7 fusion.66
  197.7 8.0 fusion.63
  208.8 9.4 convolution_convert_fusion
  220.3 15.9 reduce-window.6
  238.7 8.1 scatter_custom_fusion
  246.9 58.5 %reduce-scatter.5.cloned.1.call-done = bf16[256,2048]{1,0:T(8,128)(2,1)} async-done(((bf16[1024,2048]{1,0:T(8,128)(2,1)}), bf16[256,2048]{1,0:T(8,128)(2,1)}) %reduce-scatter.5.cloned.1.call-update) | async-done | bytes 1048592 | tf_op jit(solution)/shard_map/reduce_scatter | solution.py:225
  311.3 21.5 %gather_fusion = bf16[2560,2048]{1,0:T(8,128)(2,1)} fusion(bf16[257,2048]{1,0:T(8,128)(2,1)} %concatenate.72, s32[3072]{0:T(1024)S(1)} %get-tuple-element.192), kind=kCustom, calls=%fused_computation | custom fusion | bytes 20981760 | tf_op jit(solution)/shard_map/gather | solution.py:267
  340.7 53.8 %all_gather.38 = bf16[2048,32]{0,1:T(8,128)(2,1)S(1)} all-gather(bf16[256,32]{0,1:T(8,128)(2,1)S(1)} %copy-done.120), channel_id=1, replica_groups=mesh['fsdp'=8,'tensor'=4] {'fsdp'}, dimensions={0}, use_global_device_ids=true | all-gather | bytes 147456 | tf_op jit(solution)/shard_map/all_gather | solution.py:155
  404.9 8.4 concatenate.75
  413.3 24.6 %gather_fusion.3 = bf16[2560,2048]{1,0:T(8,128)(2,1)} fusion(bf16[2049,2048]{1,0:T(8,128)(2,1)} %concatenate.75, s32[3072]{0:T(1024)S(1)} %get-tuple-element.191), kind=kCustom, calls=%fused_computation.3 | custom fusion | bytes 20981760 | tf_op jit(solution)/shard_map/gather | solution.py:332
  437.9 130.5 %all-to-all-done = bf16[32,80,2048]{2,1,0:T(8,128)(2,1)} async-done(((bf16[32,80,2048]{2,1,0:T(8,128)(2,1)}), bf16[32,80,2048]{2,1,0:T(8,128)(2,1)}, u32[]{:S(2)}, u32[]{:S(2)}) %all-to-all-start) | async-done | bytes 10485792 | tf_op jit(solution)/shard_map/all_to_all | solution.py:74
  575.3 14.0 fusion.40
  589.3 13.0 fusion.44
  602.3 202.7 %all-to-all-done.2 = bf16[32,80,2048]{2,1,0:T(8,128)(2,1)} async-done(((bf16[32,80,2048]{2,1,0:T(8,128)(2,1)}), bf16[32,80,2048]{2,1,0:T(8,128)(2,1)}, u32[]{:S(2)}, u32[]{:S(2)}) %all-to-all-start.2) | async-done | bytes 10485792 | tf_op jit(solution)/shard_map/all_to_all | solution.py:74
  804.9 14.2 fusion.34
  844.9 11.7 multiply_convert_fusion
  857.9 11.8 fusion.42
  871.6 11.7 fusion.38
  883.3 18.6 %add_convert_fusion = bf16[2560,2048]{1,0:T(8,128)(2,1)} fusion(f32[2560,2048]{1,0:T(8,128)} %fusion.42, f32[2560,2048]{1,0:T(8,128)} %fusion.38, bf16[2048,128]{0,1:T(8,128)(2,1)S(1)} %bitcast.484, bf16[2048,128]{0,1:T(8,128)(2,1)S(1)} %bitcast.486, f32[2560,128]{1,0:T(8,128)S(1)} %bitcast.457, f32[2560,128]{1,0:T(8,128)S(1)} %fusion.190, ...), kind=kOutput, calls=%fused_computation.8 | convolution fusion | flops 2704801792 | bytes 57409536 | tf_op jit(solution)/shard_map/dot_general | solution.py:23
  911.5 11.5 fusion.36
  923.1 11.9 add_convert_fusion.1
  935.0 202.9 %all-to-all-done.3 = bf16[32,80,2048]{2,1,0:T(8,128)(2,1)} async-done(((bf16[32,80,2048]{2,1,0:T(8,128)(2,1)}), bf16[32,80,2048]{2,1,0:T(8,128)(2,1)}, u32[]{:S(2)}, u32[]{:S(2)}) %all-to-all-start.3) | async-done | bytes 10485792 | tf_op jit(solution)/shard_map/all_to_all | solution.py:74
  1143.8 21.6 %gather_fusion.4 = bf16[2048,2048]{1,0:T(8,128)(2,1)} fusion(bf16[2560,2048]{1,0:T(8,128)(2,1)} %bitcast.67, s32[2048]{0:T(1024)S(1)} %broadcast_clamp_fusion), kind=kCustom, calls=%fused_computation.4 | custom fusion | bytes 16785408 | tf_op jit(solution)/shard_map/gather | solution.py:372
  1165.4 11.3 convert_reduce_fusion
  1176.7 197.2 %all-to-all-done.1 = bf16[32,80,2048]{2,1,0:T(8,128)(2,1)} async-done(((bf16[32,80,2048]{2,1,0:T(8,128)(2,1)}), bf16[32,80,2048]{2,1,0:T(8,128)(2,1)}, u32[]{:S(2)}, u32[]{:S(2)}) %all-to-all-start.1) | async-done | bytes 10485792 | tf_op jit(solution)/shard_map/all_to_all | solution.py:74
  1373.9 21.8 %gather_fusion.2 = bf16[2048,2048]{1,0:T(8,128)(2,1)} fusion(bf16[2560,2048]{1,0:T(8,128)(2,1)} %bitcast.59, s32[2048]{0:T(1024)S(1)} %broadcast_clamp_fusion), kind=kCustom, calls=%fused_computation.2 | custom fusion | bytes 16785408 | tf_op jit(solution)/shard_map/gather | solution.py:313
  1395.8 9.6 fusion.1
  1415.6 11.3 all_gather.40
  1427.0 66.5 %all-gather.11.cloned.1.call-done = bf16[1024,2048]{1,0:T(8,128)(2,1)} async-done(((bf16[256,2048]{1,0:T(8,128)(2,1)}), bf16[1024,2048]{1,0:T(8,128)(2,1)}) %all-gather.11.cloned.1.call-update) | async-done | bytes 4194320 | tf_op jit(solution)/shard_map/all_gather | solution.py:395
  1493.4 7.7 fusion.191
  1510.9 10.7 fusion.20
  1527.9 8.0 multiply_bitcast_fusion
  1535.9 9.5 fusion.69
  1545.4 10.7 fusion.5
  1556.2 15.8 fusion.19
  1572.0 8.2 multiply_bitcast_fusion.1
  1694.6 9.9 all-to-all-done.5
  1718.6 9.7 all-to-all-done.4
  (511 shorter events, 293.2 us)
Async XLA Ops:
  7.2 582.1 %copy-start = (bf16[1,2048,768]{2,1,0:T(8,128)(2,1)S(1)}, bf16[1,2048,768]{2,1,0:T(8,128)(2,1)}, u32[]{:S(2)}) copy-start(bf16[1,2048,768]{2,1,0:T(8,128)(2,1)} %param.47) | copy-start | bytes 9437188
  7.3 20.7 %copy-start.103 = (bf16[256,128]{1,0:T(8,128)(2,1)S(1)}, bf16[256,128]{1,0:T(8,128)(2,1)}, u32[]{:S(2)}) copy-start(bf16[256,128]{1,0:T(8,128)(2,1)} %param.44) | copy-start | bytes 196612
  7.3 88.2 %all-gather.5.cloned.1.call-start = ((), (), s32[]{:S(2)}) async-start(), calls=%async_computation.10 | async-start | bytes 5242880 | tf_op jit(solution)/shard_map/all_gather | solution.py:163
  13.4 120.7 %all-gather.7.cloned.1.call-start = ((), (), s32[]{:S(2)}) async-start(), calls=%async_computation.11 | async-start | bytes 4718592 | tf_op jit(solution)/shard_map/all_gather | solution.py:151
  14.1 194.7 %all-gather.9.cloned.1.call-start = ((), (), s32[]{:S(2)}) async-start(), calls=%async_computation.12 | async-start | bytes 4718592 | tf_op jit(solution)/shard_map/all_gather | solution.py:154
  14.9 232.0 %reduce-scatter.7.cloned.1.call-start = ((), (), s32[]{:S(2)}) async-start(), calls=%async_computation.14 | async-start | bytes 40960 | tf_op jit(solution)/shard_map/reduce_scatter | solution.py:228
  16.8 83.7 %copy-start.132 = (f32[64]{0:T(128)}, f32[64]{0:T(128)S(1)}, u32[]{:S(2)}) copy-start(f32[64]{0:T(128)S(1)} %multiply_power_fusion) | copy-start | bytes 772
  16.9 134.4 %copy-start.127 = (f32[128]{0:T(128)}, f32[128]{0:T(128)S(1)}, u32[]{:S(2)}) copy-start(f32[128]{0:T(128)S(1)} %convert_element_type.239) | copy-start | bytes 1540
  17.0 83.3 %copy-start.130 = (f32[128]{0:T(128)}, f32[128]{0:T(128)S(1)}, u32[]{:S(2)}) copy-start(f32[128]{0:T(128)S(1)} %convert_element_type.238) | copy-start | bytes 1540
  41.0 16.2 copy-start.80
  57.3 84.5 %copy-start.66 = (bf16[1024,48]{0,1:T(8,128)(2,1)}, bf16[1024,48]{0,1:T(8,128)(2,1)S(1)}, u32[]{:S(2)}) copy-start(bf16[1024,48]{0,1:T(8,128)(2,1)S(1)} %all_gather.34) | copy-start | bytes 294916
  102.1 64.0 %copy-start.49 = (bf16[1024,64]{0,1:T(8,128)(2,1)}, bf16[1024,64]{0,1:T(8,128)(2,1)S(1)}, u32[]{:S(2)}) copy-start(bf16[1024,64]{0,1:T(8,128)(2,1)S(1)} %get-tuple-element.146) | copy-start | bytes 393220
  102.1 64.0 %copy-start.51 = (bf16[1024,64]{0,1:T(8,128)(2,1)}, bf16[1024,64]{0,1:T(8,128)(2,1)S(1)}, u32[]{:S(2)}) copy-start(bf16[1024,64]{0,1:T(8,128)(2,1)S(1)} %get-tuple-element.147) | copy-start | bytes 393220
  166.1 31.6 %copy-start.85 = (f32[8,512]{1,0:T(8,128)}, f32[8,512]{1,0:T(8,128)S(1)}, u32[]{:S(2)}) copy-start(f32[8,512]{1,0:T(8,128)S(1)} %get-tuple-element.177) | copy-start | bytes 49156
  173.9 16.2 copy-start.87
  208.5 96.8 %reduce-scatter.5.cloned.1.call-start = ((), (), s32[]{:S(2)}) async-start(), calls=%async_computation.13 | async-start | bytes 5242880 | tf_op jit(solution)/shard_map/reduce_scatter | solution.py:225
  219.3 89.9 %copy-start.98 = (f32[2048]{0:T(1024)}, f32[2048]{0:T(1024)S(1)}, u32[]{:S(2)}) copy-start(f32[2048]{0:T(1024)S(1)} %convert_element_type.245) | copy-start | bytes 24580
  238.7 72.6 %copy-start.112 = (s32[2048,1]{0,1:T(1,128)}, s32[2048,1]{0,1:T(1,128)S(1)}, u32[]{:S(2)}) copy-start(s32[2048,1]{0,1:T(1,128)S(1)} %compare_select_fusion) | copy-start | bytes 24580
  308.2 24.6 %copy-start.123 = (f32[256]{0:T(256)}, f32[256]{0:T(256)S(1)}, u32[]{:S(2)}) copy-start(f32[256]{0:T(256)S(1)} %get-tuple-element.168) | copy-start | bytes 3076
  332.8 235.6 %all-to-all-start = ((bf16[32,80,2048]{2,1,0:T(8,128)(2,1)}), bf16[32,80,2048]{2,1,0:T(8,128)(2,1)}, u32[]{:S(2)}, u32[]{:S(2)}) async-start(bf16[32,80,2048]{2,1,0:T(8,128)(2,1)} %bitcast.451), calls=%async_computation.2 | async-start | bytes 20971520 | tf_op jit(solution)/shard_map/all_to_all | solution.py:74
  337.8 58.3 %copy-start.16 = (bf16[256,2048]{1,0:T(8,128)(2,1)S(1)}, bf16[256,2048]{1,0:T(8,128)(2,1)}, u32[]{:S(2)}) copy-start(bf16[256,2048]{1,0:T(8,128)(2,1)} %copy-done.15) | copy-start | bytes 3145732
  568.4 236.5 %all-to-all-start.2 = ((bf16[32,80,2048]{2,1,0:T(8,128)(2,1)}), bf16[32,80,2048]{2,1,0:T(8,128)(2,1)}, u32[]{:S(2)}, u32[]{:S(2)}) async-start(bf16[32,80,2048]{2,1,0:T(8,128)(2,1)} %bitcast.452), calls=%async_computation.4 | async-start | bytes 20971520 | tf_op jit(solution)/shard_map/all_to_all | solution.py:74
  819.2 64.1 %copy-start.12 = (f32[32,80,128]{2,1,0:T(8,128)}, f32[32,80,128]{2,1,0:T(8,128)S(1)}, u32[]{:S(2)}) copy-start(f32[32,80,128]{2,1,0:T(8,128)S(1)} %broadcast_in_dim.45) | copy-start | bytes 3932164
  819.2 14.8 slice-start.6
  826.7 18.3 %copy-start.61 = (bf16[2560,128]{1,0:T(8,128)(2,1)}, bf16[2560,128]{1,0:T(8,128)(2,1)S(1)}, u32[]{:S(2)}) copy-start(bf16[2560,128]{1,0:T(8,128)(2,1)S(1)} %fusion.32) | copy-start | bytes 1966084
  857.8 25.4 %copy-start.33 = (f32[2560,128]{1,0:T(8,128)}, f32[2560,128]{1,0:T(8,128)S(1)}, u32[]{:S(2)}) copy-start(f32[2560,128]{1,0:T(8,128)S(1)} %fusion.189) | copy-start | bytes 3932164
  901.8 236.0 %all-to-all-start.3 = ((bf16[32,80,2048]{2,1,0:T(8,128)(2,1)}), bf16[32,80,2048]{2,1,0:T(8,128)(2,1)}, u32[]{:S(2)}, u32[]{:S(2)}) async-start(bf16[32,80,2048]{2,1,0:T(8,128)(2,1)} %bitcast.450), calls=%async_computation.5 | async-start | bytes 20971520 | tf_op jit(solution)/shard_map/all_to_all | solution.py:74
  1137.9 236.1 %all-to-all-start.1 = ((bf16[32,80,2048]{2,1,0:T(8,128)(2,1)}), bf16[32,80,2048]{2,1,0:T(8,128)(2,1)}, u32[]{:S(2)}, u32[]{:S(2)}) async-start(bf16[32,80,2048]{2,1,0:T(8,128)(2,1)} %bitcast.453), calls=%async_computation.3 | async-start | bytes 20971520 | tf_op jit(solution)/shard_map/all_to_all | solution.py:74
  1143.3 350.1 %all-gather.11.cloned.1.call-start = ((), (), s32[]{:S(2)}) async-start(), calls=%async_computation.15 | async-start | bytes 5242880 | tf_op jit(solution)/shard_map/all_gather | solution.py:395
  1373.9 21.8 %copy-start.22 = (f32[256,2048]{1,0:T(8,128)S(1)}, f32[256,2048]{1,0:T(8,128)}, u32[]{:S(2)}) copy-start(f32[256,2048]{1,0:T(8,128)} %convert_element_type.258) | copy-start | bytes 6291460
  1373.9 21.8 %copy-start.63 = (f32[256,8]{1,0:T(8,128)S(1)}, f32[256,8]{1,0:T(8,128)}, u32[]{:S(2)}) copy-start(f32[256,8]{1,0:T(8,128)} %copy-done.62) | copy-start | bytes 24580
  1413.3 277.4 %reduce-scatter.11.cloned.1.call-start = ((), (), s32[]{:S(2)}) async-start(), calls=%async_computation.17 | async-start | bytes 122880 | tf_op jit(solution)/shard_map/reduce_scatter | solution.py:477
  1427.0 74.2 %copy-start.90 = (bf16[1024,16]{0,1:T(8,128)(2,1)}, bf16[1024,16]{0,1:T(8,128)(2,1)S(1)}, u32[]{:S(2)}) copy-start(bf16[1024,16]{0,1:T(8,128)(2,1)S(1)} %all_gather.40) | copy-start | bytes 98308
  1599.2 26.9 %copy-start.47 = (bf16[128,1024]{1,0:T(8,128)(2,1)}, bf16[128,1024]{1,0:T(8,128)(2,1)S(1)}, u32[]{:S(2)}) copy-start(bf16[128,1024]{1,0:T(8,128)(2,1)S(1)} %fusion.82) | copy-start | bytes 786436
  1619.4 114.0 %reduce-scatter.9.cloned.1.call-start = ((), (), s32[]{:S(2)}) async-start(), calls=%async_computation.16 | async-start | bytes 5242880 | tf_op jit(solution)/shard_map/reduce_scatter | solution.py:474
  1660.7 27.2 %copy-start.67 = (bf16[1024,48]{0,1:T(8,128)(2,1)S(1)}, bf16[1024,48]{0,1:T(8,128)(2,1)}, u32[]{:S(2)}) copy-start(bf16[1024,48]{0,1:T(8,128)(2,1)} %copy-done.66) | copy-start | bytes 294916
  1660.7 28.7 %copy-start.38 = (bf16[1024,128]{0,1:T(8,128)(2,1)S(1)}, bf16[1024,128]{0,1:T(8,128)(2,1)}, u32[]{:S(2)}) copy-start(bf16[1024,128]{0,1:T(8,128)(2,1)} %copy-done.37) | copy-start | bytes 786436
  1660.7 29.3 %copy-start.21 = (bf16[1024,1024]{0,1:T(8,128)(2,1)S(1)}, bf16[1024,1024]{0,1:T(8,128)(2,1)}, u32[]{:S(2)}) copy-start(bf16[1024,1024]{0,1:T(8,128)(2,1)} %copy-done.20) | copy-start | bytes 6291460
  1670.1 20.6 %copy-start.25 = (bf16[256,2048]{1,0:T(8,128)(2,1)S(1)}, bf16[256,2048]{1,0:T(8,128)(2,1)}, u32[]{:S(2)}) copy-start(bf16[256,2048]{1,0:T(8,128)(2,1)} %fusion.52) | copy-start | bytes 3145732
  1682.4 22.1 %all-to-all-start.5 = ((bf16[32,2,2056]{2,1,0:T(2,128)(2,1)}), bf16[32,2,2056]{2,1,0:T(2,128)(2,1)}, u32[]{:S(2)}, u32[]{:S(2)}) async-start(bf16[32,2,2056]{2,1,0:T(2,128)(2,1)} %reshape.1038), calls=%async_computation.9 | async-start | bytes 557056 | tf_op jit(solution)/shard_map/all_to_all | solution.py:74
  1690.6 18.4 %copy-start.40 = (bf16[2560,256]{1,0:T(8,128)(2,1)S(1)}, bf16[2560,256]{1,0:T(8,128)(2,1)}, u32[]{:S(2)}) copy-start(bf16[2560,256]{1,0:T(8,128)(2,1)} %copy-done.39) | copy-start | bytes 3932164
  1692.9 22.2 %copy-start.126 = (s32[32]{0:T(128)S(1)}, s32[32]{0:T(128)}, u32[]{:S(2)}) copy-start(s32[32]{0:T(128)} %copy-done.125) | copy-start | bytes 388
  1704.5 23.7 %all-to-all-start.4 = ((bf16[32,2,2816]{2,1,0:T(2,128)(2,1)}), bf16[32,2,2816]{2,1,0:T(2,128)(2,1)S(1)}, u32[]{:S(2)}, u32[]{:S(2)}) async-start(bf16[32,2,2816]{2,1,0:T(2,128)(2,1)} %reshape.1036), calls=%async_computation.8 | async-start | bytes 720896 | tf_op jit(solution)/shard_map/all_to_all | solution.py:74
  1712.7 20.7 %copy-start.77 = (bf16[2048,16]{0,1:T(8,128)(2,1)S(1)}, bf16[2048,16]{0,1:T(8,128)(2,1)}, u32[]{:S(2)}) copy-start(bf16[2048,16]{0,1:T(8,128)(2,1)} %copy-done.76) | copy-start | bytes 196612
  1712.7 20.7 %copy-start.79 = (bf16[2048,16]{0,1:T(8,128)(2,1)S(1)}, bf16[2048,16]{0,1:T(8,128)(2,1)}, u32[]{:S(2)}) copy-start(bf16[2048,16]{0,1:T(8,128)(2,1)} %copy-done.78) | copy-start | bytes 196612
  1712.7 20.7 %copy-start.81 = (bf16[2048,16]{0,1:T(8,128)(2,1)S(1)}, bf16[2048,16]{0,1:T(8,128)(2,1)}, u32[]{:S(2)}) copy-start(bf16[2048,16]{0,1:T(8,128)(2,1)} %copy-done.80) | copy-start | bytes 196612
  1712.7 20.7 %copy-start.95 = (bf16[256,48]{0,1:T(8,128)(2,1)S(1)}, bf16[256,48]{0,1:T(8,128)(2,1)}, u32[]{:S(2)}) copy-start(bf16[256,48]{0,1:T(8,128)(2,1)} %reduce-scatter.11.cloned.1.call-done) | copy-start | bytes 73732
  1712.7 20.7 %copy-start.97 = (f32[2048]{0:T(1024)S(1)}, f32[2048]{0:T(1024)}, u32[]{:S(2)}) copy-start(f32[2048]{0:T(1024)} %copy-done.96) | copy-start | bytes 24580
  (118 other events, 711.7 us)
Sparse Core Ops, SparseCore 0:
  13.5 81.9 all-gather.4
  97.3 36.7 all-gather.6
  136.0 37.4 all-gather.8
  208.7 17.1 reduce-scatter.6
  228.1 77.2 reduce-scatter.4
  1413.4 79.9 all-gather.10
  1619.5 17.2 reduce-scatter.10
  1639.2 89.4 reduce-scatter.8

commit v2 on v1

v2 whole, which is shorter than its diff:
```python
import functools
import math

import jax
import jax.numpy as jnp
from jax import lax
from jax.experimental import pallas as pl
from jax.experimental.pallas import tpu as pltpu
from jax.sharding import PartitionSpec as P

NORM_EPSILON = 1e-06
ROPE_THETA = 1000000.0
BF16 = jnp.bfloat16
F32 = jnp.float32
WINDOW = 256
MEBI = 1 << 20


def matrix_product(first_op, second_op):
    return jnp.dot(first_op, second_op, preferred_element_type=F32)


def flipped_left_operand(first_op, second_op):
    return lax.dot_general(
        first_op, second_op, (((0,), (0,)), ((), ())), preferred_element_type=F32
    )


def flipped_right_operand(first_op, second_op):
    return lax.dot_general(
        first_op, second_op, (((1,), (1,)), ((), ())), preferred_element_type=F32
    )


def norm_forward(values, gain_vec):
    factor = lax.rsqrt(jnp.mean(values * values, axis=-1, keepdims=True) + NORM_EPSILON)
    return (values * factor * gain_vec, factor)


def norm_backward(values, factor, gain_vec, upstream):
    scaled = upstream * gain_vec
    return factor * scaled - values * (factor * factor * factor) * jnp.mean(
        values * scaled, axis=-1, keepdims=True
    )


def rope_tables(sequence_length, head_width):
    half_width = head_width // 2
    inverse = jnp.power(ROPE_THETA, -2.0 * jnp.arange(half_width, dtype=F32) / head_width)
    angles = jnp.arange(sequence_length, dtype=F32)[:, None] * inverse[None, :]
    cosine, sine = jnp.cos(angles), jnp.sin(angles)
    return (
        jnp.concatenate([cosine, cosine], axis=1),
        jnp.concatenate([-sine, sine], axis=1),
    )


def swapped(values):
    return pltpu.roll(values, values.shape[-1] // 2, 1)


def route_rows(block_rows):
    return lax.all_to_all(block_rows, ("fsdp", "tensor"), split_axis=0, concat_axis=0, tiled=True)


def plane_rows(block_rows):
    return lax.all_to_all(block_rows, "fsdp", split_axis=0, concat_axis=0, tiled=True)


def params(mebibytes, axes=1):
    return pltpu.CompilerParams(
        vmem_limit_bytes=mebibytes * MEBI, dimension_semantics=("arbitrary",) * axes
    )


def whole(shape):
    rank = len(shape)
    return pl.BlockSpec(shape, lambda *_: (0,) * rank)


def head_values(linear, low, second, gain, cosine, sine):
    values = linear + matrix_product(low, second)
    normed, factor = norm_forward(values, gain)
    turned = (normed * cosine + swapped(normed) * sine).astype(BF16)
    return values, factor, turned


def head_values_gradient(values, factor, gain, cosine, sine, upstream):
    back = upstream * cosine - swapped(upstream) * sine
    return norm_backward(values, factor, gain, back).astype(BF16)


def allowed_keys(block, start, width, seg_column, seg_row):
    rows = block * WINDOW + lax.broadcasted_iota(jnp.int32, (WINDOW, width), 0)
    keys = start + lax.broadcasted_iota(jnp.int32, (WINDOW, width), 1)
    mine = seg_column[block * WINDOW : (block + 1) * WINDOW]
    theirs = seg_row[:, start : start + width]
    return (keys == rows) | ((keys < rows) & (mine == theirs) & (theirs != 0))


def block_bounds(block):
    start = max(block - 1, 0) * WINDOW
    return start, (block + 1) * WINDOW - start


def attention_forward_body(
    rank,
    scale,
    lin_ref,
    key_lin_ref,
    value_lin_ref,
    low_ref,
    q_second_ref,
    k_second_ref,
    v_second_ref,
    q_gain_ref,
    k_gain_ref,
    cos_ref,
    sin_ref,
    seg_column_ref,
    seg_row_ref,
    heads_ref,
    key_scratch,
    value_scratch,
):
    cosine, sine = cos_ref[...], sin_ref[...]

    @pl.when(pl.program_id(0) == 0)
    def _():
        key_scratch[...] = head_values(
            key_lin_ref[...],
            low_ref[:, rank : 2 * rank],
            k_second_ref[...],
            k_gain_ref[...],
            cosine,
            sine,
        )[2]
        value_scratch[...] = (
            value_lin_ref[...]
            + matrix_product(low_ref[:, 2 * rank : 3 * rank], v_second_ref[...])
        ).astype(BF16)

    query = head_values(
        lin_ref[...], low_ref[:, :rank], q_second_ref[...], q_gain_ref[...], cosine, sine
    )[2]
    seg_column, seg_row = seg_column_ref[...], seg_row_ref[...]
    for block in range(query.shape[0] // WINDOW):
        start, width = block_bounds(block)
        rows = pl.ds(block * WINDOW, WINDOW)
        scores = (
            flipped_right_operand(
                query[block * WINDOW : (block + 1) * WINDOW], key_scratch[pl.ds(start, width)]
            )
            * scale
        )
        scores = jnp.where(
            allowed_keys(block, start, width, seg_column, seg_row), scores, -1e30
        )
        expo = jnp.exp(scores - jnp.max(scores, axis=-1, keepdims=True))
        probs = (expo / jnp.sum(expo, axis=-1, keepdims=True)).astype(BF16)
        heads_ref[rows, :] = matrix_product(probs, value_scratch[pl.ds(start, width)]).astype(
            BF16
        )


def attention_forward(
    linear, low, q_second, k_second, v_second, q_gain, k_gain, tables, seg_column, seg_row, scale
):
    rows, head_dim = linear.shape[0], q_gain.shape[1]
    heads = q_second.shape[1] // head_dim
    rank = q_second.shape[0]
    column = pl.BlockSpec((rows, head_dim), lambda h: (0, h))
    return pl.pallas_call(
        functools.partial(attention_forward_body, rank, scale),
        grid=(heads,),
        out_shape=jax.ShapeDtypeStruct((rows, heads * head_dim), BF16),
        in_specs=[
            column,
            pl.BlockSpec((rows, head_dim), lambda h: (0, heads)),
            pl.BlockSpec((rows, head_dim), lambda h: (0, heads + 1)),
            whole(low.shape),
            pl.BlockSpec((rank, head_dim), lambda h: (0, h)),
            whole(k_second.shape),
            whole(v_second.shape),
            whole(q_gain.shape),
            whole(k_gain.shape),
            whole(tables[0].shape),
            whole(tables[1].shape),
            whole(seg_column.shape),
            whole(seg_row.shape),
        ],
        out_specs=column,
        scratch_shapes=[pltpu.VMEM((rows, head_dim), BF16), pltpu.VMEM((rows, head_dim), BF16)],
        compiler_params=params(40),
        cost_estimate=pl.CostEstimate(
            flops=8 * heads * rows * WINDOW * head_dim,
            transcendentals=2 * heads * rows * WINDOW,
            bytes_accessed=6 * rows * heads * head_dim,
        ),
        name="attention_forward",
    )(
        linear,
        linear,
        linear,
        low,
        q_second,
        k_second,
        v_second,
        q_gain,
        k_gain,
        *tables,
        seg_column,
        seg_row,
    )


def attention_backward_body(
    rank,
    scale,
    lin_ref,
    key_lin_ref,
    value_lin_ref,
    low_ref,
    q_second_ref,
    k_second_ref,
    v_second_ref,
    q_gain_ref,
    k_gain_ref,
    cos_ref,
    sin_ref,
    seg_column_ref,
    seg_row_ref,
    heads_ref,
    heads_grad_ref,
    low_grad_ref,
    down_ref,
    q_grad_ref,
    k_grad_ref,
    v_grad_ref,
    share_ref,
    q_second_grad_ref,
    k_second_grad_ref,
    v_second_grad_ref,
    down_grad_ref,
    key_scratch,
    value_scratch,
    key_sum,
    value_sum,
    query_sum,
    share_sum,
):
    cosine, sine = cos_ref[...], sin_ref[...]
    head = pl.program_id(0)

    @pl.when(head == 0)
    def _():
        key_scratch[...] = head_values(
            key_lin_ref[...],
            low_ref[:, rank : 2 * rank],
            k_second_ref[...],
            k_gain_ref[...],
            cosine,
            sine,
        )[2]
        value_scratch[...] = (
            value_lin_ref[...]
            + matrix_product(low_ref[:, 2 * rank : 3 * rank], v_second_ref[...])
        ).astype(BF16)
        key_sum[...] = jnp.zeros_like(key_sum)
        value_sum[...] = jnp.zeros_like(value_sum)
        share_sum[...] = jnp.zeros_like(share_sum)

    low_q = low_ref[:, :rank]
    values, factor, query = head_values(
        lin_ref[...], low_q, q_second_ref[...], q_gain_ref[...], cosine, sine
    )
    low_grad = low_grad_ref[...]
    upstream = (heads_grad_ref[...] + matrix_product(low_grad, down_ref[...])).astype(BF16)
    down_grad_ref[...] = flipped_left_operand(low_grad, heads_ref[...])
    seg_column, seg_row = seg_column_ref[...], seg_row_ref[...]
    for block in range(query.shape[0] // WINDOW):
        start, width = block_bounds(block)
        rows = pl.ds(block * WINDOW, WINDOW)
        keys = pl.ds(start, width)
        query_block = query[block * WINDOW : (block + 1) * WINDOW]
        upstream_block = upstream[block * WINDOW : (block + 1) * WINDOW]
        scores = flipped_right_operand(query_block, key_scratch[keys]) * scale
        scores = jnp.where(
            allowed_keys(block, start, width, seg_column, seg_row), scores, -1e30
        )
        expo = jnp.exp(scores - jnp.max(scores, axis=-1, keepdims=True))
        probs = expo / jnp.sum(expo, axis=-1, keepdims=True)
        prob_grad = flipped_right_operand(upstream_block, value_scratch[keys])
        score_grad = (
            probs * (prob_grad - jnp.sum(probs * prob_grad, axis=-1, keepdims=True))
        ).astype(BF16)
        value_sum[keys, :] += flipped_left_operand(probs.astype(BF16), upstream_block)
        key_sum[keys, :] += flipped_left_operand(score_grad, query_block)
        query_sum[rows, :] = matrix_product(score_grad, key_scratch[keys]) * scale
    q_grad = head_values_gradient(
        values, factor, q_gain_ref[...], cosine, sine, query_sum[...]
    )
    q_grad_ref[...] = q_grad
    q_second_grad_ref[...] = flipped_left_operand(low_q, q_grad)
    share_sum[:, :rank] += flipped_right_operand(q_grad, q_second_ref[...])

    @pl.when(head == pl.num_programs(0) - 1)
    def _():
        low_k = low_ref[:, rank : 2 * rank]
        low_v = low_ref[:, 2 * rank : 3 * rank]
        key_values, key_factor, _turned = head_values(
            key_lin_ref[...], low_k, k_second_ref[...], k_gain_ref[...], cosine, sine
        )
        k_grad = head_values_gradient(
            key_values, key_factor, k_gain_ref[...], cosine, sine, key_sum[...] * scale
        )
        v_grad = value_sum[...].astype(BF16)
        k_grad_ref[...] = k_grad
        v_grad_ref[...] = v_grad
        k_second_grad_ref[...] = flipped_left_operand(low_k, k_grad)
        v_second_grad_ref[...] = flipped_left_operand(low_v, v_grad)
        share_sum[:, rank : 2 * rank] = flipped_right_operand(k_grad, k_second_ref[...])
        share_sum[:, 2 * rank : 3 * rank] = flipped_right_operand(v_grad, v_second_ref[...])
        share_ref[...] = share_sum[...].astype(BF16)


def attention_backward(
    linear,
    low,
    q_second,
    k_second,
    v_second,
    q_gain,
    k_gain,
    tables,
    seg_column,
    seg_row,
    scale,
    heads_low,
    heads_grad,
    low_grad,
    down_first,
):
    rows, head_dim = linear.shape[0], q_gain.shape[1]
    rank, columns = q_second.shape
    heads = columns // head_dim
    column = pl.BlockSpec((rows, head_dim), lambda h: (0, h))
    narrow = pl.BlockSpec((rank, head_dim), lambda h: (0, h))
    single = (rows, head_dim)
    return pl.pallas_call(
        functools.partial(attention_backward_body, rank, scale),
        grid=(heads,),
        out_shape=(
            jax.ShapeDtypeStruct((rows, columns), BF16),
            jax.ShapeDtypeStruct(single, BF16),
            jax.ShapeDtypeStruct(single, BF16),
            jax.ShapeDtypeStruct((rows, 3 * rank), BF16),
            jax.ShapeDtypeStruct((rank, columns), F32),
            jax.ShapeDtypeStruct((rank, head_dim), F32),
            jax.ShapeDtypeStruct((rank, head_dim), F32),
            jax.ShapeDtypeStruct((rank, columns), F32),
        ),
        in_specs=[
            column,
            pl.BlockSpec((rows, head_dim), lambda h: (0, heads)),
            pl.BlockSpec((rows, head_dim), lambda h: (0, heads + 1)),
            whole(low.shape),
            narrow,
            whole(k_second.shape),
            whole(v_second.shape),
            whole(q_gain.shape),
            whole(k_gain.shape),
            whole(tables[0].shape),
            whole(tables[1].shape),
            whole(seg_column.shape),
            whole(seg_row.shape),
            column,
            column,
            whole(low_grad.shape),
            narrow,
        ],
        out_specs=(
            column,
            whole(single),
            whole(single),
            whole((rows, 3 * rank)),
            narrow,
            whole((rank, head_dim)),
            whole((rank, head_dim)),
            narrow,
        ),
        scratch_shapes=[
            pltpu.VMEM(single, BF16),
            pltpu.VMEM(single, BF16),
            pltpu.VMEM(single, F32),
            pltpu.VMEM(single, F32),
            pltpu.VMEM(single, F32),
            pltpu.VMEM((rows, 3 * rank), F32),
        ],
        compiler_params=params(48),
        cost_estimate=pl.CostEstimate(
            flops=20 * heads * rows * WINDOW * head_dim,
            transcendentals=2 * heads * rows * WINDOW,
            bytes_accessed=12 * rows * columns,
        ),
        name="attention_backward",
    )(
        linear,
        linear,
        linear,
        low,
        q_second,
        k_second,
        v_second,
        q_gain,
        k_gain,
        *tables,
        seg_column,
        seg_row,
        heads_low,
        heads_grad,
        low_grad,
        down_first,
    )


def slot_choice(ranks, slots):
    experts, tokens = ranks.shape
    places = lax.broadcasted_iota(jnp.int32, (slots, tokens), 0)
    return jnp.concatenate(
        [(places == ranks[e : e + 1, :]).astype(F32) for e in range(experts)], axis=0
    ).astype(BF16)


def to_slots_body(rank_ref, rows_ref, out_ref):
    experts, _, slots, width = out_ref.shape
    chosen = matrix_product(slot_choice(rank_ref[0], slots), rows_ref[...])
    out_ref[...] = chosen.astype(BF16).reshape(out_ref.shape)


def to_slots(ranks, rows, slots):
    blocks, experts, tokens = ranks.shape
    width = rows.shape[1]
    return pl.pallas_call(
        to_slots_body,
        grid=(blocks,),
        out_shape=jax.ShapeDtypeStruct((experts, blocks, slots, width), BF16),
        in_specs=[
            pl.BlockSpec((1, experts, tokens), lambda z: (z, 0, 0)),
            pl.BlockSpec((tokens, width), lambda z: (z, 0)),
        ],
        out_specs=pl.BlockSpec((experts, 1, slots, width), lambda z: (0, z, 0, 0)),
        compiler_params=params(40),
        cost_estimate=pl.CostEstimate(
            flops=2 * blocks * experts * slots * tokens * width,
            transcendentals=0,
            bytes_accessed=2 * blocks * width * (experts * slots + tokens),
        ),
        name="to_slots",
    )(ranks, rows)


def from_slots_body(rank_ref, slot_ref, out_ref):
    experts, _, slots, width = slot_ref.shape
    choice = slot_choice(rank_ref[0], slots)
    out_ref[...] = flipped_left_operand(
        choice, slot_ref[...].reshape(experts * slots, width)
    ).astype(BF16)


def from_slots(ranks, slotted):
    blocks, experts, tokens = ranks.shape
    slots, width = slotted.shape[2:]
    return pl.pallas_call(
        from_slots_body,
        grid=(blocks,),
        out_shape=jax.ShapeDtypeStruct((blocks * tokens, width), BF16),
        in_specs=[
            pl.BlockSpec((1, experts, tokens), lambda z: (z, 0, 0)),
            pl.BlockSpec((experts, 1, slots, width), lambda z: (0, z, 0, 0)),
        ],
        out_specs=pl.BlockSpec((tokens, width), lambda z: (z, 0)),
        compiler_params=params(40),
        cost_estimate=pl.CostEstimate(
            flops=2 * blocks * experts * slots * tokens * width,
            transcendentals=0,
            bytes_accessed=2 * blocks * width * (experts * slots + tokens),
        ),
        name="from_slots",
    )(ranks, slotted)


def ranks_of(mask):
    tokens = mask.shape[-1]
    order = jnp.arange(tokens, dtype=jnp.int32)
    before = (order[:, None] < order[None, :]).astype(BF16)
    counts = matrix_product(mask.astype(BF16), before)
    return jnp.where(mask, counts, -1.0).astype(jnp.int32)


def experts_body(
    tile,
    pick_ref,
    rows_ref,
    up_rows_ref,
    rank_ref,
    weight_ref,
    gate_w_ref,
    up_w_ref,
    down_w_ref,
    pair_in_ref,
    gate_out_ref,
    up_out_ref,
    down_in_ref,
    down_out_ref,
    y_ref,
    rows_grad_ref,
    gate_grad_ref,
    pair_in_grad_ref,
    gate_out_grad_ref,
    up_out_grad_ref,
    down_in_grad_ref,
    down_out_grad_ref,
    gate_scratch,
    up_scratch,
    inner_scratch,
    route_scratch,
    gate_lin_scratch,
    up_lin_scratch,
):
    step = pl.program_id(0)

    @pl.when(step == 0)
    def _():
        for ref in (
            pair_in_grad_ref,
            gate_out_grad_ref,
            up_out_grad_ref,
            down_in_grad_ref,
            down_out_grad_ref,
        ):
            ref[...] = jnp.zeros_like(ref)

    pick = pick_ref[step]
    row_count, width = rows_ref.shape[1:]
    hidden = gate_w_ref.shape[1]
    rank = gate_out_ref.shape[1]
    blocks, tokens = rank_ref.shape[1:]
    slots = row_count // blocks
    places = lax.broadcasted_iota(jnp.int32, (slots, tokens), 0)
    held = [places == rank_ref[0, z : z + 1, :] for z in range(blocks)]
    weight = jnp.concatenate(
        [
            jnp.sum(jnp.where(held[z], weight_ref[0, z : z + 1, :], 0.0), axis=1, keepdims=True)
            for z in range(blocks)
        ],
        axis=0,
    )
    rows = rows_ref[0]
    pair = flipped_right_operand(rows, pair_in_ref[pick]).astype(BF16)
    gate_low, up_low = pair[:, :rank], pair[:, rank:]

    @pl.loop(0, hidden // tile)
    def _(j):
        columns = pl.ds(pl.multiple_of(j * tile, tile), tile)
        gate_lin = matrix_product(rows, gate_w_ref[:, columns]) + matrix_product(
            gate_low, gate_out_ref[pick, :, columns]
        )
        up_lin = matrix_product(rows, up_w_ref[:, columns]) + matrix_product(
            up_low, up_out_ref[pick, :, columns]
        )
        gate_scratch[:, columns] = gate_lin
        up_scratch[:, columns] = up_lin
        inner_scratch[:, columns] = (gate_lin * jax.nn.sigmoid(gate_lin) * up_lin).astype(BF16)

    inner = inner_scratch[...]
    down_low = flipped_right_operand(inner, down_in_ref[pick]).astype(BF16)

    def down_step(j, total):
        columns = pl.ds(pl.multiple_of(j * tile, tile), tile)
        result = (
            matrix_product(inner, down_w_ref[:, columns])
            + matrix_product(down_low, down_out_ref[pick, :, columns])
        ).astype(BF16)
        wide = result.astype(F32)
        upstream = up_rows_ref[0, :, columns].astype(F32)
        y_ref[0, :, columns] = (weight * wide).astype(BF16)
        route_scratch[:, columns] = (weight * upstream).astype(BF16)
        return total + jnp.sum(upstream * wide, axis=1, keepdims=True)

    gate_grad = lax.fori_loop(
        0, width // tile, down_step, jnp.zeros((row_count, 1), F32)
    )
    for z in range(blocks):
        gate_grad_ref[0, z : z + 1, :] = jnp.sum(
            jnp.where(held[z], gate_grad[z * slots : (z + 1) * slots], 0.0),
            axis=0,
            keepdims=True,
        )
    route = route_scratch[...]
    down_low_grad = flipped_right_operand(route, down_out_ref[pick]).astype(BF16)
    down_in_grad_ref[pick] += flipped_left_operand(down_low_grad, inner)
    down_out_grad_ref[pick] += flipped_left_operand(down_low, route)

    @pl.loop(0, hidden // tile)
    def _(j):
        columns = pl.ds(pl.multiple_of(j * tile, tile), tile)
        inner_grad = flipped_right_operand(route, down_w_ref[columns, :]) + matrix_product(
            down_low_grad, down_in_ref[pick, :, columns]
        )
        gate_lin, up_lin = gate_scratch[:, columns], up_scratch[:, columns]
        sig = jax.nn.sigmoid(gate_lin)
        gate_lin_scratch[:, columns] = (
            inner_grad * up_lin * (sig * (1.0 + gate_lin * (1.0 - sig)))
        ).astype(BF16)
        up_lin_scratch[:, columns] = (inner_grad * (gate_lin * sig)).astype(BF16)

    gate_lin_grad, up_lin_grad = gate_lin_scratch[...], up_lin_scratch[...]
    gate_low_grad = flipped_right_operand(gate_lin_grad, gate_out_ref[pick]).astype(BF16)
    up_low_grad = flipped_right_operand(up_lin_grad, up_out_ref[pick]).astype(BF16)
    gate_out_grad_ref[pick] += flipped_left_operand(gate_low, gate_lin_grad)
    up_out_grad_ref[pick] += flipped_left_operand(up_low, up_lin_grad)
    pair_grad = jnp.concatenate([gate_low_grad, up_low_grad], axis=1)
    pair_in_grad_ref[pick] += flipped_left_operand(pair_grad, rows)

    @pl.loop(0, width // tile)
    def _(j):
        columns = pl.ds(pl.multiple_of(j * tile, tile), tile)
        rows_grad_ref[0, :, columns] = (
            flipped_right_operand(gate_lin_grad, gate_w_ref[columns, :])
            + flipped_right_operand(up_lin_grad, up_w_ref[columns, :])
            + matrix_product(pair_grad, pair_in_ref[pick, :, columns])
        ).astype(BF16)


def experts(
    picks,
    rows,
    up_rows,
    ranks,
    weights,
    gate_w,
    up_w,
    down_w,
    pair_in,
    gate_out,
    up_out,
    down_in,
    down_out,
):
    sources, row_count, width = rows.shape
    hidden = gate_w.shape[1]
    adapters, rank = gate_out.shape[:2]
    token_spec = pl.BlockSpec((1,) + ranks.shape[1:], lambda s, _: (s, 0, 0))
    row_spec = pl.BlockSpec((1, row_count, width), lambda s, _: (s, 0, 0))

    def resident(array):
        return pl.BlockSpec(
            array.shape, lambda s, _: (0,) * array.ndim, pipeline_mode=pl.Buffered(1)
        )

    grads = [
        jax.ShapeDtypeStruct(shape, F32)
        for shape in (
            (adapters, 2 * rank, width),
            (adapters, rank, hidden),
            (adapters, rank, hidden),
            (adapters, rank, hidden),
            (adapters, rank, width),
        )
    ]
    return pl.pallas_call(
        functools.partial(experts_body, 256),
        grid_spec=pltpu.PrefetchScalarGridSpec(
            num_scalar_prefetch=1,
            grid=(sources,),
            in_specs=[row_spec, row_spec, token_spec, token_spec]
            + [
                resident(array)
                for array in (gate_w, up_w, down_w, pair_in, gate_out, up_out, down_in, down_out)
            ],
            out_specs=[row_spec, row_spec, token_spec]
            + [
                pl.BlockSpec(grad.shape, lambda s, _: (0, 0, 0), pipeline_mode=pl.Buffered(1))
                for grad in grads
            ],
            scratch_shapes=[
                pltpu.VMEM((row_count, hidden), F32),
                pltpu.VMEM((row_count, hidden), F32),
                pltpu.VMEM((row_count, hidden), BF16),
                pltpu.VMEM((row_count, width), BF16),
                pltpu.VMEM((row_count, hidden), BF16),
                pltpu.VMEM((row_count, hidden), BF16),
            ],
        ),
        out_shape=[
            jax.ShapeDtypeStruct(rows.shape, BF16),
            jax.ShapeDtypeStruct(rows.shape, BF16),
            jax.ShapeDtypeStruct(ranks.shape, F32),
        ]
        + grads,
        compiler_params=params(60),
        cost_estimate=pl.CostEstimate(
            flops=12 * sources * row_count * width * hidden,
            transcendentals=4 * sources * row_count * hidden,
            bytes_accessed=8 * sources * row_count * width + 6 * width * hidden,
        ),
        name="experts",
    )(
        picks,
        rows,
        up_rows,
        ranks,
        weights,
        gate_w,
        up_w,
        down_w,
        pair_in,
        gate_out,
        up_out,
        down_in,
        down_out,
    )


def per_device(
    tokens,
    segments,
    routes,
    adapter_index,
    cotangent,
    attn_gain,
    moe_gain,
    q_gain,
    key_norm_gain,
    w_query,
    key_projection_weight,
    value_projection_weight,
    w_out,
    w_router,
    expert_gate_weight,
    expert_up_weight,
    expert_down_weight,
    query_in,
    query_out,
    key_in,
    key_second_weight,
    value_in,
    value_second_weight,
    attn_in,
    attn_out,
    router_in,
    router_out,
    gate_in,
    gate_out,
    upward_in,
    upward_out,
    downward_in,
    downward_out,
):
    tensor_count = lax.axis_size("tensor")
    fsdp_count = lax.axis_size("fsdp")
    device_count = fsdp_count * tensor_count
    tensor_pos = lax.axis_index("tensor")
    fsdp_pos = lax.axis_index("fsdp")
    zero_pos = fsdp_pos * 0
    tok_rows, model_width = tokens.shape
    seq_rows = tok_rows * tensor_count
    rank = query_in.shape[2]
    adapter_count = query_in.shape[0]
    head_dim = q_gain.shape[0]
    local_cols = query_out.shape[2]
    local_kv_cols = key_second_weight.shape[2]
    expert_count = w_router.shape[1]
    top_count = routes.shape[1]
    capacity = 5 * tok_rows * top_count // (4 * expert_count)
    slots = -(-capacity // 16) * 16
    score_scale = 1.0 / math.sqrt(head_dim)
    adapter_pick = lax.dynamic_index_in_dim(adapter_index, fsdp_pos, 0, keepdims=False)

    def select_adapter(adapter_table):
        return lax.dynamic_index_in_dim(adapter_table, adapter_pick, 0, keepdims=False)

    def transposed(adapter_table):
        return jnp.swapaxes(adapter_table, -1, -2)

    input_first = jnp.concatenate(
        [select_adapter(transposed(table)) for table in (query_in, key_in, value_in)], axis=0
    )
    q_second = select_adapter(query_out)
    k_second = select_adapter(key_second_weight)
    v_second = select_adapter(value_second_weight)
    attention_first = select_adapter(transposed(attn_in))
    attention_second = select_adapter(attn_out)
    router_first = select_adapter(transposed(router_in))
    router_second = select_adapter(router_out)
    gain_attn = attn_gain.astype(F32)
    gain_moe = moe_gain.astype(F32)
    gain_query = q_gain.astype(F32)[None, :]
    gain_key = key_norm_gain.astype(F32)[None, :]

    packed_weights = lax.all_gather(
        jnp.concatenate(
            [w_query, key_projection_weight, value_projection_weight, w_router], axis=1
        ),
        "fsdp",
        axis=0,
        tiled=True,
    )
    linear_cols = local_cols + 2 * local_kv_cols
    complete_linear = packed_weights[:, :linear_cols]
    complete_router = packed_weights[:, linear_cols:]
    full_out = lax.all_gather(w_out, "fsdp", axis=1, tiled=True)
    sequence_tokens = lax.all_gather(tokens, "tensor", axis=0, tiled=True)
    sequence_routes = lax.all_gather(routes, "tensor", axis=0, tiled=True)
    sequence_cotangent = lax.all_gather(cotangent, "tensor", axis=0, tiled=True)
    plane_experts = jnp.arange(fsdp_count, dtype=jnp.int32) * tensor_count + tensor_pos
    route_blocks = sequence_routes.reshape(tensor_count, 1, tok_rows, top_count)
    plane_mask = jnp.any(route_blocks == plane_experts[None, :, None, None], axis=-1)
    plane_ranks = ranks_of(plane_mask)
    up_rows = plane_rows(
        to_slots(plane_ranks, sequence_cotangent, slots).reshape(
            fsdp_count, tensor_count * slots, model_width
        )
    )

    token_values = tokens.astype(F32)
    attn_normed, attn_factor = norm_forward(token_values, gain_attn)
    attention_narrow = attn_normed.astype(BF16)
    sequence_normalized = norm_forward(sequence_tokens.astype(F32), gain_attn)[0].astype(BF16)
    linear = matrix_product(sequence_normalized, complete_linear)
    low = flipped_right_operand(sequence_normalized, input_first).astype(BF16)
    tables = rope_tables(seq_rows, head_dim)
    seg_row = segments
    seg_column = jnp.transpose(segments, (1, 0))
    attention_operands = (
        linear,
        low,
        q_second,
        k_second,
        v_second,
        gain_query,
        gain_key,
        tables,
        seg_column,
        seg_row,
        score_scale,
    )
    heads_narrow = attention_forward(*attention_operands)
    attention_low = flipped_right_operand(heads_narrow, attention_first).astype(BF16)
    out_part = matrix_product(heads_narrow, full_out) + matrix_product(
        attention_low, attention_second
    )
    attention_total = lax.psum_scatter(
        out_part.astype(BF16), "tensor", scatter_dimension=0, tiled=True
    ).astype(F32)
    residual_stream = token_values + attention_total
    moe_normed, moe_factor = norm_forward(residual_stream, gain_moe)
    experts_narrow = moe_normed.astype(BF16)

    router_low = flipped_right_operand(experts_narrow, router_first).astype(BF16)
    router_logits = matrix_product(experts_narrow, complete_router) + matrix_product(
        router_low, router_second
    )
    expert_ids = jnp.arange(expert_count, dtype=jnp.int32)
    chosen = jnp.any(routes[:, :, None] == expert_ids[None, None, :], axis=1)
    chosen_logits = jnp.where(chosen, router_logits, -jnp.inf)
    chosen_exp = jnp.exp(chosen_logits - jnp.max(chosen_logits, axis=-1, keepdims=True))
    gate_weights = chosen_exp / jnp.sum(chosen_exp, axis=-1, keepdims=True)
    sent_weights = jnp.transpose(jnp.where(chosen, gate_weights, -1.0), (1, 0))
    own_weights = route_rows(sent_weights).reshape(fsdp_count, tensor_count, tok_rows)
    own_ranks = ranks_of(own_weights >= 0.0)

    sequence_experts = lax.all_gather(experts_narrow, "tensor", axis=0, tiled=True)
    expert_rows = plane_rows(
        to_slots(plane_ranks, sequence_experts, slots).reshape(
            fsdp_count, tensor_count * slots, model_width
        )
    )
    gate_in_t, upward_in_t = transposed(gate_in[0]), transposed(upward_in[0])
    (
        expert_output,
        rows_grad,
        gate_dots,
        pair_in_grad,
        gate_out_grad,
        upward_out_grad,
        downward_in_grad,
        downward_out_grad,
    ) = experts(
        adapter_index,
        expert_rows,
        up_rows,
        own_ranks,
        own_weights,
        expert_gate_weight[0],
        expert_up_weight[0],
        expert_down_weight[0],
        jnp.concatenate([gate_in_t, upward_in_t], axis=1),
        gate_out[0],
        upward_out[0],
        transposed(downward_in[0]),
        downward_out[0],
    )
    gate_grad = jnp.transpose(
        route_rows(gate_dots.reshape(device_count, tok_rows)), (1, 0)
    )

    def returned(slotted):
        combined = from_slots(
            plane_ranks,
            plane_rows(slotted).reshape(fsdp_count, tensor_count, slots, model_width),
        )
        return lax.psum_scatter(combined, "tensor", scatter_dimension=0, tiled=True).astype(F32)

    moe_grad = returned(rows_grad)
    output = (residual_stream + returned(expert_output)).astype(BF16)

    out_grad = cotangent.astype(F32)
    logit_gradient = (
        gate_weights * (gate_grad - jnp.sum(gate_weights * gate_grad, axis=-1, keepdims=True))
    ).astype(BF16)
    router_low_gradient = flipped_right_operand(logit_gradient, router_second).astype(BF16)
    moe_grad = (
        moe_grad
        + flipped_right_operand(logit_gradient, complete_router)
        + matrix_product(router_low_gradient, router_first)
    )
    router_first_gradient = flipped_left_operand(router_low_gradient, experts_narrow)
    router_second_gradient = flipped_left_operand(router_low, logit_gradient)
    residual_grad = out_grad + norm_backward(residual_stream, moe_factor, gain_moe, moe_grad)

    sequence_branch = lax.all_gather(
        residual_grad.astype(BF16), "tensor", axis=0, tiled=True
    )
    attention_low_grad = flipped_right_operand(sequence_branch, attention_second).astype(BF16)
    attention_second_gradient = flipped_left_operand(attention_low, sequence_branch)
    heads_grad = flipped_right_operand(sequence_branch, full_out)
    (
        q_grad,
        k_grad,
        v_grad,
        low_share,
        q_second_gradient,
        k_second_gradient,
        v_second_gradient,
        attention_first_gradient,
    ) = attention_backward(
        *attention_operands,
        heads_narrow,
        heads_grad,
        attention_low_grad,
        attention_first,
    )
    linear_grad = jnp.concatenate([q_grad, k_grad, v_grad], axis=1)
    normed_part = flipped_right_operand(linear_grad, complete_linear) + matrix_product(
        low_share, input_first
    )
    input_first_gradient = flipped_left_operand(low_share, sequence_normalized)
    normalized_gradient = lax.psum_scatter(
        normed_part.astype(BF16), "tensor", scatter_dimension=0, tiled=True
    ).astype(F32)
    input_grad = residual_grad + norm_backward(
        token_values, attn_factor, gain_attn, normalized_gradient
    )

    source_adapter = jnp.repeat(adapter_index, tensor_count)
    owner_onehot = (
        jnp.arange(adapter_count, dtype=jnp.int32)[:, None] == source_adapter[None, :]
    ).astype(BF16)

    def to_all(addend):
        lines = addend.shape[0]
        return jnp.transpose(
            addend.astype(BF16).reshape(lines, device_count, -1), (1, 0, 2)
        ).reshape(device_count, -1)

    def to_head_owners(addend):
        lines = addend.shape[0]
        pieces = jnp.transpose(
            addend.astype(BF16).reshape(lines, fsdp_count, -1), (1, 0, 2)
        ).reshape(fsdp_count, -1)
        holder = jnp.zeros((device_count, pieces.shape[1]), BF16)
        return lax.dynamic_update_slice(holder, pieces, (tensor_pos * fsdp_count, zero_pos))

    def owner_sums(parts):
        widths = [part.shape[1] for part in parts]
        total = matrix_product(owner_onehot, route_rows(jnp.concatenate(parts, axis=1)))
        pieces = []
        start = 0
        for width in widths:
            pieces.append(total[:, start : start + width])
            start += width
        return pieces

    early = owner_sums(
        [
            to_all(router_first_gradient),
            to_all(attention_second_gradient),
            to_all(router_second_gradient),
        ]
    )
    late = owner_sums(
        [
            to_all(input_first_gradient),
            to_head_owners(q_second_gradient),
            to_head_owners(k_second_gradient),
            to_head_owners(v_second_gradient),
            to_head_owners(attention_first_gradient),
        ]
    )

    def lines_of(piece, lines):
        return piece.reshape(adapter_count, lines, -1)

    first_sums = lines_of(late[0], 3 * rank)
    return (
        output,
        input_grad,
        transposed(first_sums[:, :rank]),
        lines_of(late[1], rank),
        transposed(first_sums[:, rank : 2 * rank]),
        lines_of(late[2], rank),
        transposed(first_sums[:, 2 * rank :]),
        lines_of(late[3], rank),
        transposed(lines_of(late[4], rank)),
        lines_of(early[1], rank),
        transposed(lines_of(early[0], rank)),
        lines_of(early[2], rank),
        transposed(pair_in_grad[:, :rank])[None],
        gate_out_grad[None],
        transposed(pair_in_grad[:, rank:])[None],
        upward_out_grad[None],
        transposed(downward_in_grad)[None],
        downward_out_grad[None],
    )


def solution(mesh):
    placed = (
        P(("fsdp", "tensor"), None),
        P("fsdp", None),
        P(("fsdp", "tensor"), None),
        P(),
        P(("fsdp", "tensor"), None),
        P(),
        P(),
        P(),
        P(),
        P("fsdp", "tensor"),
        P("fsdp", "tensor"),
        P("fsdp", "tensor"),
        P("tensor", "fsdp"),
        P("fsdp", None),
        P(("fsdp", "tensor"), None, None),
        P(("fsdp", "tensor"), None, None),
        P(("fsdp", "tensor"), None, None),
        P(),
        P(None, None, "tensor"),
        P(),
        P(None, None, "tensor"),
        P(),
        P(None, None, "tensor"),
        P(None, "tensor", None),
        P(),
        P(),
        P(),
        P(("fsdp", "tensor"), None, None, None),
        P(("fsdp", "tensor"), None, None, None),
        P(("fsdp", "tensor"), None, None, None),
        P(("fsdp", "tensor"), None, None, None),
        P(("fsdp", "tensor"), None, None, None),
        P(("fsdp", "tensor"), None, None, None),
    )
    return jax.shard_map(
        per_device,
        mesh=mesh,
        in_specs=placed,
        out_specs=(
            P(("fsdp", "tensor"), None),
            P(("fsdp", "tensor"), None),
            P(None, ("fsdp", "tensor"), None),
            P(None, None, ("fsdp", "tensor")),
            P(None, ("fsdp", "tensor"), None),
            P(None, None, ("fsdp", "tensor")),
            P(None, ("fsdp", "tensor"), None),
            P(None, None, ("fsdp", "tensor")),
            P(None, ("fsdp", "tensor"), None),
            P(None, None, ("fsdp", "tensor")),
            P(None, ("fsdp", "tensor"), None),
            P(None, None, ("fsdp", "tensor")),
            P(("fsdp", "tensor"), None, None, None),
            P(("fsdp", "tensor"), None, None, None),
            P(("fsdp", "tensor"), None, None, None),
            P(("fsdp", "tensor"), None, None, None),
            P(("fsdp", "tensor"), None, None, None),
            P(("fsdp", "tensor"), None, None, None),
        ),
        check_vma=False,
    )
```

time: 1750 us -> 1230 us (0.70)
  matrix products: 354 us -> 65.1 us
  waiting for transfers between devices: 939 us -> 689 us
  Pallas kernels: 0 us -> 215 us
  local copies, waits for them, and re-layouts: 168 us -> 33.1 us
  other arithmetic: 134 us -> 26.2 us
  blocking collectives: 101 us -> 143 us
    all_to_all x6 -> x3, waiting for transfers between devices: 753 us -> 21.6 us  [route_rows(): lax.all_to_all(block_rows, ('fsdp', 'tensor'), split_axis=0, concat_axis=...]
    pallas_call x0 -> x7, Pallas kernels: none -> 215 us  [the longest x1 128 us: experts(): pl.pallas_call(functools.partial(experts_body, 256), grid_spec=pltpu.Pref...]
    reduce_scatter x4, waiting for transfers between devices: 58.6 us -> 233 us  [the longest x2 144 us: returned(): lax.psum_scatter(combined, 'tensor', scatter_dimension=0, tiled=True)]
    dot_general x35 -> x11, matrix products: 203 us -> 29.8 us  [matrix_product(): return jnp.dot(first_op, second_op, preferred_element_type=F32)]
    all_to_all x0 -> x3, waiting for transfers between devices: none -> 154 us  [plane_rows(): lax.all_to_all(block_rows, 'fsdp', split_axis=0, concat_axis=0, tiled=True)]
    all_gather x4 -> x6, waiting for transfers between devices: 126 us -> 279 us  [the longest x1 74.2 us: per_device(): lax.all_gather(residual_grad.astype(BF16), 'tensor', axis=0, tiled=True)]
    all_to_all x0 -> x2, blocking collectives: none -> 131 us  [the longest x1 123 us: plane_rows(): lax.all_to_all(block_rows, 'fsdp', split_axis=0, concat_axis=0, tiled=True)]
    gather x5 -> x0, local copies, waits for them, and re-layouts: 90.3 us -> none  [the longest x1 24.6 us: per_device(): padded_grad[slot_entry].reshape(expert_count, capacity, model_width)]
  transfers between devices with their start and end apart: 14 -> 16, of which waited for: 10 -> 14; matrix products, arithmetic and copies ran while one was open for 20% -> 8% of each run, Pallas kernels for 0% -> 7%
where the time goes in v2:
time: 1230 us; the launch traced here: 1220 us
  waiting for transfers between devices  689 us (56%)
  Pallas kernels  215 us (17%)
  blocking collectives  143 us (12%)
  matrix products  65.1 us (5%)
  local copies, waits for them, and re-layouts  33.1 us (3%)
  starting transfers between devices  31.5 us (3%)
  other arithmetic  26.2 us (2%)
  between operations  17.3 us (1%)
    all_to_all x3, waiting for transfers between devices, plane_rows(): lax.all_to_all(block_rows, 'fsdp', split_axis=0, concat_axis=0, tiled=True)  154 us
    reduce_scatter x2, waiting for transfers between devices, returned(): lax.psum_scatter(combined, 'tensor', scatter_dimension=0, tiled=True)  144 us
    pallas_call x1, Pallas kernels, experts(): pl.pallas_call(functools.partial(experts_body, 256), grid_spec=pltpu.Pref...  128 us
    all_to_all x1, blocking collectives, plane_rows(): lax.all_to_all(block_rows, 'fsdp', split_axis=0, concat_axis=0, tiled=True)  123 us
    all_gather x1, waiting for transfers between devices, per_device(): lax.all_gather(residual_grad.astype(BF16), 'tensor', axis=0, tiled=True)  74.2 us
    all_gather x1, waiting for transfers between devices, per_device(): sequence_tokens = lax.all_gather(tokens, 'tensor', axis=0, tiled=True)  67 us
    reduce_scatter x1, waiting for transfers between devices, per_device(): lax.psum_scatter(out_part.astype(BF16), 'tensor', scatter_dimension=0, ti...  66.3 us
    all_gather x1, waiting for transfers between devices, per_device(): sequence_cotangent = lax.all_gather(cotangent, 'tensor', axis=0, tiled=True)  59.2 us
  transfers between devices with their start and end apart: 16, of which 14 were waited for; matrix products, arithmetic and copies ran while one was open for 8% of the time, Pallas kernels for 7%

profile of v2, /device:TPU:16, one launch (start us, length us, event | category | flops | bytes accessed | tf_op | source)
XLA Modules:
  0.0 1220.6 jit_solution(10898631734234444166)
XLA Ops:
  8.9 2.0 pad_maximum_fusion.1
  23.1 67.0 %all-gather.7.cloned.1.call-done = bf16[1024,2048]{1,0:T(8,128)(2,1)} async-done(((bf16[256,2048]{1,0:T(8,128)(2,1)}), bf16[1024,2048]{1,0:T(8,128)(2,1)}) %all-gather.7.cloned.1.call-update) | async-done | bytes 4194320 | tf_op jit(solution)/shard_map/all_gather | solution.py:814
  90.1 3.2 fusion
  94.8 41.0 %all-gather.9.cloned.1.call-done = bf16[2048,1312]{1,0:T(8,128)(2,1)} async-done(((bf16[256,1312]{1,0:T(8,128)(2,1)}), bf16[2048,1312]{1,0:T(8,128)(2,1)}) %all-gather.9.cloned.1.call-update) | async-done | bytes 5373968 | tf_op jit(solution)/shard_map/all_gather | solution.py:802
  135.9 9.4 fusion.5.lin_ref.key_lin_ref.value_lin_ref
  145.3 21.6 %attention_forward.1.heads_ref = bf16[1024,1024]{1,0:T(8,128)(2,1)S(1)} custom-call(f32[1024,1280]{1,0:T(8,128)S(1)} %fusion.5.lin_ref.key_lin_ref.value_lin_ref, f32[1024,1280]{1,0:T(8,128)S(1)} %fusion.5.lin_ref.key_lin_ref.value_lin_ref, f32[1024,1280]{1,0:T(8,128)S(1)} %fusion.5.lin_ref.key_lin_ref.value_lin_ref, ...), custom_call_target="tpu_custom_call" | custom-call | flops 2147483648 | bytes 6291456 | tf_op jit(solution)/shard_map/attention_forward/pallas_call | solution.py:173
  167.6 7.6 all-gather.11.cloned.1.call-done
  175.2 6.3 fusion.76
  181.5 3.3 add_convert_fusion.1
  185.5 11.4 all_gather.24
  197.3 59.2 %all-gather.15.cloned.1.call-done.rows_ref = bf16[1024,2048]{1,0:T(8,128)(2,1)} async-done(((bf16[256,2048]{1,0:T(8,128)(2,1)}), bf16[1024,2048]{1,0:T(8,128)(2,1)}) %all-gather.15.cloned.1.call-update) | async-done | bytes 4194320 | tf_op jit(solution)/shard_map/all_gather | solution.py:816
  256.5 2.2 copy-done.9
  258.6 5.5 to_slots.3
  264.2 5.3 all-to-all-start.1
  269.5 66.3 %reduce-scatter.5.cloned.1.call-done = bf16[256,2048]{1,0:T(8,128)(2,1)} async-done(((bf16[1024,2048]{1,0:T(8,128)(2,1)}), bf16[256,2048]{1,0:T(8,128)(2,1)}) %reduce-scatter.5.cloned.1.call-update) | async-done | bytes 1048592 | tf_op jit(solution)/shard_map/reduce_scatter | solution.py:854
  337.5 2.6 multiply_convert_fusion
  345.2 40.8 %all-to-all-done.1.up_rows_ref = bf16[8,320,2048]{2,1,0:T(8,128)(2,1)} async-done(((bf16[8,320,2048]{2,1,0:T(8,128)(2,1)}), bf16[8,320,2048]{2,1,0:T(8,128)(2,1)}, u32[]{:S(2)}, u32[]{:S(2)}) %all-to-all-start.1) | async-done | bytes 10485792 | tf_op jit(solution)/shard_map/all_to_all | solution.py:67
  386.0 4.4 all-to-all-start.2
  390.5 29.6 %all-gather.13.cloned.1.call-done.rows_ref = bf16[1024,2048]{1,0:T(8,128)(2,1)} async-done(((bf16[256,2048]{1,0:T(8,128)(2,1)}), bf16[1024,2048]{1,0:T(8,128)(2,1)}) %all-gather.13.cloned.1.call-update) | async-done | bytes 4194320 | tf_op jit(solution)/shard_map/all_gather | solution.py:874
  420.1 2.2 copy-done.10
  422.3 5.5 to_slots.2
  427.8 5.3 all-to-all-start
  433.4 2.1 pad_maximum_fusion.pair_in_ref
  436.4 113.3 %all-to-all-done.rows_ref = bf16[8,320,2048]{2,1,0:T(8,128)(2,1)} async-done(((bf16[8,320,2048]{2,1,0:T(8,128)(2,1)}), bf16[8,320,2048]{2,1,0:T(8,128)(2,1)}, u32[]{:S(2)}, u32[]{:S(2)}) %all-to-all-start) | async-done | bytes 10485792 | tf_op jit(solution)/shard_map/all_to_all | solution.py:67
  549.7 127.9 %experts.1 = (bf16[8,320,2048]{2,1,0:T(8,128)(2,1)}, bf16[8,320,2048]{2,1,0:T(8,128)(2,1)}, f32[8,4,256]{2,1,0:T(4,128)}, f32[8,32,2048]{2,1,0:T(8,128)}, f32[8,...) custom-call(s32[8]{0:T(128)} %pick_ref.1, ...), custom_call_target="tpu_custom_call" | custom-call | flops 48318382080 | bytes 51380224 | tf_op jit(solution)/shard_map/experts/pallas_call | solution.py:672
  677.6 122.6 %all_to_all.66 = bf16[8,320,2048]{2,1,0:T(8,128)(2,1)} all-to-all(bf16[8,320,2048]{2,1,0:T(8,128)(2,1)} %get-tuple-element.35), channel_id=1, replica_groups=mesh['fsdp'=8,'tensor'=4] {'fsdp'}, dimensions={0} | all-to-all | bytes 20971520 | tf_op jit(solution)/shard_map/all_to_all | solution.py:67
  800.1 6.7 from_slots.3
  806.9 2.0 copy-done.4
  809.7 8.7 all_to_all.67
  819.4 65.7 %reduce-scatter.9.cloned.1.call-done = bf16[256,2048]{1,0:T(8,128)(2,1)} async-done(((bf16[1024,2048]{1,0:T(8,128)(2,1)}), bf16[256,2048]{1,0:T(8,128)(2,1)}) %reduce-scatter.9.cloned.1.call-update) | async-done | bytes 1048592 | tf_op jit(solution)/shard_map/reduce_scatter | solution.py:914
  887.0 2.9 fusion.13
  892.9 5.2 all-to-all-start.3
  898.1 74.2 %all-gather.17.cloned.1.call-done = bf16[1024,2048]{1,0:T(8,128)(2,1)} async-done(((bf16[256,2048]{1,0:T(8,128)(2,1)}), bf16[1024,2048]{1,0:T(8,128)(2,1)}) %all-gather.17.cloned.1.call-update) | async-done | bytes 4194320 | tf_op jit(solution)/shard_map/all_gather | solution.py:933
  972.3 3.4 convolution_convert_fusion.4
  975.9 10.1 fusion.77.heads_grad_ref
  986.0 41.2 %attention_backward.1 = (bf16[1024,1024]{1,0:T(8,128)(2,1)S(1)}, bf16[1024,128]{1,0:T(8,128)(2,1)S(1)}, bf16[1024,128]{1,0:T(8,128)(2,1)S(1)}, bf16[1024,48]{1,0...) custom-call(f32[1024,1280]{1,0:T(8,128)} %copy-done.1, ...), custom_call_target="tpu_custom_call" | custom-call | flops 5368709120 | bytes 12582912 | tf_op jit(solution)/shard_map/attention_backward/pallas_call | solution.py:350
  1027.3 7.6 fusion.3
  1035.0 3.3 add_convert_fusion
  1038.4 6.7 from_slots.2
  1050.0 2.9 convolution_convert_fusion.1
  1055.3 5.5 all-to-all-start.7
  1060.9 3.5 convolution_convert_fusion
  1069.7 5.2 all-to-all-start.6
  1074.9 3.1 slice_bitcast_fusion
  1080.4 19.7 %all-to-all-done.6 = bf16[32,2,3840]{2,1,0:T(2,128)(2,1)S(1)} async-done(((bf16[32,2,3840]{2,1,0:T(2,128)(2,1)}), bf16[32,2,3840]{2,1,0:T(2,128)(2,1)S(1)}, u32[]{:S(2)}, u32[]{:S(2)}) %all-to-all-start.6) | async-done | bytes 491552 | tf_op jit(solution)/shard_map/all_to_all | solution.py:63
  1104.9 23.1 %reduce-scatter.11.cloned.1.call-done = bf16[256,2048]{1,0:T(8,128)(2,1)} async-done(((bf16[1024,2048]{1,0:T(8,128)(2,1)}), bf16[256,2048]{1,0:T(8,128)(2,1)}) %reduce-scatter.11.cloned.1.call-update) | async-done | bytes 1048592 | tf_op jit(solution)/shard_map/reduce_scatter | solution.py:960
  1129.6 77.9 %reduce-scatter.7.cloned.1.call-done = bf16[256,2048]{1,0:T(8,128)(2,1)} async-done(((bf16[1024,2048]{1,0:T(8,128)(2,1)}), bf16[256,2048]{1,0:T(8,128)(2,1)}) %reduce-scatter.7.cloned.1.call-update) | async-done | bytes 1048592 | tf_op jit(solution)/shard_map/reduce_scatter | solution.py:914
  1207.6 6.0 fusion.16
  (215 shorter events, 50.8 us)
Async XLA Ops:
  7.2 174.3 %copy-start = (bf16[8,16,2048]{2,1,0:T(8,128)(2,1)S(1)}, bf16[8,16,2048]{2,1,0:T(8,128)(2,1)}, u32[]{:S(2)}) copy-start(bf16[8,16,2048]{2,1,0:T(8,128)(2,1)} %param.57) | copy-start | bytes 1572868
  7.2 5.1 copy-start.41
  7.2 7.0 copy-start.37
  7.2 7.0 copy-start.11
  7.2 82.8 %all-gather.7.cloned.1.call-start = ((), (), s32[]{:S(2)}) async-start(), calls=%async_computation.12 | async-start | bytes 5242880 | tf_op jit(solution)/shard_map/all_gather | solution.py:814
  8.0 127.9 %all-gather.9.cloned.1.call-start = ((), (), s32[]{:S(2)}) async-start(), calls=%async_computation.13 | async-start | bytes 6488064 | tf_op jit(solution)/shard_map/all_gather | solution.py:802
  10.9 10.4 copy-start.43
  10.9 10.3 copy-start.44
  10.9 164.3 %all-gather.11.cloned.1.call-start = ((), (), s32[]{:S(2)}) async-start(), calls=%async_computation.14 | async-start | bytes 4718592 | tf_op jit(solution)/shard_map/all_gather | solution.py:813
  11.7 244.8 %all-gather.15.cloned.1.call-start = ((), (), s32[]{:S(2)}) async-start(), calls=%async_computation.17 | async-start | bytes 5242880 | tf_op jit(solution)/shard_map/all_gather | solution.py:816
  12.3 323.6 %reduce-scatter.5.cloned.1.call-start = ((), (), s32[]{:S(2)}) async-start(), calls=%async_computation.15 | async-start | bytes 5242880 | tf_op jit(solution)/shard_map/reduce_scatter | solution.py:854
  14.2 121.6 %copy-start.24 = (f32[2048]{0:T(1024)}, f32[2048]{0:T(1024)S(1)}, u32[]{:S(2)}) copy-start(f32[2048]{0:T(1024)S(1)} %convert_element_type.102) | copy-start | bytes 24580
  22.1 72.7 %copy-start.18 = (bf16[16,2048]{1,0:T(8,128)(2,1)}, bf16[16,2048]{1,0:T(8,128)(2,1)S(1)}, u32[]{:S(2)}) copy-start(bf16[16,2048]{1,0:T(8,128)(2,1)S(1)} %dynamic-slice_bitcast_fusion.2) | copy-start | bytes 196612
  23.0 71.8 %copy-start.20 = (bf16[16,2048]{1,0:T(8,128)(2,1)}, bf16[16,2048]{1,0:T(8,128)(2,1)S(1)}, u32[]{:S(2)}) copy-start(bf16[16,2048]{1,0:T(8,128)(2,1)S(1)} %get-tuple-element.183) | copy-start | bytes 196612
  23.1 71.8 %copy-start.22 = (bf16[16,2048]{1,0:T(8,128)(2,1)}, bf16[16,2048]{1,0:T(8,128)(2,1)S(1)}, u32[]{:S(2)}) copy-start(bf16[16,2048]{1,0:T(8,128)(2,1)S(1)} %get-tuple-element.184) | copy-start | bytes 196612
  93.3 42.6 %copy-start.39 = (f32[1024]{0:T(1024)}, f32[1024]{0:T(1024)S(1)}, u32[]{:S(2)}) copy-start(f32[1024]{0:T(1024)S(1)} %add_rsqrt_fusion) | copy-start | bytes 12292
  135.9 9.5 copy-start.5
  135.9 9.5 copy-start.7
  145.3 21.6 %copy-start.1 = (f32[1024,1280]{1,0:T(8,128)}, f32[1024,1280]{1,0:T(8,128)S(1)}, u32[]{:S(2)}) copy-start(f32[1024,1280]{1,0:T(8,128)S(1)} %fusion.5.lin_ref.key_lin_ref.value_lin_ref) | copy-start | bytes 15728644
  166.9 14.6 %copy-start.2 = (bf16[1024,1024]{1,0:T(8,128)(2,1)}, bf16[1024,1024]{1,0:T(8,128)(2,1)S(1)}, u32[]{:S(2)}) copy-start(bf16[1024,1024]{1,0:T(8,128)(2,1)S(1)} %attention_forward.1.heads_ref) | copy-start | bytes 6291460
  264.2 5.3 copy-start.38
  264.2 71.7 %copy-start.12 = (bf16[256,2048]{1,0:T(8,128)(2,1)S(1)}, bf16[256,2048]{1,0:T(8,128)(2,1)}, u32[]{:S(2)}) copy-start(bf16[256,2048]{1,0:T(8,128)(2,1)} %param.33) | copy-start | bytes 3145732
  264.2 121.8 %all-to-all-start.1 = ((bf16[8,320,2048]{2,1,0:T(8,128)(2,1)}), bf16[8,320,2048]{2,1,0:T(8,128)(2,1)}, u32[]{:S(2)}, u32[]{:S(2)}) async-start(bf16[8,320,2048]{2,1,0:T(8,128)(2,1)} %bitcast.201), calls=%async_computation.2 | async-start | bytes 20971520 | tf_op jit(solution)/shard_map/all_to_all | solution.py:67
  269.5 150.6 %all-gather.13.cloned.1.call-start = ((), (), s32[]{:S(2)}) async-start(), calls=%async_computation.16 | async-start | bytes 5242880 | tf_op jit(solution)/shard_map/all_gather | solution.py:874
  337.5 552.3 %copy-start.31 = (f32[256]{0:T(256)}, f32[256]{0:T(256)S(1)}, u32[]{:S(2)}) copy-start(f32[256]{0:T(256)S(1)} %get-tuple-element.175) | copy-start | bytes 3076
  341.8 86.0 %copy-start.26 = (bf16[256,16]{0,1:T(8,128)(2,1)}, bf16[256,16]{0,1:T(8,128)(2,1)S(1)}, u32[]{:S(2)}) copy-start(bf16[256,16]{0,1:T(8,128)(2,1)S(1)} %convolution_convert_fusion.7) | copy-start | bytes 24580
  386.0 41.8 %all-to-all-start.2 = ((f32[32,1,256]{2,1,0:T(1,128)}), f32[32,1,256]{2,1,0:T(1,128)S(1)}, u32[]{:S(2)}, u32[]{:S(2)}) async-start(f32[32,1,256]{2,1,0:T(1,128)} %copy.147), calls=%async_computation.3 | async-start | bytes 65536 | tf_op jit(solution)/shard_map/all_to_all | solution.py:63
  427.8 5.6 copy-start.17
  427.8 121.8 %all-to-all-start = ((bf16[8,320,2048]{2,1,0:T(8,128)(2,1)}), bf16[8,320,2048]{2,1,0:T(8,128)(2,1)}, u32[]{:S(2)}, u32[]{:S(2)}) async-start(bf16[8,320,2048]{2,1,0:T(8,128)(2,1)} %bitcast.202), calls=%async_computation.1 | async-start | bytes 20971520 | tf_op jit(solution)/shard_map/all_to_all | solution.py:67
  433.1 451.9 %reduce-scatter.9.cloned.1.call-start = ((), (), s32[]{:S(2)}) async-start(), calls=%async_computation.19 | async-start | bytes 5242880 | tf_op jit(solution)/shard_map/reduce_scatter | solution.py:914
  435.6 114.1 %copy-start.30 = (f32[8,4,256]{2,1,0:T(4,128)}, f32[8,4,256]{2,1,0:T(4,128)S(1)}, u32[]{:S(2)}) copy-start(f32[8,4,256]{2,1,0:T(4,128)S(1)} %reshape.199.weight_ref) | copy-start | bytes 98308
  809.0 163.4 %all-gather.17.cloned.1.call-start = ((), (), s32[]{:S(2)}) async-start(), calls=%async_computation.20 | async-start | bytes 5242880 | tf_op jit(solution)/shard_map/all_gather | solution.py:933
  892.9 145.5 %all-to-all-start.3 = ((bf16[8,320,2048]{2,1,0:T(8,128)(2,1)}), bf16[8,320,2048]{2,1,0:T(8,128)(2,1)}, u32[]{:S(2)}, u32[]{:S(2)}) async-start(bf16[8,320,2048]{2,1,0:T(8,128)(2,1)} %get-tuple-element.34), calls=%async_computation.4 | async-start | bytes 20971520 | tf_op jit(solution)/shard_map/all_to_all | solution.py:67
  898.1 229.9 %reduce-scatter.11.cloned.1.call-start = ((), (), s32[]{:S(2)}) async-start(), calls=%async_computation.21 | async-start | bytes 5242880 | tf_op jit(solution)/shard_map/reduce_scatter | solution.py:960
  975.9 10.2 copy-start.6
  975.9 10.1 copy-start.8
  1027.3 7.7 copy-start.19
  1027.3 7.7 copy-start.21
  1027.3 7.7 copy-start.23
  1038.3 169.2 %reduce-scatter.7.cloned.1.call-start = ((), (), s32[]{:S(2)}) async-start(), calls=%async_computation.18 | async-start | bytes 5242880 | tf_op jit(solution)/shard_map/reduce_scatter | solution.py:914
  1047.9 30.3 %copy-start.35 = (s32[32]{0:T(128)}, s32[32]{0:T(128)S(1)}, u32[]{:S(2)}) copy-start(s32[32]{0:T(128)S(1)} %eq.51) | copy-start | bytes 388
  1049.6 11.2 copy-start.25
  1049.7 11.2 copy-start.40
  1055.3 14.3 %all-to-all-start.7 = ((bf16[32,2,1032]{2,1,0:T(2,128)(2,1)}), bf16[32,2,1032]{2,1,0:T(2,128)(2,1)S(1)}, u32[]{:S(2)}, u32[]{:S(2)}) async-start(bf16[32,2,1032]{2,1,0:T(2,128)(2,1)} %reshape.232), calls=%async_computation.11 | async-start | bytes 294912 | tf_op jit(solution)/shard_map/all_to_all | solution.py:63
  1066.9 11.1 copy-start.36
  1069.7 30.4 %all-to-all-start.6 = ((bf16[32,2,3840]{2,1,0:T(2,128)(2,1)}), bf16[32,2,3840]{2,1,0:T(2,128)(2,1)S(1)}, u32[]{:S(2)}, u32[]{:S(2)}) async-start(bf16[32,2,3840]{2,1,0:T(2,128)(2,1)} %reshape.230), calls=%async_computation.10 | async-start | bytes 983040 | tf_op jit(solution)/shard_map/all_to_all | solution.py:63
  1078.4 129.2 %copy-start.32 = (f32[256]{0:T(256)S(1)}, f32[256]{0:T(256)}, u32[]{:S(2)}) copy-start(f32[256]{0:T(256)} %copy-done.31) | copy-start | bytes 3076
  1078.4 129.2 %copy-start.34 = (f32[256]{0:T(256)S(1)}, f32[256]{0:T(256)}, u32[]{:S(2)}) copy-start(f32[256]{0:T(256)} %copy-done.33) | copy-start | bytes 3076
  (13 other events, 29.4 us)
Sparse Core Ops, SparseCore 0:
  9.6 80.3 all-gather.6
  92.5 43.2 all-gather.8
  137.7 37.4 all-gather.10
  176.6 79.7 all-gather.14
  258.6 77.2 reduce-scatter.4
  340.3 79.7 all-gather.12
  809.1 75.9 reduce-scatter.8
  893.0 79.2 all-gather.16
  1038.4 89.4 reduce-scatter.10
  1130.2 77.2 reduce-scatter.6

commit v3 on v2

--- a/solution.py
+++ b/solution.py
@@ -432,17 +432,83 @@
     ).astype(BF16)
 
 
-def to_slots_body(rank_ref, rows_ref, out_ref):
-    experts, _, slots, width = out_ref.shape
+def to_slots_body(_block_ref, rank_ref, rows_ref, out_ref):
+    slots = out_ref.shape[1]
     chosen = matrix_product(slot_choice(rank_ref[0], slots), rows_ref[...])
     out_ref[...] = chosen.astype(BF16).reshape(out_ref.shape)
 
 
-def to_slots(ranks, rows, slots):
+def to_slots(block, ranks, rows, slots):
+    experts, tokens = ranks.shape[1:]
+    width = rows.shape[1]
+    half = width // 2
+    return pl.pallas_call(
+        to_slots_body,
+        grid_spec=pltpu.PrefetchScalarGridSpec(
+            num_scalar_prefetch=1,
+            grid=(2,),
+            in_specs=[
+                pl.BlockSpec((1, experts, tokens), lambda j, at: (at[0], 0, 0)),
+                pl.BlockSpec((tokens, half), lambda j, at: (0, j)),
+            ],
+            out_specs=pl.BlockSpec((experts, slots, half), lambda j, at: (0, 0, j)),
+        ),
+        out_shape=jax.ShapeDtypeStruct((experts, slots, width), BF16),
+        compiler_params=params(32),
+        cost_estimate=pl.CostEstimate(
+            flops=2 * experts * slots * tokens * width,
+            transcendentals=0,
+            bytes_accessed=2 * width * (experts * slots + tokens),
+        ),
+        name="to_slots",
+    )(block, ranks, rows)
+
+
+def from_slots_body(_block_ref, rank_ref, slot_ref, out_ref):
+    experts, slots, width = slot_ref.shape
+    choice = slot_choice(rank_ref[0], slots)
+    out_ref[...] = flipped_left_operand(
+        choice, slot_ref[...].reshape(experts * slots, width)
+    ).astype(BF16)
+
+
+def from_slots(block, ranks, slotted):
+    experts, tokens = ranks.shape[1:]
+    slots, width = slotted.shape[1:]
+    half = width // 2
+    return pl.pallas_call(
+        from_slots_body,
+        grid_spec=pltpu.PrefetchScalarGridSpec(
+            num_scalar_prefetch=1,
+            grid=(2,),
+            in_specs=[
+                pl.BlockSpec((1, experts, tokens), lambda j, at: (at[0], 0, 0)),
+                pl.BlockSpec((experts, slots, half), lambda j, at: (0, 0, j)),
+            ],
+            out_specs=pl.BlockSpec((tokens, half), lambda j, at: (0, j)),
+        ),
+        out_shape=jax.ShapeDtypeStruct((tokens, width), BF16),
+        compiler_params=params(32),
+        cost_estimate=pl.CostEstimate(
+            flops=2 * experts * slots * tokens * width,
+            transcendentals=0,
+            bytes_accessed=2 * width * (experts * slots + tokens),
+        ),
+        name="from_slots",
+    )(block, ranks, slotted)
+
+
+def all_to_slots_body(rank_ref, rows_ref, out_ref):
+    slots = out_ref.shape[2]
+    chosen = matrix_product(slot_choice(rank_ref[0], slots), rows_ref[...])
+    out_ref[...] = chosen.astype(BF16).reshape(out_ref.shape)
+
+
+def all_to_slots(ranks, rows, slots):
     blocks, experts, tokens = ranks.shape
     width = rows.shape[1]
     return pl.pallas_call(
-        to_slots_body,
+        all_to_slots_body,
         grid=(blocks,),
         out_shape=jax.ShapeDtypeStruct((experts, blocks, slots, width), BF16),
         in_specs=[
@@ -456,11 +522,11 @@
             transcendentals=0,
             bytes_accessed=2 * blocks * width * (experts * slots + tokens),
         ),
-        name="to_slots",
+        name="all_to_slots",
     )(ranks, rows)
 
 
-def from_slots_body(rank_ref, slot_ref, out_ref):
+def all_from_slots_body(_start_ref, rank_ref, slot_ref, out_ref):
     experts, _, slots, width = slot_ref.shape
     choice = slot_choice(rank_ref[0], slots)
     out_ref[...] = flipped_left_operand(
@@ -468,26 +534,29 @@
     ).astype(BF16)
 
 
-def from_slots(ranks, slotted):
+def all_from_slots(start, ranks, slotted):
     blocks, experts, tokens = ranks.shape
     slots, width = slotted.shape[2:]
     return pl.pallas_call(
-        from_slots_body,
-        grid=(blocks,),
+        all_from_slots_body,
+        grid_spec=pltpu.PrefetchScalarGridSpec(
+            num_scalar_prefetch=1,
+            grid=(blocks,),
+            in_specs=[
+                pl.BlockSpec((1, experts, tokens), lambda z, at: ((at[0] + z) % blocks, 0, 0)),
+                pl.BlockSpec((experts, 1, slots, width), lambda z, at: (0, z, 0, 0)),
+            ],
+            out_specs=pl.BlockSpec((tokens, width), lambda z, at: ((at[0] + z) % blocks, 0)),
+        ),
         out_shape=jax.ShapeDtypeStruct((blocks * tokens, width), BF16),
-        in_specs=[
-            pl.BlockSpec((1, experts, tokens), lambda z: (z, 0, 0)),
-            pl.BlockSpec((experts, 1, slots, width), lambda z: (0, z, 0, 0)),
-        ],
-        out_specs=pl.BlockSpec((tokens, width), lambda z: (z, 0)),
         compiler_params=params(40),
         cost_estimate=pl.CostEstimate(
             flops=2 * blocks * experts * slots * tokens * width,
             transcendentals=0,
             bytes_accessed=2 * blocks * width * (experts * slots + tokens),
         ),
-        name="from_slots",
-    )(ranks, slotted)
+        name="all_from_slots",
+    )(start, ranks, slotted)
 
 
 def ranks_of(mask):
@@ -498,229 +567,813 @@
     return jnp.where(mask, counts, -1.0).astype(jnp.int32)
 
 
-def experts_body(
-    tile,
-    pick_ref,
-    rows_ref,
-    up_rows_ref,
-    rank_ref,
-    weight_ref,
-    gate_w_ref,
-    up_w_ref,
-    down_w_ref,
-    pair_in_ref,
-    gate_out_ref,
-    up_out_ref,
-    down_in_ref,
-    down_out_ref,
-    y_ref,
-    rows_grad_ref,
-    gate_grad_ref,
-    pair_in_grad_ref,
-    gate_out_grad_ref,
-    up_out_grad_ref,
-    down_in_grad_ref,
-    down_out_grad_ref,
-    gate_scratch,
-    up_scratch,
-    inner_scratch,
-    route_scratch,
-    gate_lin_scratch,
-    up_lin_scratch,
+def tiles(width, tile, body):
+    @pl.loop(0, width // tile)
+    def _(j):
+        body(pl.ds(pl.multiple_of(j * tile, tile), tile))
+
+
+def expert_math(
+    tile, rows_ref, up_ref, ranks, weights, keep_dots, sent_y, mask_ref, tables, sums, scratch
 ):
-    step = pl.program_id(0)
-
-    @pl.when(step == 0)
-    def _():
-        for ref in (
-            pair_in_grad_ref,
-            gate_out_grad_ref,
-            up_out_grad_ref,
-            down_in_grad_ref,
-            down_out_grad_ref,
-        ):
-            ref[...] = jnp.zeros_like(ref)
-
-    pick = pick_ref[step]
-    row_count, width = rows_ref.shape[1:]
-    hidden = gate_w_ref.shape[1]
-    rank = gate_out_ref.shape[1]
-    blocks, tokens = rank_ref.shape[1:]
-    slots = row_count // blocks
-    places = lax.broadcasted_iota(jnp.int32, (slots, tokens), 0)
-    held = [places == rank_ref[0, z : z + 1, :] for z in range(blocks)]
+    gate_w, up_w, down_w, pair_in, gate_out, up_out, down_in, down_out = tables
+    pair_in_sum, gate_out_sum, up_out_sum, down_in_sum, down_out_sum = sums
+    gate_lin_ref, up_lin_ref, inner_ref, route_ref, gate_grad_ref, up_grad_ref = scratch
+    sources, slots, width = rows_ref.shape
+    row_count = sources * slots
+    hidden = gate_w.shape[1]
+    broad = gate_out.shape[0]
+    places = lax.broadcasted_iota(jnp.int32, (slots, ranks.shape[1]), 0)
+
+    def held(source):
+        return places == ranks[source : source + 1, :]
+
+    def all_rows():
+        return rows_ref[...].reshape(row_count, width)
+
+    def pair_mask():
+        mask = mask_ref[...].astype(F32)
+        return jnp.concatenate([mask, mask], axis=1)
+
     weight = jnp.concatenate(
         [
-            jnp.sum(jnp.where(held[z], weight_ref[0, z : z + 1, :], 0.0), axis=1, keepdims=True)
-            for z in range(blocks)
+            jnp.sum(
+                jnp.where(held(source), weights[source : source + 1, :], 0.0),
+                axis=1,
+                keepdims=True,
+            )
+            for source in range(sources)
         ],
         axis=0,
     )
-    rows = rows_ref[0]
-    pair = flipped_right_operand(rows, pair_in_ref[pick]).astype(BF16)
-    gate_low, up_low = pair[:, :rank], pair[:, rank:]
-
-    @pl.loop(0, hidden // tile)
-    def _(j):
-        columns = pl.ds(pl.multiple_of(j * tile, tile), tile)
-        gate_lin = matrix_product(rows, gate_w_ref[:, columns]) + matrix_product(
-            gate_low, gate_out_ref[pick, :, columns]
-        )
-        up_lin = matrix_product(rows, up_w_ref[:, columns]) + matrix_product(
-            up_low, up_out_ref[pick, :, columns]
-        )
-        gate_scratch[:, columns] = gate_lin
-        up_scratch[:, columns] = up_lin
-        inner_scratch[:, columns] = (gate_lin * jax.nn.sigmoid(gate_lin) * up_lin).astype(BF16)
-
-    inner = inner_scratch[...]
-    down_low = flipped_right_operand(inner, down_in_ref[pick]).astype(BF16)
+    pair = (flipped_right_operand(all_rows(), pair_in[...]) * pair_mask()).astype(BF16)
+    gate_low, up_low = pair[:, :broad], pair[:, broad:]
+
+    def inner_step(columns):
+        rows = all_rows()
+        gate_lin = matrix_product(rows, gate_w[:, columns]) + matrix_product(
+            gate_low, gate_out[:, columns]
+        )
+        up_lin = matrix_product(rows, up_w[:, columns]) + matrix_product(
+            up_low, up_out[:, columns]
+        )
+        gate_lin_ref[:, columns] = gate_lin
+        up_lin_ref[:, columns] = up_lin
+        inner_ref[:, columns] = (gate_lin * jax.nn.sigmoid(gate_lin) * up_lin).astype(BF16)
+
+    tiles(hidden, tile, inner_step)
+    down_low = (
+        flipped_right_operand(inner_ref[...], down_in[...]) * mask_ref[...].astype(F32)
+    ).astype(BF16)
 
     def down_step(j, total):
         columns = pl.ds(pl.multiple_of(j * tile, tile), tile)
         result = (
-            matrix_product(inner, down_w_ref[:, columns])
-            + matrix_product(down_low, down_out_ref[pick, :, columns])
+            matrix_product(inner_ref[...], down_w[:, columns])
+            + matrix_product(down_low, down_out[:, columns])
         ).astype(BF16)
         wide = result.astype(F32)
-        upstream = up_rows_ref[0, :, columns].astype(F32)
-        y_ref[0, :, columns] = (weight * wide).astype(BF16)
-        route_scratch[:, columns] = (weight * upstream).astype(BF16)
+        upstream = up_ref[:, :, columns].reshape(row_count, tile).astype(F32)
+        up_ref[:, :, columns] = (weight * wide).astype(BF16).reshape(sources, slots, tile)
+        route_ref[:, columns] = (weight * upstream).astype(BF16)
         return total + jnp.sum(upstream * wide, axis=1, keepdims=True)
 
-    gate_grad = lax.fori_loop(
-        0, width // tile, down_step, jnp.zeros((row_count, 1), F32)
-    )
-    for z in range(blocks):
-        gate_grad_ref[0, z : z + 1, :] = jnp.sum(
-            jnp.where(held[z], gate_grad[z * slots : (z + 1) * slots], 0.0),
-            axis=0,
-            keepdims=True,
-        )
-    route = route_scratch[...]
-    down_low_grad = flipped_right_operand(route, down_out_ref[pick]).astype(BF16)
-    down_in_grad_ref[pick] += flipped_left_operand(down_low_grad, inner)
-    down_out_grad_ref[pick] += flipped_left_operand(down_low, route)
-
-    @pl.loop(0, hidden // tile)
-    def _(j):
-        columns = pl.ds(pl.multiple_of(j * tile, tile), tile)
-        inner_grad = flipped_right_operand(route, down_w_ref[columns, :]) + matrix_product(
-            down_low_grad, down_in_ref[pick, :, columns]
-        )
-        gate_lin, up_lin = gate_scratch[:, columns], up_scratch[:, columns]
+    gate_dots = lax.fori_loop(0, width // tile, down_step, jnp.zeros((row_count, 1), F32))
+    sent_y()
+    for source in range(sources):
+        keep_dots(
+            source,
+            jnp.sum(
+                jnp.where(held(source), gate_dots[source * slots : (source + 1) * slots], 0.0),
+                axis=0,
+                keepdims=True,
+            ),
+        )
+    down_low_grad = (
+        flipped_right_operand(route_ref[...], down_out[...]) * mask_ref[...].astype(F32)
+    ).astype(BF16)
+    down_in_sum[...] += flipped_left_operand(down_low_grad, inner_ref[...])
+
+    def down_out_step(columns):
+        down_out_sum[:, columns] += flipped_left_operand(down_low, route_ref[:, columns])
+
+    tiles(width, 2 * tile, down_out_step)
+
+    def inner_grad_step(columns):
+        inner_grad = flipped_right_operand(route_ref[...], down_w[columns, :]) + matrix_product(
+            down_low_grad, down_in[:, columns]
+        )
+        gate_lin, up_lin = gate_lin_ref[:, columns], up_lin_ref[:, columns]
         sig = jax.nn.sigmoid(gate_lin)
-        gate_lin_scratch[:, columns] = (
+        gate_grad_ref[:, columns] = (
             inner_grad * up_lin * (sig * (1.0 + gate_lin * (1.0 - sig)))
         ).astype(BF16)
-        up_lin_scratch[:, columns] = (inner_grad * (gate_lin * sig)).astype(BF16)
-
-    gate_lin_grad, up_lin_grad = gate_lin_scratch[...], up_lin_scratch[...]
-    gate_low_grad = flipped_right_operand(gate_lin_grad, gate_out_ref[pick]).astype(BF16)
-    up_low_grad = flipped_right_operand(up_lin_grad, up_out_ref[pick]).astype(BF16)
-    gate_out_grad_ref[pick] += flipped_left_operand(gate_low, gate_lin_grad)
-    up_out_grad_ref[pick] += flipped_left_operand(up_low, up_lin_grad)
-    pair_grad = jnp.concatenate([gate_low_grad, up_low_grad], axis=1)
-    pair_in_grad_ref[pick] += flipped_left_operand(pair_grad, rows)
-
-    @pl.loop(0, width // tile)
-    def _(j):
-        columns = pl.ds(pl.multiple_of(j * tile, tile), tile)
-        rows_grad_ref[0, :, columns] = (
-            flipped_right_operand(gate_lin_grad, gate_w_ref[columns, :])
-            + flipped_right_operand(up_lin_grad, up_w_ref[columns, :])
-            + matrix_product(pair_grad, pair_in_ref[pick, :, columns])
-        ).astype(BF16)
-
-
-def experts(
-    picks,
-    rows,
-    up_rows,
-    ranks,
-    weights,
-    gate_w,
-    up_w,
-    down_w,
-    pair_in,
-    gate_out,
-    up_out,
-    down_in,
-    down_out,
-):
-    sources, row_count, width = rows.shape
-    hidden = gate_w.shape[1]
-    adapters, rank = gate_out.shape[:2]
-    token_spec = pl.BlockSpec((1,) + ranks.shape[1:], lambda s, _: (s, 0, 0))
-    row_spec = pl.BlockSpec((1, row_count, width), lambda s, _: (s, 0, 0))
+        up_grad_ref[:, columns] = (inner_grad * (gate_lin * sig)).astype(BF16)
+
+    tiles(hidden, tile, inner_grad_step)
+    pair_grad = (
+        jnp.concatenate(
+            [
+                flipped_right_operand(gate_grad_ref[...], gate_out[...]),
+                flipped_right_operand(up_grad_ref[...], up_out[...]),
+            ],
+            axis=1,
+        )
+        * pair_mask()
+    ).astype(BF16)
+    gate_out_sum[...] += flipped_left_operand(gate_low, gate_grad_ref[...])
+    up_out_sum[...] += flipped_left_operand(up_low, up_grad_ref[...])
+
+    def rows_grad_step(columns):
+        before = rows_ref[:, :, columns].reshape(row_count, tile)
+        pair_in_sum[:, columns] += flipped_left_operand(pair_grad, before)
+        rows_ref[:, :, columns] = (
+            (
+                flipped_right_operand(gate_grad_ref[...], gate_w[columns, :])
+                + flipped_right_operand(up_grad_ref[...], up_w[columns, :])
+                + matrix_product(pair_grad, pair_in[:, columns])
+            )
+            .astype(BF16)
+            .reshape(sources, slots, tile)
+        )
+
+    tiles(width, tile, rows_grad_step)
+
+
+def expert_sums(tables):
+    gate_w, _up_w, _down_w, pair_in, gate_out, _up_out, down_in, down_out = tables
+    return [
+        jax.ShapeDtypeStruct(table.shape, F32)
+        for table in (pair_in, gate_out, gate_out, down_in, down_out)
+    ]
+
+
+def expert_scratch(row_count, hidden, width):
+    return [
+        pltpu.VMEM((row_count, hidden), F32),
+        pltpu.VMEM((row_count, hidden), F32),
+        pltpu.VMEM((row_count, hidden), BF16),
+        pltpu.VMEM((row_count, width), BF16),
+        pltpu.VMEM((row_count, hidden), BF16),
+        pltpu.VMEM((row_count, hidden), BF16),
+    ]
+
+
+def experts_body(_block_ref, rows_in, up_in, rank_ref, weight_ref, mask_ref, *rest):
+    tables, sums_before, rest = rest[:8], rest[8:13], rest[13:]
+    y_ref, rows_grad_ref, dots_ref = rest[:3]
+    sums, rest = rest[3:8], rest[8:]
+    for total, before in zip(sums, sums_before):
+        total[...] = before[...]
+    rows_grad_ref[...] = rows_in[...]
+    y_ref[...] = up_in[...]
+
+    def keep_dots(source, dots):
+        dots_ref[source : source + 1, :] = dots
+
+    expert_math(
+        256,
+        rows_grad_ref,
+        y_ref,
+        rank_ref[0],
+        weight_ref[0],
+        keep_dots,
+        lambda: None,
+        mask_ref,
+        tables,
+        sums,
+        rest,
+    )
+
+
+def experts(block, rows, up_rows, ranks, weights, mask, tables, sums_before):
+    sources, slots, width = rows.shape
+    hidden = tables[0].shape[1]
+    tokens = ranks.shape[2]
+    token_spec = pl.BlockSpec((1, sources, tokens), lambda _, at: (at[0], 0, 0))
 
     def resident(array):
         return pl.BlockSpec(
-            array.shape, lambda s, _: (0,) * array.ndim, pipeline_mode=pl.Buffered(1)
-        )
-
-    grads = [
-        jax.ShapeDtypeStruct(shape, F32)
-        for shape in (
-            (adapters, 2 * rank, width),
-            (adapters, rank, hidden),
-            (adapters, rank, hidden),
-            (adapters, rank, hidden),
-            (adapters, rank, width),
-        )
-    ]
+            array.shape, lambda *_: (0,) * len(array.shape), pipeline_mode=pl.Buffered(1)
+        )
+
+    sums = expert_sums(tables)
+    outs = [
+        jax.ShapeDtypeStruct(rows.shape, BF16),
+        jax.ShapeDtypeStruct(rows.shape, BF16),
+        jax.ShapeDtypeStruct((sources, tokens), F32),
+    ] + sums
+    operands = [rows, up_rows, ranks, weights, mask, *tables, *sums_before]
+    specs = (
+        [resident(rows), resident(up_rows), token_spec, token_spec, resident(mask)]
+        + [resident(table) for table in tables]
+        + [resident(each) for each in sums_before]
+    )
     return pl.pallas_call(
-        functools.partial(experts_body, 256),
+        experts_body,
         grid_spec=pltpu.PrefetchScalarGridSpec(
             num_scalar_prefetch=1,
-            grid=(sources,),
-            in_specs=[row_spec, row_spec, token_spec, token_spec]
-            + [
-                resident(array)
-                for array in (gate_w, up_w, down_w, pair_in, gate_out, up_out, down_in, down_out)
-            ],
-            out_specs=[row_spec, row_spec, token_spec]
-            + [
-                pl.BlockSpec(grad.shape, lambda s, _: (0, 0, 0), pipeline_mode=pl.Buffered(1))
-                for grad in grads
-            ],
-            scratch_shapes=[
-                pltpu.VMEM((row_count, hidden), F32),
-                pltpu.VMEM((row_count, hidden), F32),
-                pltpu.VMEM((row_count, hidden), BF16),
-                pltpu.VMEM((row_count, width), BF16),
-                pltpu.VMEM((row_count, hidden), BF16),
-                pltpu.VMEM((row_count, hidden), BF16),
-            ],
+            grid=(1,),
+            in_specs=specs,
+            out_specs=[resident(out) for out in outs],
+            scratch_shapes=expert_scratch(sources * slots, hidden, width),
         ),
-        out_shape=[
-            jax.ShapeDtypeStruct(rows.shape, BF16),
-            jax.ShapeDtypeStruct(rows.shape, BF16),
-            jax.ShapeDtypeStruct(ranks.shape, F32),
-        ]
-        + grads,
-        compiler_params=params(60),
-        cost_estimate=pl.CostEstimate(
-            flops=12 * sources * row_count * width * hidden,
-            transcendentals=4 * sources * row_count * hidden,
-            bytes_accessed=8 * sources * row_count * width + 6 * width * hidden,
-        ),
+        out_shape=outs,
+        input_output_aliases={
+            1 + len(operands) - len(sums) + at: 3 + at for at in range(len(sums))
+        },
+        compiler_params=params(63),
         name="experts",
-    )(
-        picks,
+    )(block, *operands)
+
+
+def moe_body(
+    plane,
+    line,
+    own_ref,
+    up_hbm,
+    plane_rank_ref,
+    rank_ref,
+    weight_ref,
+    mask_ref,
+    *rest,
+):
+    tables_hbm, rest = rest[:8], rest[8:]
+    total_ref, dots_ref, y_hbm, back_hbm = rest[:4]
+    sums, rest = rest[4:9], rest[9:]
+    tables, rest = rest[:8], rest[8:]
+    (
+        blocks,
+        partials,
+        partials_in,
+        sent_slots,
         rows,
         up_rows,
-        ranks,
-        weights,
-        gate_w,
-        up_w,
-        down_w,
-        pair_in,
-        gate_out,
-        up_out,
-        down_in,
-        down_out,
-    )
+        back_rows,
+        choice,
+        dots,
+        dots_back,
+        dots_pass,
+        dots_in,
+    ) = rest[:12]
+    scratch, rest = rest[12:18], rest[18:]
+    (
+        table_sem,
+        up_sem,
+        y_sem,
+        back_sem,
+        own_sem,
+        block_send,
+        block_recv,
+        row_send,
+        row_recv,
+        back_send,
+        back_recv,
+        partial_send,
+        partial_recv,
+        dots_send,
+        dots_recv,
+        dots_in_send,
+        dots_in_recv,
+    ) = rest
+    width = own_ref.shape[1]
+    slots = rows.shape[2]
+    tile = 256
+    me, at_line = lax.axis_index("fsdp"), lax.axis_index("tensor")
+
+    barrier = pltpu.get_barrier_semaphore()
+
+    @pl.loop(1, plane)
+    def _(d):
+        pl.semaphore_signal(barrier, inc=1, device_id={"fsdp": lax.rem(me + d, plane)})
+
+    @pl.loop(1, line)
+    def _(d):
+        pl.semaphore_signal(barrier, inc=1, device_id={"tensor": lax.rem(at_line + d, line)})
+
+    pl.semaphore_wait(barrier, plane + line - 2)
+
+    def block_copy(r):
+        return pltpu.make_async_remote_copy(
+            src_ref=own_ref,
+            dst_ref=blocks.at[r],
+            send_sem=block_send.at[r - 1],
+            recv_sem=block_recv.at[r - 1],
+            device_id={"tensor": lax.rem(at_line + line - r, line)},
+        )
+
+    def row_copy(r, d):
+        target = lax.rem(me + d, plane)
+        return pltpu.make_async_remote_copy(
+            src_ref=sent_slots.at[lax.rem(r, 2), target],
+            dst_ref=rows.at[r, me],
+            send_sem=row_send.at[r, d],
+            recv_sem=row_recv.at[r, d],
+            device_id={"fsdp": target},
+        )
+
+    def own_rows(r):
+        return pltpu.make_async_copy(
+            sent_slots.at[lax.rem(r, 2), me], rows.at[r, me], own_sem.at[0]
+        )
+
+    def back_copy(r, d):
+        target = lax.rem(me + d, plane)
+        return pltpu.make_async_remote_copy(
+            src_ref=rows.at[r, target],
+            dst_ref=back_hbm.at[r, me],
+            send_sem=back_send.at[r, d],
+            recv_sem=back_recv.at[r, d],
+            device_id={"fsdp": target},
+        )
+
+    def own_back(r):
+        return pltpu.make_async_copy(rows.at[r, me], back_hbm.at[r, me], own_sem.at[1])
+
+    def dots_copy(r, d):
+        target = lax.rem(me + d, plane)
+        return pltpu.make_async_remote_copy(
+            src_ref=dots.at[r, target],
+            dst_ref=dots_back.at[r, me],
+            send_sem=dots_send.at[r, d],
+            recv_sem=dots_recv.at[r, d],
+            device_id={"fsdp": target},
+        )
+
+    def dots_in_copy(r):
+        return pltpu.make_async_remote_copy(
+            src_ref=dots_pass.at[r],
+            dst_ref=dots_in.at[r],
+            send_sem=dots_in_send.at[r - 1],
+            recv_sem=dots_in_recv.at[r - 1],
+            device_id={"tensor": lax.rem(at_line + r, line)},
+        )
+
+    def partial_copy(r):
+        return pltpu.make_async_remote_copy(
+            src_ref=partials.at[r - 1],
+            dst_ref=partials_in.at[r - 1],
+            send_sem=partial_send.at[r - 1],
+            recv_sem=partial_recv.at[r - 1],
+            device_id={"tensor": lax.rem(at_line + r, line)},
+        )
+
+    def up_copy(r):
+        return pltpu.make_async_copy(
+            up_hbm.at[:, lax.rem(at_line + r, line)], up_rows, up_sem
+        )
+
+    def y_copy(r):
+        return pltpu.make_async_copy(up_rows, y_hbm.at[:, r], y_sem)
+
+    @pl.loop(1, line)
+    def _(r):
+        block_copy(r).start()
+
+    first_block = pltpu.make_async_copy(own_ref, blocks.at[0], own_sem.at[2])
+    first_block.start()
+    up_copy(0).start()
+    table_copies = [
+        pltpu.make_async_copy(source, target, table_sem.at[at])
+        for at, (source, target) in enumerate(zip(tables_hbm, tables))
+    ]
+    for each in table_copies:
+        each.start()
+    for total in sums:
+        total[...] = jnp.zeros_like(total)
+    first_block.wait()
+
+    @pl.loop(0, line + 2)
+    def _(step):
+        @pl.when(step < line)
+        def _():
+            @pl.when(step > 0)
+            def _():
+                block_copy(step).wait_recv()
+
+            @pl.when(step > 1)
+            def _():
+                @pl.loop(1, plane)
+                def _(d):
+                    row_copy(step - 2, d).wait_send()
+
+            choice[...] = slot_choice(plane_rank_ref[lax.rem(at_line + step, line)], slots)
+
+            def slot_step(columns):
+                sent_slots[lax.rem(step, 2), :, :, columns] = (
+                    matrix_product(choice[...], blocks[step, :, columns])
+                    .astype(BF16)
+                    .reshape(plane, slots, 2 * tile)
+                )
+
+            tiles(width, 2 * tile, slot_step)
+
+            @pl.loop(1, plane)
+            def _(d):
+                row_copy(step, d).start()
+
+        @pl.when((step >= 1) & (step <= line))
+        def _():
+            r = step - 1
+            block = lax.rem(at_line + r, line)
+
+            @pl.when(r == 0)
+            def _():
+                for each in table_copies:
+                    each.wait()
+
+            own_rows(r).start()
+            own_rows(r).wait()
+
+            @pl.loop(1, plane)
+            def _(d):
+                row_copy(r, d).wait_recv()
+
+            up_copy(r).wait()
+
+            def keep_dots(source, values):
+                dots[r, source] = jnp.broadcast_to(values, (8, values.shape[1]))
+
+            expert_math(
+                tile,
+                rows.at[r],
+                up_rows,
+                rank_ref[block],
+                weight_ref[block],
+                keep_dots,
+                lambda: y_copy(r).start(),
+                mask_ref,
+                tables,
+                sums,
+                scratch,
+            )
+
+            @pl.loop(1, plane)
+            def _(d):
+                dots_copy(r, d).start()
+                back_copy(r, d).start()
+
+            own_back(r).start()
+            dots_back[r, me] = dots[r, me]
+            y_copy(r).wait()
+
+            @pl.when(r + 1 < line)
+            def _():
+                up_copy(r + 1).start()
+
+            own_back(r).wait()
+
+        @pl.when(step >= 2)
+        def _():
+            r = step - 2
+
+            @pl.loop(1, plane)
+            def _(d):
+                dots_copy(r, d).wait_recv()
+                back_copy(r, d).wait_recv()
+
+            dots_pass[r] = dots_back[r, :, 0, :]
+            load = pltpu.make_async_copy(back_hbm.at[r], back_rows, back_sem)
+            load.start()
+            choice[...] = slot_choice(plane_rank_ref[lax.rem(at_line + r, line)], slots)
+            load.wait()
+
+            def combined(columns):
+                return flipped_left_operand(
+                    choice[...], back_rows[:, :, columns].reshape(plane * slots, 2 * tile)
+                )
+
+            @pl.when(r == 0)
+            def _():
+                def keep(columns):
+                    total_ref[:, columns] = combined(columns)
+
+                tiles(width, 2 * tile, keep)
+                dots_ref[at_line] = dots_pass[0]
+
+            @pl.when(r > 0)
+            def _():
+                def pass_on(columns):
+                    partials[r - 1, :, columns] = combined(columns).astype(BF16)
+
+                dots_in_copy(r).start()
+                tiles(width, 2 * tile, pass_on)
+                partial_copy(r).start()
+
+    @pl.loop(1, line)
+    def _(r):
+        dots_in_copy(r).wait_recv()
+        dots_ref[lax.rem(at_line + line - r, line)] = dots_in[r]
+        partial_copy(r).wait_recv()
+        total_ref[...] += partials_in[r - 1].astype(F32)
+
+    @pl.loop(1, line)
+    def _(r):
+        partial_copy(r).wait_send()
+        dots_in_copy(r).wait_send()
+        block_copy(r).wait_send()
+
+    @pl.loop(1, plane)
+    def _(d):
+        row_copy(line - 2, d).wait_send()
+        row_copy(line - 1, d).wait_send()
+
+    @pl.loop(0, line)
+    def _(r):
+        @pl.loop(1, plane)
+        def _(d):
+            back_copy(r, d).wait_send()
+            dots_copy(r, d).wait_send()
+
+
+def moe_layer(own, up_rows, plane_ranks, ranks, weights, mask, tables, identity):
+    line, plane, tokens = plane_ranks.shape
+    slots, width = up_rows.shape[2:]
+    hidden = tables[0].shape[1]
+    sums = expert_sums(tables)
+    anywhere = pl.BlockSpec(memory_space=pl.ANY)
+    local = pl.BlockSpec(memory_space=pltpu.VMEM)
+    grouped = (plane, slots, width)
+    dma = pltpu.SemaphoreType.DMA
+    return pl.pallas_call(
+        functools.partial(moe_body, plane, line),
+        out_shape=[
+            jax.ShapeDtypeStruct((tokens, width), F32),
+            jax.ShapeDtypeStruct((line, plane, tokens), F32),
+            jax.ShapeDtypeStruct((plane, line, slots, width), BF16),
+            jax.ShapeDtypeStruct((line,) + grouped, BF16),
+        ]
+        + sums,
+        in_specs=[anywhere, anywhere, local, local, local, local] + [anywhere] * len(tables),
+        out_specs=[local, local, anywhere, anywhere] + [local] * len(sums),
+        scratch_shapes=[pltpu.VMEM(table.shape, table.dtype) for table in tables]
+        + [
+            pltpu.VMEM((line, tokens, width), BF16),
+            pltpu.VMEM((line - 1, tokens, width), BF16),
+            pltpu.VMEM((line - 1, tokens, width), BF16),
+            pltpu.VMEM((2,) + grouped, BF16),
+            pltpu.VMEM((line,) + grouped, BF16),
+            pltpu.VMEM(grouped, BF16),
+            pltpu.VMEM(grouped, BF16),
+            pltpu.VMEM((plane * slots, tokens), BF16),
+            pltpu.VMEM((line, plane, 8, tokens), F32),
+            pltpu.VMEM((line, plane, 8, tokens), F32),
+            pltpu.VMEM((line, plane, tokens), F32),
+            pltpu.VMEM((line, plane, tokens), F32),
+        ]
+        + expert_scratch(plane * slots, hidden, width)
+        + [dma((len(tables),)), dma, dma, dma, dma((3,))]
+        + [dma((line - 1,))] * 2
+        + [dma((line, plane))] * 4
+        + [dma((line - 1,))] * 2
+        + [dma((line, plane))] * 2
+        + [dma((line - 1,))] * 2,
+        compiler_params=pltpu.CompilerParams(
+            collective_id=identity, has_side_effects=True, vmem_limit_bytes=63 * MEBI
+        ),
+        name="moe_layer",
+    )(own, up_rows, plane_ranks, ranks, weights, mask, *tables)
+
+
+def greet_line(me, count):
+    barrier = pltpu.get_barrier_semaphore()
+
+    @pl.when(me > 0)
+    def _():
+        pl.semaphore_signal(barrier, inc=1, device_id={"tensor": me - 1})
+
+    @pl.when(me < count - 1)
+    def _():
+        pl.semaphore_signal(barrier, inc=1, device_id={"tensor": me + 1})
+
+    @pl.when((me > 0) & (me < count - 1))
+    def _():
+        pl.semaphore_wait(barrier, 2)
+
+    @pl.when((me == 0) | (me == count - 1))
+    def _():
+        pl.semaphore_wait(barrier, 1)
+
+
+def gather_line_body(count, chunks, *refs):
+    arrays = len(chunks)
+    ins, outs = refs[:arrays], refs[arrays : 2 * arrays]
+    right_send, right_recv, left_send, left_recv, own_sem = refs[2 * arrays :]
+    me = lax.axis_index("tensor")
+    pieces = []
+    for at in range(arrays):
+        size = ins[at].shape[0] // chunks[at]
+        for piece in range(chunks[at]):
+            pieces.append((at, pl.ds(piece * size, size)))
+
+    def copy(at, rows, place, hop, origin, target, send, recv):
+        source = ins[at].at[rows] if hop == 0 else outs[at].at[origin, rows]
+        return pltpu.make_async_remote_copy(
+            src_ref=source,
+            dst_ref=outs[at].at[origin, rows],
+            send_sem=send.at[hop, place],
+            recv_sem=recv.at[hop, place],
+            device_id={"tensor": target},
+        )
+
+    def rightward(place, hop):
+        at, rows = pieces[place]
+        return copy(at, rows, place, hop, me - hop, me + 1, right_send, right_recv)
+
+    def leftward(place, hop):
+        at, rows = pieces[place]
+        return copy(at, rows, place, hop, me + hop, me - 1, left_send, left_recv)
+
+    greet_line(me, count)
+    own = [
+        pltpu.make_async_copy(ins[at], outs[at].at[me], own_sem.at[at]) for at in range(arrays)
+    ]
+    for hop in range(count):
+        for place in range(len(pieces)):
+            if hop > 0:
+
+                @pl.when(me - hop >= 0)
+                def _():
+                    at, rows = pieces[place]
+                    copy(
+                        at, rows, place, hop - 1, me - hop, me - 1, right_send, right_recv
+                    ).wait_recv()
+
+            if hop < count - 1:
+
+                @pl.when((me - hop >= 0) & (me + 1 < count))
+                def _():
+                    rightward(place, hop).start()
+
+            if hop > 0:
+
+                @pl.when(me + hop < count)
+                def _():
+                    at, rows = pieces[place]
+                    copy(
+                        at, rows, place, hop - 1, me + hop, me + 1, left_send, left_recv
+                    ).wait_recv()
+
+            if hop < count - 1:
+
+                @pl.when((me + hop < count) & (me > 0))
+                def _():
+                    leftward(place, hop).start()
+
+        if hop == 0:
+            for each in own:
+                each.start()
+    for each in own:
+        each.wait()
+    for hop in range(count - 1):
+        for place in range(len(pieces)):
+
+            @pl.when((me - hop >= 0) & (me + 1 < count))
+            def _():
+                rightward(place, hop).wait_send()
+
+            @pl.when((me + hop < count) & (me > 0))
+            def _():
+                leftward(place, hop).wait_send()
+
+
+def gather_line(arrays, chunks, identity):
+    count = lax.axis_size("tensor")
+    total = sum(chunks)
+    anywhere = pl.BlockSpec(memory_space=pl.ANY)
+    return pl.pallas_call(
+        functools.partial(gather_line_body, count, chunks),
+        out_shape=[jax.ShapeDtypeStruct((count,) + a.shape, a.dtype) for a in arrays],
+        in_specs=[anywhere] * len(arrays),
+        out_specs=[anywhere] * len(arrays),
+        scratch_shapes=[pltpu.SemaphoreType.DMA((count - 1, total))] * 4
+        + [pltpu.SemaphoreType.DMA((len(arrays),))],
+        compiler_params=pltpu.CompilerParams(collective_id=identity, has_side_effects=True),
+        name="gather_line",
+    )(*arrays)
+
+
+def sum_line_body(
+    count,
+    chunks,
+    part_ref,
+    out_ref,
+    left_buf,
+    right_buf,
+    right_send,
+    right_recv,
+    left_send,
+    left_recv,
+):
+    me = lax.axis_index("tensor")
+    size = part_ref.shape[1] // chunks
+
+    def rightward(rows, piece, far, source):
+        return pltpu.make_async_remote_copy(
+            src_ref=source,
+            dst_ref=left_buf.at[far - 1, rows],
+            send_sem=right_send.at[far - 1, piece],
+            recv_sem=right_recv.at[far - 1, piece],
+            device_id={"tensor": me + 1},
+        )
+
+    def leftward(rows, piece, far, source):
+        return pltpu.make_async_remote_copy(
+            src_ref=source,
+            dst_ref=right_buf.at[far - 1, rows],
+            send_sem=left_send.at[far - 1, piece],
+            recv_sem=left_recv.at[far - 1, piece],
+            device_id={"tensor": me - 1},
+        )
+
+    greet_line(me, count)
+    for far in range(count - 1, 0, -1):
+        for piece in range(chunks):
+            rows = pl.ds(piece * size, size)
+
+            @pl.when((me == 0) & (me + far < count))
+            def _():
+                rightward(rows, piece, far, part_ref.at[me + far, rows]).start()
+
+            @pl.when((me == count - 1) & (me - far >= 0))
+            def _():
+                leftward(rows, piece, far, part_ref.at[me - far, rows]).start()
+
+            if far < count - 1:
+
+                @pl.when((me > 0) & (me + far < count))
+                def _():
+                    rightward(rows, piece, far + 1, left_buf.at[far, rows]).wait_recv()
+                    left_buf[far, rows, :] = (
+                        left_buf[far, rows, :].astype(F32)
+                        + part_ref[me + far, rows, :].astype(F32)
+                    ).astype(BF16)
+                    rightward(rows, piece, far, left_buf.at[far, rows]).start()
+
+                @pl.when((me < count - 1) & (me - far >= 0))
+                def _():
+                    leftward(rows, piece, far + 1, right_buf.at[far, rows]).wait_recv()
+                    right_buf[far, rows, :] = (
+                        right_buf[far, rows, :].astype(F32)
+                        + part_ref[me - far, rows, :].astype(F32)
+                    ).astype(BF16)
+                    leftward(rows, piece, far, right_buf.at[far, rows]).start()
+
+    for piece in range(chunks):
+        rows = pl.ds(piece * size, size)
+        out_ref[rows, :] = part_ref[me, rows, :].astype(F32)
+
+        @pl.when(me > 0)
+        def _():
+            rightward(rows, piece, 1, left_buf.at[0, rows]).wait_recv()
+            out_ref[rows, :] += left_buf[0, rows, :].astype(F32)
+
+        @pl.when(me < count - 1)
+        def _():
+            leftward(rows, piece, 1, right_buf.at[0, rows]).wait_recv()
+            out_ref[rows, :] += right_buf[0, rows, :].astype(F32)
+
+    for far in range(count - 1, 0, -1):
+        for piece in range(chunks):
+            rows = pl.ds(piece * size, size)
+
+            @pl.when((me == 0) & (me + far < count))
+            def _():
+                rightward(rows, piece, far, part_ref.at[me + far, rows]).wait_send()
+
+            @pl.when((me == count - 1) & (me - far >= 0))
+            def _():
+                leftward(rows, piece, far, part_ref.at[me - far, rows]).wait_send()
+
+            if far < count - 1:
+
+                @pl.when((me > 0) & (me + far < count))
+                def _():
+                    rightward(rows, piece, far, left_buf.at[far, rows]).wait_send()
+
+                @pl.when((me < count - 1) & (me - far >= 0))
+                def _():
+                    leftward(rows, piece, far, right_buf.at[far, rows]).wait_send()
+
+
+def sum_line(part, chunks, identity):
+    count, rows, width = part.shape
+    semaphores = pltpu.SemaphoreType.DMA((count - 1, chunks))
+    return pl.pallas_call(
+        functools.partial(sum_line_body, count, chunks),
+        out_shape=jax.ShapeDtypeStruct((rows, width), F32),
+        in_specs=[pl.BlockSpec(memory_space=pltpu.VMEM)],
+        out_specs=pl.BlockSpec(memory_space=pltpu.VMEM),
+        scratch_shapes=[
+            pltpu.VMEM((count - 1, rows, width), BF16),
+            pltpu.VMEM((count - 1, rows, width), BF16),
+        ]
+        + [semaphores] * 4,
+        compiler_params=pltpu.CompilerParams(
+            collective_id=identity, has_side_effects=True, vmem_limit_bytes=32 * MEBI
+        ),
+        name="sum_line",
+    )(part)
 
 
 def per_device(
@@ -811,18 +1464,48 @@
     complete_linear = packed_weights[:, :linear_cols]
     complete_router = packed_weights[:, linear_cols:]
     full_out = lax.all_gather(w_out, "fsdp", axis=1, tiled=True)
-    sequence_tokens = lax.all_gather(tokens, "tensor", axis=0, tiled=True)
-    sequence_routes = lax.all_gather(routes, "tensor", axis=0, tiled=True)
-    sequence_cotangent = lax.all_gather(cotangent, "tensor", axis=0, tiled=True)
+    sequence_tokens, sequence_routes, sequence_cotangent = gather_line(
+        [tokens, jnp.transpose(routes, (1, 0)), cotangent], (4, 1, 4), 0
+    )
+    sequence_tokens = sequence_tokens.reshape(seq_rows, model_width)
     plane_experts = jnp.arange(fsdp_count, dtype=jnp.int32) * tensor_count + tensor_pos
-    route_blocks = sequence_routes.reshape(tensor_count, 1, tok_rows, top_count)
-    plane_mask = jnp.any(route_blocks == plane_experts[None, :, None, None], axis=-1)
+    plane_mask = jnp.any(
+        sequence_routes[:, None, :, :] == plane_experts[None, :, None, None], axis=2
+    )
     plane_ranks = ranks_of(plane_mask)
-    up_rows = plane_rows(
-        to_slots(plane_ranks, sequence_cotangent, slots).reshape(
-            fsdp_count, tensor_count * slots, model_width
-        )
-    )
+    offsets = [0] + [sign * step for step in range(1, tensor_count) for sign in (1, -1)]
+    offsets = [offset % tensor_count for offset in offsets[:tensor_count]]
+    line_blocks = [((tensor_pos + offset) % tensor_count)[None] for offset in offsets]
+
+    def fetched(block, offset):
+        if offset == 0:
+            return block
+        pairs = [((at + offset) % tensor_count, at) for at in range(tensor_count)]
+        return lax.ppermute(block, "tensor", pairs)
+
+    def delivered(block, offset):
+        if offset == 0:
+            return block
+        pairs = [(at, (at + offset) % tensor_count) for at in range(tensor_count)]
+        return lax.ppermute(block, "tensor", pairs)
+
+    def dispatched(block):
+        return [
+            plane_rows(to_slots(at, plane_ranks, fetched(block, offset), slots))
+            for offset, at in zip(offsets, line_blocks)
+        ]
+
+    in_kernel = fsdp_count * slots <= 640
+    if in_kernel:
+        slotted = all_to_slots(
+            plane_ranks, sequence_cotangent.reshape(seq_rows, model_width), slots
+        )
+        slotted, sequence_tokens = lax.optimization_barrier((slotted, sequence_tokens))
+        up_rows = plane_rows(
+            slotted.reshape(fsdp_count, tensor_count * slots, model_width)
+        ).reshape(fsdp_count, tensor_count, slots, model_width)
+    else:
+        up_rows = dispatched(cotangent)
 
     token_values = tokens.astype(F32)
     attn_normed, attn_factor = norm_forward(token_values, gain_attn)
@@ -851,9 +1534,10 @@
     out_part = matrix_product(heads_narrow, full_out) + matrix_product(
         attention_low, attention_second
     )
-    attention_total = lax.psum_scatter(
-        out_part.astype(BF16), "tensor", scatter_dimension=0, tiled=True
-    ).astype(F32)
+    attention_total = sum_line(
+        out_part.astype(BF16).reshape(tensor_count, tok_rows, model_width), 4, 1
+    )
+    up_rows, attention_total = lax.optimization_barrier((up_rows, attention_total))
     residual_stream = token_values + attention_total
     moe_normed, moe_factor = norm_forward(residual_stream, gain_moe)
     experts_narrow = moe_normed.astype(BF16)
@@ -868,53 +1552,74 @@
     chosen_exp = jnp.exp(chosen_logits - jnp.max(chosen_logits, axis=-1, keepdims=True))
     gate_weights = chosen_exp / jnp.sum(chosen_exp, axis=-1, keepdims=True)
     sent_weights = jnp.transpose(jnp.where(chosen, gate_weights, -1.0), (1, 0))
-    own_weights = route_rows(sent_weights).reshape(fsdp_count, tensor_count, tok_rows)
+    own_weights = jnp.transpose(
+        route_rows(sent_weights).reshape(fsdp_count, tensor_count, tok_rows), (1, 0, 2)
+    )
     own_ranks = ranks_of(own_weights >= 0.0)
 
-    sequence_experts = lax.all_gather(experts_narrow, "tensor", axis=0, tiled=True)
-    expert_rows = plane_rows(
-        to_slots(plane_ranks, sequence_experts, slots).reshape(
-            fsdp_count, tensor_count * slots, model_width
-        )
-    )
+    broad = adapter_count * rank
     gate_in_t, upward_in_t = transposed(gate_in[0]), transposed(upward_in[0])
-    (
-        expert_output,
-        rows_grad,
-        gate_dots,
-        pair_in_grad,
-        gate_out_grad,
-        upward_out_grad,
-        downward_in_grad,
-        downward_out_grad,
-    ) = experts(
-        adapter_index,
-        expert_rows,
-        up_rows,
-        own_ranks,
-        own_weights,
+    expert_tables = (
         expert_gate_weight[0],
         expert_up_weight[0],
         expert_down_weight[0],
-        jnp.concatenate([gate_in_t, upward_in_t], axis=1),
-        gate_out[0],
-        upward_out[0],
-        transposed(downward_in[0]),
-        downward_out[0],
-    )
-    gate_grad = jnp.transpose(
-        route_rows(gate_dots.reshape(device_count, tok_rows)), (1, 0)
-    )
+        jnp.concatenate(
+            [gate_in_t.reshape(broad, model_width), upward_in_t.reshape(broad, model_width)],
+            axis=0,
+        ),
+        gate_out[0].reshape(broad, -1),
+        upward_out[0].reshape(broad, -1),
+        transposed(downward_in[0]).reshape(broad, -1),
+        downward_out[0].reshape(broad, model_width),
+    )
+    column_adapter = jnp.arange(broad, dtype=jnp.int32) // rank
+    adapter_mask = jnp.repeat(
+        (adapter_index[:, None] == column_adapter[None, :]).astype(BF16), slots, axis=0
+    )
+    ordered = [None] * tensor_count
+    if in_kernel:
+        moe_grad, gate_dots, expert_output, _landed, *sums = moe_layer(
+            experts_narrow,
+            up_rows,
+            plane_ranks,
+            own_ranks,
+            own_weights,
+            adapter_mask,
+            expert_tables,
+            3,
+        )
+    else:
+        expert_rows = dispatched(experts_narrow)
+        expert_output, rows_grad, gate_dots = [], [], []
+        sums = [jnp.zeros(each.shape, F32) for each in expert_sums(expert_tables)]
+        for at, rows, upstream in zip(line_blocks, expert_rows, up_rows):
+            y_rows, grad_rows, dots, *sums = experts(
+                at, rows, upstream, own_ranks, own_weights, adapter_mask, expert_tables, sums
+            )
+            expert_output.append(y_rows)
+            rows_grad.append(grad_rows)
+            gate_dots.append(dots)
+        for offset, dots in zip(offsets, gate_dots):
+            ordered[offset] = dots
+        gate_dots = jnp.roll(jnp.stack(ordered), tensor_pos, axis=0)
+    pair_in_grad, gate_out_grad, upward_out_grad, downward_in_grad, downward_out_grad = sums
+    if in_kernel:
+        gate_grad = jnp.transpose(gate_dots, (2, 1, 0)).reshape(tok_rows, expert_count)
+    else:
+        gate_grad = jnp.transpose(
+            route_rows(jnp.transpose(gate_dots, (1, 0, 2)).reshape(device_count, tok_rows)),
+            (1, 0),
+        )
 
     def returned(slotted):
-        combined = from_slots(
-            plane_ranks,
-            plane_rows(slotted).reshape(fsdp_count, tensor_count, slots, model_width),
-        )
-        return lax.psum_scatter(combined, "tensor", scatter_dimension=0, tiled=True).astype(F32)
-
-    moe_grad = returned(rows_grad)
-    output = (residual_stream + returned(expert_output)).astype(BF16)
+        total = 0.0
+        for offset, at, rows in zip(offsets, line_blocks, slotted):
+            combined = from_slots(at, plane_ranks, plane_rows(rows))
+            total = total + delivered(combined, offset).astype(F32)
+        return total
+
+    if not in_kernel:
+        moe_grad = returned(rows_grad)
 
     out_grad = cotangent.astype(F32)
     logit_gradient = (
@@ -930,9 +1635,18 @@
     router_second_gradient = flipped_left_operand(router_low, logit_gradient)
     residual_grad = out_grad + norm_backward(residual_stream, moe_factor, gain_moe, moe_grad)
 
-    sequence_branch = lax.all_gather(
-        residual_grad.astype(BF16), "tensor", axis=0, tiled=True
-    )
+    (sequence_branch,) = gather_line([residual_grad.astype(BF16)], (4,), 2)
+    sequence_branch = sequence_branch.reshape(seq_rows, model_width)
+    if in_kernel:
+        back_output = plane_rows(
+            expert_output.reshape(fsdp_count, tensor_count * slots, model_width)
+        ).reshape(fsdp_count, tensor_count, slots, model_width)
+        back_output, sequence_branch = lax.optimization_barrier((back_output, sequence_branch))
+        combined = all_from_slots(tensor_pos[None], plane_ranks, back_output)
+        moe_output = lax.psum_scatter(combined, "tensor", scatter_dimension=0, tiled=True)
+        output = (residual_stream + moe_output.astype(F32)).astype(BF16)
+    else:
+        output = (residual_stream + returned(expert_output)).astype(BF16)
     attention_low_grad = flipped_right_operand(sequence_branch, attention_second).astype(BF16)
     attention_second_gradient = flipped_left_operand(attention_low, sequence_branch)
     heads_grad = flipped_right_operand(sequence_branch, full_out)
@@ -957,9 +1671,9 @@
         low_share, input_first
     )
     input_first_gradient = flipped_left_operand(low_share, sequence_normalized)
-    normalized_gradient = lax.psum_scatter(
-        normed_part.astype(BF16), "tensor", scatter_dimension=0, tiled=True
-    ).astype(F32)
+    normalized_gradient = sum_line(
+        normed_part.astype(BF16).reshape(tensor_count, tok_rows, model_width), 4, 1
+    )
     input_grad = residual_grad + norm_backward(
         token_values, attn_factor, gain_attn, normalized_gradient
     )
@@ -1027,12 +1741,12 @@
         lines_of(early[1], rank),
         transposed(lines_of(early[0], rank)),
         lines_of(early[2], rank),
-        transposed(pair_in_grad[:, :rank])[None],
-        gate_out_grad[None],
-        transposed(pair_in_grad[:, rank:])[None],
-        upward_out_grad[None],
-        transposed(downward_in_grad)[None],
-        downward_out_grad[None],
+        transposed(lines_of(pair_in_grad[:broad], rank))[None],
+        lines_of(gate_out_grad, rank)[None],
+        transposed(lines_of(pair_in_grad[broad:], rank))[None],
+        lines_of(upward_out_grad, rank)[None],
+        transposed(lines_of(downward_in_grad, rank))[None],
+        lines_of(downward_out_grad, rank)[None],
     )
 
 

time: 1230 us -> 990 us (0.80)
  waiting for transfers between devices: 689 us -> 72.3 us
  Pallas kernels: 215 us -> 717 us
  blocking collectives: 143 us -> 0 us
  local copies, waits for them, and re-layouts: 33.1 us -> 51.6 us
    pallas_call x5 -> x7, Pallas kernels: 152 us -> 654 us  [the longest x1 279 us: moe_layer(): pl.pallas_call(functools.partial(moe_body, plane, line), out_shape=[jax.S...]
    reduce_scatter x4 -> x1, waiting for transfers between devices: 233 us -> 0.01 us  [per_device(): lax.psum_scatter(combined, 'tensor', scatter_dimension=0, tiled=True)]
    all_gather x4 -> x0, waiting for transfers between devices: 230 us -> none  [the longest x1 74.2 us: per_device(): lax.all_gather(residual_grad.astype(BF16), 'tensor', axis=0, tiled=True)]
    all_to_all x2 -> x0, blocking collectives: 131 us -> none  [the longest x1 123 us: plane_rows(): lax.all_to_all(block_rows, 'fsdp', split_axis=0, concat_axis=0, tiled=True)]
    all_to_all x3 -> x2, waiting for transfers between devices: 154 us -> 23.3 us  [plane_rows(): lax.all_to_all(block_rows, 'fsdp', split_axis=0, concat_axis=0, tiled=True)]
    all_gather x1, waiting for transfers between devices: 41 us -> 0.02 us  [per_device(): lax.all_gather(jnp.concatenate([w_query, key_projection_weight, value_pro...]
    all_gather x1, waiting for transfers between devices: 7.63 us -> 43.3 us  [per_device(): full_out = lax.all_gather(w_out, 'fsdp', axis=1, tiled=True)]
    all_to_all x3, waiting for transfers between devices: 21.6 us -> 4.91 us  [route_rows(): lax.all_to_all(block_rows, ('fsdp', 'tensor'), split_axis=0, concat_axis=...]
  transfers between devices with their start and end apart: 16 -> 8, of which waited for: 14 -> 3; matrix products, arithmetic and copies ran while one was open for 8% -> 11% of each run, Pallas kernels for 7% -> 45%
where the time goes in v3:
time: 990 us; the launch traced here: 983 us
  Pallas kernels  717 us (72%)
  waiting for transfers between devices  72.3 us (7%)
  matrix products  65.8 us (7%)
  local copies, waits for them, and re-layouts  51.6 us (5%)
  starting transfers between devices  34.9 us (4%)
  other arithmetic  24.3 us (2%)
  between operations  17.4 us (2%)
    pallas_call x1, Pallas kernels, moe_layer(): pl.pallas_call(functools.partial(moe_body, plane, line), out_shape=[jax.S...  279 us
    pallas_call x2, Pallas kernels, gather_line(): pl.pallas_call(functools.partial(gather_line_body, count, chunks), out_sh...  217 us
    pallas_call x2, Pallas kernels, sum_line(): pl.pallas_call(functools.partial(sum_line_body, count, chunks), out_shape...  145 us
    all_gather x1, waiting for transfers between devices, per_device(): full_out = lax.all_gather(w_out, 'fsdp', axis=1, tiled=True)  43.3 us
    pallas_call x1, Pallas kernels, attention_backward(): pl.pallas_call(functools.partial(attention_backward_body, rank, scale), g...  41.2 us
    dot_general x8, matrix products, flipped_right_operand(): lax.dot_general(first_op, second_op, (((1,), (1,)), ((), ())), preferred_...  30.8 us
    dot_general x11, matrix products, matrix_product(): return jnp.dot(first_op, second_op, preferred_element_type=F32)  28.4 us
    unnamed x170, local copies, waits for them, and re-layouts  26.4 us
  transfers between devices with their start and end apart: 8, of which 3 were waited for; matrix products, arithmetic and copies ran while one was open for 11% of the time, Pallas kernels for 45%

profile of v3, /device:TPU:16, one launch (start us, length us, event | category | flops | bytes accessed | tf_op | source)
XLA Modules:
  0.0 983.0 jit_solution(14500958407688912570)
XLA Ops:
  8.1 2.0 pad_maximum_fusion.1
  10.2 138.2 %gather_line.2 = (bf16[4,256,2048]{2,1,0:T(8,128)(2,1)}, s32[4,8,256]{2,1,0:T(8,128)}, bf16[4,256,2048]{2,1,0:T(8,128)(2,1)}) custom-call(bf16[256,2048]{1,0:T(8,128)(2,1)} %refs_0_.1, s32[8,256]{1,0:T(8,128)} %bitcast.257, bf16[256,2048]{1,0:T(8,128)(2,1)} %refs_2_.1), custom_call_target="tpu_custom_call" | custom-call | tf_op jit(solution)/shard_map/gather_line/pallas_call | solution.py:1244
  149.5 2.2 copy-done.13
  151.7 5.6 all_to_slots.1
  157.3 5.3 all-to-all-start
  170.2 2.0 fusion.33
  178.5 9.6 fusion.5.lin_ref.key_lin_ref.value_lin_ref
  188.2 21.5 %attention_forward.1.heads_ref = bf16[1024,1024]{1,0:T(8,128)(2,1)S(1)} custom-call(f32[1024,1280]{1,0:T(8,128)S(1)} %fusion.5.lin_ref.key_lin_ref.value_lin_ref, f32[1024,1280]{1,0:T(8,128)S(1)} %fusion.5.lin_ref.key_lin_ref.value_lin_ref, f32[1024,1280]{1,0:T(8,128)S(1)} %fusion.5.lin_ref.key_lin_ref.value_lin_ref, ...), custom_call_target="tpu_custom_call" | custom-call | flops 2147483648 | bytes 6291456 | tf_op jit(solution)/shard_map/attention_forward/pallas_call | solution.py:173
  210.4 43.3 %all-gather.5.cloned.1.call-done = bf16[1024,2048]{1,0:T(8,128)(2,1)} async-done(((bf16[1024,256]{1,0:T(8,128)(2,1)}), bf16[1024,2048]{1,0:T(8,128)(2,1)}) %all-gather.5.cloned.1.call-update) | async-done | bytes 4194320 | tf_op jit(solution)/shard_map/all_gather | solution.py:1466
  253.7 6.3 fusion.74
  261.3 71.6 %sum_line.2 = f32[256,2048]{1,0:T(8,128)S(1)} custom-call(bf16[4,256,2048]{2,1,0:T(8,128)(2,1)S(1)} %bitcast.219), custom_call_target="tpu_custom_call" | custom-call | tf_op jit(solution)/shard_map/sum_line/pallas_call | solution.py:1362
  333.0 2.4 multiply_reduce_fusion.1
  337.6 1.5 fusion.27
  340.8 3.3 all-to-all-start.1
  344.2 4.9 all-to-all-done.1
  351.3 279.1 %moe_layer.1 = (f32[256,2048]{1,0:T(8,128)}, f32[4,8,256]{2,1,0:T(8,128)}, bf16[8,4,80,2048]{3,2,1,0:T(8,128)(2,1)}, bf16[4,8,80,2048]{3,2,1,0:T(8,128)(2,1)}, f...) custom-call(bf16[256,2048]{1,0:T(8,128)(2,1)} %copy-done.32, ...), custom_call_target="tpu_custom_call" | custom-call | tf_op jit(solution)/shard_map/moe_layer/pallas_call | solution.py:1098
  630.5 5.3 all-to-all-start.2
  637.4 1.6 convolution_convert_fusion.2
  639.7 2.3 convolution_add_fusion.1
  642.1 1.8 fusion.13
  643.9 2.4 fusion.70
  646.3 79.0 %gather_line.3 = bf16[4,256,2048]{2,1,0:T(8,128)(2,1)} custom-call(bf16[256,2048]{1,0:T(8,128)(2,1)} %get-tuple-element.178.refs_0_), custom_call_target="tpu_custom_call" | custom-call | tf_op jit(solution)/shard_map/gather_line/pallas_call | solution.py:1244
  725.9 3.1 fusion.71
  729.0 23.3 %all-to-all-done.2 = bf16[8,320,2048]{2,1,0:T(8,128)(2,1)} async-done(((bf16[8,320,2048]{2,1,0:T(8,128)(2,1)}), bf16[8,320,2048]{2,1,0:T(8,128)(2,1)}, u32[]{:S(2)}, u32[]{:S(2)}) %all-to-all-start.2) | async-done | bytes 10485792 | tf_op jit(solution)/shard_map/all_to_all | solution.py:67
  752.3 2.8 convolution_convert_fusion.1
  757.6 14.9 %all-to-all-start.4 = ((bf16[32,2,1032]{2,1,0:T(2,128)(2,1)}), bf16[32,2,1032]{2,1,0:T(2,128)(2,1)}, u32[]{:S(2)}, u32[]{:S(2)}) async-start(bf16[32,2,1032]{2,1,0:T(2,128)(2,1)} %reshape.293), calls=%async_computation.5 | async-start | bytes 294912 | tf_op jit(solution)/shard_map/all_to_all | solution.py:63
  772.6 6.8 all_from_slots.1
  779.4 2.1 copy-done.6
  781.5 3.4 convolution_convert_fusion.4
  785.1 10.2 %fusion.75.heads_grad_ref = f32[1024,1024]{1,0:T(8,128)} fusion(bf16[1024,2048]{1,0:T(8,128)(2,1)} %bitcast.224, bf16[1024,2048]{1,0:T(8,128)(2,1)} %all-gather.5.cloned.1.call-done), kind=kOutput, calls=%fused_computation.160 | convolution fusion | flops 4294967296 | bytes 12582912 | tf_op jit(solution)/shard_map/dot_general | solution.py:30
  795.3 41.2 %attention_backward.1 = (bf16[1024,1024]{1,0:T(8,128)(2,1)S(1)}, bf16[1024,128]{1,0:T(8,128)(2,1)S(1)}, bf16[1024,128]{1,0:T(8,128)(2,1)S(1)}, bf16[1024,48]{1,0...) custom-call(f32[1024,1280]{1,0:T(8,128)} %copy-done.1, ...), custom_call_target="tpu_custom_call" | custom-call | flops 5368709120 | bytes 12582912 | tf_op jit(solution)/shard_map/attention_backward/pallas_call | solution.py:350
  838.4 1.3 copy-done.25
  841.1 2.0 convolution_convert_fusion
  843.1 2.1 reshape.260
  845.3 1.9 copy.181
  847.2 2.0 reshape.261
  849.7 1.6 constant_dynamic-update-slice_fusion.4
  852.7 10.8 %fusion.3 = f32[1024,2048]{1,0:T(8,128)} fusion(bf16[2048,1312]{1,0:T(8,128)(2,1)} %all-gather.3.cloned.1.call-done, bf16[1024,128]{1,0:T(8,128)(2,1)} %copy-done.28, bf16[1024,128]{1,0:T(8,128)(2,1)S(1)} %copy-done.27, bf16[1024,1024]{1,0:T(8,128)(2,1)} %copy-done.25), kind=kOutput, calls=%fused_computation.7 | convolution fusion | flops 5376573440 | bytes 16252928 | tf_op jit(solution)/shard_map/dot_general | solution.py:30
  864.8 2.7 reduce.1
  867.5 1.9 reshape.291
  869.4 5.9 all-to-all-start.3
  875.3 4.6 add_convert_fusion
  880.0 73.7 %sum_line.3 = f32[256,2048]{1,0:T(8,128)S(1)} custom-call(bf16[4,256,2048]{2,1,0:T(8,128)(2,1)S(1)} %bitcast.218), custom_call_target="tpu_custom_call" | custom-call | tf_op jit(solution)/shard_map/sum_line/pallas_call | solution.py:1362
  953.7 1.3 copy-done.5
  955.4 1.5 reshape.294
  959.1 3.4 reshape.292
  962.5 1.4 fusion.23
  967.4 5.4 fusion.16
  (264 shorter events, 42.9 us)
Async XLA Ops:
  7.2 252.8 %copy-start = (bf16[8,16,2048]{2,1,0:T(8,128)(2,1)S(1)}, bf16[8,16,2048]{2,1,0:T(8,128)(2,1)}, u32[]{:S(2)}) copy-start(bf16[8,16,2048]{2,1,0:T(8,128)(2,1)} %param.57) | copy-start | bytes 1572868
  7.2 171.2 %all-gather.3.cloned.1.call-start = ((), (), s32[]{:S(2)}) async-start(), calls=%async_computation.6 | async-start | bytes 6488064 | tf_op jit(solution)/shard_map/all_gather | solution.py:1455
  149.5 7.8 copy-start.14
  157.3 8.0 copy-start.66
  157.3 8.1 copy-start.18
  157.3 9.1 copy-start.67
  157.3 12.8 %copy-start.55 = (s32[256,8]{0,1:T(8,128)S(1)}, s32[256,8]{0,1:T(8,128)}, u32[]{:S(2)}) copy-start(s32[256,8]{0,1:T(8,128)} %param.35) | copy-start | bytes 24580
  157.3 175.6 %all-to-all-start = ((bf16[8,320,2048]{2,1,0:T(8,128)(2,1)}), bf16[8,320,2048]{2,1,0:T(8,128)(2,1)}, u32[]{:S(2)}, u32[]{:S(2)}) async-start(bf16[8,320,2048]{2,1,0:T(8,128)(2,1)} %bitcast.225), calls=%async_computation | async-start | bytes 20971520 | tf_op jit(solution)/shard_map/all_to_all | solution.py:67
  162.7 10.6 %copy-start.74 = (bf16[128]{0:T(256)(128)(2,1)S(1)}, bf16[128]{0:T(256)(128)(2,1)}, u32[]{:S(2)}) copy-start(bf16[128]{0:T(256)(128)(2,1)} %param.41) | copy-start | bytes 772
  162.7 10.6 %copy-start.75 = (bf16[128]{0:T(256)(128)(2,1)S(1)}, bf16[128]{0:T(256)(128)(2,1)}, u32[]{:S(2)}) copy-start(bf16[128]{0:T(256)(128)(2,1)} %param.40) | copy-start | bytes 772
  162.7 91.0 %all-gather.5.cloned.1.call-start = ((), (), s32[]{:S(2)}) async-start(), calls=%async_computation.7 | async-start | bytes 4718592 | tf_op jit(solution)/shard_map/all_gather | solution.py:1466
  165.4 13.1 %copy-start.50 = (f32[2048]{0:T(1024)}, f32[2048]{0:T(1024)S(1)}, u32[]{:S(2)}) copy-start(f32[2048]{0:T(1024)S(1)} %convert_element_type.97) | copy-start | bytes 24580
  166.4 169.5 %copy-start.53 = (f32[2048]{0:T(1024)}, f32[2048]{0:T(1024)S(1)}, u32[]{:S(2)}) copy-start(f32[2048]{0:T(1024)S(1)} %convert_element_type.102) | copy-start | bytes 24580
  170.2 169.9 %copy-start.42 = (pred[256,32]{0,1:T(8,128)(4,1)}, pred[256,32]{0,1:T(8,128)(4,1)S(1)}, u32[]{:S(2)}) copy-start(pred[256,32]{0,1:T(8,128)(4,1)S(1)} %fusion.32) | copy-start | bytes 24580
  173.3 14.9 %copy-start.7 = (f32[1024,128]{1,0:T(8,128)}, f32[1024,128]{1,0:T(8,128)S(1)}, u32[]{:S(2)}) copy-start(f32[1024,128]{1,0:T(8,128)S(1)} %get-tuple-element.207.cos_ref) | copy-start | bytes 1572868
  173.3 14.8 %copy-start.23 = (f32[1,128]{1,0:T(1,128)}, f32[1,128]{1,0:T(1,128)S(1)}, u32[]{:S(2)}) copy-start(f32[1,128]{1,0:T(1,128)S(1)} %get-tuple-element.210.q_gain_ref) | copy-start | bytes 1540
  178.5 9.7 copy-start.9
  178.5 9.7 copy-start.11
  188.1 21.6 %copy-start.1 = (f32[1024,1280]{1,0:T(8,128)}, f32[1024,1280]{1,0:T(8,128)S(1)}, u32[]{:S(2)}) copy-start(f32[1024,1280]{1,0:T(8,128)S(1)} %fusion.5.lin_ref.key_lin_ref.value_lin_ref) | copy-start | bytes 15728644
  209.8 50.3 %copy-start.4 = (bf16[1024,1024]{1,0:T(8,128)(2,1)}, bf16[1024,1024]{1,0:T(8,128)(2,1)S(1)}, u32[]{:S(2)}) copy-start(bf16[1024,1024]{1,0:T(8,128)(2,1)S(1)} %attention_forward.1.heads_ref) | copy-start | bytes 6291460
  335.9 8.2 copy-start.72
  335.9 8.2 copy-start.76
  340.0 290.3 %copy-start.57 = (f32[256]{0:T(256)}, f32[256]{0:T(256)S(1)}, u32[]{:S(2)}) copy-start(f32[256]{0:T(256)S(1)} %get-tuple-element.200) | copy-start | bytes 3076
  340.1 290.3 %copy-start.59 = (f32[256]{0:T(256)}, f32[256]{0:T(256)S(1)}, u32[]{:S(2)}) copy-start(f32[256]{0:T(256)S(1)} %fusion.52) | copy-start | bytes 3076
  340.8 8.3 all-to-all-start.1
  630.5 121.9 %all-to-all-start.2 = ((bf16[8,320,2048]{2,1,0:T(8,128)(2,1)}), bf16[8,320,2048]{2,1,0:T(8,128)(2,1)}, u32[]{:S(2)}, u32[]{:S(2)}) async-start(bf16[8,320,2048]{2,1,0:T(8,128)(2,1)} %bitcast.226), calls=%async_computation.2 | async-start | bytes 20971520 | tf_op jit(solution)/shard_map/all_to_all | solution.py:67
  729.0 43.6 %copy-start.15 = (s32[4,8,256]{2,1,0:T(8,128)S(1)}, s32[4,8,256]{2,1,0:T(8,128)}, u32[]{:S(2)}) copy-start(s32[4,8,256]{2,1,0:T(8,128)} %copy-done.14) | copy-start | bytes 98308
  757.6 111.8 %all-to-all-start.4 = ((bf16[32,2,1032]{2,1,0:T(2,128)(2,1)}), bf16[32,2,1032]{2,1,0:T(2,128)(2,1)}, u32[]{:S(2)}, u32[]{:S(2)}) async-start(bf16[32,2,1032]{2,1,0:T(2,128)(2,1)} %reshape.293), calls=%async_computation.5 | async-start | bytes 294912 | tf_op jit(solution)/shard_map/all_to_all | solution.py:63
  772.5 194.9 %reduce-scatter.2.cloned.1.call-start = ((), (), s32[]{:S(2)}) async-start(), calls=%async_computation.8 | async-start | bytes 5242880 | tf_op jit(solution)/shard_map/reduce_scatter | solution.py:1646
  785.0 10.2 %copy-start.8 = (f32[1024,128]{1,0:T(8,128)S(1)}, f32[1024,128]{1,0:T(8,128)}, u32[]{:S(2)}) copy-start(f32[1024,128]{1,0:T(8,128)} %copy-done.7) | copy-start | bytes 1572868
  785.0 10.2 %copy-start.10 = (f32[1024,128]{1,0:T(8,128)S(1)}, f32[1024,128]{1,0:T(8,128)}, u32[]{:S(2)}) copy-start(f32[1024,128]{1,0:T(8,128)} %get-tuple-element.208.sin_ref) | copy-start | bytes 1572868
  785.0 10.2 %copy-start.12 = (s32[1024,1]{1,0:T(8,128)S(1)}, s32[1024,1]{1,0:T(8,128)}, u32[]{:S(2)}) copy-start(s32[1024,1]{1,0:T(8,128)} %copy.137.seg_column_ref) | copy-start | bytes 12292
  785.1 10.2 %copy-start.24 = (f32[1,128]{1,0:T(1,128)S(1)}, f32[1,128]{1,0:T(1,128)}, u32[]{:S(2)}) copy-start(f32[1,128]{1,0:T(1,128)} %copy-done.23) | copy-start | bytes 1540
  795.3 45.8 %copy-start.34 = (bf16[4,256,2048]{2,1,0:T(8,128)(2,1)S(1)}, bf16[4,256,2048]{2,1,0:T(8,128)(2,1)}, u32[]{:S(2)}) copy-start(bf16[4,256,2048]{2,1,0:T(8,128)(2,1)} %get-tuple-element.45) | copy-start | bytes 12582916
  795.3 45.8 %copy-start.51 = (f32[2048]{0:T(1024)S(1)}, f32[2048]{0:T(1024)}, u32[]{:S(2)}) copy-start(f32[2048]{0:T(1024)} %copy-done.50) | copy-start | bytes 24580
  795.3 45.8 %copy-start.69 = (f32[1024]{0:T(1024)S(1)}, f32[1024]{0:T(1024)}, u32[]{:S(2)}) copy-start(f32[1024]{0:T(1024)} %copy-done.68) | copy-start | bytes 12292
  841.1 8.1 copy-start.17
  841.1 8.1 copy-start.22
  841.1 8.3 copy-start.20
  843.1 9.5 copy-start.27
  863.5 11.8 %copy-start.45 = (bf16[16,2048]{1,0:T(8,128)(2,1)S(1)}, bf16[16,2048]{1,0:T(8,128)(2,1)}, u32[]{:S(2)}) copy-start(bf16[16,2048]{1,0:T(8,128)(2,1)} %copy-done.44) | copy-start | bytes 196612
  863.5 11.8 %copy-start.47 = (bf16[16,2048]{1,0:T(8,128)(2,1)S(1)}, bf16[16,2048]{1,0:T(8,128)(2,1)}, u32[]{:S(2)}) copy-start(bf16[16,2048]{1,0:T(8,128)(2,1)} %copy-done.46) | copy-start | bytes 196612
  863.5 11.8 %copy-start.49 = (bf16[16,2048]{1,0:T(8,128)(2,1)S(1)}, bf16[16,2048]{1,0:T(8,128)(2,1)}, u32[]{:S(2)}) copy-start(bf16[16,2048]{1,0:T(8,128)(2,1)} %copy-done.48) | copy-start | bytes 196612
  869.4 89.7 %all-to-all-start.3 = ((bf16[32,2,3840]{2,1,0:T(2,128)(2,1)}), bf16[32,2,3840]{2,1,0:T(2,128)(2,1)}, u32[]{:S(2)}, u32[]{:S(2)}) async-start(bf16[32,2,3840]{2,1,0:T(2,128)(2,1)} %reshape.291), calls=%async_computation.4 | async-start | bytes 983040 | tf_op jit(solution)/shard_map/all_to_all | solution.py:63
  879.9 75.1 %copy-start.31 = (bf16[256,2048]{1,0:T(8,128)(2,1)S(1)}, bf16[256,2048]{1,0:T(8,128)(2,1)}, u32[]{:S(2)}) copy-start(bf16[256,2048]{1,0:T(8,128)(2,1)} %refs_0_.1) | copy-start | bytes 3145732
  879.9 75.1 %copy-start.52 = (f32[2048]{0:T(1024)S(1)}, f32[2048]{0:T(1024)}, u32[]{:S(2)}) copy-start(f32[2048]{0:T(1024)} %copy-done.50) | copy-start | bytes 24580
  955.4 12.0 %copy-start.64 = (f32[256]{0:T(256)S(1)}, f32[256]{0:T(256)}, u32[]{:S(2)}) copy-start(f32[256]{0:T(256)} %get-tuple-element.193) | copy-start | bytes 3076
  955.4 12.0 %copy-start.65 = (f32[256]{0:T(256)S(1)}, f32[256]{0:T(256)}, u32[]{:S(2)}) copy-start(f32[256]{0:T(256)} %get-tuple-element.194) | copy-start | bytes 3076
  (37 other events, 124.7 us)
Sparse Core Ops, SparseCore 0:
  10.5 44.3 all-gather.2
  165.4 88.2 all-gather.4
  781.6 78.2 reduce-scatter.1

commit v4 on v3

--- a/solution.py
+++ b/solution.py
@@ -426,7 +426,7 @@
 
 def slot_choice(ranks, slots):
     experts, tokens = ranks.shape
-    places = lax.broadcasted_iota(jnp.int32, (slots, tokens), 0)
+    places = lax.broadcasted_iota(jnp.int32, (slots, tokens), 0).astype(ranks.dtype)
     return jnp.concatenate(
         [(places == ranks[e : e + 1, :]).astype(F32) for e in range(experts)], axis=0
     ).astype(BF16)
@@ -841,17 +841,7 @@
     tile = 256
     me, at_line = lax.axis_index("fsdp"), lax.axis_index("tensor")
 
-    barrier = pltpu.get_barrier_semaphore()
-
-    @pl.loop(1, plane)
-    def _(d):
-        pl.semaphore_signal(barrier, inc=1, device_id={"fsdp": lax.rem(me + d, plane)})
-
-    @pl.loop(1, line)
-    def _(d):
-        pl.semaphore_signal(barrier, inc=1, device_id={"tensor": lax.rem(at_line + d, line)})
-
-    pl.semaphore_wait(barrier, plane + line - 2)
+    greet_line_and_plane(line, plane)
 
     def block_copy(r):
         return pltpu.make_async_remote_copy(
@@ -1158,83 +1148,22 @@
 def gather_line_body(count, chunks, *refs):
     arrays = len(chunks)
     ins, outs = refs[:arrays], refs[arrays : 2 * arrays]
-    right_send, right_recv, left_send, left_recv, own_sem = refs[2 * arrays :]
+    semaphores, own_sem = refs[2 * arrays : -1], refs[-1]
     me = lax.axis_index("tensor")
-    pieces = []
-    for at in range(arrays):
-        size = ins[at].shape[0] // chunks[at]
-        for piece in range(chunks[at]):
-            pieces.append((at, pl.ds(piece * size, size)))
-
-    def copy(at, rows, place, hop, origin, target, send, recv):
-        source = ins[at].at[rows] if hop == 0 else outs[at].at[origin, rows]
-        return pltpu.make_async_remote_copy(
-            src_ref=source,
-            dst_ref=outs[at].at[origin, rows],
-            send_sem=send.at[hop, place],
-            recv_sem=recv.at[hop, place],
-            device_id={"tensor": target},
-        )
-
-    def rightward(place, hop):
-        at, rows = pieces[place]
-        return copy(at, rows, place, hop, me - hop, me + 1, right_send, right_recv)
-
-    def leftward(place, hop):
-        at, rows = pieces[place]
-        return copy(at, rows, place, hop, me + hop, me - 1, left_send, left_recv)
-
+    advance, finish = line_relay(me, count, ins, outs, chunks, semaphores)
     greet_line(me, count)
     own = [
         pltpu.make_async_copy(ins[at], outs[at].at[me], own_sem.at[at]) for at in range(arrays)
     ]
-    for hop in range(count):
-        for place in range(len(pieces)):
-            if hop > 0:
-
-                @pl.when(me - hop >= 0)
-                def _():
-                    at, rows = pieces[place]
-                    copy(
-                        at, rows, place, hop - 1, me - hop, me - 1, right_send, right_recv
-                    ).wait_recv()
-
-            if hop < count - 1:
-
-                @pl.when((me - hop >= 0) & (me + 1 < count))
-                def _():
-                    rightward(place, hop).start()
-
-            if hop > 0:
-
-                @pl.when(me + hop < count)
-                def _():
-                    at, rows = pieces[place]
-                    copy(
-                        at, rows, place, hop - 1, me + hop, me + 1, left_send, left_recv
-                    ).wait_recv()
-
-            if hop < count - 1:
-
-                @pl.when((me + hop < count) & (me > 0))
-                def _():
-                    leftward(place, hop).start()
-
-        if hop == 0:
-            for each in own:
-                each.start()
+    everything = tuple(range(arrays))
+    advance(0, everything)
+    for each in own:
+        each.start()
+    for hop in range(1, count):
+        advance(hop, everything)
     for each in own:
         each.wait()
-    for hop in range(count - 1):
-        for place in range(len(pieces)):
-
-            @pl.when((me - hop >= 0) & (me + 1 < count))
-            def _():
-                rightward(place, hop).wait_send()
-
-            @pl.when((me + hop < count) & (me > 0))
-            def _():
-                leftward(place, hop).wait_send()
+    finish(everything, range(count - 1))
 
 
 def gather_line(arrays, chunks, identity):
@@ -1253,107 +1182,15 @@
     )(*arrays)
 
 
-def sum_line_body(
-    count,
-    chunks,
-    part_ref,
-    out_ref,
-    left_buf,
-    right_buf,
-    right_send,
-    right_recv,
-    left_send,
-    left_recv,
-):
+def sum_line_body(count, chunks, part_ref, out_ref, left_buf, right_buf, *semaphores):
     me = lax.axis_index("tensor")
-    size = part_ref.shape[1] // chunks
-
-    def rightward(rows, piece, far, source):
-        return pltpu.make_async_remote_copy(
-            src_ref=source,
-            dst_ref=left_buf.at[far - 1, rows],
-            send_sem=right_send.at[far - 1, piece],
-            recv_sem=right_recv.at[far - 1, piece],
-            device_id={"tensor": me + 1},
-        )
-
-    def leftward(rows, piece, far, source):
-        return pltpu.make_async_remote_copy(
-            src_ref=source,
-            dst_ref=right_buf.at[far - 1, rows],
-            send_sem=left_send.at[far - 1, piece],
-            recv_sem=left_recv.at[far - 1, piece],
-            device_id={"tensor": me - 1},
-        )
-
+    advance, finish = line_sum(
+        me, count, chunks, part_ref, out_ref, left_buf, right_buf, semaphores
+    )
     greet_line(me, count)
     for far in range(count - 1, 0, -1):
-        for piece in range(chunks):
-            rows = pl.ds(piece * size, size)
-
-            @pl.when((me == 0) & (me + far < count))
-            def _():
-                rightward(rows, piece, far, part_ref.at[me + far, rows]).start()
-
-            @pl.when((me == count - 1) & (me - far >= 0))
-            def _():
-                leftward(rows, piece, far, part_ref.at[me - far, rows]).start()
-
-            if far < count - 1:
-
-                @pl.when((me > 0) & (me + far < count))
-                def _():
-                    rightward(rows, piece, far + 1, left_buf.at[far, rows]).wait_recv()
-                    left_buf[far, rows, :] = (
-                        left_buf[far, rows, :].astype(F32)
-                        + part_ref[me + far, rows, :].astype(F32)
-                    ).astype(BF16)
-                    rightward(rows, piece, far, left_buf.at[far, rows]).start()
-
-                @pl.when((me < count - 1) & (me - far >= 0))
-                def _():
-                    leftward(rows, piece, far + 1, right_buf.at[far, rows]).wait_recv()
-                    right_buf[far, rows, :] = (
-                        right_buf[far, rows, :].astype(F32)
-                        + part_ref[me - far, rows, :].astype(F32)
-                    ).astype(BF16)
-                    leftward(rows, piece, far, right_buf.at[far, rows]).start()
-
-    for piece in range(chunks):
-        rows = pl.ds(piece * size, size)
-        out_ref[rows, :] = part_ref[me, rows, :].astype(F32)
-
-        @pl.when(me > 0)
-        def _():
-            rightward(rows, piece, 1, left_buf.at[0, rows]).wait_recv()
-            out_ref[rows, :] += left_buf[0, rows, :].astype(F32)
-
-        @pl.when(me < count - 1)
-        def _():
-            leftward(rows, piece, 1, right_buf.at[0, rows]).wait_recv()
-            out_ref[rows, :] += right_buf[0, rows, :].astype(F32)
-
-    for far in range(count - 1, 0, -1):
-        for piece in range(chunks):
-            rows = pl.ds(piece * size, size)
-
-            @pl.when((me == 0) & (me + far < count))
-            def _():
-                rightward(rows, piece, far, part_ref.at[me + far, rows]).wait_send()
-
-            @pl.when((me == count - 1) & (me - far >= 0))
-            def _():
-                leftward(rows, piece, far, part_ref.at[me - far, rows]).wait_send()
-
-            if far < count - 1:
-
-                @pl.when((me > 0) & (me + far < count))
-                def _():
-                    rightward(rows, piece, far, left_buf.at[far, rows]).wait_send()
-
-                @pl.when((me < count - 1) & (me - far >= 0))
-                def _():
-                    leftward(rows, piece, far, right_buf.at[far, rows]).wait_send()
+        advance(far)
+    finish()
 
 
 def sum_line(part, chunks, identity):
@@ -1374,6 +1211,594 @@
         ),
         name="sum_line",
     )(part)
+
+
+def line_relay(me, count, ins, outs, chunks, semaphores):
+    right_send, right_recv, left_send, left_recv = semaphores
+    pieces = []
+    for at in range(len(ins)):
+        size = ins[at].shape[0] // chunks[at]
+        for piece in range(chunks[at]):
+            pieces.append((at, pl.ds(piece * size, size)))
+
+    def copy(place, hop, origin, target, send, recv):
+        at, rows = pieces[place]
+        source = ins[at].at[rows] if hop == 0 else outs[at].at[origin, rows]
+        return pltpu.make_async_remote_copy(
+            src_ref=source,
+            dst_ref=outs[at].at[origin, rows],
+            send_sem=send.at[hop, place],
+            recv_sem=recv.at[hop, place],
+            device_id={"tensor": target},
+        )
+
+    def places(arrays):
+        return [place for place in range(len(pieces)) if pieces[place][0] in arrays]
+
+    def advance(hop, arrays):
+        for place in places(arrays):
+            if hop > 0:
+
+                @pl.when(me - hop >= 0)
+                def _():
+                    copy(place, hop - 1, me - hop, me - 1, right_send, right_recv).wait_recv()
+
+            if hop < count - 1:
+
+                @pl.when((me - hop >= 0) & (me + 1 < count))
+                def _():
+                    copy(place, hop, me - hop, me + 1, right_send, right_recv).start()
+
+            if hop > 0:
+
+                @pl.when(me + hop < count)
+                def _():
+                    copy(place, hop - 1, me + hop, me + 1, left_send, left_recv).wait_recv()
+
+            if hop < count - 1:
+
+                @pl.when((me + hop < count) & (me > 0))
+                def _():
+                    copy(place, hop, me + hop, me - 1, left_send, left_recv).start()
+
+    def finish(arrays, hops):
+        for hop in hops:
+            for place in places(arrays):
+
+                @pl.when((me - hop >= 0) & (me + 1 < count))
+                def _():
+                    copy(place, hop, me - hop, me + 1, right_send, right_recv).wait_send()
+
+                @pl.when((me + hop < count) & (me > 0))
+                def _():
+                    copy(place, hop, me + hop, me - 1, left_send, left_recv).wait_send()
+
+    return advance, finish
+
+
+def line_sum(me, count, chunks, part_ref, out_ref, left_buf, right_buf, semaphores):
+    right_send, right_recv, left_send, left_recv = semaphores
+    size = part_ref.shape[1] // chunks
+
+    def rightward(rows, piece, far, source):
+        return pltpu.make_async_remote_copy(
+            src_ref=source,
+            dst_ref=left_buf.at[far - 1, rows],
+            send_sem=right_send.at[far - 1, piece],
+            recv_sem=right_recv.at[far - 1, piece],
+            device_id={"tensor": me + 1},
+        )
+
+    def leftward(rows, piece, far, source):
+        return pltpu.make_async_remote_copy(
+            src_ref=source,
+            dst_ref=right_buf.at[far - 1, rows],
+            send_sem=left_send.at[far - 1, piece],
+            recv_sem=left_recv.at[far - 1, piece],
+            device_id={"tensor": me - 1},
+        )
+
+    def added(buffer, far, rows, block):
+        buffer[far, rows, :] = (
+            buffer[far, rows, :].astype(F32) + part_ref[block, rows, :].astype(F32)
+        ).astype(BF16)
+
+    def advance(far):
+        for piece in range(chunks):
+            rows = pl.ds(piece * size, size)
+
+            @pl.when((me == 0) & (me + far < count))
+            def _():
+                rightward(rows, piece, far, part_ref.at[me + far, rows]).start()
+
+            @pl.when((me == count - 1) & (me - far >= 0))
+            def _():
+                leftward(rows, piece, far, part_ref.at[me - far, rows]).start()
+
+            if far < count - 1:
+
+                @pl.when((me > 0) & (me + far < count))
+                def _():
+                    rightward(rows, piece, far + 1, left_buf.at[far, rows]).wait_recv()
+                    added(left_buf, far, rows, me + far)
+                    rightward(rows, piece, far, left_buf.at[far, rows]).start()
+
+                @pl.when((me < count - 1) & (me - far >= 0))
+                def _():
+                    leftward(rows, piece, far + 1, right_buf.at[far, rows]).wait_recv()
+                    added(right_buf, far, rows, me - far)
+                    leftward(rows, piece, far, right_buf.at[far, rows]).start()
+
+    def finish():
+        for piece in range(chunks):
+            rows = pl.ds(piece * size, size)
+            out_ref[rows, :] = part_ref[me, rows, :].astype(F32)
+
+            @pl.when(me > 0)
+            def _():
+                rightward(rows, piece, 1, left_buf.at[0, rows]).wait_recv()
+                out_ref[rows, :] += left_buf[0, rows, :].astype(F32)
+
+            @pl.when(me < count - 1)
+            def _():
+                leftward(rows, piece, 1, right_buf.at[0, rows]).wait_recv()
+                out_ref[rows, :] += right_buf[0, rows, :].astype(F32)
+
+        for far in range(count - 1, 0, -1):
+            for piece in range(chunks):
+                rows = pl.ds(piece * size, size)
+
+                @pl.when((me == 0) & (me + far < count))
+                def _():
+                    rightward(rows, piece, far, part_ref.at[me + far, rows]).wait_send()
+
+                @pl.when((me == count - 1) & (me - far >= 0))
+                def _():
+                    leftward(rows, piece, far, part_ref.at[me - far, rows]).wait_send()
+
+                if far < count - 1:
+
+                    @pl.when((me > 0) & (me + far < count))
+                    def _():
+                        rightward(rows, piece, far, left_buf.at[far, rows]).wait_send()
+
+                    @pl.when((me < count - 1) & (me - far >= 0))
+                    def _():
+                        leftward(rows, piece, far, right_buf.at[far, rows]).wait_send()
+
+    return advance, finish
+
+
+def greet_line_and_plane(line, plane):
+    me, at_line = lax.axis_index("fsdp"), lax.axis_index("tensor")
+    barrier = pltpu.get_barrier_semaphore()
+
+    @pl.loop(1, plane)
+    def _(d):
+        pl.semaphore_signal(barrier, inc=1, device_id={"fsdp": lax.rem(me + d, plane)})
+
+    @pl.loop(1, line)
+    def _(d):
+        pl.semaphore_signal(barrier, inc=1, device_id={"tensor": lax.rem(at_line + d, line)})
+
+    pl.semaphore_wait(barrier, plane + line - 2)
+
+
+def front_body(
+    plane,
+    line,
+    scale,
+    places,
+    tokens_hbm,
+    cotangent_hbm,
+    routes_hbm,
+    weights_hbm,
+    gain_ref,
+    first_ref,
+    q_second_ref,
+    k_second_ref,
+    v_second_ref,
+    q_gain_ref,
+    k_gain_ref,
+    cos_ref,
+    sin_ref,
+    seg_column_ref,
+    seg_row_ref,
+    out_first_ref,
+    out_second_ref,
+    before_ref,
+    total_ref,
+    ranks_ref,
+    low_ref,
+    out_low_ref,
+    linear_hbm,
+    heads_hbm,
+    normed_hbm,
+    gathered_hbm,
+    up_hbm,
+    rows,
+    upstream,
+    routes,
+    weights,
+    linear,
+    heads,
+    keys,
+    values,
+    part,
+    left_buf,
+    right_buf,
+    sent_slots,
+    choice,
+    own_sem,
+    save_sem,
+    relay_right_send,
+    relay_right_recv,
+    relay_left_send,
+    relay_left_recv,
+    weight_send,
+    weight_recv,
+    pass_send,
+    pass_recv,
+    sum_right_send,
+    sum_right_recv,
+    sum_left_send,
+    sum_left_recv,
+    slot_send,
+    slot_recv,
+):
+    me, at_line = lax.axis_index("fsdp"), lax.axis_index("tensor")
+    rank = q_second_ref.shape[0]
+    head_dim = q_gain_ref.shape[1]
+    tokens, width = tokens_hbm.shape
+    slots = sent_slots.shape[2]
+    tile = 256
+    query_columns = q_second_ref.shape[1]
+    linear_columns = linear.shape[1]
+    out_start = places[1]
+
+    greet_line_and_plane(line, plane)
+
+    beside = me + 1 - 2 * lax.rem(me, 2)
+
+    def weight_copy(k):
+        target = lax.rem(me + 2 * k, plane)
+        return pltpu.make_async_remote_copy(
+            src_ref=weights_hbm,
+            dst_ref=weights.at[me],
+            send_sem=weight_send.at[k],
+            recv_sem=weight_recv.at[k],
+            device_id={"fsdp": target},
+        )
+
+    def weight_pass(k):
+        origin = lax.rem(me + plane - 2 * k, plane)
+        return pltpu.make_async_remote_copy(
+            src_ref=weights_hbm if k == 0 else weights.at[origin],
+            dst_ref=weights.at[origin],
+            send_sem=pass_send.at[k],
+            recv_sem=pass_recv.at[k],
+            device_id={"fsdp": beside},
+        )
+
+    peers = plane // 2
+    for k in range(1, peers):
+        weight_copy(k).start()
+    weight_pass(0).start()
+    locals_in = [
+        pltpu.make_async_copy(source, target, own_sem.at[at])
+        for at, (source, target) in enumerate(
+            [
+                (tokens_hbm, rows.at[at_line]),
+                (routes_hbm, routes.at[at_line]),
+                (cotangent_hbm, upstream.at[at_line]),
+                (weights_hbm, weights.at[me]),
+            ]
+        )
+    ]
+    advance, finish_relay = line_relay(
+        at_line,
+        line,
+        [tokens_hbm, routes_hbm, cotangent_hbm],
+        [rows, routes, upstream],
+        (4, 1, 4),
+        (relay_right_send, relay_right_recv, relay_left_send, relay_left_recv),
+    )
+    advance(0, (0, 1))
+    advance(0, (2,))
+    for each in locals_in:
+        each.start()
+    advance(1, (0, 1))
+    advance(2, (0, 1))
+    for k in range(1, peers):
+        weight_copy(k).wait_recv()
+        weight_pass(k).start()
+    advance(3, (0, 1))
+    for each in locals_in:
+        each.wait()
+
+    for block in range(line):
+        named = [
+            jnp.max(
+                (routes[block] == expert * line + at_line).astype(F32), axis=0, keepdims=True
+            )
+            for expert in range(plane)
+        ]
+        mask = jnp.concatenate(named, axis=0)
+        counts = matrix_product(mask.astype(BF16), before_ref[...])
+        ranks_ref[block] = jnp.where(mask > 0.0, counts, -1.0)
+
+    def slot_copy(block, d):
+        target = lax.rem(me + d, plane)
+        return pltpu.make_async_remote_copy(
+            src_ref=sent_slots.at[block, target],
+            dst_ref=up_hbm.at[me, block],
+            send_sem=slot_send.at[block, d],
+            recv_sem=slot_recv.at[block, d],
+            device_id={"fsdp": target},
+        )
+
+    def own_slots(block):
+        return pltpu.make_async_copy(
+            sent_slots.at[block, me], up_hbm.at[me, block], save_sem.at[4 + block]
+        )
+
+    def dispatch(block):
+        choice[...] = slot_choice(ranks_ref[block], slots)
+
+        def slot_step(columns):
+            sent_slots[block, :, :, columns] = (
+                matrix_product(choice[...], upstream[block, :, columns])
+                .astype(BF16)
+                .reshape(plane, slots, 2 * tile)
+            )
+
+        tiles(width, 2 * tile, slot_step)
+
+        @pl.loop(1, plane)
+        def _(d):
+            slot_copy(block, d).start()
+
+    def dispatch_at(distance):
+        if distance == 0:
+            dispatch(at_line)
+            return
+
+        @pl.when(at_line - distance >= 0)
+        def _():
+            dispatch(at_line - distance)
+
+        @pl.when(at_line + distance < line)
+        def _():
+            dispatch(at_line + distance)
+
+    dispatch_at(0)
+
+    finish_relay((0,), range(1, line - 1))
+
+    @pl.loop(0, line * tokens // 128)
+    def _(j):
+        block, at = j // (tokens // 128), pl.ds((j % (tokens // 128)) * 128, 128)
+        wide = rows[block, at, :].astype(F32)
+        rows[block, at, :] = norm_forward(wide, gain_ref[...])[0].astype(BF16)
+
+    for k in range(peers):
+        weight_pass(k).wait_recv()
+    saves = [
+        pltpu.make_async_copy(rows, normed_hbm, save_sem.at[0]),
+        pltpu.make_async_copy(weights, gathered_hbm, save_sem.at[1]),
+        pltpu.make_async_copy(linear, linear_hbm, save_sem.at[2]),
+        pltpu.make_async_copy(heads, heads_hbm, save_sem.at[3]),
+    ]
+    saves[0].start()
+    saves[1].start()
+
+    @pl.loop(0, line)
+    def _(block):
+        at = pl.ds(pl.multiple_of(block * tokens, tokens), tokens)
+        low_ref[at, :] = flipped_right_operand(rows[block], first_ref[...]).astype(BF16)
+
+        def project(columns):
+            linear[at, columns] = matrix_product(
+                rows[block], weights[:, :, columns].reshape(width, tile)
+            )
+
+        tiles(linear_columns, tile, project)
+
+    saves[2].start()
+    advance(1, (2,))
+    dispatch_at(1)
+
+    cosine, sine = cos_ref[...], sin_ref[...]
+    keys[...] = head_values(
+        linear[:, query_columns : query_columns + head_dim],
+        low_ref[:, rank : 2 * rank],
+        k_second_ref[...],
+        k_gain_ref[...],
+        cosine,
+        sine,
+    )[2]
+    values[...] = (
+        linear[:, query_columns + head_dim : query_columns + 2 * head_dim]
+        + matrix_product(low_ref[:, 2 * rank : 3 * rank], v_second_ref[...])
+    ).astype(BF16)
+
+    @pl.loop(0, query_columns // head_dim)
+    def _(head):
+        columns = pl.ds(pl.multiple_of(head * head_dim, head_dim), head_dim)
+        query = head_values(
+            linear[:, columns],
+            low_ref[:, :rank],
+            q_second_ref[:, columns],
+            q_gain_ref[...],
+            cos_ref[...],
+            sin_ref[...],
+        )[2]
+        seg_column, seg_row = seg_column_ref[...], seg_row_ref[...]
+        for block in range(query.shape[0] // WINDOW):
+            start, span = block_bounds(block)
+            scores = (
+                flipped_right_operand(
+                    query[block * WINDOW : (block + 1) * WINDOW], keys[pl.ds(start, span)]
+                )
+                * scale
+            )
+            scores = jnp.where(
+                allowed_keys(block, start, span, seg_column, seg_row), scores, -1e30
+            )
+            expo = jnp.exp(scores - jnp.max(scores, axis=-1, keepdims=True))
+            probs = (expo / jnp.sum(expo, axis=-1, keepdims=True)).astype(BF16)
+            heads[pl.ds(block * WINDOW, WINDOW), columns] = matrix_product(
+                probs, values[pl.ds(start, span)]
+            ).astype(BF16)
+
+    saves[3].start()
+    advance(2, (2,))
+    dispatch_at(2)
+
+    out_low_ref[...] = flipped_right_operand(heads[...], out_first_ref[...]).astype(BF16)
+
+    @pl.loop(0, line)
+    def _(block):
+        at = pl.ds(pl.multiple_of(block * tokens, tokens), tokens)
+
+        @pl.loop(0, plane)
+        def _(shard):
+            wide = width // plane
+            columns = pl.ds(pl.multiple_of(shard * wide, wide), wide)
+            part[block, :, columns] = (
+                flipped_right_operand(heads[at, :], weights[shard, :, out_start:])
+                + matrix_product(out_low_ref[at, :], out_second_ref[:, columns])
+            ).astype(BF16)
+
+    advance_sum, finish_sum = line_sum(
+        at_line,
+        line,
+        4,
+        part,
+        total_ref,
+        left_buf,
+        right_buf,
+        (sum_right_send, sum_right_recv, sum_left_send, sum_left_recv),
+    )
+    for far in range(line - 1, 0, -1):
+        advance_sum(far)
+        if far == 2:
+            advance(3, (2,))
+            dispatch_at(3)
+    finish_sum()
+
+    for block in range(line):
+        own_slots(block).start()
+    for each in saves:
+        each.wait()
+    finish_relay((0,), (0,))
+    finish_relay((1, 2), range(line - 1))
+    for k in range(1, peers):
+        weight_copy(k).wait_send()
+    for k in range(peers):
+        weight_pass(k).wait_send()
+
+    @pl.loop(0, line)
+    def _(block):
+        @pl.loop(1, plane)
+        def _(d):
+            slot_copy(block, d).wait_recv()
+            slot_copy(block, d).wait_send()
+
+    for block in range(line):
+        own_slots(block).wait()
+
+
+def front(
+    tokens,
+    cotangent,
+    routes,
+    packed,
+    gain,
+    first,
+    q_second,
+    k_second,
+    v_second,
+    q_gain,
+    k_gain,
+    tables,
+    seg_column,
+    seg_row,
+    out_first,
+    out_second,
+    scale,
+    slots,
+    places,
+    identity,
+):
+    line, plane = lax.axis_size("tensor"), lax.axis_size("fsdp")
+    count, width = tokens.shape
+    all_rows = line * count
+    rank, query_columns = q_second.shape
+    head_dim = q_gain.shape[1]
+    linear_columns = query_columns + 2 * head_dim
+    order = jnp.arange(count, dtype=jnp.int32)
+    before = (order[:, None] < order[None, :]).astype(BF16)
+    anywhere = pl.BlockSpec(memory_space=pl.ANY)
+    local = pl.BlockSpec(memory_space=pltpu.VMEM)
+    dma = pltpu.SemaphoreType.DMA
+    up_shape = (plane, line, slots, width)
+    operands = [
+        gain,
+        first,
+        q_second,
+        k_second,
+        v_second,
+        q_gain,
+        k_gain,
+        *tables,
+        seg_column,
+        seg_row,
+        out_first,
+        out_second,
+        before,
+    ]
+    return pl.pallas_call(
+        functools.partial(front_body, plane, line, scale, places),
+        out_shape=[
+            jax.ShapeDtypeStruct((count, width), F32),
+            jax.ShapeDtypeStruct((line, plane, count), F32),
+            jax.ShapeDtypeStruct((all_rows, 3 * rank), BF16),
+            jax.ShapeDtypeStruct((all_rows, rank), BF16),
+            jax.ShapeDtypeStruct((all_rows, linear_columns), F32),
+            jax.ShapeDtypeStruct((all_rows, query_columns), BF16),
+            jax.ShapeDtypeStruct((line, count, width), BF16),
+            jax.ShapeDtypeStruct((plane,) + packed.shape, BF16),
+            jax.ShapeDtypeStruct(up_shape, BF16),
+        ],
+        in_specs=[anywhere] * 4 + [local] * len(operands),
+        out_specs=[local] * 4 + [anywhere] * 5,
+        scratch_shapes=[
+            pltpu.VMEM((line, count, width), BF16),
+            pltpu.VMEM((line, count, width), BF16),
+            pltpu.VMEM((line,) + routes.shape, jnp.int32),
+            pltpu.VMEM((plane,) + packed.shape, BF16),
+            pltpu.VMEM((all_rows, linear_columns), F32),
+            pltpu.VMEM((all_rows, query_columns), BF16),
+            pltpu.VMEM((all_rows, head_dim), BF16),
+            pltpu.VMEM((all_rows, head_dim), BF16),
+            pltpu.VMEM((line, count, width), BF16),
+            pltpu.VMEM((line - 1, count, width), BF16),
+            pltpu.VMEM((line - 1, count, width), BF16),
+            pltpu.VMEM((line, plane, slots, width), BF16),
+            pltpu.VMEM((plane * slots, count), BF16),
+            dma((4,)),
+            dma((4 + line,)),
+        ]
+        + [dma((line - 1, 9))] * 4
+        + [dma((plane // 2,))] * 4
+        + [dma((line - 1, 4))] * 4
+        + [dma((line, plane))] * 2,
+        compiler_params=pltpu.CompilerParams(
+            collective_id=identity, has_side_effects=True, vmem_limit_bytes=63 * MEBI
+        ),
+        name="front",
+    )(tokens, cotangent, routes, packed, *operands)
 
 
 def per_device(
@@ -1452,27 +1877,25 @@
     gain_query = q_gain.astype(F32)[None, :]
     gain_key = key_norm_gain.astype(F32)[None, :]
 
-    packed_weights = lax.all_gather(
-        jnp.concatenate(
-            [w_query, key_projection_weight, value_projection_weight, w_router], axis=1
-        ),
-        "fsdp",
-        axis=0,
-        tiled=True,
-    )
+    in_kernel = fsdp_count * slots <= 640
     linear_cols = local_cols + 2 * local_kv_cols
-    complete_linear = packed_weights[:, :linear_cols]
-    complete_router = packed_weights[:, linear_cols:]
-    full_out = lax.all_gather(w_out, "fsdp", axis=1, tiled=True)
-    sequence_tokens, sequence_routes, sequence_cotangent = gather_line(
-        [tokens, jnp.transpose(routes, (1, 0)), cotangent], (4, 1, 4), 0
-    )
-    sequence_tokens = sequence_tokens.reshape(seq_rows, model_width)
-    plane_experts = jnp.arange(fsdp_count, dtype=jnp.int32) * tensor_count + tensor_pos
-    plane_mask = jnp.any(
-        sequence_routes[:, None, :, :] == plane_experts[None, :, None, None], axis=2
-    )
-    plane_ranks = ranks_of(plane_mask)
+    router_pad = -(-expert_count // 128) * 128
+    out_start = linear_cols + router_pad
+    packed = jnp.concatenate(
+        [
+            w_query,
+            key_projection_weight,
+            value_projection_weight,
+            jnp.pad(w_router, ((0, 0), (0, router_pad - expert_count))),
+            jnp.transpose(w_out, (1, 0)),
+        ],
+        axis=1,
+    )
+    tables = rope_tables(seq_rows, head_dim)
+    seg_row = segments
+    seg_column = jnp.transpose(segments, (1, 0))
+    token_values = tokens.astype(F32)
+    attn_normed, attn_factor = norm_forward(token_values, gain_attn)
     offsets = [0] + [sign * step for step in range(1, tensor_count) for sign in (1, -1)]
     offsets = [offset % tensor_count for offset in offsets[:tensor_count]]
     line_blocks = [((tensor_pos + offset) % tensor_count)[None] for offset in offsets]
@@ -1495,27 +1918,62 @@
             for offset, at in zip(offsets, line_blocks)
         ]
 
-    in_kernel = fsdp_count * slots <= 640
     if in_kernel:
-        slotted = all_to_slots(
-            plane_ranks, sequence_cotangent.reshape(seq_rows, model_width), slots
-        )
-        slotted, sequence_tokens = lax.optimization_barrier((slotted, sequence_tokens))
-        up_rows = plane_rows(
-            slotted.reshape(fsdp_count, tensor_count * slots, model_width)
-        ).reshape(fsdp_count, tensor_count, slots, model_width)
+        (
+            attention_total,
+            plane_ranks,
+            low,
+            attention_low,
+            linear,
+            heads_narrow,
+            sequence_normalized,
+            gathered,
+            up_rows,
+        ) = front(
+            tokens,
+            cotangent,
+            jnp.transpose(routes, (1, 0)),
+            packed,
+            gain_attn[None, :],
+            input_first,
+            q_second,
+            k_second,
+            v_second,
+            gain_query,
+            gain_key,
+            tables,
+            seg_column,
+            seg_row,
+            attention_first,
+            attention_second,
+            score_scale,
+            slots,
+            (linear_cols, out_start),
+            0,
+        )
+        sequence_normalized = sequence_normalized.reshape(seq_rows, model_width)
+        gathered = gathered.reshape(model_width, -1)
     else:
+        gathered = lax.all_gather(packed, "fsdp", axis=0, tiled=True)
+        sequence_tokens, sequence_routes = gather_line(
+            [tokens, jnp.transpose(routes, (1, 0))], (4, 1), 0
+        )
+        sequence_tokens = sequence_tokens.reshape(seq_rows, model_width)
+        plane_experts = jnp.arange(fsdp_count, dtype=jnp.int32) * tensor_count + tensor_pos
+        plane_ranks = ranks_of(
+            jnp.any(
+                sequence_routes[:, None, :, :] == plane_experts[None, :, None, None], axis=2
+            )
+        )
         up_rows = dispatched(cotangent)
-
-    token_values = tokens.astype(F32)
-    attn_normed, attn_factor = norm_forward(token_values, gain_attn)
-    attention_narrow = attn_normed.astype(BF16)
-    sequence_normalized = norm_forward(sequence_tokens.astype(F32), gain_attn)[0].astype(BF16)
-    linear = matrix_product(sequence_normalized, complete_linear)
-    low = flipped_right_operand(sequence_normalized, input_first).astype(BF16)
-    tables = rope_tables(seq_rows, head_dim)
-    seg_row = segments
-    seg_column = jnp.transpose(segments, (1, 0))
+        sequence_normalized = norm_forward(sequence_tokens.astype(F32), gain_attn)[0].astype(
+            BF16
+        )
+        linear = matrix_product(sequence_normalized, gathered[:, :linear_cols])
+        low = flipped_right_operand(sequence_normalized, input_first).astype(BF16)
+    complete_linear = gathered[:, :linear_cols]
+    complete_router = gathered[:, linear_cols : linear_cols + expert_count]
+    full_out_t = gathered[:, out_start:]
     attention_operands = (
         linear,
         low,
@@ -1529,15 +1987,15 @@
         seg_row,
         score_scale,
     )
-    heads_narrow = attention_forward(*attention_operands)
-    attention_low = flipped_right_operand(heads_narrow, attention_first).astype(BF16)
-    out_part = matrix_product(heads_narrow, full_out) + matrix_product(
-        attention_low, attention_second
-    )
-    attention_total = sum_line(
-        out_part.astype(BF16).reshape(tensor_count, tok_rows, model_width), 4, 1
-    )
-    up_rows, attention_total = lax.optimization_barrier((up_rows, attention_total))
+    if not in_kernel:
+        heads_narrow = attention_forward(*attention_operands)
+        attention_low = flipped_right_operand(heads_narrow, attention_first).astype(BF16)
+        out_part = flipped_right_operand(heads_narrow, full_out_t) + matrix_product(
+            attention_low, attention_second
+        )
+        attention_total = sum_line(
+            out_part.astype(BF16).reshape(tensor_count, tok_rows, model_width), 4, 1
+        )
     residual_stream = token_values + attention_total
     moe_normed, moe_factor = norm_forward(residual_stream, gain_moe)
     experts_narrow = moe_normed.astype(BF16)
@@ -1641,15 +2099,16 @@
         back_output = plane_rows(
             expert_output.reshape(fsdp_count, tensor_count * slots, model_width)
         ).reshape(fsdp_count, tensor_count, slots, model_width)
-        back_output, sequence_branch = lax.optimization_barrier((back_output, sequence_branch))
-        combined = all_from_slots(tensor_pos[None], plane_ranks, back_output)
-        moe_output = lax.psum_scatter(combined, "tensor", scatter_dimension=0, tiled=True)
-        output = (residual_stream + moe_output.astype(F32)).astype(BF16)
     else:
         output = (residual_stream + returned(expert_output)).astype(BF16)
     attention_low_grad = flipped_right_operand(sequence_branch, attention_second).astype(BF16)
     attention_second_gradient = flipped_left_operand(attention_low, sequence_branch)
-    heads_grad = flipped_right_operand(sequence_branch, full_out)
+    heads_grad = matrix_product(sequence_branch, full_out_t)
+    if in_kernel:
+        back_output, heads_grad = lax.optimization_barrier((back_output, heads_grad))
+        combined = all_from_slots(tensor_pos[None], plane_ranks, back_output)
+        moe_output = lax.psum_scatter(combined, "tensor", scatter_dimension=0, tiled=True)
+        output = (residual_stream + moe_output.astype(F32)).astype(BF16)
     (
         q_grad,
         k_grad,

time: 990 us -> 871 us (0.88)
  waiting for transfers between devices: 72.3 us -> 25.9 us
  matrix products: 65.8 us -> 33 us
  Pallas kernels: 717 us -> 696 us
  local copies, waits for them, and re-layouts: 51.6 us -> 39.2 us
    pallas_call x2 -> x1, Pallas kernels: 27.1 us -> 220 us  [front(): pl.pallas_call(functools.partial(front_body, plane, line, scale, places),...]
    pallas_call x2 -> x1, Pallas kernels: 217 us -> 78.8 us  [gather_line(): pl.pallas_call(functools.partial(gather_line_body, count, chunks), out_sh...]
    pallas_call x2 -> x1, Pallas kernels: 145 us -> 71 us  [sum_line(): pl.pallas_call(functools.partial(sum_line_body, count, chunks), out_shape...]
    all_gather x2 -> x0, waiting for transfers between devices: 43.3 us -> none  [the longest x1 43.3 us: per_device(): full_out = lax.all_gather(w_out, 'fsdp', axis=1, tiled=True)]
    dot_general x8 -> x5, matrix products: 30.8 us -> 11.6 us  [flipped_right_operand(): lax.dot_general(first_op, second_op, (((1,), (1,)), ((), ())), preferred_...]
    dot_general x11 -> x8, matrix products: 28.4 us -> 17.2 us  [matrix_product(): return jnp.dot(first_op, second_op, preferred_element_type=F32)]
    unnamed x170 -> x129, local copies, waits for them, and re-layouts: 26.4 us -> 17.4 us
    all_to_all x2 -> x1, waiting for transfers between devices: 23.3 us -> 16.4 us  [plane_rows(): lax.all_to_all(block_rows, 'fsdp', split_axis=0, concat_axis=0, tiled=True)]
  transfers between devices with their start and end apart: 8 -> 5, of which waited for: 3 -> 3; matrix products, arithmetic and copies ran while one was open for 11% -> 6% of each run, Pallas kernels for 45% -> 22%
where the time goes in v4:
time: 871 us; the launch traced here: 861 us
  Pallas kernels  696 us (80%)
  local copies, waits for them, and re-layouts  39.2 us (5%)
  matrix products  33 us (4%)
  starting transfers between devices  28.5 us (3%)
  waiting for transfers between devices  25.9 us (3%)
  other arithmetic  20.8 us (2%)
  between operations  17.2 us (2%)
    pallas_call x1, Pallas kernels, moe_layer(): pl.pallas_call(functools.partial(moe_body, plane, line), out_shape=[jax.S...  279 us
    pallas_call x1, Pallas kernels, front(): pl.pallas_call(functools.partial(front_body, plane, line, scale, places),...  220 us
    pallas_call x1, Pallas kernels, gather_line(): pl.pallas_call(functools.partial(gather_line_body, count, chunks), out_sh...  78.8 us
    pallas_call x1, Pallas kernels, sum_line(): pl.pallas_call(functools.partial(sum_line_body, count, chunks), out_shape...  71 us
    pallas_call x1, Pallas kernels, attention_backward(): pl.pallas_call(functools.partial(attention_backward_body, rank, scale), g...  41 us
    all_to_all x3, starting transfers between devices, route_rows(): lax.all_to_all(block_rows, ('fsdp', 'tensor'), split_axis=0, concat_axis=...  22.7 us
    unnamed x129, local copies, waits for them, and re-layouts  17.4 us
  transfers between devices with their start and end apart: 5, of which 3 were waited for; matrix products, arithmetic and copies ran while one was open for 6% of the time, Pallas kernels for 22%

profile of v4, /device:TPU:16, one launch (start us, length us, event | category | flops | bytes accessed | tf_op | source)
XLA Modules:
  0.0 860.9 jit_solution(16145827354583229384)
XLA Ops:
  7.3 1.3 dynamic_slice.38
  11.3 0.9 dynamic-slice_bitcast_fusion.3
  12.1 1.5 dynamic-slice_bitcast_fusion.out_second_ref
  13.6 1.4 dynamic-slice_bitcast_fusion.4.out_first_ref.down_ref
  15.0 1.4 dynamic-slice_bitcast_fusion.5.q_second_ref
  16.4 2.0 fusion.29
  18.9 1.0 copy.137.seg_column_ref
  20.0 0.8 constant_dynamic-update-slice_fusion.2
  21.2 0.9 dynamic-slice_bitcast_fusion.1
  22.1 1.3 dynamic-slice_bitcast_fusion.6
  27.4 1.3 pad_maximum_fusion.1
  28.7 219.6 %front.1 = (f32[256,2048]{1,0:T(8,128)}, f32[4,8,256]{2,1,0:T(8,128)}, bf16[1024,48]{1,0:T(8,128)(2,1)}, bf16[1024,16]{1,0:T(8,128)(2,1)}, f32[1024,1280]{1,0:T(...) custom-call(bf16[256,2048]{1,0:T(8,128)(2,1)} %tokens_hbm.1, ...), custom_call_target="tpu_custom_call" | custom-call | tf_op jit(solution)/shard_map/front/pallas_call | solution.py:1761
  248.4 2.4 multiply_reduce_fusion.1
  251.6 1.9 fusion.23
  253.8 0.9 fusion.46
  255.5 3.0 all-to-all-start
  258.5 1.0 pad_maximum_fusion.rest_3_
  259.7 4.0 all-to-all-done
  265.8 279.1 %moe_layer.1 = (f32[256,2048]{1,0:T(8,128)}, f32[4,8,256]{2,1,0:T(8,128)}, bf16[8,4,80,2048]{3,2,1,0:T(8,128)(2,1)}, bf16[4,8,80,2048]{3,2,1,0:T(8,128)(2,1)}, f...) custom-call(bf16[256,2048]{1,0:T(8,128)(2,1)} %copy-done.24, ...), custom_call_target="tpu_custom_call" | custom-call | tf_op jit(solution)/shard_map/moe_layer/pallas_call | solution.py:1088
  544.9 5.3 all-to-all-start.1
  551.8 1.7 convolution_add_fusion.1
  553.8 0.9 fusion.10
  555.1 2.3 fusion.55
  557.4 78.8 %gather_line.1 = bf16[4,256,2048]{2,1,0:T(8,128)(2,1)} custom-call(bf16[256,2048]{1,0:T(8,128)(2,1)} %get-tuple-element.182.refs_0_), custom_call_target="tpu_custom_call" | custom-call | tf_op jit(solution)/shard_map/gather_line/pallas_call | solution.py:1173
  636.2 2.9 convolution_convert_fusion.1
  640.4 10.0 %fusion.2.heads_grad_ref = f32[1024,1024]{1,0:T(8,128)} fusion(bf16[1024,2048]{1,0:T(8,128)(2,1)} %bitcast.212, bf16[2048,2432]{1,0:T(8,128)(2,1)} %bitcast.244), kind=kOutput, calls=%fused_computation.3 | convolution fusion | flops 4294967296 | bytes 12582912 | tf_op jit(solution)/shard_map/dot_general | solution.py:20
  650.4 16.4 %all-to-all-done.1 = bf16[8,320,2048]{2,1,0:T(8,128)(2,1)} async-done(((bf16[8,320,2048]{2,1,0:T(8,128)(2,1)}), bf16[8,320,2048]{2,1,0:T(8,128)(2,1)}, u32[]{:S(2)}, u32[]{:S(2)}) %all-to-all-start.1) | async-done | bytes 10485792 | tf_op jit(solution)/shard_map/all_to_all | solution.py:67
  666.8 6.7 all_from_slots.1
  673.6 2.0 copy-done.2
  676.9 0.8 reshape.267
  677.7 14.6 %all-to-all-start.3 = ((bf16[32,2,1032]{2,1,0:T(2,128)(2,1)}), bf16[32,2,1032]{2,1,0:T(2,128)(2,1)S(1)}, u32[]{:S(2)}, u32[]{:S(2)}) async-start(bf16[32,2,1032]{2,1,0:T(2,128)(2,1)} %reshape.267), calls=%async_computation.4 | async-start | bytes 294912 | tf_op jit(solution)/shard_map/all_to_all | solution.py:63
  692.3 1.5 fusion.56
  693.7 1.5 copy-done.23
  695.3 1.2 convolution_convert_fusion.3
  696.7 5.5 all-to-all-done.3
  704.6 41.0 %attention_backward.1 = (bf16[1024,1024]{1,0:T(8,128)(2,1)S(1)}, bf16[1024,128]{1,0:T(8,128)(2,1)S(1)}, bf16[1024,128]{1,0:T(8,128)(2,1)S(1)}, bf16[1024,48]{1,0...) custom-call(f32[1024,1280]{1,0:T(8,128)} %get-tuple-element.53.lin_r, ...), custom_call_target="tpu_custom_call" | custom-call | flops 5368709120 | bytes 12582912 | tf_op jit(solution)/shard_map/attention_backward/pallas_call | solution.py:350
  745.6 1.4 copy-done.16
  747.0 0.9 convolution_convert_fusion
  750.1 2.0 reduce.1
  752.2 0.9 reshape.265
  753.0 5.1 all-to-all-start.2
  758.2 7.6 fusion
  765.8 1.2 add_convert_fusion
  767.1 71.0 %sum_line.1 = f32[256,2048]{1,0:T(8,128)S(1)} custom-call(bf16[4,256,2048]{2,1,0:T(8,128)(2,1)S(1)} %bitcast.209), custom_call_target="tpu_custom_call" | custom-call | tf_op jit(solution)/shard_map/sum_line/pallas_call | solution.py:1199
  838.5 1.7 reshape.266
  840.2 1.4 fusion.19
  845.1 5.4 fusion.13
  852.8 1.0 copy.208
  (205 shorter events, 25.4 us)
Async XLA Ops:
  7.2 246.3 %copy-start = (bf16[8,2048,16]{1,2,0:T(8,128)(2,1)S(1)}, bf16[8,2048,16]{1,2,0:T(8,128)(2,1)}, u32[]{:S(2)}) copy-start(bf16[8,2048,16]{1,2,0:T(8,128)(2,1)} %param.58) | copy-start | bytes 1572868
  7.2 11.1 %copy-start.49 = (bf16[2048]{0:T(1024)(128)(2,1)S(1)}, bf16[2048]{0:T(1024)(128)(2,1)}, u32[]{:S(2)}) copy-start(bf16[2048]{0:T(1024)(128)(2,1)} %param.38) | copy-start | bytes 12292
  7.2 11.7 %copy-start.10 = (s32[1,1024]{1,0:T(1,128)S(1)}, s32[1,1024]{1,0:T(1,128)}, u32[]{:S(2)}) copy-start(s32[1,1024]{1,0:T(1,128)} %seg_row_ref.3) | copy-start | bytes 12292
  7.2 12.7 %copy-start.35 = (bf16[256,1024]{1,0:T(8,128)(2,1)S(1)}, bf16[256,1024]{1,0:T(8,128)(2,1)}, u32[]{:S(2)}) copy-start(bf16[256,1024]{1,0:T(8,128)(2,1)} %param.42) | copy-start | bytes 1572868
  7.2 13.6 %copy-start.48 = (bf16[256,32]{0,1:T(8,128)(2,1)S(1)}, bf16[256,32]{0,1:T(8,128)(2,1)}, u32[]{:S(2)}) copy-start(bf16[256,32]{0,1:T(8,128)(2,1)} %param.46) | copy-start | bytes 49156
  7.2 13.7 %copy-start.36 = (bf16[1024,256]{1,0:T(8,128)(2,1)S(1)}, bf16[1024,256]{1,0:T(8,128)(2,1)}, u32[]{:S(2)}) copy-start(bf16[1024,256]{1,0:T(8,128)(2,1)} %param.45) | copy-start | bytes 1572868
  16.3 4.8 copy-start.46
  16.3 7.1 copy-start.52
  16.3 7.1 copy-start.53
  16.3 7.6 copy-start.44
  16.3 8.3 copy-start.45
  22.1 6.6 copy-start.32
  251.5 7.0 copy-start.37
  251.6 7.0 copy-start.38
  253.5 6.1 copy-start.51
  255.5 8.2 all-to-all-start
  544.9 6.0 copy-start.47
  544.9 6.9 copy-start.29
  544.9 121.9 %all-to-all-start.1 = ((bf16[8,320,2048]{2,1,0:T(8,128)(2,1)}), bf16[8,320,2048]{2,1,0:T(8,128)(2,1)}, u32[]{:S(2)}, u32[]{:S(2)}) async-start(bf16[8,320,2048]{2,1,0:T(8,128)(2,1)} %bitcast.214), calls=%async_computation.1 | async-start | bytes 20971520 | tf_op jit(solution)/shard_map/all_to_all | solution.py:67
  550.3 294.8 %reduce-scatter.2.cloned.1.call-start = ((), (), s32[]{:S(2)}) async-start(), calls=%async_computation.5 | async-start | bytes 5242880 | tf_op jit(solution)/shard_map/reduce_scatter | solution.py:2110
  557.4 78.8 %copy-start.42 = (bf16[1024,16]{1,0:T(8,128)(2,1)S(1)}, bf16[1024,16]{1,0:T(8,128)(2,1)}, u32[]{:S(2)}) copy-start(bf16[1024,16]{1,0:T(8,128)(2,1)} %get-tuple-element.66) | copy-start | bytes 98308
  636.2 3.4 copy-start.25
  640.4 26.4 %copy-start.9 = (f32[4,8,256]{2,1,0:T(8,128)S(1)}, f32[4,8,256]{2,1,0:T(8,128)}, u32[]{:S(2)}) copy-start(f32[4,8,256]{2,1,0:T(8,128)} %get-tuple-element.46.plane_rank_ref.rank_ref) | copy-start | bytes 98308
  675.5 16.7 %copy-start.28 = (f32[256,2048]{1,0:T(8,128)S(1)}, f32[256,2048]{1,0:T(8,128)}, u32[]{:S(2)}) copy-start(f32[256,2048]{1,0:T(8,128)} %get-tuple-element.67) | copy-start | bytes 6291460
  675.5 18.2 %copy-start.34 = (bf16[16,2048]{1,0:T(8,128)(2,1)S(1)}, bf16[16,2048]{1,0:T(8,128)(2,1)}, u32[]{:S(2)}) copy-start(bf16[16,2048]{1,0:T(8,128)(2,1)} %dynamic-slice_bitcast_fusion.out_second_ref) | copy-start | bytes 196612
  677.7 24.5 %all-to-all-start.3 = ((bf16[32,2,1032]{2,1,0:T(2,128)(2,1)}), bf16[32,2,1032]{2,1,0:T(2,128)(2,1)S(1)}, u32[]{:S(2)}, u32[]{:S(2)}) async-start(bf16[32,2,1032]{2,1,0:T(2,128)(2,1)} %reshape.267), calls=%async_computation.4 | async-start | bytes 294912 | tf_op jit(solution)/shard_map/all_to_all | solution.py:63
  692.3 2.9 copy-start.23
  695.2 9.3 %copy-start.3 = (f32[1024,128]{1,0:T(8,128)S(1)}, f32[1024,128]{1,0:T(8,128)}, u32[]{:S(2)}) copy-start(f32[1024,128]{1,0:T(8,128)} %get-tuple-element.211.cos_ref) | copy-start | bytes 1572868
  695.2 9.3 %copy-start.4 = (f32[1024,128]{1,0:T(8,128)S(1)}, f32[1024,128]{1,0:T(8,128)}, u32[]{:S(2)}) copy-start(f32[1024,128]{1,0:T(8,128)} %get-tuple-element.212.sin_ref) | copy-start | bytes 1572868
  695.2 9.3 %copy-start.5 = (s32[1024,1]{1,0:T(8,128)S(1)}, s32[1024,1]{1,0:T(8,128)}, u32[]{:S(2)}) copy-start(s32[1024,1]{1,0:T(8,128)} %copy.137.seg_column_ref) | copy-start | bytes 12292
  695.2 9.3 %copy-start.6 = (bf16[16,1024]{1,0:T(8,128)(2,1)S(1)}, bf16[16,1024]{1,0:T(8,128)(2,1)}, u32[]{:S(2)}) copy-start(bf16[16,1024]{1,0:T(8,128)(2,1)} %dynamic-slice_bitcast_fusion.4.out_first_ref.down_ref) | copy-start | bytes 98308
  695.2 9.3 %copy-start.7 = (bf16[16,1024]{1,0:T(8,128)(2,1)S(1)}, bf16[16,1024]{1,0:T(8,128)(2,1)}, u32[]{:S(2)}) copy-start(bf16[16,1024]{1,0:T(8,128)(2,1)} %dynamic-slice_bitcast_fusion.5.q_second_ref) | copy-start | bytes 98308
  695.2 9.3 %copy-start.8 = (bf16[1024,48]{1,0:T(8,128)(2,1)S(1)}, bf16[1024,48]{1,0:T(8,128)(2,1)}, u32[]{:S(2)}) copy-start(bf16[1024,48]{1,0:T(8,128)(2,1)} %get-tuple-element.54.low_ref) | copy-start | bytes 294916
  695.3 9.3 %copy-start.11 = (s32[1,1024]{1,0:T(1,128)S(1)}, s32[1,1024]{1,0:T(1,128)}, u32[]{:S(2)}) copy-start(s32[1,1024]{1,0:T(1,128)} %seg_row_ref.3) | copy-start | bytes 12292
  695.3 9.3 %copy-start.12 = (bf16[16,128]{1,0:T(8,128)(2,1)S(1)}, bf16[16,128]{1,0:T(8,128)(2,1)}, u32[]{:S(2)}) copy-start(bf16[16,128]{1,0:T(8,128)(2,1)} %get-tuple-element.209.v_second_ref) | copy-start | bytes 12292
  695.3 9.3 %copy-start.13 = (bf16[16,128]{1,0:T(8,128)(2,1)S(1)}, bf16[16,128]{1,0:T(8,128)(2,1)}, u32[]{:S(2)}) copy-start(bf16[16,128]{1,0:T(8,128)(2,1)} %get-tuple-element.210.k_second_ref) | copy-start | bytes 12292
  695.3 9.3 %copy-start.14 = (f32[1,128]{1,0:T(1,128)S(1)}, f32[1,128]{1,0:T(1,128)}, u32[]{:S(2)}) copy-start(f32[1,128]{1,0:T(1,128)} %get-tuple-element.213.k_gain_ref) | copy-start | bytes 1540
  695.3 9.3 %copy-start.15 = (f32[1,128]{1,0:T(1,128)S(1)}, f32[1,128]{1,0:T(1,128)}, u32[]{:S(2)}) copy-start(f32[1,128]{1,0:T(1,128)} %get-tuple-element.214.q_gain_ref) | copy-start | bytes 1540
  704.6 42.4 %copy-start.26 = (bf16[4,256,2048]{2,1,0:T(8,128)(2,1)S(1)}, bf16[4,256,2048]{2,1,0:T(8,128)(2,1)}, u32[]{:S(2)}) copy-start(bf16[4,256,2048]{2,1,0:T(8,128)(2,1)} %get-tuple-element.61) | copy-start | bytes 12582916
  749.2 9.0 %copy-start.17 = (bf16[1024,1024]{1,0:T(8,128)(2,1)S(1)}, bf16[1024,1024]{1,0:T(8,128)(2,1)}, u32[]{:S(2)}) copy-start(bf16[1024,1024]{1,0:T(8,128)(2,1)} %copy-done.16) | copy-start | bytes 6291460
  753.0 85.5 %all-to-all-start.2 = ((bf16[32,2,3840]{2,1,0:T(2,128)(2,1)}), bf16[32,2,3840]{2,1,0:T(2,128)(2,1)S(1)}, u32[]{:S(2)}, u32[]{:S(2)}) async-start(bf16[32,2,3840]{2,1,0:T(2,128)(2,1)} %reshape.265), calls=%async_computation.3 | async-start | bytes 983040 | tf_op jit(solution)/shard_map/all_to_all | solution.py:63
  758.2 7.6 copy-start.33
  767.1 71.0 %copy-start.22 = (bf16[256,2048]{1,0:T(8,128)(2,1)S(1)}, bf16[256,2048]{1,0:T(8,128)(2,1)}, u32[]{:S(2)}) copy-start(bf16[256,2048]{1,0:T(8,128)(2,1)} %tokens_hbm.1) | copy-start | bytes 3145732
  767.1 71.0 %copy-start.43 = (f32[2048]{0:T(1024)S(1)}, f32[2048]{0:T(1024)}, u32[]{:S(2)}) copy-start(f32[2048]{0:T(1024)} %convert_element_type.80) | copy-start | bytes 24580
  845.1 5.5 copy-start.41
  845.1 6.2 copy-start.40
  845.1 7.0 copy-start.39
  850.6 3.2 copy-start.1
  (11 other events, 21.1 us)
Sparse Core Ops, SparseCore 0:
  675.7 89.8 reduce-scatter.1

commit v5 on v4

--- a/solution.py
+++ b/solution.py
@@ -1801,6 +1801,485 @@
     )(tokens, cotangent, routes, packed, *operands)
 
 
+def back_body(
+    plane,
+    line,
+    scale,
+    places,
+    moe_total_ref,
+    dots_ref,
+    gates_ref,
+    residual_ref,
+    cotangent_ref,
+    moe_gain_ref,
+    router_ref,
+    router_first_ref,
+    router_second_ref,
+    router_low_ref,
+    moe_rows_ref,
+    ranks_ref,
+    low_ref,
+    out_low_ref,
+    first_out_ref,
+    second_out_ref,
+    q_second_ref,
+    k_second_ref,
+    v_second_ref,
+    q_gain_ref,
+    k_gain_ref,
+    cos_ref,
+    sin_ref,
+    seg_column_ref,
+    seg_row_ref,
+    linear_hbm,
+    heads_hbm,
+    normed_hbm,
+    gathered_hbm,
+    y_hbm,
+    output_ref,
+    residual_grad_ref,
+    share_ref,
+    linear_grad_ref,
+    rows_out_ref,
+    heads_out_ref,
+    narrow_out_ref,
+    router_out_ref,
+    y_in_hbm,
+    branch_own,
+    branch,
+    out_weights,
+    linear,
+    heads,
+    normed,
+    upstream,
+    out_low_grad,
+    keys,
+    values,
+    key_sum,
+    value_sum,
+    query_sum,
+    share_sum,
+    second_sum,
+    y_rows,
+    partials,
+    partials_in,
+    result,
+    choice,
+    load_sem,
+    y_sem,
+    relay_right_send,
+    relay_right_recv,
+    relay_left_send,
+    relay_left_recv,
+    y_send,
+    y_recv,
+    partial_send,
+    partial_recv,
+):
+    me, at_line = lax.axis_index("fsdp"), lax.axis_index("tensor")
+    tokens, width = residual_ref.shape
+    rank, query_columns = q_second_ref.shape
+    head_dim = q_gain_ref.shape[1]
+    slots = y_rows.shape[1]
+    tile = 256
+
+    greet_line_and_plane(line, plane)
+
+    def y_copy(r, d):
+        target = lax.rem(me + d, plane)
+        return pltpu.make_async_remote_copy(
+            src_ref=y_hbm.at[target, r],
+            dst_ref=y_in_hbm.at[r, me],
+            send_sem=y_send.at[r, d],
+            recv_sem=y_recv.at[r, d],
+            device_id={"fsdp": target},
+        )
+
+    def own_y(r):
+        return pltpu.make_async_copy(y_hbm.at[me, r], y_in_hbm.at[r, me], y_sem.at[r])
+
+    def partial_copy(r):
+        return pltpu.make_async_remote_copy(
+            src_ref=partials.at[r - 1],
+            dst_ref=partials_in.at[r - 1],
+            send_sem=partial_send.at[r - 1],
+            recv_sem=partial_recv.at[r - 1],
+            device_id={"tensor": lax.rem(at_line + r, line)},
+        )
+
+    for r in list(range(1, line)) + [0]:
+
+        @pl.loop(1, plane)
+        def _(d):
+            y_copy(r, d).start()
+
+    for r in range(line):
+        own_y(r).start()
+    loads = [
+        pltpu.make_async_copy(source, target, load_sem.at[at])
+        for at, (source, target) in enumerate(
+            [
+                (gathered_hbm.at[:, :, pl.ds(places[1], query_columns)], out_weights),
+                (linear_hbm, linear),
+                (heads_hbm, heads),
+                (normed_hbm, normed),
+            ]
+        )
+    ]
+    for each in loads:
+        each.start()
+
+    def combine(r):
+        @pl.loop(1, plane)
+        def _(d):
+            y_copy(r, d).wait_recv()
+
+        own_y(r).wait()
+        load = pltpu.make_async_copy(y_in_hbm.at[r], y_rows, y_sem.at[line])
+        load.start()
+        choice[...] = slot_choice(ranks_ref[lax.rem(at_line + r, line)], slots)
+        load.wait()
+
+        def combined(columns):
+            total = flipped_left_operand(
+                choice[...], y_rows[:, :, columns].reshape(plane * slots, 2 * tile)
+            )
+            if r == 0:
+                result[:, columns] = total
+            else:
+                partials[r - 1, :, columns] = total.astype(BF16)
+
+        tiles(width, 2 * tile, combined)
+        if r > 0:
+            partial_copy(r).start()
+
+    gates = gates_ref[...]
+    dots = dots_ref[...]
+    logit_grad = (gates * (dots - jnp.sum(gates * dots, axis=0, keepdims=True))).astype(BF16)
+    router_low_grad = matrix_product(router_second_ref[...], logit_grad).astype(BF16)
+    rows_out_ref[4 * rank :, :] = matrix_product(router_low_grad, moe_rows_ref[...]).astype(BF16)
+    router_out_ref[...] = flipped_right_operand(router_low_ref[...], logit_grad)
+    half = tokens // 2
+    for part in range(2):
+        rows = pl.ds(part * half, half)
+        columns = slice(part * half, (part + 1) * half)
+        moe_grad = (
+            moe_total_ref[rows, :]
+            + flipped_left_operand(logit_grad[:, columns], router_ref[...])
+            + flipped_left_operand(router_low_grad[:, columns], router_first_ref[...])
+        )
+        residual = residual_ref[rows, :]
+        factor = lax.rsqrt(
+            jnp.mean(residual * residual, axis=-1, keepdims=True) + NORM_EPSILON
+        )
+        residual_grad = cotangent_ref[rows, :].astype(F32) + norm_backward(
+            residual, factor, moe_gain_ref[...], moe_grad
+        )
+        residual_grad_ref[rows, :] = residual_grad
+        branch_own[rows, :] = residual_grad.astype(BF16)
+    branch[at_line] = branch_own[...]
+
+    advance, finish_relay = line_relay(
+        at_line,
+        line,
+        [branch_own],
+        [branch],
+        (4,),
+        (relay_right_send, relay_right_recv, relay_left_send, relay_left_recv),
+    )
+    advance(0, (0,))
+    second_sum[...] = jnp.zeros_like(second_sum)
+    loads[0].wait()
+
+    def head_gradients(block):
+        at = pl.ds(pl.multiple_of(block * tokens, tokens), tokens)
+        low_grad = flipped_right_operand(branch[block], second_out_ref[...]).astype(BF16)
+        out_low_grad[at, :] = low_grad
+        second_sum[...] += flipped_left_operand(out_low_ref[at, :], branch[block])
+
+        def project(columns):
+            upstream[at, columns] = (
+                matrix_product(branch[block], out_weights[:, :, columns].reshape(width, tile))
+                + matrix_product(low_grad, first_out_ref[:, columns])
+            ).astype(BF16)
+
+        tiles(query_columns, tile, project)
+
+    head_gradients(at_line)
+    for each in loads[1:]:
+        each.wait()
+    cosine, sine = cos_ref[...], sin_ref[...]
+    key_columns = slice(query_columns, query_columns + head_dim)
+    value_columns = slice(query_columns + head_dim, query_columns + 2 * head_dim)
+    keys[...] = head_values(
+        linear[:, key_columns],
+        low_ref[:, rank : 2 * rank],
+        k_second_ref[...],
+        k_gain_ref[...],
+        cosine,
+        sine,
+    )[2]
+    values[...] = (
+        linear[:, value_columns]
+        + matrix_product(low_ref[:, 2 * rank : 3 * rank], v_second_ref[...])
+    ).astype(BF16)
+    key_sum[...] = jnp.zeros_like(key_sum)
+    value_sum[...] = jnp.zeros_like(value_sum)
+    share_sum[...] = jnp.zeros_like(share_sum)
+    for hop in range(1, line):
+        advance(hop, (0,))
+
+        @pl.when(at_line - hop >= 0)
+        def _():
+            head_gradients(at_line - hop)
+
+        @pl.when(at_line + hop < line)
+        def _():
+            head_gradients(at_line + hop)
+
+        if hop < line - 1:
+            combine(hop)
+    rows_out_ref[3 * rank : 4 * rank, :] = second_sum[...].astype(BF16)
+
+    head_count = query_columns // head_dim
+
+    @pl.loop(0, head_count)
+    def _(head):
+        columns = pl.ds(pl.multiple_of(head * head_dim, head_dim), head_dim)
+        low_q = low_ref[:, :rank]
+        lines, factor, query = head_values(
+            linear[:, columns],
+            low_q,
+            q_second_ref[:, columns],
+            q_gain_ref[...],
+            cos_ref[...],
+            sin_ref[...],
+        )
+        heads_out_ref[rank:, columns] = flipped_left_operand(
+            out_low_grad[...], heads[:, columns]
+        ).astype(BF16)
+        seg_column, seg_row = seg_column_ref[...], seg_row_ref[...]
+        for block in range(query.shape[0] // WINDOW):
+            start, span = block_bounds(block)
+            at, near = pl.ds(block * WINDOW, WINDOW), pl.ds(start, span)
+            query_block = query[block * WINDOW : (block + 1) * WINDOW]
+            upstream_block = upstream[at, columns]
+            scores = flipped_right_operand(query_block, keys[near]) * scale
+            scores = jnp.where(
+                allowed_keys(block, start, span, seg_column, seg_row), scores, -1e30
+            )
+            expo = jnp.exp(scores - jnp.max(scores, axis=-1, keepdims=True))
+            probs = expo / jnp.sum(expo, axis=-1, keepdims=True)
+            prob_grad = flipped_right_operand(upstream_block, values[near])
+            score_grad = (
+                probs * (prob_grad - jnp.sum(probs * prob_grad, axis=-1, keepdims=True))
+            ).astype(BF16)
+            value_sum[near, :] += flipped_left_operand(probs.astype(BF16), upstream_block)
+            key_sum[near, :] += flipped_left_operand(score_grad, query_block)
+            query_sum[at, :] = matrix_product(score_grad, keys[near]) * scale
+        q_grad = head_values_gradient(
+            lines, factor, q_gain_ref[...], cos_ref[...], sin_ref[...], query_sum[...]
+        )
+        linear_grad_ref[:, columns] = q_grad
+        heads_out_ref[:rank, columns] = flipped_left_operand(low_q, q_grad).astype(BF16)
+        share_sum[:, :rank] += flipped_right_operand(q_grad, q_second_ref[:, columns])
+
+        @pl.when(head == head_count // 2 - 1)
+        def _():
+            combine(line - 1)
+
+    low_k = low_ref[:, rank : 2 * rank]
+    low_v = low_ref[:, 2 * rank : 3 * rank]
+    key_lines, key_factor, _turned = head_values(
+        linear[:, key_columns], low_k, k_second_ref[...], k_gain_ref[...], cosine, sine
+    )
+    k_grad = head_values_gradient(
+        key_lines, key_factor, k_gain_ref[...], cosine, sine, key_sum[...] * scale
+    )
+    v_grad = value_sum[...].astype(BF16)
+    linear_grad_ref[:, key_columns] = k_grad
+    linear_grad_ref[:, value_columns] = v_grad
+    narrow_out_ref[:rank, :] = flipped_left_operand(low_k, k_grad).astype(BF16)
+    narrow_out_ref[rank:, :] = flipped_left_operand(low_v, v_grad).astype(BF16)
+    share_sum[:, rank : 2 * rank] = flipped_right_operand(k_grad, k_second_ref[...])
+    share_sum[:, 2 * rank :] = flipped_right_operand(v_grad, v_second_ref[...])
+    share_ref[...] = share_sum[...].astype(BF16)
+
+    def first_gradient(columns):
+        rows_out_ref[: 3 * rank, columns] = flipped_left_operand(
+            share_ref[...], normed[:, columns]
+        ).astype(BF16)
+
+    tiles(width, 2 * tile, first_gradient)
+    combine(0)
+    for r in range(1, line):
+        partial_copy(r).wait_recv()
+        result[...] += partials_in[r - 1].astype(F32)
+    output_ref[...] = (residual_ref[...] + result[...]).astype(BF16)
+    finish_relay((0,), range(line - 1))
+    for r in range(1, line):
+        partial_copy(r).wait_send()
+    for r in range(line):
+
+        @pl.loop(1, plane)
+        def _(d):
+            y_copy(r, d).wait_send()
+
+
+def back(scale, places, slots, identity, hbm_operands, operands):
+    line, plane = lax.axis_size("tensor"), lax.axis_size("fsdp")
+    linear, heads, normed, gathered, _y = hbm_operands
+    count, width = operands[0].shape
+    all_rows, linear_columns = linear.shape
+    query_columns = heads.shape[1]
+    head_dim = (linear_columns - query_columns) // 2
+    rank = operands[13].shape[1]
+    experts_count = line * plane
+    anywhere = pl.BlockSpec(memory_space=pl.ANY)
+    local = pl.BlockSpec(memory_space=pltpu.VMEM)
+    dma = pltpu.SemaphoreType.DMA
+    single = (all_rows, head_dim)
+    block = (count, width)
+    return pl.pallas_call(
+        functools.partial(back_body, plane, line, scale, places),
+        out_shape=[
+            jax.ShapeDtypeStruct(block, BF16),
+            jax.ShapeDtypeStruct(block, F32),
+            jax.ShapeDtypeStruct((all_rows, 3 * rank), BF16),
+            jax.ShapeDtypeStruct((all_rows, linear_columns), BF16),
+            jax.ShapeDtypeStruct((5 * rank, width), BF16),
+            jax.ShapeDtypeStruct((2 * rank, query_columns), BF16),
+            jax.ShapeDtypeStruct((2 * rank, head_dim), BF16),
+            jax.ShapeDtypeStruct((rank, experts_count), F32),
+            jax.ShapeDtypeStruct((line, plane, slots, width), BF16),
+        ],
+        in_specs=[local] * len(operands) + [anywhere] * len(hbm_operands),
+        out_specs=[local] * 8 + [anywhere],
+        scratch_shapes=[
+            pltpu.VMEM(block, BF16),
+            pltpu.VMEM((line,) + block, BF16),
+            pltpu.VMEM((plane, width // plane, query_columns), BF16),
+            pltpu.VMEM((all_rows, linear_columns), F32),
+            pltpu.VMEM((all_rows, query_columns), BF16),
+            pltpu.VMEM((all_rows, width), BF16),
+            pltpu.VMEM((all_rows, query_columns), BF16),
+            pltpu.VMEM((all_rows, rank), BF16),
+            pltpu.VMEM(single, BF16),
+            pltpu.VMEM(single, BF16),
+            pltpu.VMEM(single, F32),
+            pltpu.VMEM(single, F32),
+            pltpu.VMEM(single, F32),
+            pltpu.VMEM((all_rows, 3 * rank), F32),
+            pltpu.VMEM((rank, width), F32),
+            pltpu.VMEM((plane, slots, width), BF16),
+            pltpu.VMEM((line - 1,) + block, BF16),
+            pltpu.VMEM((line - 1,) + block, BF16),
+            pltpu.VMEM(block, F32),
+            pltpu.VMEM((plane * slots, count), BF16),
+            dma((4,)),
+            dma((line + 1,)),
+        ]
+        + [dma((line - 1, 4))] * 4
+        + [dma((line, plane))] * 2
+        + [dma((line - 1,))] * 2,
+        compiler_params=pltpu.CompilerParams(
+            collective_id=identity, has_side_effects=True, vmem_limit_bytes=63 * MEBI
+        ),
+        name="back",
+    )(*operands, *hbm_operands)
+
+
+def last_body(
+    line,
+    linear_grad_ref,
+    share_ref,
+    first_ref,
+    residual_grad_ref,
+    tokens_ref,
+    gain_ref,
+    gathered_hbm,
+    input_grad_ref,
+    weights,
+    part,
+    left_buf,
+    right_buf,
+    load_sem,
+    *semaphores,
+):
+    at_line = lax.axis_index("tensor")
+    tokens, width = tokens_ref.shape
+    linear_columns = linear_grad_ref.shape[1]
+    load = pltpu.make_async_copy(
+        gathered_hbm.at[:, :, pl.ds(0, linear_columns)], weights, load_sem
+    )
+    load.start()
+    greet_line(at_line, line)
+    load.wait()
+    shards, wide = weights.shape[:2]
+
+    def normed_gradient(block):
+        at = pl.ds(pl.multiple_of(block * tokens, tokens), tokens)
+
+        @pl.loop(0, shards)
+        def _(shard):
+            columns = pl.ds(pl.multiple_of(shard * wide, wide), wide)
+            part[block, :, columns] = (
+                flipped_right_operand(linear_grad_ref[at, :], weights[shard])
+                + matrix_product(share_ref[at, :], first_ref[:, columns])
+            ).astype(BF16)
+
+    advance, finish = line_sum(
+        at_line, line, 4, part, input_grad_ref, left_buf, right_buf, semaphores
+    )
+    for far in range(line - 1, 0, -1):
+
+        @pl.when(at_line + far < line)
+        def _():
+            normed_gradient(at_line + far)
+
+        @pl.when(at_line - far >= 0)
+        def _():
+            normed_gradient(at_line - far)
+
+        advance(far)
+    normed_gradient(at_line)
+    finish()
+    half = tokens // 2
+    for at in range(2):
+        rows = pl.ds(at * half, half)
+        values = tokens_ref[rows, :].astype(F32)
+        factor = lax.rsqrt(jnp.mean(values * values, axis=-1, keepdims=True) + NORM_EPSILON)
+        input_grad_ref[rows, :] = residual_grad_ref[rows, :] + norm_backward(
+            values, factor, gain_ref[...], input_grad_ref[rows, :]
+        )
+
+
+def last(linear_grad, share, first, residual_grad, tokens, gain, gathered, identity):
+    line = lax.axis_size("tensor")
+    count, width = tokens.shape
+    anywhere = pl.BlockSpec(memory_space=pl.ANY)
+    local = pl.BlockSpec(memory_space=pltpu.VMEM)
+    dma = pltpu.SemaphoreType.DMA
+    return pl.pallas_call(
+        functools.partial(last_body, line),
+        out_shape=jax.ShapeDtypeStruct((count, width), F32),
+        in_specs=[local] * 6 + [anywhere],
+        out_specs=local,
+        scratch_shapes=[
+            pltpu.VMEM(gathered.shape[:2] + (linear_grad.shape[1],), BF16),
+            pltpu.VMEM((line, count, width), BF16),
+            pltpu.VMEM((line - 1, count, width), BF16),
+            pltpu.VMEM((line - 1, count, width), BF16),
+            dma,
+        ]
+        + [dma((line - 1, 4))] * 4,
+        compiler_params=pltpu.CompilerParams(
+            collective_id=identity, has_side_effects=True, vmem_limit_bytes=48 * MEBI
+        ),
+        name="last",
+    )(linear_grad, share, first, residual_grad, tokens, gain, gathered)
+
+
 def per_device(
     tokens,
     segments,
@@ -1952,6 +2431,7 @@
             0,
         )
         sequence_normalized = sequence_normalized.reshape(seq_rows, model_width)
+        gathered_blocks = gathered
         gathered = gathered.reshape(model_width, -1)
     else:
         gathered = lax.all_gather(packed, "fsdp", axis=0, tiled=True)
@@ -2062,80 +2542,133 @@
         gate_dots = jnp.roll(jnp.stack(ordered), tensor_pos, axis=0)
     pair_in_grad, gate_out_grad, upward_out_grad, downward_in_grad, downward_out_grad = sums
     if in_kernel:
-        gate_grad = jnp.transpose(gate_dots, (2, 1, 0)).reshape(tok_rows, expert_count)
+
+        def by_line(table):
+            lines = table.reshape(fsdp_count, tensor_count, -1)
+            return jnp.transpose(lines, (1, 0, 2)).reshape(expert_count, -1)
+
+        (
+            output,
+            residual_grad,
+            low_share,
+            linear_grad,
+            row_grads,
+            head_grads,
+            narrow_grads,
+            router_grads,
+            _landed,
+        ) = back(
+            score_scale,
+            (linear_cols, out_start),
+            slots,
+            4,
+            (linear, heads_narrow, sequence_normalized, gathered_blocks, expert_output),
+            (
+                moe_grad,
+                gate_dots.reshape(expert_count, tok_rows),
+                by_line(jnp.transpose(gate_weights, (1, 0))),
+                residual_stream,
+                cotangent,
+                gain_moe[None, :],
+                by_line(jnp.transpose(complete_router, (1, 0))),
+                router_first,
+                jnp.transpose(by_line(jnp.transpose(router_second, (1, 0))), (1, 0)),
+                jnp.transpose(router_low, (1, 0)),
+                experts_narrow,
+                plane_ranks,
+                low,
+                attention_low,
+                attention_first,
+                attention_second,
+                q_second,
+                k_second,
+                v_second,
+                gain_query,
+                gain_key,
+                *tables,
+                seg_column,
+                seg_row,
+            ),
+        )
+        router_second_gradient = jnp.transpose(
+            router_grads.reshape(rank, tensor_count, fsdp_count), (0, 2, 1)
+        ).reshape(rank, expert_count)
+        input_grad = last(
+            linear_grad,
+            low_share,
+            input_first,
+            residual_grad,
+            tokens,
+            gain_attn[None, :],
+            gathered_blocks,
+            5,
+        )
     else:
         gate_grad = jnp.transpose(
-            route_rows(jnp.transpose(gate_dots, (1, 0, 2)).reshape(device_count, tok_rows)),
-            (1, 0),
-        )
-
-    def returned(slotted):
-        total = 0.0
-        for offset, at, rows in zip(offsets, line_blocks, slotted):
-            combined = from_slots(at, plane_ranks, plane_rows(rows))
-            total = total + delivered(combined, offset).astype(F32)
-        return total
-
-    if not in_kernel:
+            route_rows(jnp.transpose(gate_dots, (1, 0, 2)).reshape(device_count, tok_rows)), (1, 0)
+        )
+
+        def returned(slotted):
+            total = 0.0
+            for offset, at, rows in zip(offsets, line_blocks, slotted):
+                combined = from_slots(at, plane_ranks, plane_rows(rows))
+                total = total + delivered(combined, offset).astype(F32)
+            return total
+
         moe_grad = returned(rows_grad)
 
-    out_grad = cotangent.astype(F32)
-    logit_gradient = (
-        gate_weights * (gate_grad - jnp.sum(gate_weights * gate_grad, axis=-1, keepdims=True))
-    ).astype(BF16)
-    router_low_gradient = flipped_right_operand(logit_gradient, router_second).astype(BF16)
-    moe_grad = (
-        moe_grad
-        + flipped_right_operand(logit_gradient, complete_router)
-        + matrix_product(router_low_gradient, router_first)
-    )
-    router_first_gradient = flipped_left_operand(router_low_gradient, experts_narrow)
-    router_second_gradient = flipped_left_operand(router_low, logit_gradient)
-    residual_grad = out_grad + norm_backward(residual_stream, moe_factor, gain_moe, moe_grad)
-
-    (sequence_branch,) = gather_line([residual_grad.astype(BF16)], (4,), 2)
-    sequence_branch = sequence_branch.reshape(seq_rows, model_width)
-    if in_kernel:
-        back_output = plane_rows(
-            expert_output.reshape(fsdp_count, tensor_count * slots, model_width)
-        ).reshape(fsdp_count, tensor_count, slots, model_width)
-    else:
+        out_grad = cotangent.astype(F32)
+        logit_gradient = (
+            gate_weights * (gate_grad - jnp.sum(gate_weights * gate_grad, axis=-1, keepdims=True))
+        ).astype(BF16)
+        router_low_gradient = flipped_right_operand(logit_gradient, router_second).astype(BF16)
+        moe_grad = (
+            moe_grad
+            + flipped_right_operand(logit_gradient, complete_router)
+            + matrix_product(router_low_gradient, router_first)
+        )
+        router_first_gradient = flipped_left_operand(router_low_gradient, experts_narrow)
+        router_second_gradient = flipped_left_operand(router_low, logit_gradient)
+        residual_grad = out_grad + norm_backward(residual_stream, moe_factor, gain_moe, moe_grad)
+
+        (sequence_branch,) = gather_line([residual_grad.astype(BF16)], (4,), 2)
+        sequence_branch = sequence_branch.reshape(seq_rows, model_width)
         output = (residual_stream + returned(expert_output)).astype(BF16)
-    attention_low_grad = flipped_right_operand(sequence_branch, attention_second).astype(BF16)
-    attention_second_gradient = flipped_left_operand(attention_low, sequence_branch)
-    heads_grad = matrix_product(sequence_branch, full_out_t)
-    if in_kernel:
-        back_output, heads_grad = lax.optimization_barrier((back_output, heads_grad))
-        combined = all_from_slots(tensor_pos[None], plane_ranks, back_output)
-        moe_output = lax.psum_scatter(combined, "tensor", scatter_dimension=0, tiled=True)
-        output = (residual_stream + moe_output.astype(F32)).astype(BF16)
-    (
-        q_grad,
-        k_grad,
-        v_grad,
-        low_share,
-        q_second_gradient,
-        k_second_gradient,
-        v_second_gradient,
-        attention_first_gradient,
-    ) = attention_backward(
-        *attention_operands,
-        heads_narrow,
-        heads_grad,
-        attention_low_grad,
-        attention_first,
-    )
-    linear_grad = jnp.concatenate([q_grad, k_grad, v_grad], axis=1)
-    normed_part = flipped_right_operand(linear_grad, complete_linear) + matrix_product(
-        low_share, input_first
-    )
-    input_first_gradient = flipped_left_operand(low_share, sequence_normalized)
-    normalized_gradient = sum_line(
-        normed_part.astype(BF16).reshape(tensor_count, tok_rows, model_width), 4, 1
-    )
-    input_grad = residual_grad + norm_backward(
-        token_values, attn_factor, gain_attn, normalized_gradient
-    )
+        attention_low_grad = flipped_right_operand(sequence_branch, attention_second).astype(BF16)
+        attention_second_gradient = flipped_left_operand(attention_low, sequence_branch)
+        heads_grad = matrix_product(sequence_branch, full_out_t)
+        (
+            q_grad,
+            k_grad,
+            v_grad,
+            low_share,
+            q_second_gradient,
+            k_second_gradient,
+            v_second_gradient,
+            attention_first_gradient,
+        ) = attention_backward(
+            *attention_operands,
+            heads_narrow,
+            heads_grad,
+            attention_low_grad,
+            attention_first,
+        )
+        linear_grad = jnp.concatenate([q_grad, k_grad, v_grad], axis=1)
+        normed_part = flipped_right_operand(linear_grad, complete_linear) + matrix_product(
+            low_share, input_first
+        )
+        input_first_gradient = flipped_left_operand(low_share, sequence_normalized)
+        normalized_gradient = sum_line(
+            normed_part.astype(BF16).reshape(tensor_count, tok_rows, model_width), 4, 1
+        )
+        input_grad = residual_grad + norm_backward(
+            token_values, attn_factor, gain_attn, normalized_gradient
+        )
+        row_grads = jnp.concatenate(
+            [input_first_gradient, attention_second_gradient, router_first_gradient], axis=0
+        )
+        head_grads = jnp.concatenate([q_second_gradient, attention_first_gradient], axis=0)
+        narrow_grads = jnp.concatenate([k_second_gradient, v_second_gradient], axis=0)
 
     source_adapter = jnp.repeat(adapter_index, tensor_count)
     owner_onehot = (
@@ -2166,40 +2699,38 @@
             start += width
         return pieces
 
-    early = owner_sums(
+    row_sums, head_sums, narrow_sums, router_sums = owner_sums(
         [
-            to_all(router_first_gradient),
-            to_all(attention_second_gradient),
+            to_all(row_grads),
+            to_head_owners(head_grads),
+            to_head_owners(narrow_grads),
             to_all(router_second_gradient),
         ]
     )
-    late = owner_sums(
-        [
-            to_all(input_first_gradient),
-            to_head_owners(q_second_gradient),
-            to_head_owners(k_second_gradient),
-            to_head_owners(v_second_gradient),
-            to_head_owners(attention_first_gradient),
-        ]
-    )
 
     def lines_of(piece, lines):
         return piece.reshape(adapter_count, lines, -1)
 
-    first_sums = lines_of(late[0], 3 * rank)
+    row_sums = lines_of(row_sums, 5 * rank)
+    head_sums = lines_of(head_sums, 2 * rank)
+    narrow_sums = lines_of(narrow_sums, 2 * rank)
+
+    def factor_rows(at):
+        return row_sums[:, at * rank : (at + 1) * rank]
+
     return (
         output,
         input_grad,
-        transposed(first_sums[:, :rank]),
-        lines_of(late[1], rank),
-        transposed(first_sums[:, rank : 2 * rank]),
-        lines_of(late[2], rank),
-        transposed(first_sums[:, 2 * rank :]),
-        lines_of(late[3], rank),
-        transposed(lines_of(late[4], rank)),
-        lines_of(early[1], rank),
-        transposed(lines_of(early[0], rank)),
-        lines_of(early[2], rank),
+        transposed(factor_rows(0)),
+        head_sums[:, :rank],
+        transposed(factor_rows(1)),
+        narrow_sums[:, :rank],
+        transposed(factor_rows(2)),
+        narrow_sums[:, rank:],
+        transposed(head_sums[:, rank:]),
+        factor_rows(3),
+        transposed(factor_rows(4)),
+        lines_of(router_sums, rank),
         transposed(lines_of(pair_in_grad[:broad], rank))[None],
         lines_of(gate_out_grad, rank)[None],
         transposed(lines_of(pair_in_grad[broad:], rank))[None],

time: 871 us -> 845 us (0.970)
  Pallas kernels: 696 us -> 738 us
  matrix products: 33 us -> 3.01 us
  waiting for transfers between devices: 25.9 us -> 0.35 us
  between operations: 17.2 us -> 3.44 us
  other arithmetic: 20.8 us -> 10.7 us
  starting transfers between devices: 28.5 us -> 37.8 us
    pallas_call x4 -> x2, Pallas kernels: 197 us -> 239 us  [the longest x1 159 us: back(): pl.pallas_call(functools.partial(back_body, plane, line, scale, places),...]
    all_to_all x1 -> x0, waiting for transfers between devices: 16.4 us -> none  [plane_rows(): lax.all_to_all(block_rows, 'fsdp', split_axis=0, concat_axis=0, tiled=True)]
    all_to_all x3 -> x2, starting transfers between devices: 22.7 us -> 37.8 us  [route_rows(): lax.all_to_all(block_rows, ('fsdp', 'tensor'), split_axis=0, concat_axis=...]
    dot_general x8 -> x4, matrix products: 17.2 us -> 2.63 us  [matrix_product(): return jnp.dot(first_op, second_op, preferred_element_type=F32)]
    dot_general x5 -> x1, matrix products: 11.6 us -> 0.37 us  [flipped_right_operand(): lax.dot_general(first_op, second_op, (((1,), (1,)), ((), ())), preferred_...]
    all_to_all x3 -> x2, waiting for transfers between devices: 9.45 us -> 0.35 us  [route_rows(): lax.all_to_all(block_rows, ('fsdp', 'tensor'), split_axis=0, concat_axis=...]
    unnamed x129 -> x89, local copies, waits for them, and re-layouts: 17.4 us -> 18.7 us
  transfers between devices with their start and end apart: 5 -> 2, of which waited for: 3 -> 1; matrix products, arithmetic and copies ran while one was open for 6% -> 1% of each run, Pallas kernels for 22% -> 10%
where the time goes in v5:
time: 845 us; the launch traced here: 834 us
  Pallas kernels  738 us (87%)
  local copies, waits for them, and re-layouts  41.2 us (5%)
  starting transfers between devices  37.8 us (4%)
  other arithmetic  10.7 us (1%)
    pallas_call x1, Pallas kernels, moe_layer(): pl.pallas_call(functools.partial(moe_body, plane, line), out_shape=[jax.S...  279 us
    pallas_call x1, Pallas kernels, front(): pl.pallas_call(functools.partial(front_body, plane, line, scale, places),...  219 us
    pallas_call x1, Pallas kernels, back(): pl.pallas_call(functools.partial(back_body, plane, line, scale, places),...  159 us
    pallas_call x1, Pallas kernels, last(): pl.pallas_call(functools.partial(last_body, line), out_shape=jax.ShapeDty...  79.9 us
    all_to_all x2, starting transfers between devices, route_rows(): lax.all_to_all(block_rows, ('fsdp', 'tensor'), split_axis=0, concat_axis=...  37.8 us
    unnamed x89, local copies, waits for them, and re-layouts  18.7 us
  transfers between devices with their start and end apart: 2, of which 1 were waited for; matrix products, arithmetic and copies ran while one was open for 1% of the time, Pallas kernels for 10%

profile of v5, /device:TPU:16, one launch (start us, length us, event | category | flops | bytes accessed | tf_op | source)
XLA Modules:
  0.0 834.1 jit_solution(1403965913584449542)
XLA Ops:
  0.7 1.4 dynamic_slice.38
  3.4 0.7 fusion.7.before_ref
  4.7 0.6 dynamic-slice_bitcast_fusion.1.out_second_ref.second_out_ref
  5.4 1.4 dynamic-slice_bitcast_fusion.5.out_first_ref.first_out_ref
  6.7 1.4 dynamic-slice_bitcast_fusion.6.q_second_ref
  8.1 2.0 fusion.10
  10.1 1.8 copy.124.seg_column_ref
  12.5 0.8 constant_dynamic-update-slice_fusion.2
  13.7 0.9 dynamic-slice_bitcast_fusion
  14.6 0.9 dynamic-slice_bitcast_fusion.3
  15.5 1.3 dynamic-slice_bitcast_fusion.7
  18.7 0.6 pad_dynamic-update-slice_fusion
  19.3 0.8 bitcast_dynamic-update-slice_fusion.weights_hbm
  20.1 0.7 pad_maximum_fusion.3.first_ref
  20.8 1.3 pad_maximum_fusion.1
  22.1 219.4 %front.1 = (f32[256,2048]{1,0:T(8,128)}, f32[4,8,256]{2,1,0:T(8,128)}, bf16[1024,48]{1,0:T(8,128)(2,1)}, bf16[1024,16]{1,0:T(8,128)(2,1)}, f32[1024,1280]{1,0:T(...) custom-call(bf16[256,2048]{1,0:T(8,128)(2,1)} %tokens_ref.1, ...), custom_call_target="tpu_custom_call" | custom-call | tf_op jit(solution)/shard_map/front/pallas_call | solution.py:1761
  241.6 2.2 multiply_reduce_fusion
  245.5 1.5 fusion.20
  246.9 0.7 constant_dynamic-slice_fusion
  247.9 0.6 copy.127
  248.5 3.4 all-to-all-start
  252.0 1.1 pad_maximum_fusion.rest_3_
  253.1 1.1 slice.64
  255.2 0.7 copy.164
  255.9 0.7 copy.132
  257.7 0.8 fusion.rank_ref
  258.4 0.7 broadcast_in_dim.78
  259.1 279.0 %moe_layer.1 = (f32[256,2048]{1,0:T(8,128)}, f32[4,8,256]{2,1,0:T(8,128)}, bf16[8,4,80,2048]{3,2,1,0:T(8,128)(2,1)}, bf16[4,8,80,2048]{3,2,1,0:T(8,128)(2,1)}, f...) custom-call(bf16[256,2048]{1,0:T(8,128)(2,1)} %copy-done.9, ...), custom_call_target="tpu_custom_call" | custom-call | tf_op jit(solution)/shard_map/moe_layer/pallas_call | solution.py:1088
  538.2 159.2 %back.1 = (bf16[256,2048]{1,0:T(8,128)(2,1)}, f32[256,2048]{1,0:T(8,128)}, bf16[1024,48]{1,0:T(8,128)(2,1)}, bf16[1024,1280]{1,0:T(8,128)(2,1)}, bf16[80,2048]{1...) custom-call(f32[256,2048]{1,0:T(8,128)} %get-tuple-element.47.moe_to, ...), custom_call_target="tpu_custom_call" | custom-call | tf_op jit(solution)/shard_map/back/pallas_call | solution.py:2143
  697.4 1.6 reshape.186
  701.0 1.1 reduce.1
  702.1 1.4 reshape.205
  703.5 34.4 %all-to-all-start.1 = ((bf16[32,2,4872]{2,1,0:T(2,128)(2,1)}), bf16[32,2,4872]{2,1,0:T(2,128)(2,1)S(1)}, u32[]{:S(2)}, u32[]{:S(2)}) async-start(bf16[32,2,4872]{2,1,0:T(2,128)(2,1)} %reshape.205), calls=%async_computation.1 | async-start | bytes 1277952 | tf_op jit(solution)/shard_map/all_to_all | solution.py:63
  738.1 1.6 copy-done.5
  739.6 79.9 %last.1 = f32[256,2048]{1,0:T(8,128)S(1)} custom-call(bf16[1024,1280]{1,0:T(8,128)(2,1)} %get-tuple-element.56.linear_grad_ref, bf16[1024,48]{1,0:T(8,128)(2,1)S(1)} %copy-done.7, bf16[48,2048]{1,0:T(8,128)(2,1)S(1)} %copy-done.6, f32[256,2048]{1,0:T(8,128)S(1)} %copy-done.5, bf16[256,2048]{1,0:T(8,128)(2,1)S(1)} %copy-done.2, f32[1,2048]{1,0:T(1,128)S(1)} %bitcast.182, ...), custom_call_target="tpu_custom_call" | custom-call | tf_op jit(solution)/shard_map/last/pallas_call | solution.py:2263
  819.5 1.3 copy-done.3
  820.9 1.5 fusion.23
  822.4 0.8 reshape.206
  824.2 0.7 slice_bitcast_fusion.1
  824.9 0.6 copy.165
  825.6 0.6 copy.146
  826.3 0.7 fusion.25
  827.0 2.3 copy.182
  829.3 1.3 copy.183
  830.6 0.7 copy.184
  831.4 0.7 copy.185
  832.1 0.7 copy.186
  832.9 1.0 copy.187
  (121 shorter events, 9.8 us)
Async XLA Ops:
  0.7 4.1 copy-start
  0.7 11.2 %copy-start.30 = (bf16[2048]{0:T(1024)(128)(2,1)S(1)}, bf16[2048]{0:T(1024)(128)(2,1)}, u32[]{:S(2)}) copy-start(bf16[2048]{0:T(1024)(128)(2,1)} %param.38) | copy-start | bytes 12292
  0.7 11.8 %copy-start.14 = (bf16[256,1024]{1,0:T(8,128)(2,1)S(1)}, bf16[256,1024]{1,0:T(8,128)(2,1)}, u32[]{:S(2)}) copy-start(bf16[256,1024]{1,0:T(8,128)(2,1)} %param.42) | copy-start | bytes 1572868
  0.7 12.6 %copy-start.27 = (bf16[256,32]{0,1:T(8,128)(2,1)S(1)}, bf16[256,32]{0,1:T(8,128)(2,1)}, u32[]{:S(2)}) copy-start(bf16[256,32]{0,1:T(8,128)(2,1)} %param.46) | copy-start | bytes 49156
  0.7 12.7 %copy-start.15 = (bf16[1024,256]{1,0:T(8,128)(2,1)S(1)}, bf16[1024,256]{1,0:T(8,128)(2,1)}, u32[]{:S(2)}) copy-start(bf16[1024,256]{1,0:T(8,128)(2,1)} %param.45) | copy-start | bytes 1572868
  8.1 5.5 copy-start.26
  8.1 8.7 %copy-start.33 = (bf16[128]{0:T(256)(128)(2,1)S(1)}, bf16[128]{0:T(256)(128)(2,1)}, u32[]{:S(2)}) copy-start(bf16[128]{0:T(256)(128)(2,1)} %param.41) | copy-start | bytes 772
  8.1 8.7 %copy-start.34 = (bf16[128]{0:T(256)(128)(2,1)S(1)}, bf16[128]{0:T(256)(128)(2,1)}, u32[]{:S(2)}) copy-start(bf16[128]{0:T(256)(128)(2,1)} %param.40) | copy-start | bytes 772
  8.1 9.3 %copy-start.23 = (bf16[256,128]{1,0:T(8,128)(2,1)S(1)}, bf16[256,128]{1,0:T(8,128)(2,1)}, u32[]{:S(2)}) copy-start(bf16[256,128]{1,0:T(8,128)(2,1)} %param.43) | copy-start | bytes 196612
  10.1 8.0 copy-start.24
  14.6 229.5 %copy-start.13 = (bf16[16,2048]{1,0:T(8,128)(2,1)}, bf16[16,2048]{1,0:T(8,128)(2,1)S(1)}, u32[]{:S(2)}) copy-start(bf16[16,2048]{1,0:T(8,128)(2,1)S(1)} %get-tuple-element.178.router_first_ref) | copy-start | bytes 196612
  241.6 2.3 copy-start.31
  243.8 1.3 copy-start.10
  243.8 1.3 copy-start.21
  244.1 1.4 copy-start.9
  244.1 7.9 copy-start.16
  244.1 7.9 copy-start.17
  245.1 9.1 %copy-start.22 = (bf16[256,16]{0,1:T(8,128)(2,1)}, bf16[256,16]{0,1:T(8,128)(2,1)S(1)}, u32[]{:S(2)}) copy-start(bf16[256,16]{0,1:T(8,128)(2,1)S(1)} %convolution_convert_fusion) | copy-start | bytes 24580
  245.1 7.9 copy-start.32
  248.5 8.4 %all-to-all-start = ((f32[32,1,256]{2,1,0:T(1,128)}), f32[32,1,256]{2,1,0:T(1,128)S(1)}, u32[]{:S(2)}, u32[]{:S(2)}) async-start(f32[32,1,256]{2,1,0:T(1,128)} %copy.127), calls=%async_computation | async-start | bytes 65536 | tf_op jit(solution)/shard_map/all_to_all | solution.py:63
  697.4 2.4 copy-start.25
  697.4 2.4 copy-start.28
  697.4 2.8 copy-start.29
  700.4 37.6 %copy-start.2 = (bf16[256,2048]{1,0:T(8,128)(2,1)S(1)}, bf16[256,2048]{1,0:T(8,128)(2,1)}, u32[]{:S(2)}) copy-start(bf16[256,2048]{1,0:T(8,128)(2,1)} %tokens_ref.1) | copy-start | bytes 3145732
  700.4 37.6 %copy-start.6 = (bf16[48,2048]{1,0:T(8,128)(2,1)S(1)}, bf16[48,2048]{1,0:T(8,128)(2,1)}, u32[]{:S(2)}) copy-start(bf16[48,2048]{1,0:T(8,128)(2,1)} %pad_maximum_fusion.3.first_ref) | copy-start | bytes 589828
  700.5 37.6 %copy-start.7 = (bf16[1024,48]{1,0:T(8,128)(2,1)S(1)}, bf16[1024,48]{1,0:T(8,128)(2,1)}, u32[]{:S(2)}) copy-start(bf16[1024,48]{1,0:T(8,128)(2,1)} %get-tuple-element.57.share_ref) | copy-start | bytes 294916
  700.5 37.6 %copy-start.8 = (f32[2048]{0:T(1024)S(1)}, f32[2048]{0:T(1024)}, u32[]{:S(2)}) copy-start(f32[2048]{0:T(1024)} %broadcast_in_dim.86) | copy-start | bytes 24580
  703.5 118.9 %all-to-all-start.1 = ((bf16[32,2,4872]{2,1,0:T(2,128)(2,1)}), bf16[32,2,4872]{2,1,0:T(2,128)(2,1)S(1)}, u32[]{:S(2)}, u32[]{:S(2)}) async-start(bf16[32,2,4872]{2,1,0:T(2,128)(2,1)} %reshape.205), calls=%async_computation.1 | async-start | bytes 1277952 | tf_op jit(solution)/shard_map/all_to_all | solution.py:63
  738.0 1.6 copy-start.5
  739.6 81.2 %copy-start.11 = (f32[256,2048]{1,0:T(8,128)S(1)}, f32[256,2048]{1,0:T(8,128)}, u32[]{:S(2)}) copy-start(f32[256,2048]{1,0:T(8,128)} %get-tuple-element.63) | copy-start | bytes 6291460
  819.5 1.3 copy-start.3
  824.1 5.2 copy-start.4
  829.3 1.3 copy-start.20
  829.3 2.1 copy-start.19
  829.3 2.8 copy-start.18
  829.3 4.6 copy-start.1
  830.6 2.2 copy-start.12

commit v6 on v5

--- a/solution.py
+++ b/solution.py
@@ -567,6 +567,177 @@
     return jnp.where(mask, counts, -1.0).astype(jnp.int32)
 
 
+def line_relay(me, count, ins, outs, chunks, semaphores):
+    right_send, right_recv, left_send, left_recv = semaphores
+    pieces = []
+    for at in range(len(ins)):
+        size = ins[at].shape[0] // chunks[at]
+        for piece in range(chunks[at]):
+            pieces.append((at, pl.ds(piece * size, size)))
+
+    def copy(place, hop, origin, target, send, recv):
+        at, rows = pieces[place]
+        source = ins[at].at[rows] if hop == 0 else outs[at].at[origin, rows]
+        return pltpu.make_async_remote_copy(
+            src_ref=source,
+            dst_ref=outs[at].at[origin, rows],
+            send_sem=send.at[hop, place],
+            recv_sem=recv.at[hop, place],
+            device_id={"tensor": target},
+        )
+
+    def places(arrays):
+        return [place for place in range(len(pieces)) if pieces[place][0] in arrays]
+
+    def advance(hop, arrays):
+        for place in places(arrays):
+            if hop > 0:
+
+                @pl.when(me - hop >= 0)
+                def _():
+                    copy(place, hop - 1, me - hop, me - 1, right_send, right_recv).wait_recv()
+
+            if hop < count - 1:
+
+                @pl.when((me - hop >= 0) & (me + 1 < count))
+                def _():
+                    copy(place, hop, me - hop, me + 1, right_send, right_recv).start()
+
+            if hop > 0:
+
+                @pl.when(me + hop < count)
+                def _():
+                    copy(place, hop - 1, me + hop, me + 1, left_send, left_recv).wait_recv()
+
+            if hop < count - 1:
+
+                @pl.when((me + hop < count) & (me > 0))
+                def _():
+                    copy(place, hop, me + hop, me - 1, left_send, left_recv).start()
+
+    def finish(arrays, hops):
+        for hop in hops:
+            for place in places(arrays):
+
+                @pl.when((me - hop >= 0) & (me + 1 < count))
+                def _():
+                    copy(place, hop, me - hop, me + 1, right_send, right_recv).wait_send()
+
+                @pl.when((me + hop < count) & (me > 0))
+                def _():
+                    copy(place, hop, me + hop, me - 1, left_send, left_recv).wait_send()
+
+    return advance, finish
+
+
+def line_sum(me, count, chunks, part_ref, out_ref, left_buf, right_buf, semaphores):
+    right_send, right_recv, left_send, left_recv = semaphores
+    size = part_ref.shape[1] // chunks
+
+    def rightward(rows, piece, far, source):
+        return pltpu.make_async_remote_copy(
+            src_ref=source,
+            dst_ref=left_buf.at[far - 1, rows],
+            send_sem=right_send.at[far - 1, piece],
+            recv_sem=right_recv.at[far - 1, piece],
+            device_id={"tensor": me + 1},
+        )
+
+    def leftward(rows, piece, far, source):
+        return pltpu.make_async_remote_copy(
+            src_ref=source,
+            dst_ref=right_buf.at[far - 1, rows],
+            send_sem=left_send.at[far - 1, piece],
+            recv_sem=left_recv.at[far - 1, piece],
+            device_id={"tensor": me - 1},
+        )
+
+    def added(buffer, far, rows, block):
+        buffer[far, rows, :] = (
+            buffer[far, rows, :].astype(F32) + part_ref[block, rows, :].astype(F32)
+        ).astype(BF16)
+
+    def advance(far):
+        for piece in range(chunks):
+            rows = pl.ds(piece * size, size)
+
+            @pl.when((me == 0) & (me + far < count))
+            def _():
+                rightward(rows, piece, far, part_ref.at[me + far, rows]).start()
+
+            @pl.when((me == count - 1) & (me - far >= 0))
+            def _():
+                leftward(rows, piece, far, part_ref.at[me - far, rows]).start()
+
+            if far < count - 1:
+
+                @pl.when((me > 0) & (me + far < count))
+                def _():
+                    rightward(rows, piece, far + 1, left_buf.at[far, rows]).wait_recv()
+                    added(left_buf, far, rows, me + far)
+                    rightward(rows, piece, far, left_buf.at[far, rows]).start()
+
+                @pl.when((me < count - 1) & (me - far >= 0))
+                def _():
+                    leftward(rows, piece, far + 1, right_buf.at[far, rows]).wait_recv()
+                    added(right_buf, far, rows, me - far)
+                    leftward(rows, piece, far, right_buf.at[far, rows]).start()
+
+    def finish():
+        for piece in range(chunks):
+            rows = pl.ds(piece * size, size)
+            out_ref[rows, :] = part_ref[me, rows, :].astype(F32)
+
+            @pl.when(me > 0)
+            def _():
+                rightward(rows, piece, 1, left_buf.at[0, rows]).wait_recv()
+                out_ref[rows, :] += left_buf[0, rows, :].astype(F32)
+
+            @pl.when(me < count - 1)
+            def _():
+                leftward(rows, piece, 1, right_buf.at[0, rows]).wait_recv()
+                out_ref[rows, :] += right_buf[0, rows, :].astype(F32)
+
+        for far in range(count - 1, 0, -1):
+            for piece in range(chunks):
+                rows = pl.ds(piece * size, size)
+
+                @pl.when((me == 0) & (me + far < count))
+                def _():
+                    rightward(rows, piece, far, part_ref.at[me + far, rows]).wait_send()
+
+                @pl.when((me == count - 1) & (me - far >= 0))
+                def _():
+                    leftward(rows, piece, far, part_ref.at[me - far, rows]).wait_send()
+
+                if far < count - 1:
+
+                    @pl.when((me > 0) & (me + far < count))
+                    def _():
+                        rightward(rows, piece, far, left_buf.at[far, rows]).wait_send()
+
+                    @pl.when((me < count - 1) & (me - far >= 0))
+                    def _():
+                        leftward(rows, piece, far, right_buf.at[far, rows]).wait_send()
+
+    return advance, finish
+
+
+def greet_line_and_plane(line, plane):
+    me, at_line = lax.axis_index("fsdp"), lax.axis_index("tensor")
+    barrier = pltpu.get_barrier_semaphore()
+
+    @pl.loop(1, plane)
+    def _(d):
+        pl.semaphore_signal(barrier, inc=1, device_id={"fsdp": lax.rem(me + d, plane)})
+
+    @pl.loop(1, line)
+    def _(d):
+        pl.semaphore_signal(barrier, inc=1, device_id={"tensor": lax.rem(at_line + d, line)})
+
+    pl.semaphore_wait(barrier, plane + line - 2)
+
+
 def tiles(width, tile, body):
     @pl.loop(0, width // tile)
     def _(j):
@@ -823,8 +994,10 @@
         y_sem,
         back_sem,
         own_sem,
-        block_send,
-        block_recv,
+        relay_right_send,
+        relay_right_recv,
+        relay_left_send,
+        relay_left_recv,
         row_send,
         row_recv,
         back_send,
@@ -843,189 +1016,210 @@
 
     greet_line_and_plane(line, plane)
 
-    def block_copy(r):
-        return pltpu.make_async_remote_copy(
-            src_ref=own_ref,
-            dst_ref=blocks.at[r],
-            send_sem=block_send.at[r - 1],
-            recv_sem=block_recv.at[r - 1],
-            device_id={"tensor": lax.rem(at_line + line - r, line)},
-        )
-
-    def row_copy(r, d):
+    orders = [sorted(range(line), key=lambda block: abs(block - at)) for at in range(line)]
+
+    def place_of(step):
+        result = 0
+        for at in range(line):
+            for k in range(line):
+                result = jnp.where((at_line == at) & (step == k), orders[at][k], result)
+        return result
+
+    advance, finish_relay = line_relay(
+        at_line,
+        line,
+        [own_ref],
+        [blocks],
+        (4,),
+        (relay_right_send, relay_right_recv, relay_left_send, relay_left_recv),
+    )
+
+    def row_copy(step, block, d):
         target = lax.rem(me + d, plane)
         return pltpu.make_async_remote_copy(
-            src_ref=sent_slots.at[lax.rem(r, 2), target],
-            dst_ref=rows.at[r, me],
-            send_sem=row_send.at[r, d],
-            recv_sem=row_recv.at[r, d],
+            src_ref=sent_slots.at[lax.rem(step, 2), target],
+            dst_ref=rows.at[block, me],
+            send_sem=row_send.at[block, d],
+            recv_sem=row_recv.at[block, d],
             device_id={"fsdp": target},
         )
 
-    def own_rows(r):
+    def own_rows(step, block):
         return pltpu.make_async_copy(
-            sent_slots.at[lax.rem(r, 2), me], rows.at[r, me], own_sem.at[0]
-        )
-
-    def back_copy(r, d):
+            sent_slots.at[lax.rem(step, 2), me], rows.at[block, me], own_sem.at[0]
+        )
+
+    def back_copy(block, d):
         target = lax.rem(me + d, plane)
         return pltpu.make_async_remote_copy(
-            src_ref=rows.at[r, target],
-            dst_ref=back_hbm.at[r, me],
-            send_sem=back_send.at[r, d],
-            recv_sem=back_recv.at[r, d],
+            src_ref=rows.at[block, target],
+            dst_ref=back_hbm.at[block, me],
+            send_sem=back_send.at[block, d],
+            recv_sem=back_recv.at[block, d],
             device_id={"fsdp": target},
         )
 
-    def own_back(r):
-        return pltpu.make_async_copy(rows.at[r, me], back_hbm.at[r, me], own_sem.at[1])
-
-    def dots_copy(r, d):
+    def own_back(block):
+        return pltpu.make_async_copy(
+            rows.at[block, me], back_hbm.at[block, me], own_sem.at[1]
+        )
+
+    def dots_copy(block, d):
         target = lax.rem(me + d, plane)
         return pltpu.make_async_remote_copy(
-            src_ref=dots.at[r, target],
-            dst_ref=dots_back.at[r, me],
-            send_sem=dots_send.at[r, d],
-            recv_sem=dots_recv.at[r, d],
+            src_ref=dots.at[block, target],
+            dst_ref=dots_back.at[block, me],
+            send_sem=dots_send.at[block, d],
+            recv_sem=dots_recv.at[block, d],
             device_id={"fsdp": target},
         )
 
-    def dots_in_copy(r):
+    def dots_in_copy(block, sender):
         return pltpu.make_async_remote_copy(
-            src_ref=dots_pass.at[r],
-            dst_ref=dots_in.at[r],
-            send_sem=dots_in_send.at[r - 1],
-            recv_sem=dots_in_recv.at[r - 1],
-            device_id={"tensor": lax.rem(at_line + r, line)},
-        )
-
-    def partial_copy(r):
+            src_ref=dots_pass.at[block],
+            dst_ref=dots_in.at[sender],
+            send_sem=dots_in_send.at[block],
+            recv_sem=dots_in_recv.at[sender],
+            device_id={"tensor": block},
+        )
+
+    def partial_copy(block, sender):
         return pltpu.make_async_remote_copy(
-            src_ref=partials.at[r - 1],
-            dst_ref=partials_in.at[r - 1],
-            send_sem=partial_send.at[r - 1],
-            recv_sem=partial_recv.at[r - 1],
-            device_id={"tensor": lax.rem(at_line + r, line)},
-        )
-
-    def up_copy(r):
-        return pltpu.make_async_copy(
-            up_hbm.at[:, lax.rem(at_line + r, line)], up_rows, up_sem
-        )
-
-    def y_copy(r):
-        return pltpu.make_async_copy(up_rows, y_hbm.at[:, r], y_sem)
-
-    @pl.loop(1, line)
-    def _(r):
-        block_copy(r).start()
-
-    first_block = pltpu.make_async_copy(own_ref, blocks.at[0], own_sem.at[2])
+            src_ref=partials.at[block],
+            dst_ref=partials_in.at[sender],
+            send_sem=partial_send.at[block],
+            recv_sem=partial_recv.at[sender],
+            device_id={"tensor": block},
+        )
+
+    def up_copy(block):
+        return pltpu.make_async_copy(up_hbm.at[:, block], up_rows, up_sem)
+
+    def y_copy(block):
+        return pltpu.make_async_copy(up_rows, y_hbm.at[:, block], y_sem)
+
+    advance(0, (0,))
+    first_block = pltpu.make_async_copy(own_ref, blocks.at[at_line], own_sem.at[2])
     first_block.start()
-    up_copy(0).start()
+    up_copy(at_line).start()
     table_copies = [
         pltpu.make_async_copy(source, target, table_sem.at[at])
         for at, (source, target) in enumerate(zip(tables_hbm, tables))
     ]
     for each in table_copies:
         each.start()
+    first_block.wait()
+
+    def dispatch(step):
+        block = place_of(step)
+        if step > 1:
+            before = place_of(step - 2)
+
+            @pl.loop(1, plane)
+            def _(d):
+                row_copy(step - 2, before, d).wait_send()
+
+        choice[...] = slot_choice(plane_rank_ref[block], slots)
+
+        def slot_step(columns):
+            sent_slots[step % 2, :, :, columns] = (
+                matrix_product(choice[...], blocks[block, :, columns])
+                .astype(BF16)
+                .reshape(plane, slots, 2 * tile)
+            )
+
+        tiles(width, 2 * tile, slot_step)
+
+        @pl.loop(1, plane)
+        def _(d):
+            row_copy(step, block, d).start()
+
+        own = own_rows(step, block)
+        own.start()
+        own.wait()
+
+    dispatch(0)
     for total in sums:
         total[...] = jnp.zeros_like(total)
-    first_block.wait()
+    advance(1, (0,))
+    dispatch(1)
+    for each in table_copies:
+        each.wait()
+
+    def send_back(block):
+        @pl.loop(1, plane)
+        def _(d):
+            dots_copy(block, d).start()
+            back_copy(block, d).start()
+
+        own = own_back(block)
+        own.start()
+        dots_back[block, me] = dots[block, me]
+        own.wait()
 
     @pl.loop(0, line + 2)
     def _(step):
         @pl.when(step < line)
         def _():
-            @pl.when(step > 0)
-            def _():
-                block_copy(step).wait_recv()
-
-            @pl.when(step > 1)
-            def _():
-                @pl.loop(1, plane)
-                def _(d):
-                    row_copy(step - 2, d).wait_send()
-
-            choice[...] = slot_choice(plane_rank_ref[lax.rem(at_line + step, line)], slots)
-
-            def slot_step(columns):
-                sent_slots[lax.rem(step, 2), :, :, columns] = (
-                    matrix_product(choice[...], blocks[step, :, columns])
-                    .astype(BF16)
-                    .reshape(plane, slots, 2 * tile)
-                )
-
-            tiles(width, 2 * tile, slot_step)
+            block = place_of(step)
 
             @pl.loop(1, plane)
             def _(d):
-                row_copy(step, d).start()
-
-        @pl.when((step >= 1) & (step <= line))
-        def _():
-            r = step - 1
-            block = lax.rem(at_line + r, line)
-
-            @pl.when(r == 0)
-            def _():
-                for each in table_copies:
-                    each.wait()
-
-            own_rows(r).start()
-            own_rows(r).wait()
-
-            @pl.loop(1, plane)
-            def _(d):
-                row_copy(r, d).wait_recv()
-
-            up_copy(r).wait()
+                row_copy(step, block, d).wait_recv()
+
+            up_copy(block).wait()
 
             def keep_dots(source, values):
-                dots[r, source] = jnp.broadcast_to(values, (8, values.shape[1]))
+                dots[block, source] = jnp.broadcast_to(values, (8, values.shape[1]))
 
             expert_math(
                 tile,
-                rows.at[r],
+                rows.at[block],
                 up_rows,
                 rank_ref[block],
                 weight_ref[block],
                 keep_dots,
-                lambda: y_copy(r).start(),
+                lambda: y_copy(block).start(),
                 mask_ref,
                 tables,
                 sums,
                 scratch,
             )
 
+            @pl.when(step > 0)
+            def _():
+                send_back(block)
+
+            @pl.when(step == line - 1)
+            def _():
+                send_back(at_line)
+
+            y_copy(block).wait()
+
+            @pl.when(step + 1 < line)
+            def _():
+                up_copy(place_of(step + 1)).start()
+
+            for late in range(2, line):
+
+                @pl.when(step == late - 2)
+                def _():
+                    advance(late, (0,))
+                    dispatch(late)
+
+        @pl.when(step >= 2)
+        def _():
+            block = place_of(lax.rem(step - 1, line))
+
             @pl.loop(1, plane)
             def _(d):
-                dots_copy(r, d).start()
-                back_copy(r, d).start()
-
-            own_back(r).start()
-            dots_back[r, me] = dots[r, me]
-            y_copy(r).wait()
-
-            @pl.when(r + 1 < line)
-            def _():
-                up_copy(r + 1).start()
-
-            own_back(r).wait()
-
-        @pl.when(step >= 2)
-        def _():
-            r = step - 2
-
-            @pl.loop(1, plane)
-            def _(d):
-                dots_copy(r, d).wait_recv()
-                back_copy(r, d).wait_recv()
-
-            dots_pass[r] = dots_back[r, :, 0, :]
-            load = pltpu.make_async_copy(back_hbm.at[r], back_rows, back_sem)
+                dots_copy(block, d).wait_recv()
+                back_copy(block, d).wait_recv()
+
+            dots_pass[block] = dots_back[block, :, 0, :]
+            load = pltpu.make_async_copy(back_hbm.at[block], back_rows, back_sem)
             load.start()
-            choice[...] = slot_choice(plane_rank_ref[lax.rem(at_line + r, line)], slots)
+            choice[...] = slot_choice(plane_rank_ref[block], slots)
             load.wait()
 
             def combined(columns):
@@ -1033,47 +1227,51 @@
                     choice[...], back_rows[:, :, columns].reshape(plane * slots, 2 * tile)
                 )
 
-            @pl.when(r == 0)
+            @pl.when(step == line + 1)
             def _():
                 def keep(columns):
                     total_ref[:, columns] = combined(columns)
 
                 tiles(width, 2 * tile, keep)
-                dots_ref[at_line] = dots_pass[0]
-
-            @pl.when(r > 0)
+                dots_ref[at_line] = dots_pass[at_line]
+
+            @pl.when(step < line + 1)
             def _():
+                dots_in_copy(block, at_line).start()
+
                 def pass_on(columns):
-                    partials[r - 1, :, columns] = combined(columns).astype(BF16)
-
-                dots_in_copy(r).start()
+                    partials[block, :, columns] = combined(columns).astype(BF16)
+
                 tiles(width, 2 * tile, pass_on)
-                partial_copy(r).start()
+                partial_copy(block, at_line).start()
 
     @pl.loop(1, line)
-    def _(r):
-        dots_in_copy(r).wait_recv()
-        dots_ref[lax.rem(at_line + line - r, line)] = dots_in[r]
-        partial_copy(r).wait_recv()
-        total_ref[...] += partials_in[r - 1].astype(F32)
+    def _(step):
+        sender = place_of(step)
+        dots_in_copy(sender, sender).wait_recv()
+        dots_ref[sender] = dots_in[sender]
+        partial_copy(sender, sender).wait_recv()
+        total_ref[...] += partials_in[sender].astype(F32)
 
     @pl.loop(1, line)
-    def _(r):
-        partial_copy(r).wait_send()
-        dots_in_copy(r).wait_send()
-        block_copy(r).wait_send()
-
-    @pl.loop(1, plane)
-    def _(d):
-        row_copy(line - 2, d).wait_send()
-        row_copy(line - 1, d).wait_send()
-
-    @pl.loop(0, line)
-    def _(r):
+    def _(step):
+        block = place_of(step)
+        partial_copy(block, at_line).wait_send()
+        dots_in_copy(block, at_line).wait_send()
+
+    finish_relay((0,), range(line - 1))
+    for step in (line - 2, line - 1):
+
         @pl.loop(1, plane)
         def _(d):
-            back_copy(r, d).wait_send()
-            dots_copy(r, d).wait_send()
+            row_copy(step, place_of(step), d).wait_send()
+
+    @pl.loop(0, line)
+    def _(block):
+        @pl.loop(1, plane)
+        def _(d):
+            back_copy(block, d).wait_send()
+            dots_copy(block, d).wait_send()
 
 
 def moe_layer(own, up_rows, plane_ranks, ranks, weights, mask, tables, identity):
@@ -1099,8 +1297,8 @@
         scratch_shapes=[pltpu.VMEM(table.shape, table.dtype) for table in tables]
         + [
             pltpu.VMEM((line, tokens, width), BF16),
-            pltpu.VMEM((line - 1, tokens, width), BF16),
-            pltpu.VMEM((line - 1, tokens, width), BF16),
+            pltpu.VMEM((line, tokens, width), BF16),
+            pltpu.VMEM((line, tokens, width), BF16),
             pltpu.VMEM((2,) + grouped, BF16),
             pltpu.VMEM((line,) + grouped, BF16),
             pltpu.VMEM(grouped, BF16),
@@ -1113,11 +1311,11 @@
         ]
         + expert_scratch(plane * slots, hidden, width)
         + [dma((len(tables),)), dma, dma, dma, dma((3,))]
-        + [dma((line - 1,))] * 2
+        + [dma((line - 1, 4))] * 4
         + [dma((line, plane))] * 4
-        + [dma((line - 1,))] * 2
+        + [dma((line,))] * 2
         + [dma((line, plane))] * 2
-        + [dma((line - 1,))] * 2,
+        + [dma((line,))] * 2,
         compiler_params=pltpu.CompilerParams(
             collective_id=identity, has_side_effects=True, vmem_limit_bytes=63 * MEBI
         ),
@@ -1211,177 +1409,6 @@
         ),
         name="sum_line",
     )(part)
-
-
-def line_relay(me, count, ins, outs, chunks, semaphores):
-    right_send, right_recv, left_send, left_recv = semaphores
-    pieces = []
-    for at in range(len(ins)):
-        size = ins[at].shape[0] // chunks[at]
-        for piece in range(chunks[at]):
-            pieces.append((at, pl.ds(piece * size, size)))
-
-    def copy(place, hop, origin, target, send, recv):
-        at, rows = pieces[place]
-        source = ins[at].at[rows] if hop == 0 else outs[at].at[origin, rows]
-        return pltpu.make_async_remote_copy(
-            src_ref=source,
-            dst_ref=outs[at].at[origin, rows],
-            send_sem=send.at[hop, place],
-            recv_sem=recv.at[hop, place],
-            device_id={"tensor": target},
-        )
-
-    def places(arrays):
-        return [place for place in range(len(pieces)) if pieces[place][0] in arrays]
-
-    def advance(hop, arrays):
-        for place in places(arrays):
-            if hop > 0:
-
-                @pl.when(me - hop >= 0)
-                def _():
-                    copy(place, hop - 1, me - hop, me - 1, right_send, right_recv).wait_recv()
-
-            if hop < count - 1:
-
-                @pl.when((me - hop >= 0) & (me + 1 < count))
-                def _():
-                    copy(place, hop, me - hop, me + 1, right_send, right_recv).start()
-
-            if hop > 0:
-
-                @pl.when(me + hop < count)
-                def _():
-                    copy(place, hop - 1, me + hop, me + 1, left_send, left_recv).wait_recv()
-
-            if hop < count - 1:
-
-                @pl.when((me + hop < count) & (me > 0))
-                def _():
-                    copy(place, hop, me + hop, me - 1, left_send, left_recv).start()
-
-    def finish(arrays, hops):
-        for hop in hops:
-            for place in places(arrays):
-
-                @pl.when((me - hop >= 0) & (me + 1 < count))
-                def _():
-                    copy(place, hop, me - hop, me + 1, right_send, right_recv).wait_send()
-
-                @pl.when((me + hop < count) & (me > 0))
-                def _():
-                    copy(place, hop, me + hop, me - 1, left_send, left_recv).wait_send()
-
-    return advance, finish
-
-
-def line_sum(me, count, chunks, part_ref, out_ref, left_buf, right_buf, semaphores):
-    right_send, right_recv, left_send, left_recv = semaphores
-    size = part_ref.shape[1] // chunks
-
-    def rightward(rows, piece, far, source):
-        return pltpu.make_async_remote_copy(
-            src_ref=source,
-            dst_ref=left_buf.at[far - 1, rows],
-            send_sem=right_send.at[far - 1, piece],
-            recv_sem=right_recv.at[far - 1, piece],
-            device_id={"tensor": me + 1},
-        )
-
-    def leftward(rows, piece, far, source):
-        return pltpu.make_async_remote_copy(
-            src_ref=source,
-            dst_ref=right_buf.at[far - 1, rows],
-            send_sem=left_send.at[far - 1, piece],
-            recv_sem=left_recv.at[far - 1, piece],
-            device_id={"tensor": me - 1},
-        )
-
-    def added(buffer, far, rows, block):
-        buffer[far, rows, :] = (
-            buffer[far, rows, :].astype(F32) + part_ref[block, rows, :].astype(F32)
-        ).astype(BF16)
-
-    def advance(far):
-        for piece in range(chunks):
-            rows = pl.ds(piece * size, size)
-
-            @pl.when((me == 0) & (me + far < count))
-            def _():
-                rightward(rows, piece, far, part_ref.at[me + far, rows]).start()
-
-            @pl.when((me == count - 1) & (me - far >= 0))
-            def _():
-                leftward(rows, piece, far, part_ref.at[me - far, rows]).start()
-
-            if far < count - 1:
-
-                @pl.when((me > 0) & (me + far < count))
-                def _():
-                    rightward(rows, piece, far + 1, left_buf.at[far, rows]).wait_recv()
-                    added(left_buf, far, rows, me + far)
-                    rightward(rows, piece, far, left_buf.at[far, rows]).start()
-
-                @pl.when((me < count - 1) & (me - far >= 0))
-                def _():
-                    leftward(rows, piece, far + 1, right_buf.at[far, rows]).wait_recv()
-                    added(right_buf, far, rows, me - far)
-                    leftward(rows, piece, far, right_buf.at[far, rows]).start()
-
-    def finish():
-        for piece in range(chunks):
-            rows = pl.ds(piece * size, size)
-            out_ref[rows, :] = part_ref[me, rows, :].astype(F32)
-
-            @pl.when(me > 0)
-            def _():
-                rightward(rows, piece, 1, left_buf.at[0, rows]).wait_recv()
-                out_ref[rows, :] += left_buf[0, rows, :].astype(F32)
-
-            @pl.when(me < count - 1)
-            def _():
-                leftward(rows, piece, 1, right_buf.at[0, rows]).wait_recv()
-                out_ref[rows, :] += right_buf[0, rows, :].astype(F32)
-
-        for far in range(count - 1, 0, -1):
-            for piece in range(chunks):
-                rows = pl.ds(piece * size, size)
-
-                @pl.when((me == 0) & (me + far < count))
-                def _():
-                    rightward(rows, piece, far, part_ref.at[me + far, rows]).wait_send()
-
-                @pl.when((me == count - 1) & (me - far >= 0))
-                def _():
-                    leftward(rows, piece, far, part_ref.at[me - far, rows]).wait_send()
-
-                if far < count - 1:
-
-                    @pl.when((me > 0) & (me + far < count))
-                    def _():
-                        rightward(rows, piece, far, left_buf.at[far, rows]).wait_send()
-
-                    @pl.when((me < count - 1) & (me - far >= 0))
-                    def _():
-                        leftward(rows, piece, far, right_buf.at[far, rows]).wait_send()
-
-    return advance, finish
-
-
-def greet_line_and_plane(line, plane):
-    me, at_line = lax.axis_index("fsdp"), lax.axis_index("tensor")
-    barrier = pltpu.get_barrier_semaphore()
-
-    @pl.loop(1, plane)
-    def _(d):
-        pl.semaphore_signal(barrier, inc=1, device_id={"fsdp": lax.rem(me + d, plane)})
-
-    @pl.loop(1, line)
-    def _(d):
-        pl.semaphore_signal(barrier, inc=1, device_id={"tensor": lax.rem(at_line + d, line)})
-
-    pl.semaphore_wait(barrier, plane + line - 2)
 
 
 def front_body(
@@ -1504,11 +1531,11 @@
         (relay_right_send, relay_right_recv, relay_left_send, relay_left_recv),
     )
     advance(0, (0, 1))
-    advance(0, (2,))
     for each in locals_in:
         each.start()
     advance(1, (0, 1))
     advance(2, (0, 1))
+    advance(0, (2,))
     for k in range(1, peers):
         weight_copy(k).wait_recv()
         weight_pass(k).start()
@@ -1862,7 +1889,8 @@
     second_sum,
     y_rows,
     partials,
-    partials_in,
+    left_buf,
+    right_buf,
     result,
     choice,
     load_sem,
@@ -1873,8 +1901,10 @@
     relay_left_recv,
     y_send,
     y_recv,
-    partial_send,
-    partial_recv,
+    sum_right_send,
+    sum_right_recv,
+    sum_left_send,
+    sum_left_recv,
 ):
     me, at_line = lax.axis_index("fsdp"), lax.axis_index("tensor")
     tokens, width = residual_ref.shape
@@ -1885,36 +1915,50 @@
 
     greet_line_and_plane(line, plane)
 
-    def y_copy(r, d):
+    orders = [sorted(range(line), key=lambda block: abs(block - at)) for at in range(line)]
+
+    def place_of(step):
+        result = 0
+        for at in range(line):
+            result = jnp.where(at_line == at, orders[at][step], result)
+        return result
+
+    def y_copy(block, d):
         target = lax.rem(me + d, plane)
         return pltpu.make_async_remote_copy(
-            src_ref=y_hbm.at[target, r],
-            dst_ref=y_in_hbm.at[r, me],
-            send_sem=y_send.at[r, d],
-            recv_sem=y_recv.at[r, d],
+            src_ref=y_hbm.at[target, block],
+            dst_ref=y_in_hbm.at[block, me],
+            send_sem=y_send.at[block, d],
+            recv_sem=y_recv.at[block, d],
             device_id={"fsdp": target},
         )
 
-    def own_y(r):
-        return pltpu.make_async_copy(y_hbm.at[me, r], y_in_hbm.at[r, me], y_sem.at[r])
-
-    def partial_copy(r):
-        return pltpu.make_async_remote_copy(
-            src_ref=partials.at[r - 1],
-            dst_ref=partials_in.at[r - 1],
-            send_sem=partial_send.at[r - 1],
-            recv_sem=partial_recv.at[r - 1],
-            device_id={"tensor": lax.rem(at_line + r, line)},
-        )
-
-    for r in list(range(1, line)) + [0]:
+    def own_y(block):
+        return pltpu.make_async_copy(
+            y_hbm.at[me, block], y_in_hbm.at[block, me], y_sem.at[block]
+        )
+
+    def send_y(step):
+        block = place_of(step)
 
         @pl.loop(1, plane)
         def _(d):
-            y_copy(r, d).start()
-
-    for r in range(line):
-        own_y(r).start()
+            y_copy(block, d).start()
+
+        own_y(block).start()
+
+    send_y(line - 1)
+    send_y(line - 2)
+    advance_sum, finish_sum = line_sum(
+        at_line,
+        line,
+        4,
+        partials,
+        result,
+        left_buf,
+        right_buf,
+        (sum_right_send, sum_right_recv, sum_left_send, sum_left_recv),
+    )
     loads = [
         pltpu.make_async_copy(source, target, load_sem.at[at])
         for at, (source, target) in enumerate(
@@ -1929,29 +1973,30 @@
     for each in loads:
         each.start()
 
-    def combine(r):
+    def combine(step):
+        block = place_of(step)
+
         @pl.loop(1, plane)
         def _(d):
-            y_copy(r, d).wait_recv()
-
-        own_y(r).wait()
-        load = pltpu.make_async_copy(y_in_hbm.at[r], y_rows, y_sem.at[line])
+            y_copy(block, d).wait_recv()
+
+        own_y(block).wait()
+        if step > 1:
+            send_y(step - 2)
+        load = pltpu.make_async_copy(y_in_hbm.at[block], y_rows, y_sem.at[line])
         load.start()
-        choice[...] = slot_choice(ranks_ref[lax.rem(at_line + r, line)], slots)
+        choice[...] = slot_choice(ranks_ref[block], slots)
         load.wait()
 
         def combined(columns):
             total = flipped_left_operand(
                 choice[...], y_rows[:, :, columns].reshape(plane * slots, 2 * tile)
             )
-            if r == 0:
-                result[:, columns] = total
-            else:
-                partials[r - 1, :, columns] = total.astype(BF16)
+            partials[block, :, columns] = total.astype(BF16)
 
         tiles(width, 2 * tile, combined)
-        if r > 0:
-            partial_copy(r).start()
+        if step > 0:
+            advance_sum(step)
 
     gates = gates_ref[...]
     dots = dots_ref[...]
@@ -2038,7 +2083,7 @@
             head_gradients(at_line + hop)
 
         if hop < line - 1:
-            combine(hop)
+            combine(line - hop)
     rows_out_ref[3 * rank : 4 * rank, :] = second_sum[...].astype(BF16)
 
     head_count = query_columns // head_dim
@@ -2086,7 +2131,7 @@
 
         @pl.when(head == head_count // 2 - 1)
         def _():
-            combine(line - 1)
+            combine(1)
 
     low_k = low_ref[:, rank : 2 * rank]
     low_v = low_ref[:, 2 * rank : 3 * rank]
@@ -2112,18 +2157,14 @@
 
     tiles(width, 2 * tile, first_gradient)
     combine(0)
-    for r in range(1, line):
-        partial_copy(r).wait_recv()
-        result[...] += partials_in[r - 1].astype(F32)
+    finish_sum()
     output_ref[...] = (residual_ref[...] + result[...]).astype(BF16)
     finish_relay((0,), range(line - 1))
-    for r in range(1, line):
-        partial_copy(r).wait_send()
-    for r in range(line):
+    for block in range(line):
 
         @pl.loop(1, plane)
         def _(d):
-            y_copy(r, d).wait_send()
+            y_copy(block, d).wait_send()
 
 
 def back(scale, places, slots, identity, hbm_operands, operands):
@@ -2172,6 +2213,7 @@
             pltpu.VMEM((all_rows, 3 * rank), F32),
             pltpu.VMEM((rank, width), F32),
             pltpu.VMEM((plane, slots, width), BF16),
+            pltpu.VMEM((line,) + block, BF16),
             pltpu.VMEM((line - 1,) + block, BF16),
             pltpu.VMEM((line - 1,) + block, BF16),
             pltpu.VMEM(block, F32),
@@ -2181,7 +2223,7 @@
         ]
         + [dma((line - 1, 4))] * 4
         + [dma((line, plane))] * 2
-        + [dma((line - 1,))] * 2,
+        + [dma((line - 1, 4))] * 4,
         compiler_params=pltpu.CompilerParams(
             collective_id=identity, has_side_effects=True, vmem_limit_bytes=63 * MEBI
         ),

time: 845 us -> 770 us (0.911)
  Pallas kernels: 738 us -> 691 us
  starting transfers between devices: 37.8 us -> 9.41 us
    all_to_all x2, starting transfers between devices: 37.8 us -> 9.41 us  [route_rows(): lax.all_to_all(block_rows, ('fsdp', 'tensor'), split_axis=0, concat_axis=...]
    pallas_call x1, Pallas kernels: 279 us -> 258 us  [moe_layer(): pl.pallas_call(functools.partial(moe_body, plane, line), out_shape=[jax.S...]
    pallas_call x1, Pallas kernels: 219 us -> 206 us  [front(): pl.pallas_call(functools.partial(front_body, plane, line, scale, places),...]
    pallas_call x1, Pallas kernels: 159 us -> 147 us  [back(): pl.pallas_call(functools.partial(back_body, plane, line, scale, places),...]
  transfers between devices with their start and end apart: 2 -> 2, of which waited for: 1 -> 1; matrix products, arithmetic and copies ran while one was open for 1% -> 1% of each run, Pallas kernels for 10% -> 11%
where the time goes in v6:
time: 770 us; the launch traced here: 759 us
  Pallas kernels  691 us (90%)
  local copies, waits for them, and re-layouts  41.2 us (5%)
  other arithmetic  10.7 us (1%)
  starting transfers between devices  9.41 us (1%)
    pallas_call x1, Pallas kernels, moe_layer(): pl.pallas_call(functools.partial(moe_body, plane, line), out_shape=[jax.S...  258 us
    pallas_call x1, Pallas kernels, front(): pl.pallas_call(functools.partial(front_body, plane, line, scale, places),...  206 us
    pallas_call x1, Pallas kernels, back(): pl.pallas_call(functools.partial(back_body, plane, line, scale, places),...  147 us
    pallas_call x1, Pallas kernels, last(): pl.pallas_call(functools.partial(last_body, line), out_shape=jax.ShapeDty...  79.9 us
    unnamed x89, local copies, waits for them, and re-layouts  18.7 us
  transfers between devices with their start and end apart: 2, of which 1 were waited for; matrix products, arithmetic and copies ran while one was open for 1% of the time, Pallas kernels for 11%

profile of v6, /device:TPU:16, one launch (start us, length us, event | category | flops | bytes accessed | tf_op | source)
XLA Modules:
  0.0 759.3 jit_solution(12325786967688022687)
XLA Ops:
  0.7 1.4 dynamic_slice.38
  3.4 0.7 fusion.7.before_ref
  4.7 0.6 dynamic-slice_bitcast_fusion.1.out_second_ref.second_out_ref
  5.4 1.4 dynamic-slice_bitcast_fusion.5.out_first_ref.first_out_ref
  6.7 1.4 dynamic-slice_bitcast_fusion.6.q_second_ref
  8.1 2.0 fusion.10
  10.1 1.8 copy.124.seg_column_ref
  12.5 0.8 constant_dynamic-update-slice_fusion.2
  13.7 0.9 dynamic-slice_bitcast_fusion
  14.6 0.9 dynamic-slice_bitcast_fusion.3
  15.5 1.3 dynamic-slice_bitcast_fusion.7
  18.7 0.6 pad_dynamic-update-slice_fusion
  19.3 0.8 bitcast_dynamic-update-slice_fusion.weights_hbm
  20.1 0.7 pad_maximum_fusion.3.first_ref
  20.8 1.3 pad_maximum_fusion.1
  22.1 205.8 %front.1 = (f32[256,2048]{1,0:T(8,128)}, f32[4,8,256]{2,1,0:T(8,128)}, bf16[1024,48]{1,0:T(8,128)(2,1)}, bf16[1024,16]{1,0:T(8,128)(2,1)}, f32[1024,1280]{1,0:T(...) custom-call(bf16[256,2048]{1,0:T(8,128)(2,1)} %tokens_ref.1, ...), custom_call_target="tpu_custom_call" | custom-call | tf_op jit(solution)/shard_map/front/pallas_call | solution.py:1788
  228.0 2.2 multiply_reduce_fusion
  231.9 1.5 fusion.20
  233.3 0.7 constant_dynamic-slice_fusion
  234.3 0.6 copy.127
  234.9 3.4 all-to-all-start
  238.4 1.1 pad_maximum_fusion.rest_3_
  239.5 1.1 slice.64
  241.6 0.7 copy.164
  242.3 0.7 copy.132
  244.1 0.8 fusion.rank_ref
  244.8 0.7 broadcast_in_dim.78
  245.5 258.2 %moe_layer.1 = (f32[256,2048]{1,0:T(8,128)}, f32[4,8,256]{2,1,0:T(8,128)}, bf16[8,4,80,2048]{3,2,1,0:T(8,128)(2,1)}, bf16[4,8,80,2048]{3,2,1,0:T(8,128)(2,1)}, f...) custom-call(bf16[256,2048]{1,0:T(8,128)(2,1)} %copy-done.9, ...), custom_call_target="tpu_custom_call" | custom-call | tf_op jit(solution)/shard_map/moe_layer/pallas_call | solution.py:1286
  503.7 147.1 %back.1 = (bf16[256,2048]{1,0:T(8,128)(2,1)}, f32[256,2048]{1,0:T(8,128)}, bf16[1024,48]{1,0:T(8,128)(2,1)}, bf16[1024,1280]{1,0:T(8,128)(2,1)}, bf16[80,2048]{1...) custom-call(f32[256,2048]{1,0:T(8,128)} %get-tuple-element.47.moe_to, ...), custom_call_target="tpu_custom_call" | custom-call | tf_op jit(solution)/shard_map/back/pallas_call | solution.py:2184
  650.9 1.6 reshape.186
  654.4 1.1 reduce.1
  655.5 1.4 reshape.205
  656.9 6.0 all-to-all-start.1
  663.1 1.6 copy-done.5
  664.7 79.9 %last.1 = f32[256,2048]{1,0:T(8,128)S(1)} custom-call(bf16[1024,1280]{1,0:T(8,128)(2,1)} %get-tuple-element.56.linear_grad_ref, bf16[1024,48]{1,0:T(8,128)(2,1)S(1)} %copy-done.7, bf16[48,2048]{1,0:T(8,128)(2,1)S(1)} %copy-done.6, f32[256,2048]{1,0:T(8,128)S(1)} %copy-done.5, bf16[256,2048]{1,0:T(8,128)(2,1)S(1)} %copy-done.2, f32[1,2048]{1,0:T(1,128)S(1)} %bitcast.182, ...), custom_call_target="tpu_custom_call" | custom-call | tf_op jit(solution)/shard_map/last/pallas_call | solution.py:2305
  744.6 1.3 copy-done.3
  745.9 1.5 fusion.23
  747.5 0.8 reshape.206
  749.2 0.7 slice_bitcast_fusion.1
  750.0 0.6 copy.165
  750.6 0.6 copy.146
  751.4 0.7 fusion.25
  752.0 2.3 copy.182
  754.3 1.3 copy.183
  755.7 0.7 copy.184
  756.4 0.7 copy.185
  757.2 0.7 copy.186
  757.9 1.0 copy.187
  (121 shorter events, 9.8 us)
Async XLA Ops:
  0.7 4.1 copy-start
  0.7 11.2 %copy-start.30 = (bf16[2048]{0:T(1024)(128)(2,1)S(1)}, bf16[2048]{0:T(1024)(128)(2,1)}, u32[]{:S(2)}) copy-start(bf16[2048]{0:T(1024)(128)(2,1)} %param.38) | copy-start | bytes 12292
  0.7 11.8 %copy-start.14 = (bf16[256,1024]{1,0:T(8,128)(2,1)S(1)}, bf16[256,1024]{1,0:T(8,128)(2,1)}, u32[]{:S(2)}) copy-start(bf16[256,1024]{1,0:T(8,128)(2,1)} %param.42) | copy-start | bytes 1572868
  0.7 12.6 %copy-start.27 = (bf16[256,32]{0,1:T(8,128)(2,1)S(1)}, bf16[256,32]{0,1:T(8,128)(2,1)}, u32[]{:S(2)}) copy-start(bf16[256,32]{0,1:T(8,128)(2,1)} %param.46) | copy-start | bytes 49156
  0.7 12.7 %copy-start.15 = (bf16[1024,256]{1,0:T(8,128)(2,1)S(1)}, bf16[1024,256]{1,0:T(8,128)(2,1)}, u32[]{:S(2)}) copy-start(bf16[1024,256]{1,0:T(8,128)(2,1)} %param.45) | copy-start | bytes 1572868
  8.1 5.5 copy-start.26
  8.1 8.7 %copy-start.33 = (bf16[128]{0:T(256)(128)(2,1)S(1)}, bf16[128]{0:T(256)(128)(2,1)}, u32[]{:S(2)}) copy-start(bf16[128]{0:T(256)(128)(2,1)} %param.41) | copy-start | bytes 772
  8.1 8.7 %copy-start.34 = (bf16[128]{0:T(256)(128)(2,1)S(1)}, bf16[128]{0:T(256)(128)(2,1)}, u32[]{:S(2)}) copy-start(bf16[128]{0:T(256)(128)(2,1)} %param.40) | copy-start | bytes 772
  8.1 9.3 %copy-start.23 = (bf16[256,128]{1,0:T(8,128)(2,1)S(1)}, bf16[256,128]{1,0:T(8,128)(2,1)}, u32[]{:S(2)}) copy-start(bf16[256,128]{1,0:T(8,128)(2,1)} %param.43) | copy-start | bytes 196612
  10.1 8.0 %copy-start.24 = (bf16[256,128]{1,0:T(8,128)(2,1)S(1)}, bf16[256,128]{1,0:T(8,128)(2,1)}, u32[]{:S(2)}) copy-start(bf16[256,128]{1,0:T(8,128)(2,1)} %param.44) | copy-start | bytes 196612
  14.6 215.9 %copy-start.13 = (bf16[16,2048]{1,0:T(8,128)(2,1)}, bf16[16,2048]{1,0:T(8,128)(2,1)S(1)}, u32[]{:S(2)}) copy-start(bf16[16,2048]{1,0:T(8,128)(2,1)S(1)} %get-tuple-element.178.router_first_ref) | copy-start | bytes 196612
  228.0 2.3 copy-start.31
  230.2 1.3 copy-start.10
  230.2 1.3 copy-start.21
  230.5 1.4 copy-start.9
  230.5 7.9 %copy-start.16 = (bf16[1,8,2048,16]{2,3,1,0:T(8,128)(2,1)S(1)}, bf16[1,8,2048,16]{2,3,1,0:T(8,128)(2,1)}, u32[]{:S(2)}) copy-start(bf16[1,8,2048,16]{2,3,1,0:T(8,128)(2,1)} %param.62) | copy-start | bytes 1572868
  230.5 7.9 %copy-start.17 = (bf16[1,8,2048,16]{2,3,1,0:T(8,128)(2,1)S(1)}, bf16[1,8,2048,16]{2,3,1,0:T(8,128)(2,1)}, u32[]{:S(2)}) copy-start(bf16[1,8,2048,16]{2,3,1,0:T(8,128)(2,1)} %param.60) | copy-start | bytes 1572868
  231.5 9.1 %copy-start.22 = (bf16[256,16]{0,1:T(8,128)(2,1)}, bf16[256,16]{0,1:T(8,128)(2,1)S(1)}, u32[]{:S(2)}) copy-start(bf16[256,16]{0,1:T(8,128)(2,1)S(1)} %convolution_convert_fusion) | copy-start | bytes 24580
  231.5 7.9 %copy-start.32 = (s32[8]{0:T(128)S(1)}, s32[8]{0:T(128)}, u32[]{:S(2)}) copy-start(s32[8]{0:T(128)} %param.36) | copy-start | bytes 100
  234.9 8.4 %all-to-all-start = ((f32[32,1,256]{2,1,0:T(1,128)}), f32[32,1,256]{2,1,0:T(1,128)S(1)}, u32[]{:S(2)}, u32[]{:S(2)}) async-start(f32[32,1,256]{2,1,0:T(1,128)} %copy.127), calls=%async_computation | async-start | bytes 65536 | tf_op jit(solution)/shard_map/all_to_all | solution.py:63
  650.9 2.4 copy-start.25
  650.9 2.4 copy-start.28
  650.9 2.8 copy-start.29
  653.9 9.2 %copy-start.2 = (bf16[256,2048]{1,0:T(8,128)(2,1)S(1)}, bf16[256,2048]{1,0:T(8,128)(2,1)}, u32[]{:S(2)}) copy-start(bf16[256,2048]{1,0:T(8,128)(2,1)} %tokens_ref.1) | copy-start | bytes 3145732
  653.9 9.2 %copy-start.6 = (bf16[48,2048]{1,0:T(8,128)(2,1)S(1)}, bf16[48,2048]{1,0:T(8,128)(2,1)}, u32[]{:S(2)}) copy-start(bf16[48,2048]{1,0:T(8,128)(2,1)} %pad_maximum_fusion.3.first_ref) | copy-start | bytes 589828
  653.9 9.2 %copy-start.7 = (bf16[1024,48]{1,0:T(8,128)(2,1)S(1)}, bf16[1024,48]{1,0:T(8,128)(2,1)}, u32[]{:S(2)}) copy-start(bf16[1024,48]{1,0:T(8,128)(2,1)} %get-tuple-element.57.share_ref) | copy-start | bytes 294916
  653.9 9.2 %copy-start.8 = (f32[2048]{0:T(1024)S(1)}, f32[2048]{0:T(1024)}, u32[]{:S(2)}) copy-start(f32[2048]{0:T(1024)} %broadcast_in_dim.86) | copy-start | bytes 24580
  656.9 90.5 %all-to-all-start.1 = ((bf16[32,2,4872]{2,1,0:T(2,128)(2,1)}), bf16[32,2,4872]{2,1,0:T(2,128)(2,1)S(1)}, u32[]{:S(2)}, u32[]{:S(2)}) async-start(bf16[32,2,4872]{2,1,0:T(2,128)(2,1)} %reshape.205), calls=%async_computation.1 | async-start | bytes 1277952 | tf_op jit(solution)/shard_map/all_to_all | solution.py:63
  663.1 1.6 copy-start.5
  664.7 81.2 %copy-start.11 = (f32[256,2048]{1,0:T(8,128)S(1)}, f32[256,2048]{1,0:T(8,128)}, u32[]{:S(2)}) copy-start(f32[256,2048]{1,0:T(8,128)} %get-tuple-element.63) | copy-start | bytes 6291460
  744.6 1.3 copy-start.3
  749.1 5.2 copy-start.4
  754.3 1.3 copy-start.20
  754.3 2.1 copy-start.19
  754.3 2.8 copy-start.18
  754.3 4.6 copy-start.1
  755.7 2.2 copy-start.12

commit v7 on v6

--- a/solution.py
+++ b/solution.py
@@ -3,6 +3,7 @@
 
 import jax
 import jax.numpy as jnp
+import numpy as np
 from jax import lax
 from jax.experimental import pallas as pl
 from jax.experimental.pallas import tpu as pltpu
@@ -46,12 +47,14 @@
 
 def rope_tables(sequence_length, head_width):
     half_width = head_width // 2
-    inverse = jnp.power(ROPE_THETA, -2.0 * jnp.arange(half_width, dtype=F32) / head_width)
-    angles = jnp.arange(sequence_length, dtype=F32)[:, None] * inverse[None, :]
-    cosine, sine = jnp.cos(angles), jnp.sin(angles)
+    inverse = np.power(
+        np.float32(ROPE_THETA), -2.0 * np.arange(half_width, dtype=np.float32) / head_width
+    ).astype(np.float32)
+    angles = np.arange(sequence_length, dtype=np.float32)[:, None] * inverse[None, :]
+    cosine, sine = np.cos(angles), np.sin(angles)
     return (
-        jnp.concatenate([cosine, cosine], axis=1),
-        jnp.concatenate([-sine, sine], axis=1),
+        jnp.asarray(np.concatenate([cosine, cosine], axis=1)),
+        jnp.asarray(np.concatenate([-sine, sine], axis=1)),
     )
 
 
@@ -71,6 +74,31 @@
     return pltpu.CompilerParams(
         vmem_limit_bytes=mebibytes * MEBI, dimension_semantics=("arbitrary",) * axes
     )
+
+
+def staged(body, lead, count):
+    def kernel(*refs):
+        semaphores, held = refs[-1], refs[-1 - count : -1]
+        copies = [
+            pltpu.make_async_copy(source, target, semaphores.at[at])
+            for at, (source, target) in enumerate(zip(refs[lead : lead + count], held))
+        ]
+        for each in copies:
+            each.start()
+
+        def ready():
+            for each in copies:
+                each.wait()
+
+        body(ready, *refs[:lead], *held, *refs[lead + count : -1 - count])
+
+    return kernel
+
+
+def staging(operands):
+    return [pltpu.VMEM(operand.shape, operand.dtype) for operand in operands] + [
+        pltpu.SemaphoreType.DMA((len(operands),))
+    ]
 
 
 def whole(shape):
@@ -754,7 +782,7 @@
     row_count = sources * slots
     hidden = gate_w.shape[1]
     broad = gate_out.shape[0]
-    places = lax.broadcasted_iota(jnp.int32, (slots, ranks.shape[1]), 0)
+    places = lax.broadcasted_iota(jnp.int32, (slots, ranks.shape[1]), 0).astype(ranks.dtype)
 
     def held(source):
         return places == ranks[source : source + 1, :]
@@ -961,10 +989,10 @@
 def moe_body(
     plane,
     line,
+    ready,
     own_ref,
     up_hbm,
     plane_rank_ref,
-    rank_ref,
     weight_ref,
     mask_ref,
     *rest,
@@ -986,8 +1014,11 @@
         dots_back,
         dots_pass,
         dots_in,
-    ) = rest[:12]
-    scratch, rest = rest[12:18], rest[18:]
+        line_weights,
+        weight_pass,
+        weight_land,
+    ) = rest[:15]
+    scratch, rest = rest[15:21], rest[21:]
     (
         table_sem,
         up_sem,
@@ -1008,6 +1039,10 @@
         dots_recv,
         dots_in_send,
         dots_in_recv,
+        line_weight_send,
+        line_weight_recv,
+        weight_send,
+        weight_recv,
     ) = rest
     width = own_ref.shape[1]
     slots = rows.shape[2]
@@ -1098,6 +1133,29 @@
     def y_copy(block):
         return pltpu.make_async_copy(up_rows, y_hbm.at[:, block], y_sem)
 
+    def line_weight_copy(target, sender):
+        return pltpu.make_async_remote_copy(
+            src_ref=weight_ref.at[target],
+            dst_ref=line_weights.at[sender],
+            send_sem=line_weight_send.at[target],
+            recv_sem=line_weight_recv.at[sender],
+            device_id={"tensor": target},
+        )
+
+    def weight_copy(block, d):
+        target = lax.rem(me + d, plane)
+        return pltpu.make_async_remote_copy(
+            src_ref=weight_pass.at[block, target],
+            dst_ref=weight_land.at[block, me],
+            send_sem=weight_send.at[block, d],
+            recv_sem=weight_recv.at[block, d],
+            device_id={"fsdp": target},
+        )
+
+    ready()
+    for step in range(1, line):
+        line_weight_copy(place_of(step), at_line).start()
+    line_weights[at_line] = weight_ref[at_line]
     advance(0, (0,))
     first_block = pltpu.make_async_copy(own_ref, blocks.at[at_line], own_sem.at[2])
     first_block.start()
@@ -1119,6 +1177,18 @@
             def _(d):
                 row_copy(step - 2, before, d).wait_send()
 
+        if step > 0:
+            line_weight_copy(block, block).wait_recv()
+        for target in range(plane):
+            weight_pass[block, target] = jnp.broadcast_to(
+                line_weights[block, target : target + 1, :], weight_pass.shape[2:]
+            )
+        weight_land[block, me] = weight_pass[block, me]
+
+        @pl.loop(1, plane)
+        def _(d):
+            weight_copy(block, d).start()
+
         choice[...] = slot_choice(plane_rank_ref[block], slots)
 
         def slot_step(columns):
@@ -1165,8 +1235,21 @@
 
             @pl.loop(1, plane)
             def _(d):
+                weight_copy(block, d).wait_recv()
                 row_copy(step, block, d).wait_recv()
 
+            gates = weight_land[block, :, 0, :]
+            count = gates.shape[1]
+            earlier = lax.broadcasted_iota(jnp.int32, (count, count), 0)
+            before = (
+                (earlier < lax.broadcasted_iota(jnp.int32, (count, count), 1))
+                .astype(F32)
+                .astype(BF16)
+            )
+            held = gates >= 0.0
+            ranks = jnp.where(
+                held, matrix_product(held.astype(F32).astype(BF16), before), -1.0
+            )
             up_copy(block).wait()
 
             def keep_dots(source, values):
@@ -1176,8 +1259,8 @@
                 tile,
                 rows.at[block],
                 up_rows,
-                rank_ref[block],
-                weight_ref[block],
+                ranks,
+                gates,
                 keep_dots,
                 lambda: y_copy(block).start(),
                 mask_ref,
@@ -1272,9 +1355,13 @@
         def _(d):
             back_copy(block, d).wait_send()
             dots_copy(block, d).wait_send()
-
-
-def moe_layer(own, up_rows, plane_ranks, ranks, weights, mask, tables, identity):
+            weight_copy(block, d).wait_send()
+
+    for step in range(1, line):
+        line_weight_copy(place_of(step), at_line).wait_send()
+
+
+def moe_layer(own, up_rows, plane_ranks, weights, mask, tables, identity):
     line, plane, tokens = plane_ranks.shape
     slots, width = up_rows.shape[2:]
     hidden = tables[0].shape[1]
@@ -1284,7 +1371,7 @@
     grouped = (plane, slots, width)
     dma = pltpu.SemaphoreType.DMA
     return pl.pallas_call(
-        functools.partial(moe_body, plane, line),
+        staged(functools.partial(moe_body, plane, line), 2, 3),
         out_shape=[
             jax.ShapeDtypeStruct((tokens, width), F32),
             jax.ShapeDtypeStruct((line, plane, tokens), F32),
@@ -1292,7 +1379,7 @@
             jax.ShapeDtypeStruct((line,) + grouped, BF16),
         ]
         + sums,
-        in_specs=[anywhere, anywhere, local, local, local, local] + [anywhere] * len(tables),
+        in_specs=[anywhere] * (5 + len(tables)),
         out_specs=[local, local, anywhere, anywhere] + [local] * len(sums),
         scratch_shapes=[pltpu.VMEM(table.shape, table.dtype) for table in tables]
         + [
@@ -1308,6 +1395,9 @@
             pltpu.VMEM((line, plane, 8, tokens), F32),
             pltpu.VMEM((line, plane, tokens), F32),
             pltpu.VMEM((line, plane, tokens), F32),
+            pltpu.VMEM((line, plane, tokens), F32),
+            pltpu.VMEM((line, plane, 8, tokens), F32),
+            pltpu.VMEM((line, plane, 8, tokens), F32),
         ]
         + expert_scratch(plane * slots, hidden, width)
         + [dma((len(tables),)), dma, dma, dma, dma((3,))]
@@ -1315,12 +1405,14 @@
         + [dma((line, plane))] * 4
         + [dma((line,))] * 2
         + [dma((line, plane))] * 2
-        + [dma((line,))] * 2,
+        + [dma((line,))] * 4
+        + [dma((line, plane))] * 2
+        + staging([plane_ranks, weights, mask]),
         compiler_params=pltpu.CompilerParams(
             collective_id=identity, has_side_effects=True, vmem_limit_bytes=63 * MEBI
         ),
         name="moe_layer",
-    )(own, up_rows, plane_ranks, ranks, weights, mask, *tables)
+    )(own, up_rows, plane_ranks, weights, mask, *tables)
 
 
 def greet_line(me, count):
@@ -1416,6 +1508,7 @@
     line,
     scale,
     places,
+    ready,
     tokens_hbm,
     cotangent_hbm,
     routes_hbm,
@@ -1543,6 +1636,8 @@
     for each in locals_in:
         each.wait()
 
+    ready()
+
     for block in range(line):
         named = [
             jnp.max(
@@ -1786,7 +1881,9 @@
         before,
     ]
     return pl.pallas_call(
-        functools.partial(front_body, plane, line, scale, places),
+        staged(
+            functools.partial(front_body, plane, line, scale, places), 4, len(operands)
+        ),
         out_shape=[
             jax.ShapeDtypeStruct((count, width), F32),
             jax.ShapeDtypeStruct((line, plane, count), F32),
@@ -1798,7 +1895,7 @@
             jax.ShapeDtypeStruct((plane,) + packed.shape, BF16),
             jax.ShapeDtypeStruct(up_shape, BF16),
         ],
-        in_specs=[anywhere] * 4 + [local] * len(operands),
+        in_specs=[anywhere] * (4 + len(operands)),
         out_specs=[local] * 4 + [anywhere] * 5,
         scratch_shapes=[
             pltpu.VMEM((line, count, width), BF16),
@@ -1820,7 +1917,8 @@
         + [dma((line - 1, 9))] * 4
         + [dma((plane // 2,))] * 4
         + [dma((line - 1, 4))] * 4
-        + [dma((line, plane))] * 2,
+        + [dma((line, plane))] * 2
+        + staging(operands),
         compiler_params=pltpu.CompilerParams(
             collective_id=identity, has_side_effects=True, vmem_limit_bytes=63 * MEBI
         ),
@@ -1839,7 +1937,6 @@
     residual_ref,
     cotangent_ref,
     moe_gain_ref,
-    router_ref,
     router_first_ref,
     router_second_ref,
     router_low_ref,
@@ -1867,14 +1964,12 @@
     residual_grad_ref,
     share_ref,
     linear_grad_ref,
-    rows_out_ref,
-    heads_out_ref,
-    narrow_out_ref,
-    router_out_ref,
+    owned_ref,
     y_in_hbm,
     branch_own,
     branch,
     out_weights,
+    router_weights,
     linear,
     heads,
     normed,
@@ -1893,6 +1988,10 @@
     right_buf,
     result,
     choice,
+    rows_out_ref,
+    heads_out_ref,
+    narrow_out_ref,
+    router_out_ref,
     load_sem,
     y_sem,
     relay_right_send,
@@ -1963,6 +2062,10 @@
         pltpu.make_async_copy(source, target, load_sem.at[at])
         for at, (source, target) in enumerate(
             [
+                (
+                    gathered_hbm.at[:, :, pl.ds(places[0], places[1] - places[0])],
+                    router_weights,
+                ),
                 (gathered_hbm.at[:, :, pl.ds(places[1], query_columns)], out_weights),
                 (linear_hbm, linear),
                 (heads_hbm, heads),
@@ -1998,10 +2101,25 @@
         if step > 0:
             advance_sum(step)
 
+    loads[0].wait()
+    router_ref = router_weights[...].reshape(width, -1)
     gates = gates_ref[...]
     dots = dots_ref[...]
     logit_grad = (gates * (dots - jnp.sum(gates * dots, axis=0, keepdims=True))).astype(BF16)
-    router_low_grad = matrix_product(router_second_ref[...], logit_grad).astype(BF16)
+    experts_count, lanes = gates.shape[0], router_ref.shape[1]
+    wide_logit_grad = jnp.transpose(
+        jnp.concatenate(
+            [
+                logit_grad.astype(F32),
+                jnp.zeros((lanes - experts_count, tokens), F32),
+            ],
+            axis=0,
+        ),
+        (1, 0),
+    ).astype(BF16)
+    router_low_grad = matrix_product(
+        router_second_ref[:, :experts_count], logit_grad
+    ).astype(BF16)
     rows_out_ref[4 * rank :, :] = matrix_product(router_low_grad, moe_rows_ref[...]).astype(BF16)
     router_out_ref[...] = flipped_right_operand(router_low_ref[...], logit_grad)
     half = tokens // 2
@@ -2010,7 +2128,7 @@
         columns = slice(part * half, (part + 1) * half)
         moe_grad = (
             moe_total_ref[rows, :]
-            + flipped_left_operand(logit_grad[:, columns], router_ref[...])
+            + flipped_right_operand(wide_logit_grad[columns], router_ref)
             + flipped_left_operand(router_low_grad[:, columns], router_first_ref[...])
         )
         residual = residual_ref[rows, :]
@@ -2034,7 +2152,7 @@
     )
     advance(0, (0,))
     second_sum[...] = jnp.zeros_like(second_sum)
-    loads[0].wait()
+    loads[1].wait()
 
     def head_gradients(block):
         at = pl.ds(pl.multiple_of(block * tokens, tokens), tokens)
@@ -2051,7 +2169,7 @@
         tiles(query_columns, tile, project)
 
     head_gradients(at_line)
-    for each in loads[1:]:
+    for each in loads[2:]:
         each.wait()
     cosine, sine = cos_ref[...], sin_ref[...]
     key_columns = slice(query_columns, query_columns + head_dim)
@@ -2156,6 +2274,23 @@
         ).astype(BF16)
 
     tiles(width, 2 * tile, first_gradient)
+
+    pieces, lines, lanes_out = owned_ref.shape
+    row_lines, span = rows_out_ref.shape[0], width // pieces
+    owned_ref[...] = jnp.zeros_like(owned_ref)
+    for piece in range(pieces):
+        owned_ref[piece, :row_lines, :span] = rows_out_ref[:, piece * span : (piece + 1) * span]
+        at = (piece % line) * plane + piece // line
+        owned_ref[piece, :rank, span : span + 1] = router_out_ref[:, at : at + 1].astype(BF16)
+    narrow_span = head_dim // plane
+    for piece in range(plane):
+        owner = at_line * plane + piece
+        owned_ref[owner, row_lines:, :] = heads_out_ref[
+            :, piece * lanes_out : (piece + 1) * lanes_out
+        ]
+        owned_ref[owner, : 2 * rank, span + rank : span + rank + narrow_span] = narrow_out_ref[
+            :, piece * narrow_span : (piece + 1) * narrow_span
+        ]
     combine(0)
     finish_sum()
     output_ref[...] = (residual_ref[...] + result[...]).astype(BF16)
@@ -2174,7 +2309,7 @@
     all_rows, linear_columns = linear.shape
     query_columns = heads.shape[1]
     head_dim = (linear_columns - query_columns) // 2
-    rank = operands[13].shape[1]
+    rank = operands[12].shape[1]
     experts_count = line * plane
     anywhere = pl.BlockSpec(memory_space=pl.ANY)
     local = pl.BlockSpec(memory_space=pltpu.VMEM)
@@ -2188,18 +2323,16 @@
             jax.ShapeDtypeStruct(block, F32),
             jax.ShapeDtypeStruct((all_rows, 3 * rank), BF16),
             jax.ShapeDtypeStruct((all_rows, linear_columns), BF16),
-            jax.ShapeDtypeStruct((5 * rank, width), BF16),
-            jax.ShapeDtypeStruct((2 * rank, query_columns), BF16),
-            jax.ShapeDtypeStruct((2 * rank, head_dim), BF16),
-            jax.ShapeDtypeStruct((rank, experts_count), F32),
+            jax.ShapeDtypeStruct((experts_count, 7 * rank, head_dim), BF16),
             jax.ShapeDtypeStruct((line, plane, slots, width), BF16),
         ],
         in_specs=[local] * len(operands) + [anywhere] * len(hbm_operands),
-        out_specs=[local] * 8 + [anywhere],
+        out_specs=[local] * 5 + [anywhere],
         scratch_shapes=[
             pltpu.VMEM(block, BF16),
             pltpu.VMEM((line,) + block, BF16),
             pltpu.VMEM((plane, width // plane, query_columns), BF16),
+            pltpu.VMEM((plane, width // plane, places[1] - places[0]), BF16),
             pltpu.VMEM((all_rows, linear_columns), F32),
             pltpu.VMEM((all_rows, query_columns), BF16),
             pltpu.VMEM((all_rows, width), BF16),
@@ -2218,7 +2351,11 @@
             pltpu.VMEM((line - 1,) + block, BF16),
             pltpu.VMEM(block, F32),
             pltpu.VMEM((plane * slots, count), BF16),
-            dma((4,)),
+            pltpu.VMEM((5 * rank, width), BF16),
+            pltpu.VMEM((2 * rank, query_columns), BF16),
+            pltpu.VMEM((2 * rank, head_dim), BF16),
+            pltpu.VMEM((rank, experts_count), F32),
+            dma((5,)),
             dma((line + 1,)),
         ]
         + [dma((line - 1, 4))] * 4
@@ -2233,6 +2370,7 @@
 
 def last_body(
     line,
+    ready,
     linear_grad_ref,
     share_ref,
     first_ref,
@@ -2256,6 +2394,7 @@
     )
     load.start()
     greet_line(at_line, line)
+    ready()
     load.wait()
     shards, wide = weights.shape[:2]
 
@@ -2302,10 +2441,11 @@
     anywhere = pl.BlockSpec(memory_space=pl.ANY)
     local = pl.BlockSpec(memory_space=pltpu.VMEM)
     dma = pltpu.SemaphoreType.DMA
+    operands = [linear_grad, share, first, residual_grad, tokens, gain]
     return pl.pallas_call(
-        functools.partial(last_body, line),
+        staged(functools.partial(last_body, line), 0, 6),
         out_shape=jax.ShapeDtypeStruct((count, width), F32),
-        in_specs=[local] * 6 + [anywhere],
+        in_specs=[anywhere] * 7,
         out_specs=local,
         scratch_shapes=[
             pltpu.VMEM(gathered.shape[:2] + (linear_grad.shape[1],), BF16),
@@ -2314,12 +2454,236 @@
             pltpu.VMEM((line - 1, count, width), BF16),
             dma,
         ]
-        + [dma((line - 1, 4))] * 4,
+        + [dma((line - 1, 4))] * 4
+        + staging(operands),
         compiler_params=pltpu.CompilerParams(
-            collective_id=identity, has_side_effects=True, vmem_limit_bytes=48 * MEBI
+            collective_id=identity, has_side_effects=True, vmem_limit_bytes=63 * MEBI
         ),
         name="last",
-    )(linear_grad, share, first, residual_grad, tokens, gain, gathered)
+    )(*operands, gathered)
+
+
+def prepare_body(
+    _adapters_ref,
+    _place_ref,
+    query_in_ref,
+    key_in_ref,
+    value_in_ref,
+    query_out_ref,
+    key_out_ref,
+    value_out_ref,
+    attn_in_ref,
+    attn_out_ref,
+    router_in_ref,
+    router_out_ref,
+    w_query_ref,
+    w_key_ref,
+    w_value_ref,
+    w_router_ref,
+    w_out_ref,
+    order_ref,
+    segments_ref,
+    first_ref,
+    q_second_ref,
+    k_second_ref,
+    v_second_ref,
+    out_first_ref,
+    out_second_ref,
+    router_first_ref,
+    router_second_ref,
+    packed_ref,
+    seg_column_ref,
+):
+    rank = query_in_ref.shape[1]
+    for at, ref in enumerate((query_in_ref, key_in_ref, value_in_ref)):
+        first_ref[at * rank : (at + 1) * rank, :] = ref[0]
+    q_second_ref[...] = query_out_ref[0]
+    k_second_ref[...] = key_out_ref[0]
+    v_second_ref[...] = value_out_ref[0]
+    out_first_ref[...] = attn_in_ref[0]
+    out_second_ref[...] = attn_out_ref[0]
+    router_first_ref[...] = router_in_ref[0]
+    router_second_ref[...] = matrix_product(router_out_ref[0], order_ref[...]).astype(BF16)
+    start = 0
+    for ref in (w_query_ref, w_key_ref, w_value_ref):
+        width = ref.shape[1]
+        packed_ref[:, start : start + width] = ref[...]
+        start += width
+    width = order_ref.shape[1]
+    packed_ref[:, start : start + width] = flipped_left_operand(
+        w_router_ref[...], order_ref[...]
+    ).astype(BF16)
+    start += width
+    for at in range(0, w_out_ref.shape[0], 256):
+        packed_ref[:, start + at : start + at + 256] = jnp.transpose(
+            w_out_ref[at : at + 256, :], (1, 0)
+        )
+    marks = jnp.broadcast_to(segments_ref[...].astype(F32), (8, segments_ref.shape[1]))
+    seg_column_ref[...] = jnp.transpose(marks, (1, 0))[:, :1].astype(jnp.int32)
+
+
+def prepare(adapters, place, tables, weights, order, segments):
+    def chosen(table):
+        return pl.BlockSpec(
+            (1,) + table.shape[1:], lambda _, adapter, at: (adapter[at[0]], 0, 0)
+        )
+
+    def resident(shape):
+        return pl.BlockSpec(tuple(shape), lambda *_: (0,) * len(shape))
+
+    rank = tables[0].shape[1]
+    columns = sum(w.shape[1] for w in weights[:3]) + order.shape[1] + weights[4].shape[0]
+    shapes = [
+        ((3 * rank, tables[0].shape[2]), BF16),
+        (tables[3].shape[1:], BF16),
+        (tables[4].shape[1:], BF16),
+        (tables[5].shape[1:], BF16),
+        (tables[6].shape[1:], BF16),
+        (tables[7].shape[1:], BF16),
+        (tables[8].shape[1:], BF16),
+        ((rank, order.shape[1]), BF16),
+        ((weights[0].shape[0], columns), BF16),
+        ((segments.shape[1], 1), jnp.int32),
+    ]
+    return pl.pallas_call(
+        prepare_body,
+        grid_spec=pltpu.PrefetchScalarGridSpec(
+            num_scalar_prefetch=2,
+            grid=(1,),
+            in_specs=[chosen(table) for table in tables]
+            + [resident(w.shape) for w in weights]
+            + [resident(order.shape), resident(segments.shape)],
+            out_specs=[resident(shape) for shape, _ in shapes],
+        ),
+        out_shape=[jax.ShapeDtypeStruct(shape, dtype) for shape, dtype in shapes],
+        compiler_params=params(63),
+        name="prepare",
+    )(adapters, place, *tables, *weights, order, segments)
+
+
+def router_body(
+    line,
+    total_ref,
+    tokens_ref,
+    gain_ref,
+    weights_ref,
+    first_ref,
+    second_ref,
+    routes_ref,
+    residual_ref,
+    rows_ref,
+    gates_ref,
+    sent_ref,
+    low_ref,
+):
+    count, width = tokens_ref.shape
+    residual = total_ref[...] + tokens_ref[...].astype(F32)
+    residual_ref[...] = residual
+    rows_ref[...] = norm_forward(residual, gain_ref[...])[0].astype(BF16)
+    low_ref[...] = flipped_right_operand(first_ref[...], rows_ref[...]).astype(BF16)
+    logits = matrix_product(rows_ref[...], weights_ref[...].reshape(width, -1))
+    logits = jnp.transpose(logits, (1, 0)) + flipped_left_operand(second_ref[...], low_ref[...])
+    experts_count = gates_ref.shape[0]
+    plane = experts_count // line
+    logits = logits[:experts_count]
+    at = lax.broadcasted_iota(jnp.int32, (experts_count, count), 0)
+    names = (at % plane) * line + at // plane
+    chosen = jnp.zeros((experts_count, count), jnp.bool_)
+    for k in range(routes_ref.shape[0]):
+        chosen = chosen | (names == routes_ref[k : k + 1, :])
+    peak = jnp.max(jnp.where(chosen, logits, -jnp.inf), axis=0, keepdims=True)
+    expo = jnp.where(chosen, jnp.exp(jnp.where(chosen, logits - peak, 0.0)), 0.0)
+    gates = expo / jnp.sum(expo, axis=0, keepdims=True)
+    gates_ref[...] = gates
+    sent = jnp.where(chosen, gates, -1.0)
+    for group in range(line):
+        sent_ref[group] = sent[group * plane : (group + 1) * plane]
+
+
+def router(total, tokens, gain, gathered, column, first, second, routes):
+    line, plane = lax.axis_size("tensor"), lax.axis_size("fsdp")
+    count, width = tokens.shape
+    lanes = second.shape[1]
+
+    def resident(shape):
+        return pl.BlockSpec(tuple(shape), lambda *_: (0,) * len(shape))
+
+    shapes = [
+        ((count, width), F32),
+        ((count, width), BF16),
+        ((line * plane, count), F32),
+        ((line, plane, count), F32),
+        ((first.shape[0], count), BF16),
+    ]
+    return pl.pallas_call(
+        functools.partial(router_body, line),
+        grid=(1,),
+        in_specs=[
+            resident(total.shape),
+            resident(tokens.shape),
+            resident(gain.shape),
+            pl.BlockSpec(gathered.shape[:2] + (lanes,), lambda _: (0, 0, column // lanes)),
+            resident(first.shape),
+            resident(second.shape),
+            resident(routes.shape),
+        ],
+        out_specs=[resident(shape) for shape, _ in shapes],
+        out_shape=[jax.ShapeDtypeStruct(shape, dtype) for shape, dtype in shapes],
+        compiler_params=params(63),
+        name="router",
+    )(total, tokens, gain, gathered, first, second, routes)
+
+
+def owners_body(spans, adapters_ref, pieces_ref, *refs):
+    outs, total = refs[:-1], refs[-1]
+    span, narrow_span = spans
+    sources = adapters_ref.shape[0]
+    group = pieces_ref.shape[0] // sources
+    rank = outs[0].shape[1]
+    total[...] = jnp.zeros_like(total)
+
+    @pl.loop(0, sources)
+    def _(source):
+        addend = pieces_ref[source * group].astype(F32)
+        for at in range(1, group):
+            addend = addend + pieces_ref[source * group + at].astype(F32)
+        total[adapters_ref[source]] += addend
+
+    for at in range(5):
+        outs[at][...] = total[:, at * rank : (at + 1) * rank, :span]
+    outs[5][...] = total[:, :rank, span : span + 1]
+    outs[6][...] = total[:, 5 * rank : 6 * rank, :]
+    outs[7][...] = total[:, 6 * rank :, :]
+    columns = slice(span + rank, span + rank + narrow_span)
+    outs[8][...] = total[:, :rank, columns]
+    outs[9][...] = total[:, rank : 2 * rank, columns]
+
+
+def owners(adapters, pieces, adapter_count, rank, span, narrow_span):
+    lanes = pieces.shape[2]
+    shapes = (
+        [(adapter_count, rank, span)] * 5
+        + [(adapter_count, rank, 1)]
+        + [(adapter_count, rank, lanes)] * 2
+        + [(adapter_count, rank, narrow_span)] * 2
+    )
+
+    def resident(shape):
+        return pl.BlockSpec(tuple(shape), lambda *_: (0,) * len(shape))
+
+    return pl.pallas_call(
+        functools.partial(owners_body, (span, narrow_span)),
+        grid_spec=pltpu.PrefetchScalarGridSpec(
+            num_scalar_prefetch=1,
+            grid=(1,),
+            in_specs=[resident(pieces.shape)],
+            out_specs=[resident(shape) for shape in shapes],
+            scratch_shapes=[pltpu.VMEM((adapter_count,) + pieces.shape[1:], F32)],
+        ),
+        out_shape=[jax.ShapeDtypeStruct(shape, F32) for shape in shapes],
+        compiler_params=params(63),
+        name="owners",
+    )(adapters, pieces)
 
 
 def per_device(
@@ -2383,16 +2747,6 @@
     def transposed(adapter_table):
         return jnp.swapaxes(adapter_table, -1, -2)
 
-    input_first = jnp.concatenate(
-        [select_adapter(transposed(table)) for table in (query_in, key_in, value_in)], axis=0
-    )
-    q_second = select_adapter(query_out)
-    k_second = select_adapter(key_second_weight)
-    v_second = select_adapter(value_second_weight)
-    attention_first = select_adapter(transposed(attn_in))
-    attention_second = select_adapter(attn_out)
-    router_first = select_adapter(transposed(router_in))
-    router_second = select_adapter(router_out)
     gain_attn = attn_gain.astype(F32)
     gain_moe = moe_gain.astype(F32)
     gain_query = q_gain.astype(F32)[None, :]
@@ -2402,19 +2756,73 @@
     linear_cols = local_cols + 2 * local_kv_cols
     router_pad = -(-expert_count // 128) * 128
     out_start = linear_cols + router_pad
-    packed = jnp.concatenate(
-        [
-            w_query,
-            key_projection_weight,
-            value_projection_weight,
-            jnp.pad(w_router, ((0, 0), (0, router_pad - expert_count))),
-            jnp.transpose(w_out, (1, 0)),
-        ],
-        axis=1,
-    )
     tables = rope_tables(seq_rows, head_dim)
     seg_row = segments
-    seg_column = jnp.transpose(segments, (1, 0))
+    routes_t = jnp.transpose(routes, (1, 0))
+    if in_kernel:
+        expert_order = np.zeros((expert_count, router_pad), np.float32)
+        places = np.arange(expert_count)
+        expert_order[
+            (places % fsdp_count) * tensor_count + places // fsdp_count, places
+        ] = 1.0
+        (
+            input_first,
+            q_second,
+            k_second,
+            v_second,
+            attention_first,
+            attention_second,
+            router_first,
+            router_second,
+            packed,
+            seg_column,
+        ) = prepare(
+            adapter_index,
+            fsdp_pos[None],
+            [
+                transposed(query_in),
+                transposed(key_in),
+                transposed(value_in),
+                query_out,
+                key_second_weight,
+                value_second_weight,
+                transposed(attn_in),
+                attn_out,
+                transposed(router_in),
+                router_out,
+            ],
+            [
+                w_query,
+                key_projection_weight,
+                value_projection_weight,
+                jnp.transpose(w_router, (1, 0)),
+                w_out,
+            ],
+            jnp.asarray(expert_order, BF16),
+            segments,
+        )
+    else:
+        input_first = jnp.concatenate(
+            [select_adapter(transposed(table)) for table in (query_in, key_in, value_in)], axis=0
+        )
+        q_second = select_adapter(query_out)
+        k_second = select_adapter(key_second_weight)
+        v_second = select_adapter(value_second_weight)
+        attention_first = select_adapter(transposed(attn_in))
+        attention_second = select_adapter(attn_out)
+        router_first = select_adapter(transposed(router_in))
+        router_second = select_adapter(router_out)
+        packed = jnp.concatenate(
+            [
+                w_query,
+                key_projection_weight,
+                value_projection_weight,
+                jnp.pad(w_router, ((0, 0), (0, router_pad - expert_count))),
+                jnp.transpose(w_out, (1, 0)),
+            ],
+            axis=1,
+        )
+        seg_column = jnp.transpose(segments, (1, 0))
     token_values = tokens.astype(F32)
     attn_normed, attn_factor = norm_forward(token_values, gain_attn)
     offsets = [0] + [sign * step for step in range(1, tensor_count) for sign in (1, -1)]
@@ -2453,7 +2861,7 @@
         ) = front(
             tokens,
             cotangent,
-            jnp.transpose(routes, (1, 0)),
+            routes_t,
             packed,
             gain_attn[None, :],
             input_first,
@@ -2473,8 +2881,6 @@
             0,
         )
         sequence_normalized = sequence_normalized.reshape(seq_rows, model_width)
-        gathered_blocks = gathered
-        gathered = gathered.reshape(model_width, -1)
     else:
         gathered = lax.all_gather(packed, "fsdp", axis=0, tiled=True)
         sequence_tokens, sequence_routes = gather_line(
@@ -2493,9 +2899,9 @@
         )
         linear = matrix_product(sequence_normalized, gathered[:, :linear_cols])
         low = flipped_right_operand(sequence_normalized, input_first).astype(BF16)
-    complete_linear = gathered[:, :linear_cols]
-    complete_router = gathered[:, linear_cols : linear_cols + expert_count]
-    full_out_t = gathered[:, out_start:]
+        complete_linear = gathered[:, :linear_cols]
+        complete_router = gathered[:, linear_cols : linear_cols + expert_count]
+        full_out_t = gathered[:, out_start:]
     attention_operands = (
         linear,
         low,
@@ -2518,24 +2924,36 @@
         attention_total = sum_line(
             out_part.astype(BF16).reshape(tensor_count, tok_rows, model_width), 4, 1
         )
-    residual_stream = token_values + attention_total
-    moe_normed, moe_factor = norm_forward(residual_stream, gain_moe)
-    experts_narrow = moe_normed.astype(BF16)
-
-    router_low = flipped_right_operand(experts_narrow, router_first).astype(BF16)
-    router_logits = matrix_product(experts_narrow, complete_router) + matrix_product(
-        router_low, router_second
-    )
-    expert_ids = jnp.arange(expert_count, dtype=jnp.int32)
-    chosen = jnp.any(routes[:, :, None] == expert_ids[None, None, :], axis=1)
-    chosen_logits = jnp.where(chosen, router_logits, -jnp.inf)
-    chosen_exp = jnp.exp(chosen_logits - jnp.max(chosen_logits, axis=-1, keepdims=True))
-    gate_weights = chosen_exp / jnp.sum(chosen_exp, axis=-1, keepdims=True)
-    sent_weights = jnp.transpose(jnp.where(chosen, gate_weights, -1.0), (1, 0))
-    own_weights = jnp.transpose(
-        route_rows(sent_weights).reshape(fsdp_count, tensor_count, tok_rows), (1, 0, 2)
-    )
-    own_ranks = ranks_of(own_weights >= 0.0)
+    if in_kernel:
+        residual_stream, experts_narrow, gate_weights, sent_weights, router_low = router(
+            attention_total,
+            tokens,
+            gain_moe[None, :],
+            gathered,
+            linear_cols,
+            router_first,
+            router_second,
+            routes_t,
+        )
+    else:
+        residual_stream = token_values + attention_total
+        moe_normed, moe_factor = norm_forward(residual_stream, gain_moe)
+        experts_narrow = moe_normed.astype(BF16)
+
+        router_low = flipped_right_operand(experts_narrow, router_first).astype(BF16)
+        router_logits = matrix_product(experts_narrow, complete_router) + matrix_product(
+            router_low, router_second
+        )
+        expert_ids = jnp.arange(expert_count, dtype=jnp.int32)
+        chosen = jnp.any(routes[:, :, None] == expert_ids[None, None, :], axis=1)
+        chosen_logits = jnp.where(chosen, router_logits, -jnp.inf)
+        chosen_exp = jnp.exp(chosen_logits - jnp.max(chosen_logits, axis=-1, keepdims=True))
+        gate_weights = chosen_exp / jnp.sum(chosen_exp, axis=-1, keepdims=True)
+        sent_weights = jnp.transpose(jnp.where(chosen, gate_weights, -1.0), (1, 0))
+        own_weights = jnp.transpose(
+            route_rows(sent_weights).reshape(fsdp_count, tensor_count, tok_rows), (1, 0, 2)
+        )
+        own_ranks = ranks_of(own_weights >= 0.0)
 
     broad = adapter_count * rank
     gate_in_t, upward_in_t = transposed(gate_in[0]), transposed(upward_in[0])
@@ -2562,8 +2980,7 @@
             experts_narrow,
             up_rows,
             plane_ranks,
-            own_ranks,
-            own_weights,
+            sent_weights,
             adapter_mask,
             expert_tables,
             3,
@@ -2584,38 +3001,29 @@
         gate_dots = jnp.roll(jnp.stack(ordered), tensor_pos, axis=0)
     pair_in_grad, gate_out_grad, upward_out_grad, downward_in_grad, downward_out_grad = sums
     if in_kernel:
-
-        def by_line(table):
-            lines = table.reshape(fsdp_count, tensor_count, -1)
-            return jnp.transpose(lines, (1, 0, 2)).reshape(expert_count, -1)
-
         (
             output,
             residual_grad,
             low_share,
             linear_grad,
-            row_grads,
-            head_grads,
-            narrow_grads,
-            router_grads,
+            owned,
             _landed,
         ) = back(
             score_scale,
             (linear_cols, out_start),
             slots,
             4,
-            (linear, heads_narrow, sequence_normalized, gathered_blocks, expert_output),
+            (linear, heads_narrow, sequence_normalized, gathered, expert_output),
             (
                 moe_grad,
                 gate_dots.reshape(expert_count, tok_rows),
-                by_line(jnp.transpose(gate_weights, (1, 0))),
+                gate_weights,
                 residual_stream,
                 cotangent,
                 gain_moe[None, :],
-                by_line(jnp.transpose(complete_router, (1, 0))),
                 router_first,
-                jnp.transpose(by_line(jnp.transpose(router_second, (1, 0))), (1, 0)),
-                jnp.transpose(router_low, (1, 0)),
+                router_second,
+                router_low,
                 experts_narrow,
                 plane_ranks,
                 low,
@@ -2632,9 +3040,7 @@
                 seg_row,
             ),
         )
-        router_second_gradient = jnp.transpose(
-            router_grads.reshape(rank, tensor_count, fsdp_count), (0, 2, 1)
-        ).reshape(rank, expert_count)
+        owned = route_rows(owned)
         input_grad = last(
             linear_grad,
             low_share,
@@ -2642,7 +3048,7 @@
             residual_grad,
             tokens,
             gain_attn[None, :],
-            gathered_blocks,
+            gathered,
             5,
         )
     else:
@@ -2712,67 +3118,89 @@
         head_grads = jnp.concatenate([q_second_gradient, attention_first_gradient], axis=0)
         narrow_grads = jnp.concatenate([k_second_gradient, v_second_gradient], axis=0)
 
-    source_adapter = jnp.repeat(adapter_index, tensor_count)
-    owner_onehot = (
-        jnp.arange(adapter_count, dtype=jnp.int32)[:, None] == source_adapter[None, :]
-    ).astype(BF16)
-
-    def to_all(addend):
-        lines = addend.shape[0]
-        return jnp.transpose(
-            addend.astype(BF16).reshape(lines, device_count, -1), (1, 0, 2)
-        ).reshape(device_count, -1)
-
-    def to_head_owners(addend):
-        lines = addend.shape[0]
-        pieces = jnp.transpose(
-            addend.astype(BF16).reshape(lines, fsdp_count, -1), (1, 0, 2)
-        ).reshape(fsdp_count, -1)
-        holder = jnp.zeros((device_count, pieces.shape[1]), BF16)
-        return lax.dynamic_update_slice(holder, pieces, (tensor_pos * fsdp_count, zero_pos))
-
-    def owner_sums(parts):
-        widths = [part.shape[1] for part in parts]
-        total = matrix_product(owner_onehot, route_rows(jnp.concatenate(parts, axis=1)))
-        pieces = []
-        start = 0
-        for width in widths:
-            pieces.append(total[:, start : start + width])
-            start += width
-        return pieces
-
-    row_sums, head_sums, narrow_sums, router_sums = owner_sums(
-        [
-            to_all(row_grads),
-            to_head_owners(head_grads),
-            to_head_owners(narrow_grads),
-            to_all(router_second_gradient),
-        ]
-    )
-
     def lines_of(piece, lines):
         return piece.reshape(adapter_count, lines, -1)
 
-    row_sums = lines_of(row_sums, 5 * rank)
-    head_sums = lines_of(head_sums, 2 * rank)
-    narrow_sums = lines_of(narrow_sums, 2 * rank)
-
-    def factor_rows(at):
-        return row_sums[:, at * rank : (at + 1) * rank]
-
+    if in_kernel:
+        (
+            query_in_sum,
+            key_in_sum,
+            value_in_sum,
+            attn_out_sum,
+            router_in_sum,
+            router_out_sum,
+            query_out_sum,
+            attn_in_sum,
+            key_out_sum,
+            value_out_sum,
+        ) = owners(
+            adapter_index,
+            owned,
+            adapter_count,
+            rank,
+            model_width // device_count,
+            local_kv_cols // fsdp_count,
+        )
+    else:
+        source_adapter = jnp.repeat(adapter_index, tensor_count)
+        owner_onehot = (
+            jnp.arange(adapter_count, dtype=jnp.int32)[:, None] == source_adapter[None, :]
+        ).astype(BF16)
+
+        def to_all(addend):
+            lines = addend.shape[0]
+            return jnp.transpose(
+                addend.astype(BF16).reshape(lines, device_count, -1), (1, 0, 2)
+            ).reshape(device_count, -1)
+
+        def to_head_owners(addend):
+            lines = addend.shape[0]
+            pieces = jnp.transpose(
+                addend.astype(BF16).reshape(lines, fsdp_count, -1), (1, 0, 2)
+            ).reshape(fsdp_count, -1)
+            holder = jnp.zeros((device_count, pieces.shape[1]), BF16)
+            return lax.dynamic_update_slice(holder, pieces, (tensor_pos * fsdp_count, zero_pos))
+
+        def owner_sums(parts):
+            widths = [part.shape[1] for part in parts]
+            total = matrix_product(owner_onehot, route_rows(jnp.concatenate(parts, axis=1)))
+            pieces = []
+            start = 0
+            for width in widths:
+                pieces.append(total[:, start : start + width])
+                start += width
+            return pieces
+
+        row_sums, head_sums, narrow_sums, router_sums = owner_sums(
+            [
+                to_all(row_grads),
+                to_head_owners(head_grads),
+                to_head_owners(narrow_grads),
+                to_all(router_second_gradient),
+            ]
+        )
+        row_sums = lines_of(row_sums, 5 * rank)
+        head_sums = lines_of(head_sums, 2 * rank)
+        narrow_sums = lines_of(narrow_sums, 2 * rank)
+        query_in_sum, key_in_sum, value_in_sum, attn_out_sum, router_in_sum = [
+            row_sums[:, at * rank : (at + 1) * rank] for at in range(5)
+        ]
+        query_out_sum, attn_in_sum = head_sums[:, :rank], head_sums[:, rank:]
+        key_out_sum, value_out_sum = narrow_sums[:, :rank], narrow_sums[:, rank:]
+        router_out_sum = lines_of(router_sums, rank)
     return (
         output,
         input_grad,
-        transposed(factor_rows(0)),
-        head_sums[:, :rank],
-        transposed(factor_rows(1)),
-        narrow_sums[:, :rank],
-        transposed(factor_rows(2)),
-        narrow_sums[:, rank:],
-        transposed(head_sums[:, rank:]),
-        factor_rows(3),
-        transposed(factor_rows(4)),
-        lines_of(router_sums, rank),
+        transposed(query_in_sum),
+        query_out_sum,
+        transposed(key_in_sum),
+        key_out_sum,
+        transposed(value_in_sum),
+        value_out_sum,
+        transposed(attn_in_sum),
+        attn_out_sum,
+        transposed(router_in_sum),
+        router_out_sum,
         transposed(lines_of(pair_in_grad[:broad], rank))[None],
         lines_of(gate_out_grad, rank)[None],
         transposed(lines_of(pair_in_grad[broad:], rank))[None],

time: 770 us -> 742 us (0.964)
  local copies, waits for them, and re-layouts: 41.2 us -> 13.2 us
  Pallas kernels: 691 us -> 709 us
    pallas_call x3 -> x6, Pallas kernels: 544 us -> 562 us  [the longest x1 259 us: moe_layer(): pl.pallas_call(staged(functools.partial(moe_body, plane, line), 2, 3), ou...]
    unnamed x89 -> x19, local copies, waits for them, and re-layouts: 18.7 us -> 9.47 us
  transfers between devices with their start and end apart: 2 -> 1, of which waited for: 1 -> 0; matrix products, arithmetic and copies ran while one was open for 1% -> 0% of each run, Pallas kernels for 11% -> 12%
where the time goes in v7:
time: 742 us; the launch traced here: 735 us
  Pallas kernels  709 us (96%)
  local copies, waits for them, and re-layouts  13.2 us (2%)
  other arithmetic  7.5 us (1%)
    pallas_call x1, Pallas kernels, moe_layer(): pl.pallas_call(staged(functools.partial(moe_body, plane, line), 2, 3), ou...  259 us
    pallas_call x1, Pallas kernels, front(): pl.pallas_call(staged(functools.partial(front_body, plane, line, scale, p...  205 us
    pallas_call x1, Pallas kernels, back(): pl.pallas_call(functools.partial(back_body, plane, line, scale, places),...  147 us
    pallas_call x1, Pallas kernels, last(): pl.pallas_call(staged(functools.partial(last_body, line), 0, 6), out_shap...  87.6 us
  transfers between devices with their start and end apart: 1, of which 0 were waited for; matrix products, arithmetic and copies ran while one was open for 0% of the time, Pallas kernels for 12%

profile of v7, /device:TPU:16, one launch (start us, length us, event | category | flops | bytes accessed | tf_op | source)
XLA Modules:
  0.0 735.2 jit_solution(8627650367436381731)
XLA Ops:
  0.7 0.7 fusion.refs_17_
  1.3 1.3 broadcast_in_dim.54
  2.6 1.3 broadcast_in_dim.57
  3.9 1.2 bitcast_convert_fusion
  5.2 0.7 compare_convert_fusion
  5.9 2.3 pad_maximum_fusion.refs_8_
  8.2 3.8 prepare.1
  12.0 204.6 %front.1 = (f32[256,2048]{1,0:T(8,128)}, f32[4,8,256]{2,1,0:T(8,128)}, bf16[1024,48]{1,0:T(8,128)(2,1)}, bf16[1024,16]{1,0:T(8,128)(2,1)}, f32[1024,1280]{1,0:T(...) custom-call(bf16[256,2048]{1,0:T(8,128)(2,1)} %refs_4_.1, ...), custom_call_target="tpu_custom_call" | custom-call | tf_op jit(solution)/shard_map/front/pallas_call | solution.py:1883
  216.6 4.1 router.1
  220.7 0.7 broadcast_in_dim.50
  221.4 258.8 %moe_layer.1 = (f32[256,2048]{1,0:T(8,128)}, f32[4,8,256]{2,1,0:T(8,128)}, bf16[8,4,80,2048]{3,2,1,0:T(8,128)(2,1)}, bf16[4,8,80,2048]{3,2,1,0:T(8,128)(2,1)}, f...) custom-call(bf16[256,2048]{1,0:T(8,128)(2,1)} %get-tuple-element.77., ...), custom_call_target="tpu_custom_call" | custom-call | tf_op jit(solution)/shard_map/moe_layer/pallas_call | solution.py:1373
  480.2 147.1 %back.1 = (bf16[256,2048]{1,0:T(8,128)(2,1)}, f32[256,2048]{1,0:T(8,128)}, bf16[1024,48]{1,0:T(8,128)(2,1)}, bf16[1024,1280]{1,0:T(8,128)(2,1)}, bf16[32,112,128...) custom-call(f32[256,2048]{1,0:T(8,128)} %get-tuple-element.81.moe_total_ref, f32[32,256]{1,0:T(8,128)} %bitcast.91, ...), custom_call_target="tpu_custom_call" | custom-call | tf_op jit(solution)/shard_map/back/pallas_call | solution.py:2319
  627.3 4.5 all-to-all-start
  631.8 87.6 %last.1 = f32[256,2048]{1,0:T(8,128)} custom-call(bf16[1024,1280]{1,0:T(8,128)(2,1)} %get-tuple-element.93.refs_0_, bf16[1024,48]{1,0:T(8,128)(2,1)} %get-tuple-element.94.refs_1_, bf16[48,2048]{1,0:T(8,128)(2,1)} %get-tuple-element.66.refs_5_.refs_2_, f32[256,2048]{1,0:T(8,128)} %get-tuple-element.95.refs_3_, bf16[256,2048]{1,0:T(8,128)(2,1)} %refs_4_.1, ...), custom_call_target="tpu_custom_call" | custom-call | tf_op jit(solution)/shard_map/last/pallas_call | solution.py:2445
  719.4 3.1 fusion.1
  722.4 0.0 all-to-all-done.pieces_ref
  722.5 0.0 copy-start.1
  722.5 0.9 copy-done.1
  723.4 2.9 owners.1
  726.2 0.0 copy-start
  726.2 1.7 copy.54
  727.9 2.3 copy.61
  730.2 0.0 copy-done
  730.2 0.0 copy-start.5
  730.2 0.0 copy-start.4
  730.2 0.0 copy-start.3
  730.3 1.3 copy.62
  731.6 0.0 copy-done.5
  731.6 0.0 copy-start.2
  731.6 0.7 copy.63
  732.3 0.0 copy-done.4
  732.3 0.7 copy.64
  733.1 0.0 copy-done.3
  733.1 0.7 copy.65
  733.8 0.0 copy-done.2
  733.8 1.0 copy.66
  (1 shorter events, 0.0 us)
Async XLA Ops:
  627.3 95.2 %all-to-all-start = ((bf16[32,112,128]{2,1,0:T(8,128)(2,1)}), bf16[32,112,128]{2,1,0:T(8,128)(2,1)S(1)}, u32[]{:S(2)}, u32[]{:S(2)}) async-start(bf16[32,112,128]{2,1,0:T(8,128)(2,1)} %get-tuple-element.96), calls=%async_computation | async-start | bytes 1835008 | tf_op jit(solution)/shard_map/all_to_all | solution.py:66
  722.5 0.9 copy-start.1
  726.2 4.0 copy-start
  730.2 1.3 copy-start.5
  730.2 2.1 copy-start.4
  730.2 2.8 copy-start.3
  731.6 2.2 copy-start.2

commit v8 on v7

--- a/solution.py
+++ b/solution.py
@@ -1779,8 +1779,7 @@
 
     out_low_ref[...] = flipped_right_operand(heads[...], out_first_ref[...]).astype(BF16)
 
-    @pl.loop(0, line)
-    def _(block):
+    def output_part(block):
         at = pl.ds(pl.multiple_of(block * tokens, tokens), tokens)
 
         @pl.loop(0, plane)
@@ -1803,10 +1802,20 @@
         (sum_right_send, sum_right_recv, sum_left_send, sum_left_recv),
     )
     for far in range(line - 1, 0, -1):
+
+        @pl.when(at_line + far < line)
+        def _():
+            output_part(at_line + far)
+
+        @pl.when(at_line - far >= 0)
+        def _():
+            output_part(at_line - far)
+
         advance_sum(far)
         if far == 2:
             advance(3, (2,))
             dispatch_at(3)
+    output_part(at_line)
     finish_sum()
 
     for block in range(line):

time: 742 us -> 735 us (level)
  Pallas kernels: 709 us -> 701 us
    pallas_call x1, Pallas kernels: 205 us -> 197 us  [front(): pl.pallas_call(staged(functools.partial(front_body, plane, line, scale, p...]
where the time goes in v8:
time: 735 us; the launch traced here: 727 us
  Pallas kernels  701 us (95%)
  local copies, waits for them, and re-layouts  13.2 us (2%)
  other arithmetic  7.5 us (1%)
    pallas_call x1, Pallas kernels, moe_layer(): pl.pallas_call(staged(functools.partial(moe_body, plane, line), 2, 3), ou...  259 us
    pallas_call x1, Pallas kernels, front(): pl.pallas_call(staged(functools.partial(front_body, plane, line, scale, p...  197 us
    pallas_call x1, Pallas kernels, back(): pl.pallas_call(functools.partial(back_body, plane, line, scale, places),...  147 us
    pallas_call x1, Pallas kernels, last(): pl.pallas_call(staged(functools.partial(last_body, line), 0, 6), out_shap...  87.6 us
  transfers between devices with their start and end apart: 1, of which 0 were waited for; matrix products, arithmetic and copies ran while one was open for 0% of the time, Pallas kernels for 12%

profile of v8, /device:TPU:16, one launch (start us, length us, event | category | flops | bytes accessed | tf_op | source)
XLA Modules:
  0.0 727.2 jit_solution(9313398417808255646)
XLA Ops:
  0.7 0.7 fusion.refs_17_
  1.3 1.3 broadcast_in_dim.54
  2.6 1.3 broadcast_in_dim.57
  3.9 1.2 bitcast_convert_fusion
  5.2 0.7 compare_convert_fusion
  5.9 2.3 pad_maximum_fusion.refs_8_
  8.2 3.8 prepare.1
  12.0 196.6 %front.1 = (f32[256,2048]{1,0:T(8,128)}, f32[4,8,256]{2,1,0:T(8,128)}, bf16[1024,48]{1,0:T(8,128)(2,1)}, bf16[1024,16]{1,0:T(8,128)(2,1)}, f32[1024,1280]{1,0:T(...) custom-call(bf16[256,2048]{1,0:T(8,128)(2,1)} %refs_4_.1, ...), custom_call_target="tpu_custom_call" | custom-call | tf_op jit(solution)/shard_map/front/pallas_call | solution.py:1892
  208.6 4.1 router.1
  212.7 0.7 broadcast_in_dim.50
  213.4 258.8 %moe_layer.1 = (f32[256,2048]{1,0:T(8,128)}, f32[4,8,256]{2,1,0:T(8,128)}, bf16[8,4,80,2048]{3,2,1,0:T(8,128)(2,1)}, bf16[4,8,80,2048]{3,2,1,0:T(8,128)(2,1)}, f...) custom-call(bf16[256,2048]{1,0:T(8,128)(2,1)} %get-tuple-element.77., ...), custom_call_target="tpu_custom_call" | custom-call | tf_op jit(solution)/shard_map/moe_layer/pallas_call | solution.py:1373
  472.2 147.1 %back.1 = (bf16[256,2048]{1,0:T(8,128)(2,1)}, f32[256,2048]{1,0:T(8,128)}, bf16[1024,48]{1,0:T(8,128)(2,1)}, bf16[1024,1280]{1,0:T(8,128)(2,1)}, bf16[32,112,128...) custom-call(f32[256,2048]{1,0:T(8,128)} %get-tuple-element.81.moe_total_ref, f32[32,256]{1,0:T(8,128)} %bitcast.91, ...), custom_call_target="tpu_custom_call" | custom-call | tf_op jit(solution)/shard_map/back/pallas_call | solution.py:2328
  619.3 4.5 all-to-all-start
  623.8 87.6 %last.1 = f32[256,2048]{1,0:T(8,128)} custom-call(bf16[1024,1280]{1,0:T(8,128)(2,1)} %get-tuple-element.93.refs_0_, bf16[1024,48]{1,0:T(8,128)(2,1)} %get-tuple-element.94.refs_1_, bf16[48,2048]{1,0:T(8,128)(2,1)} %get-tuple-element.66.refs_5_.refs_2_, f32[256,2048]{1,0:T(8,128)} %get-tuple-element.95.refs_3_, bf16[256,2048]{1,0:T(8,128)(2,1)} %refs_4_.1, ...), custom_call_target="tpu_custom_call" | custom-call | tf_op jit(solution)/shard_map/last/pallas_call | solution.py:2454
  711.4 3.1 fusion.1
  714.5 0.0 all-to-all-done.pieces_ref
  714.5 0.0 copy-start.1
  714.5 0.9 copy-done.1
  715.4 2.9 owners.1
  718.3 0.0 copy-start
  718.3 1.7 copy.54
  719.9 2.3 copy.61
  722.3 0.0 copy-done
  722.3 0.0 copy-start.5
  722.3 0.0 copy-start.4
  722.3 0.0 copy-start.3
  722.3 1.3 copy.62
  723.6 0.0 copy-done.5
  723.6 0.0 copy-start.2
  723.6 0.7 copy.63
  724.3 0.0 copy-done.4
  724.3 0.7 copy.64
  725.1 0.0 copy-done.3
  725.1 0.7 copy.65
  725.8 0.0 copy-done.2
  725.8 1.0 copy.66
  (1 shorter events, 0.0 us)
Async XLA Ops:
  619.3 95.2 %all-to-all-start = ((bf16[32,112,128]{2,1,0:T(8,128)(2,1)}), bf16[32,112,128]{2,1,0:T(8,128)(2,1)S(1)}, u32[]{:S(2)}, u32[]{:S(2)}) async-start(bf16[32,112,128]{2,1,0:T(8,128)(2,1)} %get-tuple-element.96), calls=%async_computation | async-start | bytes 1835008 | tf_op jit(solution)/shard_map/all_to_all | solution.py:66
  714.5 0.9 copy-start.1
  718.3 4.0 copy-start
  722.3 1.3 copy-start.5
  722.3 2.1 copy-start.4
  722.3 2.8 copy-start.3
  723.6 2.2 copy-start.2
